TPU v7x, 512 devices: a whole 4x4x16 slice. The times are simulated.
512 devices in a mesh: dp: 16 (over y_hi, x, core), fsdp: 32 (over y_lo, z).
Axes of the slice: x: 4, y: 4 (y_hi: 2, y_lo: 2; y = y_hi * 2 + y_lo), z: 16, core: 2. Of those that a mesh axis runs over, the one named last changes fastest.
Arguments:
- hidden: bfloat16 [512, 256, 4096], P(('dp', 'fsdp')), may hold values from -40 to 40
- lengths: int32 [512], P(('dp', 'fsdp')), may hold values from 64 to 256
- list_ids: int32 [512], P('dp'), may hold values from 0 to 1023, as said below
- list_owner: int32 [1024], replicated, may hold values from 0 to 15, as said below
- attn_gain: float32 [4096], replicated, may hold values from 0.25 to 1.75
- final_gain: float32 [4096], replicated, may hold values from 0.25 to 1.75
- w_query: bfloat16 [4096, 2048], P('fsdp'), may hold values from -24 to 24
- w_key: bfloat16 [4096, 512], P('fsdp'), may hold values from -1 to 1
- w_value: bfloat16 [4096, 512], P('fsdp'), may hold values from -0.09375 to 0.09375
- w_out: bfloat16 [2048, 4096], P('fsdp'), may hold values from -0.125 to 0.125
Outputs:
- inbox: bfloat16 [16, 16, 4, 4096], P('dp', None, None, 'fsdp')
Inputs may be any that keep to these rules, and one draw needn't show every extreme that they name: Positions from lengths[p] on are padding. `list_ids`: in each aligned block of 32 passages (those of one index of dp), at most 4 passages name lists of one owner, and in every block some owner is named by exactly 4 passages. `list_owner`: every owner holds exactly 64 lists.
All inputs are finite; a program needn't handle non-finite values.
Results may differ from a plain program's by a relative error of at most 0.0029.
The roundings to bfloat16 on the way count: a program that leaves them out, or rounds other values in their place, can miss the bound.
Values may be sent and summed in bfloat16 or wider, within the bound.
No kernel may reach another device: no remote copies, remote signals or barrier semaphores. Data moves between devices by JAX's collectives and lax.ppermute only.
A program may use at most 64 MiB of HBM per device.

v0:
```python
import math

import jax
import jax.numpy as jnp
from jax import lax
from jax.sharding import PartitionSpec as P

HEADS = 16
KV_HEADS = 4
HEAD = 128


def cut_along(shard, dim, count):
    before, after = (shard.shape[:dim], shard.shape[dim + 1 :])
    return jnp.moveaxis(shard.reshape(*before, count, -1, *after), dim, 0)


def sent_and_summed(shard, axis, dim):
    count = lax.axis_size(axis)
    blocks = lax.all_to_all(cut_along(shard, dim, count), axis, 0, 0, tiled=True)
    return jnp.sum(blocks, axis=0)


def in_one_piece(arrays, axis, dim, along):
    widths = [a.shape[along] for a in arrays]
    both = jnp.concatenate(arrays, axis=along)
    whole = lax.all_gather(both, axis, axis=dim, tiled=True)
    return tuple(jnp.split(whole, [sum(widths[:k]) for k in range(1, len(widths))], axis=along))


def rope_tables(positions, head_width):
    halfway = head_width // 2
    frequency = 10000.0 ** (-jnp.arange(halfway, dtype=jnp.float32) * 2.0 / head_width)
    angles = positions.astype(jnp.float32)[..., None] * frequency
    return (jnp.cos(angles), jnp.sin(angles))


def rotate(vectors, cosine_table, sine_table):
    halfway = vectors.shape[-1] // 2
    first_half = vectors[..., :halfway]
    second_half = vectors[..., halfway:]
    return jnp.concatenate(
        [
            first_half * cosine_table - second_half * sine_table,
            second_half * cosine_table + first_half * sine_table,
        ],
        axis=-1,
    )


def project_queries(last_normed, w_query, last_position):
    slices = lax.all_to_all(last_normed, "fsdp", split_axis=1, concat_axis=0, tiled=True)
    summed = sent_and_summed(
        jnp.dot(slices, w_query, preferred_element_type=jnp.float32), "fsdp", 0
    )
    shaped = summed.reshape(last_normed.shape[0], HEADS, HEAD)
    query_cos, query_sin = rope_tables(last_position, HEAD)
    rotated = rotate(shaped, query_cos[:, None, :], query_sin[:, None, :])
    return (rotated * (1.0 / math.sqrt(HEAD))).astype(jnp.bfloat16)


def attend(queries, key_rows, lengths):
    passages = queries.shape[0]
    grouped = queries.reshape(passages, KV_HEADS, HEADS // KV_HEADS, HEAD)
    scores = jnp.einsum("pkgd,ptkd->pkgt", grouped, key_rows, preferred_element_type=jnp.float32)
    visible = jnp.arange(key_rows.shape[1])[None, None, None, :] < lengths[:, None, None, None]
    scores = jnp.where(visible, scores, -jnp.inf)
    powers = jnp.exp(scores - jnp.max(scores, axis=-1, keepdims=True))
    return (powers / jnp.sum(powers, axis=-1, keepdims=True)).astype(jnp.bfloat16)


def weigh_values(weights, value_rows):
    passages = weights.shape[0]
    context = jnp.einsum(
        "pkgt,ptkd->pkgd", weights.astype(jnp.float32), value_rows, precision=lax.Precision.HIGHEST
    )
    return context.reshape(passages, HEADS * HEAD).astype(jnp.bfloat16)


def local(
    hidden, lengths, list_ids, list_owner, attn_gain, final_gain, w_query, w_key, w_value, w_out
):
    passages, seq_len, model_width = hidden.shape
    floats = hidden.astype(jnp.float32)
    normed = (
        floats * lax.rsqrt(jnp.mean(floats * floats, axis=-1, keepdims=True) + 1e-05) * attn_gain
    ).astype(jnp.bfloat16)
    flat_rows = normed.reshape(passages * seq_len, model_width)
    last_position = lengths - 1
    last_normed = jnp.take_along_axis(normed, last_position[:, None, None], axis=1)[:, 0, :]
    last_input = jnp.take_along_axis(hidden, last_position[:, None, None], axis=1)[:, 0, :].astype(
        jnp.float32
    )
    cosine_table, sine_table = rope_tables(jnp.arange(seq_len), HEAD)

    def add_rows(weight_piece):
        return jnp.dot(flat_rows, weight_piece, preferred_element_type=jnp.float32)

    pieces = in_one_piece((w_key, w_value), "fsdp", 0, 1)
    key_sum = add_rows(pieces[0])
    value_sum = add_rows(pieces[1])
    shaped = key_sum.reshape(passages, seq_len, KV_HEADS, HEAD)
    key_rows = rotate(shaped, cosine_table[:, None, :], sine_table[:, None, :]).astype(jnp.bfloat16)
    queries = project_queries(last_normed, w_query, last_position)
    weights = attend(queries, key_rows, lengths)
    context = weigh_values(weights, value_sum.reshape(passages, seq_len, KV_HEADS, HEAD))
    context_part = lax.all_to_all(context, "fsdp", split_axis=1, concat_axis=0, tiled=True)
    mixed_out = sent_and_summed(
        jnp.dot(context_part, w_out, preferred_element_type=jnp.float32), "fsdp", 0
    )
    residual = last_input + mixed_out
    scaled = residual * final_gain
    embedded = (
        scaled * lax.rsqrt(jnp.mean(scaled * scaled, axis=-1, keepdims=True) + 1e-06)
    ).astype(jnp.bfloat16)
    feature_slab = lax.all_to_all(embedded, "fsdp", split_axis=1, concat_axis=0, tiled=True)
    owner_count = lax.axis_size("dp")
    capacity = max(2, 2 * lax.axis_size("fsdp") * passages // owner_count)
    list_index = jnp.arange(list_owner.shape[0])
    owners = jnp.sum(
        jnp.where(list_ids[:, None] == list_index[None, :], list_owner[None, :], 0), axis=1
    )
    owner_marks = (owners[:, None] == jnp.arange(owner_count)[None, :]).astype(jnp.int32)
    slot_rank = jnp.sum((jnp.cumsum(owner_marks, axis=0) - owner_marks) * owner_marks, axis=1)
    select = (
        (owners[None, None, :] == jnp.arange(owner_count)[:, None, None])
        & (slot_rank[None, None, :] == jnp.arange(capacity)[None, :, None])
    ).astype(jnp.bfloat16)
    outgoing = jnp.einsum(
        "osr,rd->osd", select, feature_slab, preferred_element_type=jnp.float32
    ).astype(jnp.bfloat16)
    return lax.all_to_all(outgoing[:, None], "dp", split_axis=0, concat_axis=1, tiled=True)


def solution(mesh):
    in_specs = (
        P(("dp", "fsdp"), None, None),
        P(("dp", "fsdp")),
        P("dp"),
        P(),
        P(),
        P(),
        P("fsdp", None),
        P("fsdp", None),
        P("fsdp", None),
        P("fsdp", None),
    )
    out_specs = P("dp", None, None, "fsdp")
    return jax.shard_map(local, mesh=mesh, in_specs=in_specs, out_specs=out_specs, check_vma=False)
```

profile of v0, /device:TPU:1, one launch (start us, length us, event | category | flops | bytes accessed | tf_op | source)
XLA Modules:
  0.0 289.3 jit_solution(12676240735359500580)
XLA Ops:
  6.5 0.0 copy-start
  6.5 0.0 all-gather.2.cloned.1.call-start
  6.5 1.8 pad_maximum_fusion
  8.4 0.0 all-gather.2.cloned.1.call-update
  9.1 2.1 fusion.1
  11.2 0.0 copy-done.1
  11.2 1.3 fusion.3
  12.5 0.0 copy-start.2
  12.5 1.3 copy-done.2
  13.9 29.0 %all_to_all.67 = bf16[1,32,128]{2,0,1:T(2,128)(2,1)S(1)} all-to-all(bf16[1,32,128]{2,0,1:T(2,128)(2,1)S(1)} %fusion.21), channel_id=1, replica_groups=mesh['dp'=16,'fsdp'=32] {'fsdp'}, dimensions={1} | all-to-all | bytes 16384 | tf_op jit(solution)/shard_map/all_to_all | solution.py:52
  42.9 0.0 copy-done.3
  42.9 0.2 convolution_bitcast_fusion.1
  43.1 1.0 copy.28
  44.1 3.9 %all-to-all-start.1 = ((f32[32,1,2048]{2,1,0:T(1,128)}), f32[32,1,2048]{2,1,0:T(1,128)S(1)}, u32[]{:S(2)}, u32[]{:S(2)}) async-start(f32[32,1,2048]{2,1,0:T(1,128)} %copy.28), calls=%async_computation.1 | async-start | bytes 524288 | tf_op jit(solution)/shard_map/all_to_all | solution.py:20
  48.0 0.5 iota_compare_fusion.4
  48.5 0.3 multiply_cosine_fusion
  48.9 21.9 %all-to-all-done.1 = f32[32,1,2048]{2,1,0:T(1,128)S(1)} async-done(((f32[32,1,2048]{2,1,0:T(1,128)}), f32[32,1,2048]{2,1,0:T(1,128)S(1)}, u32[]{:S(2)}, u32[]{:S(2)}) %all-to-all-start.1) | async-done | bytes 262176 | tf_op jit(solution)/shard_map/all_to_all | solution.py:20
  70.8 0.2 reduce_sum.66
  70.9 0.7 multiply_subtract_fusion
  71.6 82.0 %all-gather.2.cloned.1.call-done = bf16[4096,1024]{1,0:T(8,128)(2,1)} async-done(((bf16[128,1024]{1,0:T(8,128)(2,1)}), bf16[4096,1024]{1,0:T(8,128)(2,1)}) %all-gather.2.cloned.1.call-update) | async-done | bytes 8388624 | tf_op jit(solution)/shard_map/all_gather | solution.py:27
  153.6 5.7 %slice_bitcast_fusion.1 = (bf16[512,4096]{0,1:T(8,128)(2,1)}, bf16[512,4096]{0,1:T(8,128)(2,1)}) fusion(bf16[4096,1024]{1,0:T(8,128)(2,1)} %all-gather.2.cloned.1.call-done), kind=kLoop, calls=%fused_computation.8 | loop fusion | bytes 16777216 | tf_op jit(solution)/shard_map/dot_general | solution.py:97
  159.3 6.4 %copy.31 = bf16[512,4096]{1,0:T(8,128)(2,1)} copy(bf16[512,4096]{0,1:T(8,128)(2,1)} %get-tuple-element.18) | data formatting | bytes 8388608 | tf_op jit(solution)/shard_map/dot_general | solution.py:97
  165.7 4.1 %fusion.4 = f32[256,4,128]{2,0,1:T(8,128)S(1)} fusion(bf16[4,128,4096]{2,1,0:T(8,128)(2,1)} %bitcast.58, bf16[1,256,4096]{2,1,0:T(8,128)(2,1)} %copy-done.2), kind=kOutput, calls=%fused_computation.10 | convolution fusion | flops 1073741824 | bytes 6815744 | tf_op jit(solution)/shard_map/dot_general | solution.py:97
  169.9 6.4 %copy.29 = bf16[512,4096]{1,0:T(8,128)(2,1)} copy(bf16[512,4096]{0,1:T(8,128)(2,1)} %get-tuple-element.17) | data formatting | bytes 8388608 | tf_op jit(solution)/shard_map/dot_general | solution.py:97
  176.3 4.1 %fusion.8 = f32[1,256,4,128]{1,3,2,0:T(8,128)S(1)} fusion(bf16[4,128,4096]{2,1,0:T(8,128)(2,1)} %bitcast.57, bf16[1,256,4096]{2,1,0:T(8,128)(2,1)} %copy-done.2), kind=kOutput, calls=%fused_computation.14 | convolution fusion | flops 1073741824 | bytes 6815744 | tf_op jit(solution)/shard_map/dot_general | solution.py:97
  180.4 0.0 copy-start.4
  180.4 0.1 fusion.17
  180.5 1.1 fusion.54
  181.6 0.3 convolution_convert_fusion.1
  181.9 0.1 convert_element_type.85
  181.9 16.7 %all_to_all.68 = bf16[1,32,64]{2,0,1:T(2,128)(2,1)S(1)} all-to-all(bf16[1,32,64]{2,0,1:T(2,128)(2,1)S(1)} %convert_element_type.85), channel_id=1, replica_groups=mesh['dp'=16,'fsdp'=32] {'fsdp'}, dimensions={1} | all-to-all | bytes 8192 | tf_op jit(solution)/shard_map/all_to_all | solution.py:107
  198.7 0.2 convolution_bitcast_fusion
  198.9 1.3 copy.33
  200.2 3.9 %all-to-all-start.3 = ((f32[32,1,4096]{2,1,0:T(1,128)}), f32[32,1,4096]{2,1,0:T(1,128)S(1)}, u32[]{:S(2)}, u32[]{:S(2)}) async-start(f32[32,1,4096]{2,1,0:T(1,128)} %copy.33), calls=%async_computation.3 | async-start | bytes 1048576 | tf_op jit(solution)/shard_map/all_to_all | solution.py:20
  204.1 0.9 select_reduce_fusion
  205.0 0.1 fusion.22
  205.1 0.1 reduce_window_sum.11
  205.2 0.2 select_reduce_fusion.1
  205.4 20.7 %all-to-all-done.3 = f32[32,1,4096]{2,1,0:T(1,128)S(1)} async-done(((f32[32,1,4096]{2,1,0:T(1,128)}), f32[32,1,4096]{2,1,0:T(1,128)S(1)}, u32[]{:S(2)}, u32[]{:S(2)}) %all-to-all-start.3) | async-done | bytes 524320 | tf_op jit(solution)/shard_map/all_to_all | solution.py:20
  226.1 0.4 reduce_sum.68
  226.5 0.0 copy-done.4
  226.5 0.6 multiply_reduce_fusion
  227.8 0.6 copy.34
  228.4 3.8 %all-to-all-start.4 = ((bf16[1,32,128]{2,0,1:T(2,128)(2,1)}), bf16[1,32,128]{2,0,1:T(2,128)(2,1)S(1)}, u32[]{:S(2)}, u32[]{:S(2)}) async-start(bf16[1,32,128]{2,0,1:T(2,128)(2,1)} %copy.34), calls=%async_computation.4 | async-start | bytes 32768 | tf_op jit(solution)/shard_map/all_to_all | solution.py:116
  232.3 13.1 %all-to-all-done.4 = bf16[1,32,128]{2,0,1:T(2,128)(2,1)S(1)} async-done(((bf16[1,32,128]{2,0,1:T(2,128)(2,1)}), bf16[1,32,128]{2,0,1:T(2,128)(2,1)S(1)}, u32[]{:S(2)}, u32[]{:S(2)}) %all-to-all-start.4) | async-done | bytes 8224 | tf_op jit(solution)/shard_map/all_to_all | solution.py:116
  245.4 0.1 fusion.12
  245.5 36.4 %all_to_all.69 = bf16[16,1,4,128]{3,2,1,0:T(4,128)(2,1)S(1)} all-to-all(bf16[16,1,4,128]{3,2,1,0:T(4,128)(2,1)S(1)} %copy.35), channel_id=1, replica_groups=mesh['dp'=16,'fsdp'=32] {'dp'}, dimensions={0} | all-to-all | bytes 32768 | tf_op jit(solution)/shard_map/all_to_all | solution.py:132
  281.9 0.6 copy.54
  (13 shorter events, 0.2 us)
Async XLA Ops:
  6.5 192.2 %copy-start = (bf16[64,4096]{1,0:T(8,128)(2,1)S(1)}, bf16[64,4096]{1,0:T(8,128)(2,1)}, u32[]{:S(2)}) copy-start(bf16[64,4096]{1,0:T(8,128)(2,1)} %param.21) | copy-start | bytes 1572868
  6.5 4.6 %copy-start.1 = (bf16[1,256,4096]{2,1,0:T(8,128)(2,1)S(1)}, bf16[1,256,4096]{2,1,0:T(8,128)(2,1)}, u32[]{:S(2)}) copy-start(bf16[1,256,4096]{2,1,0:T(8,128)(2,1)} %param.12) | copy-start | bytes 6291460
  6.5 36.4 %copy-start.3 = (bf16[128,2048]{1,0:T(8,128)(2,1)S(1)}, bf16[128,2048]{1,0:T(8,128)(2,1)}, u32[]{:S(2)}) copy-start(bf16[128,2048]{1,0:T(8,128)(2,1)} %param.18) | copy-start | bytes 1572868
  6.5 147.1 %all-gather.2.cloned.1.call-start = ((), (), s32[]{:S(2)}) async-start(), calls=%async_computation.6 | async-start | bytes 8650752 | tf_op jit(solution)/shard_map/all_gather | solution.py:27
  12.5 1.4 copy-start.2
  44.1 26.7 %all-to-all-start.1 = ((f32[32,1,2048]{2,1,0:T(1,128)}), f32[32,1,2048]{2,1,0:T(1,128)S(1)}, u32[]{:S(2)}, u32[]{:S(2)}) async-start(f32[32,1,2048]{2,1,0:T(1,128)} %copy.28), calls=%async_computation.1 | async-start | bytes 524288 | tf_op jit(solution)/shard_map/all_to_all | solution.py:20
  180.4 46.1 %copy-start.4 = (f32[4096]{0:T(1024)S(1)}, f32[4096]{0:T(1024)}, u32[]{:S(2)}) copy-start(f32[4096]{0:T(1024)} %param.17) | copy-start | bytes 49156
  200.2 25.9 %all-to-all-start.3 = ((f32[32,1,4096]{2,1,0:T(1,128)}), f32[32,1,4096]{2,1,0:T(1,128)S(1)}, u32[]{:S(2)}, u32[]{:S(2)}) async-start(f32[32,1,4096]{2,1,0:T(1,128)} %copy.33), calls=%async_computation.3 | async-start | bytes 1048576 | tf_op jit(solution)/shard_map/all_to_all | solution.py:20
  228.4 17.0 %all-to-all-start.4 = ((bf16[1,32,128]{2,0,1:T(2,128)(2,1)}), bf16[1,32,128]{2,0,1:T(2,128)(2,1)S(1)}, u32[]{:S(2)}, u32[]{:S(2)}) async-start(bf16[1,32,128]{2,0,1:T(2,128)(2,1)} %copy.34), calls=%async_computation.4 | async-start | bytes 32768 | tf_op jit(solution)/shard_map/all_to_all | solution.py:116
Sparse Core Ops, SparseCore 0:
  9.4 144.1 all-gather.1
where the time goes:
time: 290 us; the launch traced here: 289 us
  waiting for transfers between devices  138 us (48%)
  blocking collectives  82.1 us (28%)
  local copies, waits for them, and re-layouts  23.5 us (8%)
  between operations  14.9 us (5%)
  starting transfers between devices  11.6 us (4%)
  matrix products  10.1 us (3%)
  other arithmetic  9.33 us (3%)
    all_gather x1, waiting for transfers between devices, in_one_piece(): whole = lax.all_gather(both, axis, axis=dim, tiled=True)  82 us
    all_to_all x2, waiting for transfers between devices, sent_and_summed(): lax.all_to_all(cut_along(shard, dim, count), axis, 0, 0, tiled=True)  42.6 us
    all_to_all x1, blocking collectives, local(): lax.all_to_all(outgoing[:, None], 'dp', split_axis=0, concat_axis=1, tile...  36.4 us
    all_to_all x1, blocking collectives, project_queries(): lax.all_to_all(last_normed, 'fsdp', split_axis=1, concat_axis=0, tiled=True)  29 us
    dot_general x3, local copies, waits for them, and re-layouts, add_rows(): return jnp.dot(flat_rows, weight_piece, preferred_element_type=jnp.float32)  18.5 us
    all_to_all x1, blocking collectives, local(): lax.all_to_all(context, 'fsdp', split_axis=1, concat_axis=0, tiled=True)  16.7 us
    all_to_all x1, waiting for transfers between devices, local(): lax.all_to_all(embedded, 'fsdp', split_axis=1, concat_axis=0, tiled=True)  13.1 us
    dot_general x2, matrix products, add_rows(): return jnp.dot(flat_rows, weight_piece, preferred_element_type=jnp.float32)  8.21 us
  transfers between devices with their start and end apart: 4, of which 4 were waited for; matrix products, arithmetic and copies ran while one was open for 3% of the time, Pallas kernels for 0%

commit v1 on v0

v1 whole, which is shorter than its diff:
```python
import math

import jax
import jax.numpy as jnp
from jax import lax
from jax.experimental import pallas as pl
from jax.experimental.pallas import tpu as pltpu
from jax.sharding import PartitionSpec as P

HEADS = 16
KV_HEADS = 4
HEAD = 128
X = 4
Y_LO = 2
Z = 16
BOTH = ("dp", "fsdp")

bf16 = jnp.bfloat16
f32 = jnp.float32


def dp_index(y_hi, x, core):
    return (y_hi * X + x) * 2 + core


def fsdp_index(y_lo, z):
    return y_lo * Z + z


Z_GROUPS = [[fsdp_index(yl, z) for z in range(Z)] for yl in range(Y_LO)]
CORE_SWAP = [(d, d ^ 1) for d in range(16)]
Y_LO_SWAP = [(i, i ^ Z) for i in range(32)]


def x_shift(step):
    return [
        (dp_index(yh, x, c), dp_index(yh, (x + step) % X, c))
        for yh in range(2)
        for x in range(X)
        for c in range(2)
    ]


def y_shift(step):
    pairs = []
    for y in range(4):
        to = (y + step) % 4
        for x in range(X):
            for z in range(Z):
                for c in range(2):
                    pairs.append(
                        (
                            dp_index(y // 2, x, c) * 32 + fsdp_index(y % 2, z),
                            dp_index(to // 2, x, c) * 32 + fsdp_index(to % 2, z),
                        )
                    )
    return pairs


def rope_tables(positions, head_width):
    halfway = head_width // 2
    frequency = 10000.0 ** (-jnp.arange(halfway, dtype=f32) * 2.0 / head_width)
    angles = positions.astype(f32)[..., None] * frequency
    cosine, sine = jnp.cos(angles), jnp.sin(angles)
    return (
        jnp.concatenate([cosine, cosine], axis=-1),
        jnp.concatenate([-sine, sine], axis=-1),
    )


def plane_gather(piece, x):
    plus = lax.ppermute(piece, "dp", x_shift(1))
    minus = lax.ppermute(piece, "dp", x_shift(-1))
    far = lax.ppermute(piece, "dp", x_shift(2))
    received = jnp.stack([piece, plus, far, minus])
    own = jnp.take(received, (x - jnp.arange(X)) % X, axis=0)
    low = lax.ppermute(own[:2], BOTH, y_shift(-1))
    high = lax.ppermute(own[2:], BOTH, y_shift(1))
    return own, low, high


def fill(scratch, own, low, high, y_lo, sem):
    copies = []
    for x in range(X):
        copies.append(
            pltpu.make_async_copy(own.at[x], scratch.at[y_lo, :, x], sem.at[x])
        )
        half = low if x < 2 else high
        copies.append(
            pltpu.make_async_copy(half.at[x % 2], scratch.at[1 - y_lo, :, x], sem.at[X + x])
        )
    for copy in copies:
        copy.start()
    for copy in copies:
        copy.wait()


def attend_body(
    y_lo_ref, len_ref, normed_ref, other_ref, q_ref, cos_ref, sin_ref, own, low, high, u_ref, w_ref, sem
):
    y_lo = y_lo_ref[0]
    fill(w_ref, own, low, high, y_lo, sem)
    weight = w_ref[...].reshape(Y_LO * Z * X * 32, 256)
    cosine, sine = cos_ref[...], sin_ref[...]
    for p, rows_ref in enumerate((normed_ref, other_ref)):
        rows = rows_ref[...]
        keys = jnp.dot(rows, weight, preferred_element_type=f32)
        scores = []
        for g in range(2):
            part = keys[:, g * HEAD : (g + 1) * HEAD]
            turned = (part * cosine + pltpu.roll(part, HEAD // 2, 1) * sine).astype(bf16)
            scores.append(
                lax.dot_general(
                    q_ref[p, g], turned, (((1,), (1,)), ((), ())), preferred_element_type=f32
                )[:4]
            )
        scores = jnp.concatenate(scores, axis=0)
        place = lax.broadcasted_iota(jnp.int32, scores.shape, 1)
        scores = jnp.where(place < len_ref[p], scores, -jnp.inf)
        powers = jnp.exp(scores - jnp.max(scores, axis=-1, keepdims=True))
        weights = (powers / jnp.sum(powers, axis=-1, keepdims=True)).astype(bf16)
        u_ref[p] = jnp.dot(weights, rows, preferred_element_type=f32)


def attend(y_lo, lengths, normed, other, q, cosine, sine, pieces):
    vmem = pl.BlockSpec(memory_space=pltpu.VMEM)
    smem = pl.BlockSpec(memory_space=pltpu.SMEM)
    anywhere = pl.BlockSpec(memory_space=pl.ANY)
    return pl.pallas_call(
        attend_body,
        out_shape=jax.ShapeDtypeStruct((2, 8, normed.shape[1]), f32),
        in_specs=[smem, smem, vmem, vmem, vmem, vmem, vmem, anywhere, anywhere, anywhere],
        out_specs=vmem,
        scratch_shapes=[
            pltpu.VMEM((Y_LO, Z, X, 32, 256), bf16),
            pltpu.SemaphoreType.DMA((2 * X,)),
        ],
        compiler_params=pltpu.CompilerParams(vmem_limit_bytes=40 << 20),
        name="attend",
    )(y_lo, lengths, normed, other, q, cosine, sine, *pieces)


def weigh_body(y_lo_ref, u_ref, own, low, high, out_ref, w_ref, sem):
    fill(w_ref, own, low, high, y_lo_ref[0], sem)
    weight = w_ref[...].reshape(Y_LO * Z * X * 32, 256)
    u = u_ref[...].reshape(16, -1)
    first = u.astype(bf16)
    rest = u - first.astype(f32)
    second = rest.astype(bf16)
    third = (rest - second.astype(f32)).astype(bf16)
    parts = [jnp.dot(t, weight, preferred_element_type=f32) for t in (third, second, first)]
    total = parts[0] + parts[1] + parts[2]
    kind = (lax.broadcasted_iota(jnp.int32, (16, HEAD), 0) // 4) % 2
    out_ref[...] = jnp.where(kind == 0, total[:, :HEAD], total[:, HEAD:]).astype(bf16)


def weigh(y_lo, u, pieces):
    vmem = pl.BlockSpec(memory_space=pltpu.VMEM)
    smem = pl.BlockSpec(memory_space=pltpu.SMEM)
    anywhere = pl.BlockSpec(memory_space=pl.ANY)
    return pl.pallas_call(
        weigh_body,
        out_shape=jax.ShapeDtypeStruct((16, HEAD), bf16),
        in_specs=[smem, vmem, anywhere, anywhere, anywhere],
        out_specs=vmem,
        scratch_shapes=[
            pltpu.VMEM((Y_LO, Z, X, 32, 256), bf16),
            pltpu.SemaphoreType.DMA((2 * X,)),
        ],
        compiler_params=pltpu.CompilerParams(vmem_limit_bytes=40 << 20),
        name="weigh",
    )(y_lo, u, *pieces)


def local(
    hidden, lengths, list_ids, list_owner, attn_gain, final_gain, w_query, w_key, w_value, w_out
):
    _, seq_len, width = hidden.shape
    dp, fsdp = lax.axis_index("dp"), lax.axis_index("fsdp")
    core, x = dp % 2, (dp // 2) % X
    y_lo = fsdp // Z
    last = lengths[0] - 1

    w_query_other = lax.ppermute(w_query, "fsdp", Y_LO_SWAP)
    last_input = lax.dynamic_slice(hidden, (0, last, 0), (1, 1, width))[0]

    def norm(rows):
        floats = rows.astype(f32)
        return (
            floats * lax.rsqrt(jnp.mean(floats * floats, axis=-1, keepdims=True) + 1e-05) * attn_gain
        ).astype(bf16)

    last_normed = norm(last_input)
    halves = last_normed.reshape(Y_LO, Z, HEAD)
    halves = jnp.where(y_lo == 0, halves, halves[::-1])
    features = jnp.transpose(halves, (1, 0, 2)).reshape(Z, 1, 2 * HEAD)

    units = jnp.concatenate(
        [lax.dynamic_slice(w, (x * 32, core * 256), (32, 256)) for w in (w_key, w_value)], axis=0
    )
    outgoing = jnp.concatenate(
        [
            jnp.broadcast_to(units, (Z, 64, 256)),
            jnp.broadcast_to(features, (Z, 16, 256)),
        ],
        axis=1,
    )
    arrived = lax.all_to_all(outgoing, "fsdp", 0, 0, tiled=True, axis_index_groups=Z_GROUPS)
    key_piece, value_piece, rows = arrived[:, :32], arrived[:, 32:64], arrived[:, 64]

    query_parts = jnp.dot(rows[:, :HEAD], w_query, preferred_element_type=f32) + jnp.dot(
        rows[:, HEAD:], w_query_other, preferred_element_type=f32
    )
    query_sum = jnp.sum(
        lax.all_to_all(
            query_parts.reshape(Z, HEADS, HEAD), "fsdp", 0, 0, tiled=True, axis_index_groups=Z_GROUPS
        ),
        axis=0,
    )
    query_cos, query_sin = rope_tables(last[None], HEAD)
    turned = query_sum * query_cos + jnp.roll(query_sum, HEAD // 2, axis=1) * query_sin
    queries = (turned * (1.0 / math.sqrt(HEAD))).astype(bf16).reshape(2, 8, HEAD)
    mine = lax.dynamic_index_in_dim(queries, core, 0, keepdims=False)
    give = jnp.concatenate(
        [
            lax.dynamic_index_in_dim(queries, 1 - core, 0, keepdims=False),
            jnp.broadcast_to(lengths.astype(bf16)[:, None], (8, HEAD)),
        ],
        axis=0,
    )
    got = lax.ppermute(give, "dp", CORE_SWAP)
    both_queries = jnp.stack([mine, got[:8]]).reshape(2, 2, 4, HEAD)
    both_queries = jnp.concatenate([both_queries, both_queries], axis=2)
    both_lengths = jnp.concatenate([lengths, got[8, :1].astype(jnp.int32)])

    normed = norm(hidden[0])
    other = lax.ppermute(normed, "dp", CORE_SWAP)
    key_pieces = plane_gather(key_piece, x)
    value_pieces = plane_gather(value_piece, x)
    cosine, sine = rope_tables(jnp.arange(seq_len), HEAD)
    y_lo_one = y_lo[None].astype(jnp.int32)
    u = attend(y_lo_one, both_lengths, normed, other, both_queries, cosine, sine, key_pieces)
    context = weigh(y_lo_one, u, value_pieces)
    swapped = lax.ppermute(context[8:], "dp", CORE_SWAP)
    halves = (context[:8], swapped)
    context = jnp.where(
        core == 0, jnp.concatenate(halves, axis=0), jnp.concatenate(halves[::-1], axis=0)
    ).reshape(1, HEADS * HEAD)

    slabs = width // HEAD
    columns = jnp.transpose(w_out.reshape(-1, slabs, HEAD), (1, 0, 2))
    columns = jnp.concatenate(
        [columns, jnp.broadcast_to(last_input.reshape(slabs, 1, HEAD), (slabs, 16, HEAD))], axis=1
    )
    columns = lax.all_to_all(columns, "fsdp", 0, 0, tiled=True)
    out_weight = columns[:, :-16].reshape(HEADS * HEAD, HEAD)
    slab_input = columns[:, -16].astype(f32)

    contexts = lax.all_to_all(
        jnp.broadcast_to(context.reshape(1, HEADS, HEAD), (slabs, HEADS, HEAD)), "fsdp", 0, 0, tiled=True
    ).reshape(slabs, HEADS * HEAD)
    residual = slab_input + jnp.dot(contexts, out_weight, preferred_element_type=f32)
    gain = lax.dynamic_slice(final_gain, (fsdp * HEAD,), (HEAD,))
    scaled = residual * gain
    partial = jnp.sum(scaled * scaled, axis=-1)
    squares = lax.all_to_all(
        jnp.broadcast_to(partial[None, None, :], (slabs, 1, slabs)), "fsdp", 0, 0, tiled=True
    )
    mean = jnp.sum(squares, axis=0)[0] / width
    slab = (scaled * lax.rsqrt(mean + 1e-06)[:, None]).astype(bf16)

    owner_count = lax.axis_size("dp")
    capacity = 4
    list_index = jnp.arange(list_owner.shape[0])
    owners = jnp.sum(
        jnp.where(list_ids[:, None] == list_index[None, :], list_owner[None, :], 0), axis=1
    )
    owner_marks = (owners[:, None] == jnp.arange(owner_count)[None, :]).astype(jnp.int32)
    slot_rank = jnp.sum((jnp.cumsum(owner_marks, axis=0) - owner_marks) * owner_marks, axis=1)
    select = (
        (owners[None, None, :] == jnp.arange(owner_count)[:, None, None])
        & (slot_rank[None, None, :] == jnp.arange(capacity)[None, :, None])
    ).astype(bf16)
    outgoing = jnp.einsum("osr,rd->osd", select, slab, preferred_element_type=f32).astype(bf16)
    return lax.all_to_all(outgoing[:, None], "dp", split_axis=0, concat_axis=1, tiled=True)


def solution(mesh):
    in_specs = (
        P(("dp", "fsdp"), None, None),
        P(("dp", "fsdp")),
        P("dp"),
        P(),
        P(),
        P(),
        P("fsdp", None),
        P("fsdp", None),
        P("fsdp", None),
        P("fsdp", None),
    )
    out_specs = P("dp", None, None, "fsdp")
    return jax.shard_map(local, mesh=mesh, in_specs=in_specs, out_specs=out_specs, check_vma=False)
```

time: 290 us -> 215 us (0.74)
  starting transfers between devices: 11.6 us -> 104 us
  waiting for transfers between devices: 138 us -> 54.9 us
  blocking collectives: 82.1 us -> 15.9 us
  between operations: 14.9 us -> 2.46 us
  local copies, waits for them, and re-layouts: 23.5 us -> 12.3 us
  Pallas kernels: 0 us -> 8 us
  matrix products: 10.1 us -> 2.96 us
  other arithmetic: 9.33 us -> 13.5 us
    all_gather x1 -> x0, waiting for transfers between devices: 82 us -> none  [in_one_piece(): whole = lax.all_gather(both, axis, axis=dim, tiled=True)]
    all_to_all x3 -> x5, starting transfers between devices: 11.6 us -> 58.3 us  [the longest x1 15.7 us: local(): lax.all_to_all(outgoing, 'fsdp', 0, 0, tiled=True, axis_index_groups=Z_GR...]
    all_to_all x2 -> x0, blocking collectives: 45.7 us -> none  [the longest x1 29 us: project_queries(): lax.all_to_all(last_normed, 'fsdp', split_axis=1, concat_axis=0, tiled=True)]
    ppermute x0 -> x14, starting transfers between devices: none -> 45.3 us  [the longest x2 9.36 us: plane_gather(): low = lax.ppermute(own[:2], BOTH, y_shift(-1))]
    all_to_all x1, blocking collectives: 36.4 us -> 15.9 us  [local(): lax.all_to_all(outgoing[:, None], 'dp', split_axis=0, concat_axis=1, tile...]
    dot_general x3 -> x0, local copies, waits for them, and re-layouts: 18.5 us -> none  [add_rows(): return jnp.dot(flat_rows, weight_piece, preferred_element_type=jnp.float32)]
    all_to_all x3 -> x5, waiting for transfers between devices: 55.7 us -> 46.2 us  [the longest x1 22 us: local(): lax.all_to_all(outgoing, 'fsdp', 0, 0, tiled=True, axis_index_groups=Z_GR...]
    ppermute x0 -> x14, waiting for transfers between devices: none -> 8.72 us  [the longest x2 5.96 us: plane_gather(): low = lax.ppermute(own[:2], BOTH, y_shift(-1))]
  transfers between devices with their start and end apart: 4 -> 19, of which waited for: 4 -> 8; matrix products, arithmetic and copies ran while one was open for 3% -> 10% of each run, Pallas kernels for 0% -> 4%
where the time goes in v1:
time: 215 us; the launch traced here: 214 us
  starting transfers between devices  104 us (48%)
  waiting for transfers between devices  54.9 us (26%)
  blocking collectives  15.9 us (7%)
  other arithmetic  13.5 us (6%)
  local copies, waits for them, and re-layouts  12.3 us (6%)
  Pallas kernels  8 us (4%)
  matrix products  2.96 us (1%)
  between operations  2.46 us (1%)
    all_to_all x1, waiting for transfers between devices, local(): lax.all_to_all(outgoing, 'fsdp', 0, 0, tiled=True, axis_index_groups=Z_GR...  22 us
    all_to_all x1, blocking collectives, local(): lax.all_to_all(outgoing[:, None], 'dp', split_axis=0, concat_axis=1, tile...  15.9 us
    all_to_all x1, starting transfers between devices, local(): lax.all_to_all(outgoing, 'fsdp', 0, 0, tiled=True, axis_index_groups=Z_GR...  15.7 us
    all_to_all x1, starting transfers between devices, local(): columns = lax.all_to_all(columns, 'fsdp', 0, 0, tiled=True)  13.2 us
    all_to_all x1, starting transfers between devices, local(): lax.all_to_all(jnp.broadcast_to(context.reshape(1, HEADS, HEAD), (slabs,...  12.6 us
    all_to_all x1, starting transfers between devices, local(): lax.all_to_all(query_parts.reshape(Z, HEADS, HEAD), 'fsdp', 0, 0, tiled=T...  12.4 us
    all_to_all x1, waiting for transfers between devices, local(): lax.all_to_all(jnp.broadcast_to(partial[None, None, :], (slabs, 1, slabs)...  12.1 us
    all_to_all x1, waiting for transfers between devices, local(): lax.all_to_all(jnp.broadcast_to(context.reshape(1, HEADS, HEAD), (slabs,...  12.1 us
  transfers between devices with their start and end apart: 19, of which 8 were waited for; matrix products, arithmetic and copies ran while one was open for 10% of the time, Pallas kernels for 4%

profile of v1, /device:TPU:1, one launch (start us, length us, event | category | flops | bytes accessed | tf_op | source)
XLA Modules:
  0.0 213.6 jit_solution(11634868680535110226)
XLA Ops:
  0.0 0.8 dynamic_slice.20
  0.8 0.7 dynamic_slice.21
  2.2 1.5 multiply_reduce_fusion.1
  4.2 0.9 convert_multiply_fusion.2
  5.1 0.7 multiply_convert_fusion.1
  5.9 0.9 pad_maximum_fusion.3
  6.8 15.7 %all-to-all-start.1 = ((bf16[16,80,256]{2,1,0:T(8,128)(2,1)}), bf16[16,80,256]{2,1,0:T(8,128)(2,1)S(1)}, u32[]{:S(2)}, u32[]{:S(2)}) async-start(bf16[16,80,256]{2,1,0:T(8,128)(2,1)} %pad_maximum_fusion.3), calls=%async_computation.1 | async-start | bytes 1310720 | tf_op jit(solution)/shard_map/all_to_all | solution.py:208
  22.5 3.2 %collective-permute-start = (bf16[128,2048]{1,0:T(8,128)(2,1)}, bf16[128,2048]{1,0:T(8,128)(2,1)}, u32[]{:S(2)}, u32[]{:S(2)}) collective-permute-start(bf16[128,2048]{1,0:T(8,128)(2,1)} %param.18), channel_id=1, source_target_pairs={{0,16},{1,17},{2,18},{3,19},{4,20},{5,21},{6,22},{7,23},{8,24},{9,... | collective-permute-start | bytes 1572872 | tf_op jit(solution)/shard_map/ppermute | solution.py:184
  27.2 2.0 fusion.2.normed_ref
  29.2 22.0 %all-to-all-done.1 = bf16[16,80,256]{2,1,0:T(8,128)(2,1)S(1)} async-done(((bf16[16,80,256]{2,1,0:T(8,128)(2,1)}), bf16[16,80,256]{2,1,0:T(8,128)(2,1)S(1)}, u32[]{:S(2)}, u32[]{:S(2)}) %all-to-all-start.1) | async-done | bytes 655392 | tf_op jit(solution)/shard_map/all_to_all | solution.py:208
  51.4 3.1 %collective-permute-start.3 = (bf16[16,32,256]{2,1,0:T(8,128)(2,1)S(1)}, bf16[16,32,256]{2,1,0:T(8,128)(2,1)S(1)}, u32[]{:S(2)}, u32[]{:S(2)}) collective-permute-start(bf16[16,32,256]{2,1,0:T(8,128)(2,1)S(1)} %get-tuple-element.13), channel_id=1, source_target_pairs={{0,64},{32,96},{64,128},{96,160},{128,192},{160,224},{192,0},{224,... | collective-permute-start | bytes 786440 | tf_op jit(solution)/shard_map/ppermute | solution.py:72
  54.5 1.2 fusion.21
  55.8 1.2 fusion.3
  57.7 12.4 %all-to-all-start.2 = ((f32[16,16,128]{2,1,0:T(8,128)}), f32[16,16,128]{2,1,0:T(8,128)S(1)}, u32[]{:S(2)}, u32[]{:S(2)}) async-start(f32[16,16,128]{2,1,0:T(8,128)} %bitcast.42), calls=%async_computation.2 | async-start | bytes 262144 | tf_op jit(solution)/shard_map/all_to_all | solution.py:215
  70.1 4.4 %collective-permute-start.4 = (bf16[16,32,256]{2,1,0:T(8,128)(2,1)S(1)}, bf16[16,32,256]{2,1,0:T(8,128)(2,1)S(1)}, u32[]{:S(2)}, u32[]{:S(2)}) collective-permute-start(bf16[16,32,256]{2,1,0:T(8,128)(2,1)S(1)} %get-tuple-element.13), channel_id=1, source_target_pairs={{0,128},{32,160},{64,192},{96,224},{128,0},{160,32},{192,64},{224,... | collective-permute-start | bytes 786440 | tf_op jit(solution)/shard_map/ppermute | solution.py:74
  74.4 3.1 %collective-permute-start.5 = (bf16[16,32,256]{2,1,0:T(8,128)(2,1)S(1)}, bf16[16,32,256]{2,1,0:T(8,128)(2,1)}, u32[]{:S(2)}, u32[]{:S(2)}) collective-permute-start(bf16[16,32,256]{2,1,0:T(8,128)(2,1)S(1)} %get-tuple-element.13), channel_id=1, source_target_pairs={{0,192},{32,224},{64,0},{96,32},{128,64},{160,96},{192,128},{224,1... | collective-permute-start | bytes 786440 | tf_op jit(solution)/shard_map/ppermute | solution.py:73
  78.1 2.2 %collective-permute-start.8 = (bf16[16,32,256]{2,1,0:T(8,128)(2,1)S(1)}, bf16[16,32,256]{2,1,0:T(8,128)(2,1)S(1)}, u32[]{:S(2)}, u32[]{:S(2)}) collective-permute-start(bf16[16,32,256]{2,1,0:T(8,128)(2,1)S(1)} %get-tuple-element.12), channel_id=1, source_target_pairs={{0,64},{32,96},{64,128},{96,160},{128,192},{160,224},{192,0},{224,... | collective-permute-start | bytes 786440 | tf_op jit(solution)/shard_map/ppermute | solution.py:72
  80.3 2.8 %collective-permute-start.9 = (bf16[16,32,256]{2,1,0:T(8,128)(2,1)S(1)}, bf16[16,32,256]{2,1,0:T(8,128)(2,1)S(1)}, u32[]{:S(2)}, u32[]{:S(2)}) collective-permute-start(bf16[16,32,256]{2,1,0:T(8,128)(2,1)S(1)} %get-tuple-element.12), channel_id=1, source_target_pairs={{0,128},{32,160},{64,192},{96,224},{128,0},{160,32},{192,64},{224,... | collective-permute-start | bytes 786440 | tf_op jit(solution)/shard_map/ppermute | solution.py:74
  83.2 3.4 %collective-permute-start.10 = (bf16[16,32,256]{2,1,0:T(8,128)(2,1)S(1)}, bf16[16,32,256]{2,1,0:T(8,128)(2,1)}, u32[]{:S(2)}, u32[]{:S(2)}) collective-permute-start(bf16[16,32,256]{2,1,0:T(8,128)(2,1)S(1)} %get-tuple-element.12), channel_id=1, source_target_pairs={{0,192},{32,224},{64,0},{96,32},{128,64},{160,96},{192,128},{224,1... | collective-permute-start | bytes 786440 | tf_op jit(solution)/shard_map/ppermute | solution.py:73
  87.2 1.1 copy.28
  88.3 4.2 %collective-permute-start.2 = (bf16[256,4096]{1,0:T(8,128)(2,1)}, bf16[256,4096]{1,0:T(8,128)(2,1)}, u32[]{:S(2)}, u32[]{:S(2)}) collective-permute-start(bf16[256,4096]{1,0:T(8,128)(2,1)} %fusion.2.normed_ref), channel_id=1, source_target_pairs={{0,32},{32,0},{64,96},{96,64},{128,160},{160,128},{192,224},{224,1... | collective-permute-start | bytes 6291464 | tf_op jit(solution)/shard_map/ppermute | solution.py:237
  92.5 1.2 pad_maximum_fusion
  94.3 13.2 %all-to-all-start = ((bf16[32,80,128]{2,1,0:T(8,128)(2,1)}), bf16[32,80,128]{2,1,0:T(8,128)(2,1)}, u32[]{:S(2)}, u32[]{:S(2)}) async-start(bf16[32,80,128]{2,1,0:T(8,128)(2,1)} %copy.28), calls=%async_computation | async-start | bytes 1310720 | tf_op jit(solution)/shard_map/all_to_all | solution.py:255
  107.5 1.1 pad_maximum_fusion.1
  108.6 1.6 gather_fusion.1
  110.2 1.5 broadcast_select_fusion
  111.7 1.0 fusion.29
  112.7 4.5 %collective-permute-start.6 = (bf16[2,16,32,256]{3,2,1,0:T(8,128)(2,1)}, bf16[2,16,32,256]{3,2,1,0:T(8,128)(2,1)S(1)}, u32[]{:S(2)}, u32[]{:S(2)}) collective-permute-start(bf16[2,16,32,256]{3,2,1,0:T(8,128)(2,1)} %get-tuple-element.9), channel_id=1, source_target_pairs={{0,272},{32,304},{1,273},{33,305},{2,274},{34,306},{3,275},{35,307... | collective-permute-start | bytes 1572872 | tf_op jit(solution)/shard_map/ppermute | solution.py:77
  117.3 1.9 collective-permute-start.7
  119.4 2.8 %collective-permute-start.1 = (bf16[16,128]{1,0:T(8,128)(2,1)S(1)}, bf16[16,128]{1,0:T(8,128)(2,1)S(1)}, u32[]{:S(2)}, u32[]{:S(2)}) collective-permute-start(bf16[16,128]{1,0:T(8,128)(2,1)S(1)} %concatenate.62), channel_id=1, source_target_pairs={{0,32},{32,0},{64,96},{96,64},{128,160},{160,128},{192,224},{224,1... | collective-permute-start | bytes 12296 | tf_op jit(solution)/shard_map/ppermute | solution.py:231
  122.2 4.9 %collective-permute-start.11 = (bf16[2,16,32,256]{3,2,1,0:T(8,128)(2,1)S(1)}, bf16[2,16,32,256]{3,2,1,0:T(8,128)(2,1)S(1)}, u32[]{:S(2)}, u32[]{:S(2)}) collective-permute-start(bf16[2,16,32,256]{3,2,1,0:T(8,128)(2,1)S(1)} %get-tuple-element.7), channel_id=1, source_target_pairs={{0,272},{32,304},{1,273},{33,305},{2,274},{34,306},{3,275},{35,307... | collective-permute-start | bytes 1572872 | tf_op jit(solution)/shard_map/ppermute | solution.py:77
  127.1 1.9 collective-permute-start.12
  131.0 1.3 collective-permute-done.6.low
  132.3 1.3 collective-permute-done.7.high
  133.6 6.8 %attend.1.u_ref = f32[2,8,4096]{2,1,0:T(8,128)S(1)} custom-call(s32[1]{0:T(128)} %bitcast.4.y_lo_ref, s32[2]{0:T(128)S(1)} %pad_add_fusion.len_ref, bf16[256,4096]{1,0:T(8,128)(2,1)} %fusion.2.normed_ref, bf16[256,4096]{1,0:T(8,128)(2,1)} %collective-permute-done.2.other_ref, bf16[2,2,8,128]{3,2,1,0:T(8,128)(2,1)S(1)} %maximum_maximum_fusion.q_ref, ...), custom_call_target="tpu_custom_call" | custom-call | tf_op jit(solution)/shard_map/attend/pallas_call | solution.py:129
  140.4 4.7 %collective-permute-done.11.low = bf16[2,16,32,256]{3,2,1,0:T(8,128)(2,1)S(1)} collective-permute-done((bf16[2,16,32,256]{3,2,1,0:T(8,128)(2,1)S(1)}, bf16[2,16,32,256]{3,2,1,0:T(8,128)(2,1)S(1)}, u32[]{:S(2)}, u32[]{:S(2)}) %collective-permute-start.11) | collective-permute-done | bytes 524320 | tf_op jit(solution)/shard_map/ppermute | solution.py:77
  145.1 0.9 collective-permute-done.12.high
  146.0 1.2 weigh.1
  147.2 3.0 %collective-permute-start.13 = (bf16[8,128]{1,0:T(8,128)(2,1)S(1)}, bf16[8,128]{1,0:T(8,128)(2,1)S(1)}, u32[]{:S(2)}, u32[]{:S(2)}) collective-permute-start(bf16[8,128]{1,0:T(8,128)(2,1)S(1)} %get-tuple-element.17), channel_id=1, source_target_pairs={{0,32},{32,0},{64,96},{96,64},{128,160},{160,128},{192,224},{224,1... | collective-permute-start | bytes 6152 | tf_op jit(solution)/shard_map/ppermute | solution.py:244
  151.0 0.7 broadcast_in_dim.50
  151.7 12.6 %all-to-all-start.3 = ((bf16[32,16,128]{2,1,0:T(8,128)(2,1)}), bf16[32,16,128]{2,1,0:T(8,128)(2,1)S(1)}, u32[]{:S(2)}, u32[]{:S(2)}) async-start(bf16[32,16,128]{2,1,0:T(8,128)(2,1)} %broadcast_in_dim.50), calls=%async_computation.3 | async-start | bytes 262144 | tf_op jit(solution)/shard_map/all_to_all | solution.py:259
  164.4 0.8 dynamic_slice.24
  165.4 1.1 slice.90
  166.4 0.9 slice.74
  167.3 12.1 %all-to-all-done.3 = bf16[32,16,128]{2,1,0:T(8,128)(2,1)S(1)} async-done(((bf16[32,16,128]{2,1,0:T(8,128)(2,1)}), bf16[32,16,128]{2,1,0:T(8,128)(2,1)S(1)}, u32[]{:S(2)}, u32[]{:S(2)}) %all-to-all-start.3) | async-done | bytes 131104 | tf_op jit(solution)/shard_map/all_to_all | solution.py:259
  180.3 4.4 %all-to-all-start.4 = ((f32[32,1,32]{2,1,0:T(1,128)}), f32[32,1,32]{2,1,0:T(1,128)S(1)}, u32[]{:S(2)}, u32[]{:S(2)}) async-start(f32[32,1,32]{2,1,0:T(1,128)} %broadcast_in_dim.51), calls=%async_computation.4 | async-start | bytes 32768 | tf_op jit(solution)/shard_map/all_to_all | solution.py:266
  184.7 12.1 %all-to-all-done.4 = f32[32,1,32]{2,1,0:T(1,128)S(1)} async-done(((f32[32,1,32]{2,1,0:T(1,128)}), f32[32,1,32]{2,1,0:T(1,128)S(1)}, u32[]{:S(2)}, u32[]{:S(2)}) %all-to-all-start.4) | async-done | bytes 4128 | tf_op jit(solution)/shard_map/all_to_all | solution.py:266
  197.0 15.9 %all_to_all.37 = bf16[16,1,4,128]{3,2,1,0:T(4,128)(2,1)S(1)} all-to-all(bf16[16,1,4,128]{3,2,1,0:T(4,128)(2,1)S(1)} %copy.32), channel_id=1, replica_groups=mesh['dp'=16,'fsdp'=32] {'dp'}, dimensions={0} | all-to-all | bytes 32768 | tf_op jit(solution)/shard_map/all_to_all | solution.py:285
  (81 shorter events, 8.6 us)
Async XLA Ops:
  0.0 25.7 %copy-start.1 = (bf16[64,4096]{1,0:T(8,128)(2,1)S(1)}, bf16[64,4096]{1,0:T(8,128)(2,1)}, u32[]{:S(2)}) copy-start(bf16[64,4096]{1,0:T(8,128)(2,1)} %param.21) | copy-start | bytes 1572868
  5.8 20.0 %copy-start = (bf16[1,256,4096]{2,1,0:T(8,128)(2,1)S(1)}, bf16[1,256,4096]{2,1,0:T(8,128)(2,1)}, u32[]{:S(2)}) copy-start(bf16[1,256,4096]{2,1,0:T(8,128)(2,1)} %param.12) | copy-start | bytes 6291460
  6.8 44.5 %all-to-all-start.1 = ((bf16[16,80,256]{2,1,0:T(8,128)(2,1)}), bf16[16,80,256]{2,1,0:T(8,128)(2,1)S(1)}, u32[]{:S(2)}, u32[]{:S(2)}) async-start(bf16[16,80,256]{2,1,0:T(8,128)(2,1)} %pad_maximum_fusion.3), calls=%async_computation.1 | async-start | bytes 1310720 | tf_op jit(solution)/shard_map/all_to_all | solution.py:208
  22.5 33.2 %collective-permute-start = (bf16[128,2048]{1,0:T(8,128)(2,1)}, bf16[128,2048]{1,0:T(8,128)(2,1)}, u32[]{:S(2)}, u32[]{:S(2)}) collective-permute-start(bf16[128,2048]{1,0:T(8,128)(2,1)} %param.18), channel_id=1, source_target_pairs={{0,16},{1,17},{2,18},{3,19},{4,20},{5,21},{6,22},{7,23},{8,24},{9,... | collective-permute-start | bytes 1572872 | tf_op jit(solution)/shard_map/ppermute | solution.py:184
  25.8 1.4 copy-start.3
  29.2 59.1 %copy-start.6 = (s32[4]{0:T(128)S(1)}, s32[4]{0:T(128)}, u32[]{:S(2)}) copy-start(s32[4]{0:T(128)} %compare_select_fusion) | copy-start | bytes 52
  51.4 31.8 %collective-permute-start.3 = (bf16[16,32,256]{2,1,0:T(8,128)(2,1)S(1)}, bf16[16,32,256]{2,1,0:T(8,128)(2,1)S(1)}, u32[]{:S(2)}, u32[]{:S(2)}) collective-permute-start(bf16[16,32,256]{2,1,0:T(8,128)(2,1)S(1)} %get-tuple-element.13), channel_id=1, source_target_pairs={{0,64},{32,96},{64,128},{96,160},{128,192},{160,224},{192,0},{224,... | collective-permute-start | bytes 786440 | tf_op jit(solution)/shard_map/ppermute | solution.py:72
  57.7 36.6 %all-to-all-start.2 = ((f32[16,16,128]{2,1,0:T(8,128)}), f32[16,16,128]{2,1,0:T(8,128)S(1)}, u32[]{:S(2)}, u32[]{:S(2)}) async-start(f32[16,16,128]{2,1,0:T(8,128)} %bitcast.42), calls=%async_computation.2 | async-start | bytes 262144 | tf_op jit(solution)/shard_map/all_to_all | solution.py:215
  70.1 18.2 %collective-permute-start.4 = (bf16[16,32,256]{2,1,0:T(8,128)(2,1)S(1)}, bf16[16,32,256]{2,1,0:T(8,128)(2,1)S(1)}, u32[]{:S(2)}, u32[]{:S(2)}) collective-permute-start(bf16[16,32,256]{2,1,0:T(8,128)(2,1)S(1)} %get-tuple-element.13), channel_id=1, source_target_pairs={{0,128},{32,160},{64,192},{96,224},{128,0},{160,32},{192,64},{224,... | collective-permute-start | bytes 786440 | tf_op jit(solution)/shard_map/ppermute | solution.py:74
  74.4 18.0 %collective-permute-start.5 = (bf16[16,32,256]{2,1,0:T(8,128)(2,1)S(1)}, bf16[16,32,256]{2,1,0:T(8,128)(2,1)}, u32[]{:S(2)}, u32[]{:S(2)}) collective-permute-start(bf16[16,32,256]{2,1,0:T(8,128)(2,1)S(1)} %get-tuple-element.13), channel_id=1, source_target_pairs={{0,192},{32,224},{64,0},{96,32},{128,64},{160,96},{192,128},{224,1... | collective-permute-start | bytes 786440 | tf_op jit(solution)/shard_map/ppermute | solution.py:73
  78.1 29.4 %collective-permute-start.8 = (bf16[16,32,256]{2,1,0:T(8,128)(2,1)S(1)}, bf16[16,32,256]{2,1,0:T(8,128)(2,1)S(1)}, u32[]{:S(2)}, u32[]{:S(2)}) collective-permute-start(bf16[16,32,256]{2,1,0:T(8,128)(2,1)S(1)} %get-tuple-element.12), channel_id=1, source_target_pairs={{0,64},{32,96},{64,128},{96,160},{128,192},{160,224},{192,0},{224,... | collective-permute-start | bytes 786440 | tf_op jit(solution)/shard_map/ppermute | solution.py:72
  80.3 27.2 %collective-permute-start.9 = (bf16[16,32,256]{2,1,0:T(8,128)(2,1)S(1)}, bf16[16,32,256]{2,1,0:T(8,128)(2,1)S(1)}, u32[]{:S(2)}, u32[]{:S(2)}) collective-permute-start(bf16[16,32,256]{2,1,0:T(8,128)(2,1)S(1)} %get-tuple-element.12), channel_id=1, source_target_pairs={{0,128},{32,160},{64,192},{96,224},{128,0},{160,32},{192,64},{224,... | collective-permute-start | bytes 786440 | tf_op jit(solution)/shard_map/ppermute | solution.py:74
  83.1 9.4 %copy-start.2 = (bf16[16,32,256]{2,1,0:T(8,128)(2,1)}, bf16[16,32,256]{2,1,0:T(8,128)(2,1)S(1)}, u32[]{:S(2)}) copy-start(bf16[16,32,256]{2,1,0:T(8,128)(2,1)S(1)} %collective-permute-done.3) | copy-start | bytes 786436
  83.2 24.3 %collective-permute-start.10 = (bf16[16,32,256]{2,1,0:T(8,128)(2,1)S(1)}, bf16[16,32,256]{2,1,0:T(8,128)(2,1)}, u32[]{:S(2)}, u32[]{:S(2)}) collective-permute-start(bf16[16,32,256]{2,1,0:T(8,128)(2,1)S(1)} %get-tuple-element.12), channel_id=1, source_target_pairs={{0,192},{32,224},{64,0},{96,32},{128,64},{160,96},{192,128},{224,1... | collective-permute-start | bytes 786440 | tf_op jit(solution)/shard_map/ppermute | solution.py:73
  88.3 42.7 %collective-permute-start.2 = (bf16[256,4096]{1,0:T(8,128)(2,1)}, bf16[256,4096]{1,0:T(8,128)(2,1)}, u32[]{:S(2)}, u32[]{:S(2)}) collective-permute-start(bf16[256,4096]{1,0:T(8,128)(2,1)} %fusion.2.normed_ref), channel_id=1, source_target_pairs={{0,32},{32,0},{64,96},{96,64},{128,160},{160,128},{192,224},{224,1... | collective-permute-start | bytes 6291464 | tf_op jit(solution)/shard_map/ppermute | solution.py:237
  94.3 56.7 %all-to-all-start = ((bf16[32,80,128]{2,1,0:T(8,128)(2,1)}), bf16[32,80,128]{2,1,0:T(8,128)(2,1)}, u32[]{:S(2)}, u32[]{:S(2)}) async-start(bf16[32,80,128]{2,1,0:T(8,128)(2,1)} %copy.28), calls=%async_computation | async-start | bytes 1310720 | tf_op jit(solution)/shard_map/all_to_all | solution.py:255
  111.7 7.6 %copy-start.7 = (f32[128]{0:T(128)S(1)}, f32[128]{0:T(128)}, u32[]{:S(2)}) copy-start(f32[128]{0:T(128)} %maximum_bitcast_fusion) | copy-start | bytes 1540
  111.7 7.6 %copy-start.8 = (f32[128]{0:T(128)S(1)}, f32[128]{0:T(128)}, u32[]{:S(2)}) copy-start(f32[128]{0:T(128)} %maximum_bitcast_fusion.1) | copy-start | bytes 1540
  112.7 19.5 %collective-permute-start.6 = (bf16[2,16,32,256]{3,2,1,0:T(8,128)(2,1)}, bf16[2,16,32,256]{3,2,1,0:T(8,128)(2,1)S(1)}, u32[]{:S(2)}, u32[]{:S(2)}) collective-permute-start(bf16[2,16,32,256]{3,2,1,0:T(8,128)(2,1)} %get-tuple-element.9), channel_id=1, source_target_pairs={{0,272},{32,304},{1,273},{33,305},{2,274},{34,306},{3,275},{35,307... | collective-permute-start | bytes 1572872 | tf_op jit(solution)/shard_map/ppermute | solution.py:77
  117.3 16.3 %collective-permute-start.7 = (bf16[2,16,32,256]{3,2,1,0:T(8,128)(2,1)}, bf16[2,16,32,256]{3,2,1,0:T(8,128)(2,1)S(1)}, u32[]{:S(2)}, u32[]{:S(2)}) collective-permute-start(bf16[2,16,32,256]{3,2,1,0:T(8,128)(2,1)} %get-tuple-element.8), channel_id=1, source_target_pairs={{0,16},{32,48},{1,17},{33,49},{2,18},{34,50},{3,19},{35,51},{4,20}... | collective-permute-start | bytes 1572872 | tf_op jit(solution)/shard_map/ppermute | solution.py:78
  119.4 7.7 %collective-permute-start.1 = (bf16[16,128]{1,0:T(8,128)(2,1)S(1)}, bf16[16,128]{1,0:T(8,128)(2,1)S(1)}, u32[]{:S(2)}, u32[]{:S(2)}) collective-permute-start(bf16[16,128]{1,0:T(8,128)(2,1)S(1)} %concatenate.62), channel_id=1, source_target_pairs={{0,32},{32,0},{64,96},{96,64},{128,160},{160,128},{192,224},{224,1... | collective-permute-start | bytes 12296 | tf_op jit(solution)/shard_map/ppermute | solution.py:231
  122.2 22.9 %collective-permute-start.11 = (bf16[2,16,32,256]{3,2,1,0:T(8,128)(2,1)S(1)}, bf16[2,16,32,256]{3,2,1,0:T(8,128)(2,1)S(1)}, u32[]{:S(2)}, u32[]{:S(2)}) collective-permute-start(bf16[2,16,32,256]{3,2,1,0:T(8,128)(2,1)S(1)} %get-tuple-element.7), channel_id=1, source_target_pairs={{0,272},{32,304},{1,273},{33,305},{2,274},{34,306},{3,275},{35,307... | collective-permute-start | bytes 1572872 | tf_op jit(solution)/shard_map/ppermute | solution.py:77
  127.1 18.9 %collective-permute-start.12 = (bf16[2,16,32,256]{3,2,1,0:T(8,128)(2,1)S(1)}, bf16[2,16,32,256]{3,2,1,0:T(8,128)(2,1)S(1)}, u32[]{:S(2)}, u32[]{:S(2)}) collective-permute-start(bf16[2,16,32,256]{3,2,1,0:T(8,128)(2,1)S(1)} %get-tuple-element.6), channel_id=1, source_target_pairs={{0,16},{32,48},{1,17},{33,49},{2,18},{34,50},{3,19},{35,51},{4,20}... | collective-permute-start | bytes 1572872 | tf_op jit(solution)/shard_map/ppermute | solution.py:78
  140.4 9.8 %copy-start.4 = (s32[1024]{0:T(1024)S(1)}, s32[1024]{0:T(1024)}, u32[]{:S(2)}) copy-start(s32[1024]{0:T(1024)} %param.15) | copy-start | bytes 12292
  140.4 9.8 %copy-start.5 = (s32[32]{0:T(128)S(1)}, s32[32]{0:T(128)}, u32[]{:S(2)}) copy-start(s32[32]{0:T(128)} %param.14) | copy-start | bytes 388
  147.2 3.9 %collective-permute-start.13 = (bf16[8,128]{1,0:T(8,128)(2,1)S(1)}, bf16[8,128]{1,0:T(8,128)(2,1)S(1)}, u32[]{:S(2)}, u32[]{:S(2)}) collective-permute-start(bf16[8,128]{1,0:T(8,128)(2,1)S(1)} %get-tuple-element.17), channel_id=1, source_target_pairs={{0,32},{32,0},{64,96},{96,64},{128,160},{160,128},{192,224},{224,1... | collective-permute-start | bytes 6152 | tf_op jit(solution)/shard_map/ppermute | solution.py:244
  151.7 27.7 %all-to-all-start.3 = ((bf16[32,16,128]{2,1,0:T(8,128)(2,1)}), bf16[32,16,128]{2,1,0:T(8,128)(2,1)S(1)}, u32[]{:S(2)}, u32[]{:S(2)}) async-start(bf16[32,16,128]{2,1,0:T(8,128)(2,1)} %broadcast_in_dim.50), calls=%async_computation.3 | async-start | bytes 262144 | tf_op jit(solution)/shard_map/all_to_all | solution.py:259
  180.3 16.5 %all-to-all-start.4 = ((f32[32,1,32]{2,1,0:T(1,128)}), f32[32,1,32]{2,1,0:T(1,128)S(1)}, u32[]{:S(2)}, u32[]{:S(2)}) async-start(f32[32,1,32]{2,1,0:T(1,128)} %broadcast_in_dim.51), calls=%async_computation.4 | async-start | bytes 32768 | tf_op jit(solution)/shard_map/all_to_all | solution.py:266

commit v2 on v1

v2 whole, which is shorter than its diff:
```python
import math

import jax
import jax.numpy as jnp
from jax import lax
from jax.experimental import pallas as pl
from jax.experimental.pallas import tpu as pltpu
from jax.sharding import PartitionSpec as P

HEADS = 16
KV_HEADS = 4
HEAD = 128
X = 4
Y_LO = 2
Z = 16
BOTH = ("dp", "fsdp")

bf16 = jnp.bfloat16
f32 = jnp.float32
VMEM = pl.BlockSpec(memory_space=pltpu.VMEM)
SMEM = pl.BlockSpec(memory_space=pltpu.SMEM)
HBM = pl.BlockSpec(memory_space=pltpu.HBM)


def dp_index(y_hi, x, core):
    return (y_hi * X + x) * 2 + core


def fsdp_index(y_lo, z):
    return y_lo * Z + z


Z_GROUPS = [[fsdp_index(yl, z) for z in range(Z)] for yl in range(Y_LO)]
CORE_Z_GROUPS = [
    [dp_index(yh, x, c) * 32 + fsdp_index(yl, z) for c in range(2) for z in range(Z)]
    for yh in range(2)
    for x in range(X)
    for yl in range(Y_LO)
]
CROSS_SWAP = [
    (
        dp_index(yh, x, c) * 32 + fsdp_index(1 - c, z),
        dp_index(yh, x, 1 - c) * 32 + fsdp_index(c, z),
    )
    for yh in range(2)
    for x in range(X)
    for c in range(2)
    for z in range(Z)
]
CORE_SWAP = [(d, d ^ 1) for d in range(16)]
Y_LO_SWAP = [(i, i ^ Z) for i in range(32)]


def x_shift(step):
    return [
        (dp_index(yh, x, c), dp_index(yh, (x + step) % X, c))
        for yh in range(2)
        for x in range(X)
        for c in range(2)
    ]


def y_shift(step):
    pairs = []
    for y in range(4):
        to = (y + step) % 4
        for x in range(X):
            for z in range(Z):
                for c in range(2):
                    pairs.append(
                        (
                            dp_index(y // 2, x, c) * 32 + fsdp_index(y % 2, z),
                            dp_index(to // 2, x, c) * 32 + fsdp_index(to % 2, z),
                        )
                    )
    return pairs


def rope_tables(positions, head_width):
    halfway = head_width // 2
    frequency = 10000.0 ** (-jnp.arange(halfway, dtype=f32) * 2.0 / head_width)
    angles = positions.astype(f32)[..., None] * frequency
    cosine, sine = jnp.cos(angles), jnp.sin(angles)
    return (
        jnp.concatenate([cosine, cosine], axis=-1),
        jnp.concatenate([-sine, sine], axis=-1),
    )


PIECE = 136


def open_body(place_ref, hidden, gain_ref, w_key, w_value, out_ref, last_ref, block, keys, values, sem):
    last, x, core, y_lo = place_ref[0], place_ref[1], place_ref[2], place_ref[3]
    first = pl.multiple_of((last >> 3) << 3, 8)
    rows = pl.ds(pl.multiple_of(x * 32, 32), 32)
    columns = pl.ds(pl.multiple_of(core * 256, 256), 256)
    copies = [
        pltpu.make_async_copy(hidden.at[0, pl.ds(first, 8)], block, sem.at[0]),
        pltpu.make_async_copy(w_key.at[rows, columns], keys, sem.at[1]),
        pltpu.make_async_copy(w_value.at[rows, columns], values, sem.at[2]),
    ]
    for copy in copies:
        copy.start()
    copies[0].wait()
    floats = block[...].astype(f32)
    pick = lax.broadcasted_iota(jnp.int32, floats.shape, 0) == (last & 7)
    row = jnp.sum(jnp.where(pick, floats, 0.0), axis=0, keepdims=True)
    last_ref[...] = row.astype(bf16)
    normed = row * lax.rsqrt(jnp.mean(row * row, axis=-1, keepdims=True) + 1e-05) * gain_ref[...]
    normed = normed.astype(bf16).astype(f32)
    half = normed.shape[1] // 2
    place = lax.broadcasted_iota(jnp.int32, (8, HEAD), 0)
    copies[1].wait()
    copies[2].wait()
    unit = jnp.concatenate(
        [w[:, g * HEAD : (g + 1) * HEAD] for w in (keys[...], values[...]) for g in range(2)], axis=0
    )
    for z in range(Z):
        low = normed[:, z * HEAD : (z + 1) * HEAD]
        high = normed[:, half + z * HEAD : half + (z + 1) * HEAD]
        mine = jnp.where(y_lo == 0, low, high)
        other = jnp.where(y_lo == 0, high, low)
        tile = jnp.where(place == 0, mine, jnp.where(place == 1, other, 0.0))
        out_ref[z, :128, :] = unit
        out_ref[z, 128:, :] = tile.astype(bf16)


def open_payload(place, hidden, gain, w_key, w_value):
    width = hidden.shape[2]
    return pl.pallas_call(
        open_body,
        out_shape=(
            jax.ShapeDtypeStruct((Z, PIECE, HEAD), bf16),
            jax.ShapeDtypeStruct((1, width), bf16),
        ),
        in_specs=[SMEM, HBM, VMEM, HBM, HBM],
        out_specs=(VMEM, VMEM),
        scratch_shapes=[
            pltpu.VMEM((8, width), bf16),
            pltpu.VMEM((32, 256), bf16),
            pltpu.VMEM((32, 256), bf16),
            pltpu.SemaphoreType.DMA((3,)),
        ],
        compiler_params=pltpu.CompilerParams(vmem_limit_bytes=8 << 20),
        name="open",
    )(place, hidden, gain[None, :], w_key, w_value)


ROWS = 56
QUERY_ROW = 32
HIDDEN_ROW = 48


def fill_body(place_ref, w_out_ref, near_ref, far_ref, out_ref):
    core, y_lo = place_ref[2], place_ref[3]
    weight = w_out_ref[...].astype(f32)
    weight = jnp.where(core == 0, weight[:32], weight[32:]).astype(bf16)
    row = lax.broadcasted_iota(jnp.int32, (8, HEAD), 0)
    half = Z * HEAD
    near, far = (
        jnp.where(y_lo == 0, rows[:, :half], rows[:, half:])
        for rows in (near_ref[...].astype(f32), far_ref[...].astype(f32))
    )
    zeros = jnp.zeros((HIDDEN_ROW - QUERY_ROW, HEAD), bf16)
    for z in range(Z):
        cut = slice(z * HEAD, (z + 1) * HEAD)
        tile = jnp.where(row == 0, near[:, cut], jnp.where(row == 1, far[:, cut], 0.0)).astype(bf16)
        for c in range(2):
            n = c * Z + z
            out_ref[n, :QUERY_ROW, :] = weight[:, n * HEAD : (n + 1) * HEAD]
            out_ref[n, QUERY_ROW:HIDDEN_ROW, :] = zeros
            out_ref[n, HIDDEN_ROW:, :] = tile


def fill_payload(place, w_out, near, far):
    return pl.pallas_call(
        fill_body,
        out_shape=jax.ShapeDtypeStruct((2 * Z, ROWS, HEAD), bf16),
        in_specs=[SMEM, VMEM, VMEM, VMEM],
        out_specs=VMEM,
        compiler_params=pltpu.CompilerParams(vmem_limit_bytes=8 << 20),
        name="fill",
    )(place, w_out, near, far)


def query_body(arrived, near_ref, far_ref, payload, out, tile, parts, sent, sem):
    copy = pltpu.make_async_copy(arrived.at[:, pl.ds(128, 8), :], tile, sem.at[0])
    copy.start()
    copy.wait()
    features = tile[...].astype(f32)
    total = jnp.dot(
        features[:, 0, :].astype(bf16), near_ref[...], preferred_element_type=f32
    ) + jnp.dot(features[:, 1, :].astype(bf16), far_ref[...], preferred_element_type=f32)
    high = total.astype(bf16).astype(f32)
    low = total - high
    for h in range(HEADS):
        c, cut = h // 8, slice(h * HEAD, (h + 1) * HEAD)
        parts[c * Z : (c + 1) * Z, h % 8, :] = high[:, cut]
        parts[c * Z : (c + 1) * Z, 8 + h % 8, :] = low[:, cut]
    sent[...] = parts[...].astype(bf16)
    back = pltpu.make_async_copy(sent, out.at[:, pl.ds(QUERY_ROW, 16), :], sem.at[1])
    back.start()
    back.wait()


def query_payload(arrived, near, far, payload):
    return pl.pallas_call(
        query_body,
        out_shape=jax.ShapeDtypeStruct(payload.shape, bf16),
        in_specs=[HBM, VMEM, VMEM, HBM],
        out_specs=HBM,
        input_output_aliases={3: 0},
        scratch_shapes=[
            pltpu.VMEM((Z, 8, HEAD), bf16),
            pltpu.VMEM((2 * Z, 16, HEAD), f32),
            pltpu.VMEM((2 * Z, 16, HEAD), bf16),
            pltpu.SemaphoreType.DMA((2,)),
        ],
        compiler_params=pltpu.CompilerParams(vmem_limit_bytes=8 << 20),
        name="query",
    )(arrived, near, far, payload)


def attend_body(place_ref, len_ref, normed, other, cos_ref, sin_ref, parts, *refs):
    pieces, (out_ref, w_ref, q_ref, rows_ref, sem, q_sem) = refs[:8], refs[8:]
    fetch = pltpu.make_async_copy(parts.at[:, pl.ds(QUERY_ROW, 16), :], q_ref, q_sem.at[0])
    fetch.start()
    fills = [
        pltpu.make_async_copy(rows, rows_ref.at[p], q_sem.at[1 + p])
        for p, rows in enumerate((normed, other))
    ]
    x, core, y_lo = place_ref[1], place_ref[2], place_ref[3]
    copies = [[], []]
    for kind in range(2):
        for n, piece in enumerate(pieces):
            row = y_lo if n < X else 1 - y_lo
            column = (x + X - n % X) & (X - 1)
            for g in range(2):
                copies[kind].append(
                    pltpu.make_async_copy(
                        piece.at[:, pl.ds((kind * 2 + g) * 32, 32), :],
                        w_ref.at[kind, row, :, column, :, pl.ds(g * HEAD, HEAD)],
                        sem.at[kind, n, g],
                    )
                )
    for copy in fills[:1] + copies[0] + fills[1:] + copies[1]:
        copy.start()
    cosine, sine = cos_ref[...], sin_ref[...]
    fetch.wait()
    by_core = [jnp.sum(q_ref[c * Z : (c + 1) * Z].astype(f32), axis=0) for c in range(2)]
    by_core = [both[:8] + both[8:] for both in by_core]
    queries = []
    for p in range(2):
        summed = jnp.where(core == p, by_core[0], by_core[1])
        last = len_ref[p] - 1
        turned = summed * cos_ref[pl.ds(last, 1), :] + pltpu.roll(summed, HEAD // 2, 1) * sin_ref[
            pl.ds(last, 1), :
        ]
        queries.append((turned * (1.0 / math.sqrt(HEAD))).astype(bf16))
    for copy in copies[0]:
        copy.wait()
    weight = w_ref[0].reshape(Y_LO * Z * X * 32, 256)
    sums = []
    for p in range(2):
        fills[p].wait()
        rows = rows_ref[p]
        keys = jnp.dot(rows, weight, preferred_element_type=f32)
        scores = []
        for g in range(2):
            part = keys[:, g * HEAD : (g + 1) * HEAD]
            turned = (part * cosine + pltpu.roll(part, HEAD // 2, 1) * sine).astype(bf16)
            scores.append(
                lax.dot_general(
                    queries[p], turned, (((1,), (1,)), ((), ())), preferred_element_type=f32
                )
            )
        head = lax.broadcasted_iota(jnp.int32, scores[0].shape, 0)
        place = lax.broadcasted_iota(jnp.int32, scores[0].shape, 1)
        scores = jnp.where(head < 4, scores[0], scores[1])
        scores = jnp.where(place < len_ref[p], scores, -jnp.inf)
        powers = jnp.exp(scores - jnp.max(scores, axis=-1, keepdims=True))
        weights = (powers / jnp.sum(powers, axis=-1, keepdims=True)).astype(bf16)
        sums.append(jnp.dot(weights, rows, preferred_element_type=f32))
    u = jnp.concatenate(sums, axis=0)
    first = u.astype(bf16)
    rest = u - first.astype(f32)
    second = rest.astype(bf16)
    third = (rest - second.astype(f32)).astype(bf16)
    for copy in copies[1]:
        copy.wait()
    weight = w_ref[1].reshape(Y_LO * Z * X * 32, 256)
    parts = [jnp.dot(t, weight, preferred_element_type=f32) for t in (third, second, first)]
    total = parts[0] + parts[1] + parts[2]
    head = lax.broadcasted_iota(jnp.int32, (16, HEAD), 0)
    context = jnp.where((head & 7) < 4, total[:, :HEAD], total[:, HEAD:])
    turned = jnp.concatenate([context[8:], context[:8]], axis=0)
    context = jnp.where(core == 0, context, turned).astype(bf16)
    out_ref[...] = jnp.broadcast_to(context[None], out_ref.shape)


def attend(place, lengths, normed, other, cosine, sine, parts, pieces):
    return pl.pallas_call(
        attend_body,
        out_shape=jax.ShapeDtypeStruct((2 * Z, 16, HEAD), bf16),
        in_specs=[SMEM, SMEM, HBM, HBM, VMEM, VMEM] + [HBM] * 9,
        out_specs=VMEM,
        scratch_shapes=[
            pltpu.VMEM((2, Y_LO, Z, X, 32, 256), bf16),
            pltpu.VMEM((2 * Z, 16, HEAD), bf16),
            pltpu.VMEM((2, *normed.shape), bf16),
            pltpu.SemaphoreType.DMA((2, 8, 2)),
            pltpu.SemaphoreType.DMA((3,)),
        ],
        compiler_params=pltpu.CompilerParams(vmem_limit_bytes=60 << 20),
        name="attend",
    )(place, lengths, normed, other, cosine, sine, parts, *pieces)


def local(
    hidden, lengths, list_ids, list_owner, attn_gain, final_gain, w_query, w_key, w_value, w_out
):
    _, seq_len, width = hidden.shape
    dp, fsdp = lax.axis_index("dp"), lax.axis_index("fsdp")
    core, x = dp & 1, (dp >> 1) & (X - 1)
    y_lo = fsdp >> 4
    place = jnp.stack([lengths[0] - 1, x, core, y_lo]).astype(jnp.int32)

    outgoing, last_input = open_payload(place, hidden, attn_gain, w_key, w_value)

    w_query_other = lax.ppermute(w_query, "fsdp", Y_LO_SWAP)
    both_lengths = jnp.concatenate([lengths, lax.ppermute(lengths, "dp", CORE_SWAP)])
    rows, outgoing = lax.optimization_barrier((hidden[0], outgoing))
    arrived = lax.all_to_all(outgoing, "fsdp", 0, 0, tiled=True, axis_index_groups=Z_GROUPS)
    floats = rows.astype(f32)
    normed = (
        floats * lax.rsqrt(jnp.mean(floats * floats, axis=-1, keepdims=True) + 1e-05) * attn_gain
    ).astype(bf16)
    other = lax.ppermute(normed, "dp", CORE_SWAP)
    cosine, sine = rope_tables(jnp.arange(seq_len), HEAD)
    last_other = lax.ppermute(last_input, "fsdp", Y_LO_SWAP)
    payload = fill_payload(place, w_out, last_input, last_other)
    arrived, w_query_other, other, both_lengths, cosine, sine, payload = lax.optimization_barrier(
        (arrived, w_query_other, other, both_lengths, cosine, sine, payload)
    )

    plus = lax.ppermute(arrived, "dp", x_shift(1))
    minus = lax.ppermute(arrived, "dp", x_shift(-1))
    far = lax.ppermute(arrived, "dp", x_shift(2))
    y_own = lax.ppermute(arrived, BOTH, y_shift(-1))

    w_query_other, plus, minus = lax.optimization_barrier((w_query_other, plus, minus))
    payload = query_payload(arrived, w_query, w_query_other, payload)
    parts = lax.all_to_all(payload, BOTH, 0, 0, tiled=True, axis_index_groups=CORE_Z_GROUPS)

    plus, minus, far, y_own = lax.optimization_barrier((plus, minus, far, y_own))
    y_plus = lax.ppermute(plus, BOTH, y_shift(1))
    y_minus = lax.ppermute(minus, BOTH, y_shift(-1))
    y_far = lax.ppermute(far, BOTH, y_shift(1))

    pieces = (arrived, plus, far, minus, y_own, y_plus, y_far, y_minus)
    context = attend(place, both_lengths, normed, other, cosine, sine, parts, pieces)
    contexts = lax.all_to_all(context, "fsdp", 0, 0, tiled=True)

    weight = jnp.transpose(parts[:, :QUERY_ROW].reshape(2, Z, 32, HEAD), (1, 0, 2, 3))
    weight = weight.reshape(2 * Z * 32, HEAD)
    weight = jnp.where(core == y_lo, weight, lax.ppermute(weight, BOTH, CROSS_SWAP))
    inputs = lax.dynamic_slice(parts, (core * Z, HIDDEN_ROW, 0), (Z, 2, HEAD)).astype(f32)
    inputs = jnp.where(y_lo == 0, inputs, inputs[:, ::-1])
    inputs = jnp.transpose(inputs, (1, 0, 2)).reshape(2 * Z, HEAD)

    slabs = width // HEAD
    contexts = contexts.reshape(slabs, 2, 8 * HEAD)
    halves = jnp.einsum("sad,dn->asn", contexts, weight, preferred_element_type=f32)
    kept = lax.dynamic_index_in_dim(halves, core, 0, keepdims=False)
    given = lax.dynamic_index_in_dim(halves, 1 - core, 0, keepdims=False)
    residual = inputs + (kept + lax.ppermute(given, "dp", CORE_SWAP))
    gain = lax.dynamic_slice(final_gain, (fsdp * HEAD,), (HEAD,))
    scaled = residual * gain
    partial = jnp.sum(scaled * scaled, axis=-1)
    squares = lax.all_to_all(
        jnp.broadcast_to(partial[None, None, :], (slabs, 1, slabs)), "fsdp", 0, 0, tiled=True
    )
    mean = jnp.sum(squares, axis=0)[0] / width
    slab = (scaled * lax.rsqrt(mean + 1e-06)[:, None]).astype(bf16)

    owner_count = lax.axis_size("dp")
    capacity = 4
    list_index = jnp.arange(list_owner.shape[0])
    owners = jnp.sum(
        jnp.where(list_ids[:, None] == list_index[None, :], list_owner[None, :], 0), axis=1
    )
    owner_marks = (owners[:, None] == jnp.arange(owner_count)[None, :]).astype(jnp.int32)
    slot_rank = jnp.sum((jnp.cumsum(owner_marks, axis=0) - owner_marks) * owner_marks, axis=1)
    select = (
        (owners[None, None, :] == jnp.arange(owner_count)[:, None, None])
        & (slot_rank[None, None, :] == jnp.arange(capacity)[None, :, None])
    ).astype(bf16)
    outgoing = jnp.einsum("osr,rd->osd", select, slab, preferred_element_type=f32).astype(bf16)
    return lax.all_to_all(outgoing[:, None], "dp", split_axis=0, concat_axis=1, tiled=True)


def solution(mesh):
    in_specs = (
        P(("dp", "fsdp"), None, None),
        P(("dp", "fsdp")),
        P("dp"),
        P(),
        P(),
        P(),
        P("fsdp", None),
        P("fsdp", None),
        P("fsdp", None),
        P("fsdp", None),
    )
    out_specs = P("dp", None, None, "fsdp")
    return jax.shard_map(local, mesh=mesh, in_specs=in_specs, out_specs=out_specs, check_vma=False)
```

time: 215 us -> 214 us (level)
  waiting for transfers between devices: 54.9 us -> 68.8 us
  Pallas kernels: 8 us -> 14.6 us
  starting transfers between devices: 104 us -> 97.8 us
  other arithmetic: 13.5 us -> 7.33 us
  local copies, waits for them, and re-layouts: 12.3 us -> 8.91 us
  matrix products: 2.96 us -> 0.39 us
  blocking collectives: 15.9 us -> 13.6 us
    ppermute x12 -> x11, waiting for transfers between devices: 8.72 us -> 37.4 us  [the longest x1 10.3 us: local(): y_plus = lax.ppermute(plus, BOTH, y_shift(1))]
    all_to_all x1, waiting for transfers between devices: 22 us -> 4.85 us  [local(): lax.all_to_all(outgoing, 'fsdp', 0, 0, tiled=True, axis_index_groups=Z_GR...]
    ppermute x1, waiting for transfers between devices: 0.01 us -> 8.72 us  [local(): w_query_other = lax.ppermute(w_query, 'fsdp', Y_LO_SWAP)]
    all_to_all x3 -> x2, starting transfers between devices: 38.1 us -> 30 us  [the longest x1 18.5 us: local(): lax.all_to_all(payload, BOTH, 0, 0, tiled=True, axis_index_groups=CORE_Z_...]
    pallas_call x2 -> x4, Pallas kernels: 8 us -> 14.6 us  [the longest x1 10.3 us: attend(): pl.pallas_call(attend_body, out_shape=jax.ShapeDtypeStruct((2 * Z, 16, HE...]
    all_to_all x3 -> x2, waiting for transfers between devices: 12.1 us -> 5.76 us  [the longest x1 5.76 us: local(): contexts = lax.all_to_all(context, 'fsdp', 0, 0, tiled=True)]
    all_to_all x1, starting transfers between devices: 15.7 us -> 9.55 us  [local(): lax.all_to_all(outgoing, 'fsdp', 0, 0, tiled=True, axis_index_groups=Z_GR...]
    unnamed x22 -> x39, local copies, waits for them, and re-layouts: 1.42 us -> 6.43 us
  transfers between devices with their start and end apart: 19 -> 17, of which waited for: 8 -> 11; matrix products, arithmetic and copies ran while one was open for 10% -> 3% of each run, Pallas kernels for 4% -> 1%
where the time goes in v2:
time: 214 us; the launch traced here: 212 us
  starting transfers between devices  97.8 us (46%)
  waiting for transfers between devices  68.8 us (32%)
  Pallas kernels  14.6 us (7%)
  blocking collectives  13.6 us (6%)
  local copies, waits for them, and re-layouts  8.91 us (4%)
  other arithmetic  7.33 us (3%)
    all_to_all x1, starting transfers between devices, local(): lax.all_to_all(payload, BOTH, 0, 0, tiled=True, axis_index_groups=CORE_Z_...  18.5 us
    all_to_all x1, blocking collectives, local(): lax.all_to_all(outgoing[:, None], 'dp', split_axis=0, concat_axis=1, tile...  13.6 us
    all_to_all x1, waiting for transfers between devices, local(): lax.all_to_all(jnp.broadcast_to(partial[None, None, :], (slabs, 1, slabs)...  12.1 us
    all_to_all x1, starting transfers between devices, local(): contexts = lax.all_to_all(context, 'fsdp', 0, 0, tiled=True)  11.5 us
    pallas_call x1, Pallas kernels, attend(): pl.pallas_call(attend_body, out_shape=jax.ShapeDtypeStruct((2 * Z, 16, HE...  10.3 us
    ppermute x1, waiting for transfers between devices, local(): y_plus = lax.ppermute(plus, BOTH, y_shift(1))  10.3 us
    all_to_all x1, starting transfers between devices, local(): lax.all_to_all(outgoing, 'fsdp', 0, 0, tiled=True, axis_index_groups=Z_GR...  9.55 us
    ppermute x1, starting transfers between devices, local(): other = lax.ppermute(normed, 'dp', CORE_SWAP)  8.91 us
  transfers between devices with their start and end apart: 17, of which 11 were waited for; matrix products, arithmetic and copies ran while one was open for 3% of the time, Pallas kernels for 1%

profile of v2, /device:TPU:1, one launch (start us, length us, event | category | flops | bytes accessed | tf_op | source)
XLA Modules:
  0.0 212.5 jit_solution(7299102400711876206)
XLA Ops:
  0.7 1.6 copy-done
  2.3 0.9 copy-done.5
  3.2 0.9 copy-done.6
  4.1 0.7 copy-done.7
  4.9 1.7 open.1
  7.2 2.0 fusion.2.normed
  9.1 8.9 %collective-permute-start.1 = (bf16[256,4096]{1,0:T(8,128)(2,1)}, bf16[256,4096]{1,0:T(8,128)(2,1)}, u32[]{:S(2)}, u32[]{:S(2)}) collective-permute-start(bf16[256,4096]{1,0:T(8,128)(2,1)} %fusion.2.normed), channel_id=1, source_target_pairs={{0,32},{32,0},{64,96},{96,64},{128,160},{160,128},{192,224},{224,1... | collective-permute-start | bytes 6291464 | tf_op jit(solution)/shard_map/ppermute | solution.py:339
  18.0 9.6 %all-to-all-start = ((bf16[16,136,128]{2,1,0:T(8,128)(2,1)}), bf16[16,136,128]{2,1,0:T(8,128)(2,1)S(1)}, u32[]{:S(2)}, u32[]{:S(2)}) async-start(bf16[16,136,128]{2,1,0:T(8,128)(2,1)} %get-tuple-element.24), calls=%async_computation | async-start | bytes 1114112 | tf_op jit(solution)/shard_map/all_to_all | solution.py:334
  27.6 2.2 %collective-permute-start.2 = (s32[1]{0:T(128)}, s32[1]{0:T(128)}, u32[]{:S(2)}, u32[]{:S(2)}) collective-permute-start(s32[1]{0:T(128)} %param.11), channel_id=1, source_target_pairs={{0,32},{32,0},{64,96},{96,64},{128,160},{160,128},{192,224},{224,1... | collective-permute-start | bytes 20 | tf_op jit(solution)/shard_map/ppermute | solution.py:332
  29.8 3.2 %collective-permute-start.3 = (bf16[1,4096]{1,0:T(2,128)(2,1)S(1)}, bf16[1,4096]{1,0:T(2,128)(2,1)S(1)}, u32[]{:S(2)}, u32[]{:S(2)}) collective-permute-start(bf16[1,4096]{1,0:T(2,128)(2,1)S(1)} %get-tuple-element.26.near_ref), channel_id=1, source_target_pairs={{0,16},{1,17},{2,18},{3,19},{4,20},{5,21},{6,22},{7,23},{8,24},{9,... | collective-permute-start | bytes 24584 | tf_op jit(solution)/shard_map/ppermute | solution.py:341
  33.0 2.1 collective-permute-start
  35.7 0.8 pad_maximum_fusion
  36.5 1.2 pad_add_fusion.1.len_ref
  37.7 1.4 fill.1.payload
  39.2 8.7 %collective-permute-done.far_ref = bf16[128,2048]{1,0:T(8,128)(2,1)S(1)} collective-permute-done((bf16[128,2048]{1,0:T(8,128)(2,1)S(1)}, bf16[128,2048]{1,0:T(8,128)(2,1)S(1)}, u32[]{:S(2)}, u32[]{:S(2)}) %collective-permute-start) | collective-permute-done | bytes 524320 | tf_op jit(solution)/shard_map/ppermute | solution.py:331
  47.9 4.8 %all-to-all-done.arrived.refs_0_ = bf16[16,136,128]{2,1,0:T(8,128)(2,1)S(1)} async-done(((bf16[16,136,128]{2,1,0:T(8,128)(2,1)}), bf16[16,136,128]{2,1,0:T(8,128)(2,1)S(1)}, u32[]{:S(2)}, u32[]{:S(2)}) %all-to-all-start) | async-done | bytes 557088 | tf_op jit(solution)/shard_map/all_to_all | solution.py:334
  52.8 3.1 %collective-permute-start.4 = (bf16[16,136,128]{2,1,0:T(8,128)(2,1)S(1)}, bf16[16,136,128]{2,1,0:T(8,128)(2,1)S(1)}, u32[]{:S(2)}, u32[]{:S(2)}) collective-permute-start(bf16[16,136,128]{2,1,0:T(8,128)(2,1)S(1)} %all-to-all-done.arrived.refs_0_), channel_id=1, source_target_pairs={{0,64},{32,96},{64,128},{96,160},{128,192},{160,224},{192,0},{224,... | collective-permute-start | bytes 1671176 | tf_op jit(solution)/shard_map/ppermute | solution.py:347
  55.9 3.4 %collective-permute-start.5 = (bf16[16,136,128]{2,1,0:T(8,128)(2,1)S(1)}, bf16[16,136,128]{2,1,0:T(8,128)(2,1)S(1)}, u32[]{:S(2)}, u32[]{:S(2)}) collective-permute-start(bf16[16,136,128]{2,1,0:T(8,128)(2,1)S(1)} %all-to-all-done.arrived.refs_0_), channel_id=1, source_target_pairs={{0,192},{32,224},{64,0},{96,32},{128,64},{160,96},{192,128},{224,1... | collective-permute-start | bytes 1671176 | tf_op jit(solution)/shard_map/ppermute | solution.py:348
  59.3 5.0 %collective-permute-done.4.refs_1_ = bf16[16,136,128]{2,1,0:T(8,128)(2,1)S(1)} collective-permute-done((bf16[16,136,128]{2,1,0:T(8,128)(2,1)S(1)}, bf16[16,136,128]{2,1,0:T(8,128)(2,1)S(1)}, u32[]{:S(2)}, u32[]{:S(2)}) %collective-permute-start.4) | collective-permute-done | bytes 557088 | tf_op jit(solution)/shard_map/ppermute | solution.py:347
  64.2 2.2 %collective-permute-done.5.refs_3_ = bf16[16,136,128]{2,1,0:T(8,128)(2,1)S(1)} collective-permute-done((bf16[16,136,128]{2,1,0:T(8,128)(2,1)S(1)}, bf16[16,136,128]{2,1,0:T(8,128)(2,1)S(1)}, u32[]{:S(2)}, u32[]{:S(2)}) %collective-permute-start.5) | collective-permute-done | bytes 557088 | tf_op jit(solution)/shard_map/ppermute | solution.py:348
  66.5 1.1 query.1
  67.5 18.5 %all-to-all-start.1 = ((bf16[32,56,128]{2,1,0:T(8,128)(2,1)}), bf16[32,56,128]{2,1,0:T(8,128)(2,1)S(1)}, u32[]{:S(2)}, u32[]{:S(2)}) async-start(bf16[32,56,128]{2,1,0:T(8,128)(2,1)} %query.1), calls=%async_computation.1 | async-start | bytes 917504 | tf_op jit(solution)/shard_map/all_to_all | solution.py:354
  86.1 4.4 %collective-permute-start.7 = (bf16[16,136,128]{2,1,0:T(8,128)(2,1)S(1)}, bf16[16,136,128]{2,1,0:T(8,128)(2,1)S(1)}, u32[]{:S(2)}, u32[]{:S(2)}) collective-permute-start(bf16[16,136,128]{2,1,0:T(8,128)(2,1)S(1)} %all-to-all-done.arrived.refs_0_), channel_id=1, source_target_pairs={{0,128},{32,160},{64,192},{96,224},{128,0},{160,32},{192,64},{224,... | collective-permute-start | bytes 1671176 | tf_op jit(solution)/shard_map/ppermute | solution.py:349
  90.5 4.6 %collective-permute-start.8 = (bf16[16,136,128]{2,1,0:T(8,128)(2,1)S(1)}, bf16[16,136,128]{2,1,0:T(8,128)(2,1)S(1)}, u32[]{:S(2)}, u32[]{:S(2)}) collective-permute-start(bf16[16,136,128]{2,1,0:T(8,128)(2,1)S(1)} %all-to-all-done.arrived.refs_0_), channel_id=1, source_target_pairs={{0,272},{32,304},{1,273},{33,305},{2,274},{34,306},{3,275},{35,307... | collective-permute-start | bytes 1671176 | tf_op jit(solution)/shard_map/ppermute | solution.py:350
  95.1 8.4 %collective-permute-done.7.refs_2_ = bf16[16,136,128]{2,1,0:T(8,128)(2,1)S(1)} collective-permute-done((bf16[16,136,128]{2,1,0:T(8,128)(2,1)S(1)}, bf16[16,136,128]{2,1,0:T(8,128)(2,1)S(1)}, u32[]{:S(2)}, u32[]{:S(2)}) %collective-permute-start.7) | collective-permute-done | bytes 557088 | tf_op jit(solution)/shard_map/ppermute | solution.py:349
  103.5 3.1 %collective-permute-done.8.refs_4_ = bf16[16,136,128]{2,1,0:T(8,128)(2,1)S(1)} collective-permute-done((bf16[16,136,128]{2,1,0:T(8,128)(2,1)S(1)}, bf16[16,136,128]{2,1,0:T(8,128)(2,1)S(1)}, u32[]{:S(2)}, u32[]{:S(2)}) %collective-permute-start.8) | collective-permute-done | bytes 557088 | tf_op jit(solution)/shard_map/ppermute | solution.py:350
  106.6 2.7 %collective-permute-start.10 = (bf16[16,136,128]{2,1,0:T(8,128)(2,1)S(1)}, bf16[16,136,128]{2,1,0:T(8,128)(2,1)S(1)}, u32[]{:S(2)}, u32[]{:S(2)}) collective-permute-start(bf16[16,136,128]{2,1,0:T(8,128)(2,1)S(1)} %collective-permute-done.7.refs_2_), channel_id=1, source_target_pairs={{0,16},{32,48},{1,17},{33,49},{2,18},{34,50},{3,19},{35,51},{4,20}... | collective-permute-start | bytes 1671176 | tf_op jit(solution)/shard_map/ppermute | solution.py:359
  109.2 4.6 %collective-permute-start.11 = (bf16[16,136,128]{2,1,0:T(8,128)(2,1)S(1)}, bf16[16,136,128]{2,1,0:T(8,128)(2,1)S(1)}, u32[]{:S(2)}, u32[]{:S(2)}) collective-permute-start(bf16[16,136,128]{2,1,0:T(8,128)(2,1)S(1)} %collective-permute-done.5.refs_3_), channel_id=1, source_target_pairs={{0,272},{32,304},{1,273},{33,305},{2,274},{34,306},{3,275},{35,307... | collective-permute-start | bytes 1671176 | tf_op jit(solution)/shard_map/ppermute | solution.py:358
  113.8 1.9 collective-permute-start.9
  116.0 7.5 %collective-permute-done.10.refs_6_ = bf16[16,136,128]{2,1,0:T(8,128)(2,1)S(1)} collective-permute-done((bf16[16,136,128]{2,1,0:T(8,128)(2,1)S(1)}, bf16[16,136,128]{2,1,0:T(8,128)(2,1)S(1)}, u32[]{:S(2)}, u32[]{:S(2)}) %collective-permute-start.10) | collective-permute-done | bytes 557088 | tf_op jit(solution)/shard_map/ppermute | solution.py:359
  123.5 0.9 collective-permute-done.11.refs_7_
  124.4 0.8 copy-done.16
  125.2 10.3 %collective-permute-done.9.refs_5_ = bf16[16,136,128]{2,1,0:T(8,128)(2,1)} collective-permute-done((bf16[16,136,128]{2,1,0:T(8,128)(2,1)S(1)}, bf16[16,136,128]{2,1,0:T(8,128)(2,1)}, u32[]{:S(2)}, u32[]{:S(2)}) %collective-permute-start.9) | collective-permute-done | bytes 557088 | tf_op jit(solution)/shard_map/ppermute | solution.py:357
  135.5 0.8 copy-done.10
  136.4 10.3 %attend.1 = bf16[32,16,128]{2,1,0:T(8,128)(2,1)} custom-call(s32[4]{0:T(128)} %copy-done.9, s32[2]{0:T(128)} %pad_add_fusion.1.len_ref, bf16[256,4096]{1,0:T(8,128)(2,1)} %fusion.2.normed, bf16[256,4096]{1,0:T(8,128)(2,1)} %collective-permute-done.1.other, f32[256,128]{1,0:T(8,128)} %get-tuple-element.33.cos_ref, f32[256,128]{1,0:T(8,128)} %get-tuple-element.34.sin_ref, ...), custom_call_target="tpu_custom_call" | custom-call | tf_op jit(solution)/shard_map/attend/pallas_call | solution.py:303
  146.7 11.5 %all-to-all-start.2 = ((bf16[32,16,128]{2,1,0:T(8,128)(2,1)}), bf16[32,16,128]{2,1,0:T(8,128)(2,1)S(1)}, u32[]{:S(2)}, u32[]{:S(2)}) async-start(bf16[32,16,128]{2,1,0:T(8,128)(2,1)} %attend.1), calls=%async_computation.2 | async-start | bytes 262144 | tf_op jit(solution)/shard_map/all_to_all | solution.py:363
  158.2 1.0 slice.4
  159.2 5.7 %collective-permute-start.6 = (bf16[1024,128]{1,0:T(8,128)(2,1)S(1)}, bf16[1024,128]{1,0:T(8,128)(2,1)S(1)}, u32[]{:S(2)}, u32[]{:S(2)}) collective-permute-start(bf16[1024,128]{1,0:T(8,128)(2,1)S(1)} %bitcast.41), channel_id=1, source_target_pairs={{16,32},{17,33},{18,34},{19,35},{20,36},{21,37},{22,38},{23,39},{2... | collective-permute-start | bytes 786440 | tf_op jit(solution)/shard_map/ppermute | solution.py:367
  165.1 0.8 dynamic_slice.16
  166.0 0.8 dynamic-slice_convert_fusion
  166.8 5.8 %all-to-all-done.2 = bf16[32,16,128]{2,1,0:T(8,128)(2,1)S(1)} async-done(((bf16[32,16,128]{2,1,0:T(8,128)(2,1)}), bf16[32,16,128]{2,1,0:T(8,128)(2,1)S(1)}, u32[]{:S(2)}, u32[]{:S(2)}) %all-to-all-start.2) | async-done | bytes 131104 | tf_op jit(solution)/shard_map/all_to_all | solution.py:363
  172.8 5.5 %collective-permute-start.12 = (f32[32,128]{1,0:T(8,128)S(1)}, f32[32,128]{1,0:T(8,128)S(1)}, u32[]{:S(2)}, u32[]{:S(2)}) collective-permute-start(f32[32,128]{1,0:T(8,128)S(1)} %dynamic-slice_bitcast_fusion), channel_id=1, source_target_pairs={{0,32},{32,0},{64,96},{96,64},{128,160},{160,128},{192,224},{224,1... | collective-permute-start | bytes 49160 | tf_op jit(solution)/shard_map/ppermute | solution.py:377
  178.3 0.8 select_bitcast_fusion
  179.3 0.6 broadcast_in_dim.17
  179.9 6.0 %all-to-all-start.3 = ((f32[32,1,32]{2,1,0:T(1,128)}), f32[32,1,32]{2,1,0:T(1,128)S(1)}, u32[]{:S(2)}, u32[]{:S(2)}) async-start(f32[32,1,32]{2,1,0:T(1,128)} %broadcast_in_dim.17), calls=%async_computation.3 | async-start | bytes 32768 | tf_op jit(solution)/shard_map/all_to_all | solution.py:381
  185.9 12.1 %all-to-all-done.3 = f32[32,1,32]{2,1,0:T(1,128)S(1)} async-done(((f32[32,1,32]{2,1,0:T(1,128)}), f32[32,1,32]{2,1,0:T(1,128)S(1)}, u32[]{:S(2)}, u32[]{:S(2)}) %all-to-all-start.3) | async-done | bytes 4128 | tf_op jit(solution)/shard_map/all_to_all | solution.py:381
  198.2 13.6 %all_to_all.32 = bf16[16,1,4,128]{3,2,1,0:T(4,128)(2,1)S(1)} all-to-all(bf16[16,1,4,128]{3,2,1,0:T(4,128)(2,1)S(1)} %copy.31), channel_id=1, replica_groups=mesh['dp'=16,'fsdp'=32] {'dp'}, dimensions={0} | all-to-all | bytes 32768 | tf_op jit(solution)/shard_map/all_to_all | solution.py:400
  211.9 0.6 copy.37
  (61 shorter events, 2.4 us)
Async XLA Ops:
  0.7 37.0 %copy-start.9 = (s32[4]{0:T(128)}, s32[4]{0:T(128)S(1)}, u32[]{:S(2)}) copy-start(s32[4]{0:T(128)S(1)} %pad_add_fusion.place_ref) | copy-start | bytes 52
  0.7 1.6 copy-start
  2.3 0.9 copy-start.5
  3.2 0.9 copy-start.6
  4.1 0.7 copy-start.7
  4.9 1.8 copy-start.1
  4.9 2.3 %copy-start.8 = (f32[4096]{0:T(1024)S(1)}, f32[4096]{0:T(1024)}, u32[]{:S(2)}) copy-start(f32[4096]{0:T(1024)} %param.14) | copy-start | bytes 49156
  7.1 25.9 %copy-start.3 = (bf16[128,2048]{1,0:T(8,128)(2,1)S(1)}, bf16[128,2048]{1,0:T(8,128)(2,1)}, u32[]{:S(2)}) copy-start(bf16[128,2048]{1,0:T(8,128)(2,1)} %near_ref.1) | copy-start | bytes 1572868
  9.1 28.6 %copy-start.4 = (bf16[64,4096]{1,0:T(8,128)(2,1)S(1)}, bf16[64,4096]{1,0:T(8,128)(2,1)}, u32[]{:S(2)}) copy-start(bf16[64,4096]{1,0:T(8,128)(2,1)} %w_out_ref.1) | copy-start | bytes 1572868
  9.1 43.6 %collective-permute-start.1 = (bf16[256,4096]{1,0:T(8,128)(2,1)}, bf16[256,4096]{1,0:T(8,128)(2,1)}, u32[]{:S(2)}, u32[]{:S(2)}) collective-permute-start(bf16[256,4096]{1,0:T(8,128)(2,1)} %fusion.2.normed), channel_id=1, source_target_pairs={{0,32},{32,0},{64,96},{96,64},{128,160},{160,128},{192,224},{224,1... | collective-permute-start | bytes 6291464 | tf_op jit(solution)/shard_map/ppermute | solution.py:339
  18.0 34.7 %all-to-all-start = ((bf16[16,136,128]{2,1,0:T(8,128)(2,1)}), bf16[16,136,128]{2,1,0:T(8,128)(2,1)S(1)}, u32[]{:S(2)}, u32[]{:S(2)}) async-start(bf16[16,136,128]{2,1,0:T(8,128)(2,1)} %get-tuple-element.24), calls=%async_computation | async-start | bytes 1114112 | tf_op jit(solution)/shard_map/all_to_all | solution.py:334
  27.6 8.9 %collective-permute-start.2 = (s32[1]{0:T(128)}, s32[1]{0:T(128)}, u32[]{:S(2)}, u32[]{:S(2)}) collective-permute-start(s32[1]{0:T(128)} %param.11), channel_id=1, source_target_pairs={{0,32},{32,0},{64,96},{96,64},{128,160},{160,128},{192,224},{224,1... | collective-permute-start | bytes 20 | tf_op jit(solution)/shard_map/ppermute | solution.py:332
  29.8 7.9 %collective-permute-start.3 = (bf16[1,4096]{1,0:T(2,128)(2,1)S(1)}, bf16[1,4096]{1,0:T(2,128)(2,1)S(1)}, u32[]{:S(2)}, u32[]{:S(2)}) collective-permute-start(bf16[1,4096]{1,0:T(2,128)(2,1)S(1)} %get-tuple-element.26.near_ref), channel_id=1, source_target_pairs={{0,16},{1,17},{2,18},{3,19},{4,20},{5,21},{6,22},{7,23},{8,24},{9,... | collective-permute-start | bytes 24584 | tf_op jit(solution)/shard_map/ppermute | solution.py:341
  33.0 14.9 %collective-permute-start = (bf16[128,2048]{1,0:T(8,128)(2,1)S(1)}, bf16[128,2048]{1,0:T(8,128)(2,1)S(1)}, u32[]{:S(2)}, u32[]{:S(2)}) collective-permute-start(bf16[128,2048]{1,0:T(8,128)(2,1)S(1)} %copy-done.3), channel_id=1, source_target_pairs={{0,16},{1,17},{2,18},{3,19},{4,20},{5,21},{6,22},{7,23},{8,24},{9,... | collective-permute-start | bytes 1572872 | tf_op jit(solution)/shard_map/ppermute | solution.py:331
  37.7 78.0 %copy-start.17 = (s32[1024]{0:T(1024)S(1)}, s32[1024]{0:T(1024)}, u32[]{:S(2)}) copy-start(s32[1024]{0:T(1024)} %param.13) | copy-start | bytes 12292
  37.7 78.0 %copy-start.18 = (s32[32]{0:T(128)S(1)}, s32[32]{0:T(128)}, u32[]{:S(2)}) copy-start(s32[32]{0:T(128)} %param.12) | copy-start | bytes 388
  52.8 82.7 %copy-start.2 = (bf16[16,136,128]{2,1,0:T(8,128)(2,1)}, bf16[16,136,128]{2,1,0:T(8,128)(2,1)S(1)}, u32[]{:S(2)}) copy-start(bf16[16,136,128]{2,1,0:T(8,128)(2,1)S(1)} %all-to-all-done.arrived.refs_0_) | copy-start | bytes 1671172
  52.8 11.5 %collective-permute-start.4 = (bf16[16,136,128]{2,1,0:T(8,128)(2,1)S(1)}, bf16[16,136,128]{2,1,0:T(8,128)(2,1)S(1)}, u32[]{:S(2)}, u32[]{:S(2)}) collective-permute-start(bf16[16,136,128]{2,1,0:T(8,128)(2,1)S(1)} %all-to-all-done.arrived.refs_0_), channel_id=1, source_target_pairs={{0,64},{32,96},{64,128},{96,160},{128,192},{160,224},{192,0},{224,... | collective-permute-start | bytes 1671176 | tf_op jit(solution)/shard_map/ppermute | solution.py:347
  55.9 10.6 %collective-permute-start.5 = (bf16[16,136,128]{2,1,0:T(8,128)(2,1)S(1)}, bf16[16,136,128]{2,1,0:T(8,128)(2,1)S(1)}, u32[]{:S(2)}, u32[]{:S(2)}) collective-permute-start(bf16[16,136,128]{2,1,0:T(8,128)(2,1)S(1)} %all-to-all-done.arrived.refs_0_), channel_id=1, source_target_pairs={{0,192},{32,224},{64,0},{96,32},{128,64},{160,96},{192,128},{224,1... | collective-permute-start | bytes 1671176 | tf_op jit(solution)/shard_map/ppermute | solution.py:348
  64.2 71.3 %copy-start.11 = (bf16[16,136,128]{2,1,0:T(8,128)(2,1)}, bf16[16,136,128]{2,1,0:T(8,128)(2,1)S(1)}, u32[]{:S(2)}) copy-start(bf16[16,136,128]{2,1,0:T(8,128)(2,1)S(1)} %collective-permute-done.4.refs_1_) | copy-start | bytes 1671172
  66.5 69.1 %copy-start.12 = (bf16[16,136,128]{2,1,0:T(8,128)(2,1)}, bf16[16,136,128]{2,1,0:T(8,128)(2,1)S(1)}, u32[]{:S(2)}) copy-start(bf16[16,136,128]{2,1,0:T(8,128)(2,1)S(1)} %collective-permute-done.5.refs_3_) | copy-start | bytes 1671172
  67.5 68.0 %all-to-all-start.1 = ((bf16[32,56,128]{2,1,0:T(8,128)(2,1)}), bf16[32,56,128]{2,1,0:T(8,128)(2,1)S(1)}, u32[]{:S(2)}, u32[]{:S(2)}) async-start(bf16[32,56,128]{2,1,0:T(8,128)(2,1)} %query.1), calls=%async_computation.1 | async-start | bytes 917504 | tf_op jit(solution)/shard_map/all_to_all | solution.py:354
  86.1 17.4 %collective-permute-start.7 = (bf16[16,136,128]{2,1,0:T(8,128)(2,1)S(1)}, bf16[16,136,128]{2,1,0:T(8,128)(2,1)S(1)}, u32[]{:S(2)}, u32[]{:S(2)}) collective-permute-start(bf16[16,136,128]{2,1,0:T(8,128)(2,1)S(1)} %all-to-all-done.arrived.refs_0_), channel_id=1, source_target_pairs={{0,128},{32,160},{64,192},{96,224},{128,0},{160,32},{192,64},{224,... | collective-permute-start | bytes 1671176 | tf_op jit(solution)/shard_map/ppermute | solution.py:349
  90.5 16.1 %collective-permute-start.8 = (bf16[16,136,128]{2,1,0:T(8,128)(2,1)S(1)}, bf16[16,136,128]{2,1,0:T(8,128)(2,1)S(1)}, u32[]{:S(2)}, u32[]{:S(2)}) collective-permute-start(bf16[16,136,128]{2,1,0:T(8,128)(2,1)S(1)} %all-to-all-done.arrived.refs_0_), channel_id=1, source_target_pairs={{0,272},{32,304},{1,273},{33,305},{2,274},{34,306},{3,275},{35,307... | collective-permute-start | bytes 1671176 | tf_op jit(solution)/shard_map/ppermute | solution.py:350
  103.5 32.0 %copy-start.13 = (bf16[16,136,128]{2,1,0:T(8,128)(2,1)}, bf16[16,136,128]{2,1,0:T(8,128)(2,1)S(1)}, u32[]{:S(2)}) copy-start(bf16[16,136,128]{2,1,0:T(8,128)(2,1)S(1)} %collective-permute-done.7.refs_2_) | copy-start | bytes 1671172
  106.6 29.0 %copy-start.14 = (bf16[16,136,128]{2,1,0:T(8,128)(2,1)}, bf16[16,136,128]{2,1,0:T(8,128)(2,1)S(1)}, u32[]{:S(2)}) copy-start(bf16[16,136,128]{2,1,0:T(8,128)(2,1)S(1)} %collective-permute-done.8.refs_4_) | copy-start | bytes 1671172
  106.6 16.9 %collective-permute-start.10 = (bf16[16,136,128]{2,1,0:T(8,128)(2,1)S(1)}, bf16[16,136,128]{2,1,0:T(8,128)(2,1)S(1)}, u32[]{:S(2)}, u32[]{:S(2)}) collective-permute-start(bf16[16,136,128]{2,1,0:T(8,128)(2,1)S(1)} %collective-permute-done.7.refs_2_), channel_id=1, source_target_pairs={{0,16},{32,48},{1,17},{33,49},{2,18},{34,50},{3,19},{35,51},{4,20}... | collective-permute-start | bytes 1671176 | tf_op jit(solution)/shard_map/ppermute | solution.py:359
  109.2 15.1 %collective-permute-start.11 = (bf16[16,136,128]{2,1,0:T(8,128)(2,1)S(1)}, bf16[16,136,128]{2,1,0:T(8,128)(2,1)S(1)}, u32[]{:S(2)}, u32[]{:S(2)}) collective-permute-start(bf16[16,136,128]{2,1,0:T(8,128)(2,1)S(1)} %collective-permute-done.5.refs_3_), channel_id=1, source_target_pairs={{0,272},{32,304},{1,273},{33,305},{2,274},{34,306},{3,275},{35,307... | collective-permute-start | bytes 1671176 | tf_op jit(solution)/shard_map/ppermute | solution.py:358
  113.8 21.7 %collective-permute-start.9 = (bf16[16,136,128]{2,1,0:T(8,128)(2,1)S(1)}, bf16[16,136,128]{2,1,0:T(8,128)(2,1)}, u32[]{:S(2)}, u32[]{:S(2)}) collective-permute-start(bf16[16,136,128]{2,1,0:T(8,128)(2,1)S(1)} %collective-permute-done.4.refs_1_), channel_id=1, source_target_pairs={{0,16},{32,48},{1,17},{33,49},{2,18},{34,50},{3,19},{35,51},{4,20}... | collective-permute-start | bytes 1671176 | tf_op jit(solution)/shard_map/ppermute | solution.py:357
  123.5 0.9 copy-start.15
  124.4 0.8 copy-start.16
  135.5 0.8 copy-start.10
  146.7 25.9 %all-to-all-start.2 = ((bf16[32,16,128]{2,1,0:T(8,128)(2,1)}), bf16[32,16,128]{2,1,0:T(8,128)(2,1)S(1)}, u32[]{:S(2)}, u32[]{:S(2)}) async-start(bf16[32,16,128]{2,1,0:T(8,128)(2,1)} %attend.1), calls=%async_computation.2 | async-start | bytes 262144 | tf_op jit(solution)/shard_map/all_to_all | solution.py:363
  159.2 13.4 %collective-permute-start.6 = (bf16[1024,128]{1,0:T(8,128)(2,1)S(1)}, bf16[1024,128]{1,0:T(8,128)(2,1)S(1)}, u32[]{:S(2)}, u32[]{:S(2)}) collective-permute-start(bf16[1024,128]{1,0:T(8,128)(2,1)S(1)} %bitcast.41), channel_id=1, source_target_pairs={{16,32},{17,33},{18,34},{19,35},{20,36},{21,37},{22,38},{23,39},{2... | collective-permute-start | bytes 786440 | tf_op jit(solution)/shard_map/ppermute | solution.py:367
  172.8 6.3 %collective-permute-start.12 = (f32[32,128]{1,0:T(8,128)S(1)}, f32[32,128]{1,0:T(8,128)S(1)}, u32[]{:S(2)}, u32[]{:S(2)}) collective-permute-start(f32[32,128]{1,0:T(8,128)S(1)} %dynamic-slice_bitcast_fusion), channel_id=1, source_target_pairs={{0,32},{32,0},{64,96},{96,64},{128,160},{160,128},{192,224},{224,1... | collective-permute-start | bytes 49160 | tf_op jit(solution)/shard_map/ppermute | solution.py:377
  179.9 18.1 %all-to-all-start.3 = ((f32[32,1,32]{2,1,0:T(1,128)}), f32[32,1,32]{2,1,0:T(1,128)S(1)}, u32[]{:S(2)}, u32[]{:S(2)}) async-start(f32[32,1,32]{2,1,0:T(1,128)} %broadcast_in_dim.17), calls=%async_computation.3 | async-start | bytes 32768 | tf_op jit(solution)/shard_map/all_to_all | solution.py:381

commit v3 on v2

--- a/solution.py
+++ b/solution.py
@@ -51,31 +51,6 @@
 Y_LO_SWAP = [(i, i ^ Z) for i in range(32)]
 
 
-def x_shift(step):
-    return [
-        (dp_index(yh, x, c), dp_index(yh, (x + step) % X, c))
-        for yh in range(2)
-        for x in range(X)
-        for c in range(2)
-    ]
-
-
-def y_shift(step):
-    pairs = []
-    for y in range(4):
-        to = (y + step) % 4
-        for x in range(X):
-            for z in range(Z):
-                for c in range(2):
-                    pairs.append(
-                        (
-                            dp_index(y // 2, x, c) * 32 + fsdp_index(y % 2, z),
-                            dp_index(to // 2, x, c) * 32 + fsdp_index(to % 2, z),
-                        )
-                    )
-    return pairs
-
-
 def rope_tables(positions, head_width):
     halfway = head_width // 2
     frequency = 10000.0 ** (-jnp.arange(halfway, dtype=f32) * 2.0 / head_width)
@@ -87,22 +62,56 @@
     )
 
 
-PIECE = 136
-
-
-def open_body(place_ref, hidden, gain_ref, w_key, w_value, out_ref, last_ref, block, keys, values, sem):
-    last, x, core, y_lo = place_ref[0], place_ref[1], place_ref[2], place_ref[3]
-    first = pl.multiple_of((last >> 3) << 3, 8)
-    rows = pl.ds(pl.multiple_of(x * 32, 32), 32)
-    columns = pl.ds(pl.multiple_of(core * 256, 256), 256)
+def unit_body(place_ref, w_key, w_value, out, sem):
+    columns = pl.ds(pl.multiple_of(place_ref[2] * 256, 256), 256)
     copies = [
-        pltpu.make_async_copy(hidden.at[0, pl.ds(first, 8)], block, sem.at[0]),
-        pltpu.make_async_copy(w_key.at[rows, columns], keys, sem.at[1]),
-        pltpu.make_async_copy(w_value.at[rows, columns], values, sem.at[2]),
+        pltpu.make_async_copy(w.at[:, columns], out.at[:, pl.ds(k * 256, 256)], sem.at[k])
+        for k, w in enumerate((w_key, w_value))
     ]
     for copy in copies:
         copy.start()
-    copies[0].wait()
+    for copy in copies:
+        copy.wait()
+
+
+def core_unit(place, w_key, w_value):
+    return pl.pallas_call(
+        unit_body,
+        out_shape=jax.ShapeDtypeStruct((w_key.shape[0], 512), bf16),
+        in_specs=[SMEM, HBM, HBM],
+        out_specs=HBM,
+        scratch_shapes=[pltpu.SemaphoreType.DMA((2,))],
+        compiler_params=pltpu.CompilerParams(vmem_limit_bytes=1 << 20),
+        name="unit",
+    )(place, w_key, w_value)
+
+
+def pair_body(near, far, out, sem):
+    copies = [pltpu.make_async_copy(rows, out.at[k], sem.at[k]) for k, rows in enumerate((near, far))]
+    for copy in copies:
+        copy.start()
+    for copy in copies:
+        copy.wait()
+
+
+def pair(near, far):
+    return pl.pallas_call(
+        pair_body,
+        out_shape=jax.ShapeDtypeStruct((2, *near.shape), bf16),
+        in_specs=[HBM, HBM],
+        out_specs=HBM,
+        scratch_shapes=[pltpu.SemaphoreType.DMA((2,))],
+        compiler_params=pltpu.CompilerParams(vmem_limit_bytes=1 << 20),
+        name="pair",
+    )(near, far)
+
+
+def open_body(place_ref, hidden, gain_ref, out_ref, last_ref, block, sem):
+    last, y_lo = place_ref[0], place_ref[3]
+    first = pl.multiple_of((last >> 3) << 3, 8)
+    copy = pltpu.make_async_copy(hidden.at[0, pl.ds(first, 8)], block, sem.at[0])
+    copy.start()
+    copy.wait()
     floats = block[...].astype(f32)
     pick = lax.broadcasted_iota(jnp.int32, floats.shape, 0) == (last & 7)
     row = jnp.sum(jnp.where(pick, floats, 0.0), axis=0, keepdims=True)
@@ -111,40 +120,29 @@
     normed = normed.astype(bf16).astype(f32)
     half = normed.shape[1] // 2
     place = lax.broadcasted_iota(jnp.int32, (8, HEAD), 0)
-    copies[1].wait()
-    copies[2].wait()
-    unit = jnp.concatenate(
-        [w[:, g * HEAD : (g + 1) * HEAD] for w in (keys[...], values[...]) for g in range(2)], axis=0
-    )
     for z in range(Z):
         low = normed[:, z * HEAD : (z + 1) * HEAD]
         high = normed[:, half + z * HEAD : half + (z + 1) * HEAD]
         mine = jnp.where(y_lo == 0, low, high)
         other = jnp.where(y_lo == 0, high, low)
         tile = jnp.where(place == 0, mine, jnp.where(place == 1, other, 0.0))
-        out_ref[z, :128, :] = unit
-        out_ref[z, 128:, :] = tile.astype(bf16)
-
-
-def open_payload(place, hidden, gain, w_key, w_value):
+        out_ref[z] = tile.astype(bf16)
+
+
+def open_payload(place, hidden, gain):
     width = hidden.shape[2]
     return pl.pallas_call(
         open_body,
         out_shape=(
-            jax.ShapeDtypeStruct((Z, PIECE, HEAD), bf16),
+            jax.ShapeDtypeStruct((Z, 8, HEAD), bf16),
             jax.ShapeDtypeStruct((1, width), bf16),
         ),
-        in_specs=[SMEM, HBM, VMEM, HBM, HBM],
+        in_specs=[SMEM, HBM, VMEM],
         out_specs=(VMEM, VMEM),
-        scratch_shapes=[
-            pltpu.VMEM((8, width), bf16),
-            pltpu.VMEM((32, 256), bf16),
-            pltpu.VMEM((32, 256), bf16),
-            pltpu.SemaphoreType.DMA((3,)),
-        ],
-        compiler_params=pltpu.CompilerParams(vmem_limit_bytes=8 << 20),
+        scratch_shapes=[pltpu.VMEM((8, width), bf16), pltpu.SemaphoreType.DMA((1,))],
+        compiler_params=pltpu.CompilerParams(vmem_limit_bytes=4 << 20),
         name="open",
-    )(place, hidden, gain[None, :], w_key, w_value)
+    )(place, hidden, gain[None, :])
 
 
 ROWS = 56
@@ -184,11 +182,8 @@
     )(place, w_out, near, far)
 
 
-def query_body(arrived, near_ref, far_ref, payload, out, tile, parts, sent, sem):
-    copy = pltpu.make_async_copy(arrived.at[:, pl.ds(128, 8), :], tile, sem.at[0])
-    copy.start()
-    copy.wait()
-    features = tile[...].astype(f32)
+def query_body(arrived_ref, near_ref, far_ref, payload, out, parts, sent, sem):
+    features = arrived_ref[...].astype(f32)
     total = jnp.dot(
         features[:, 0, :].astype(bf16), near_ref[...], preferred_element_type=f32
     ) + jnp.dot(features[:, 1, :].astype(bf16), far_ref[...], preferred_element_type=f32)
@@ -199,7 +194,7 @@
         parts[c * Z : (c + 1) * Z, h % 8, :] = high[:, cut]
         parts[c * Z : (c + 1) * Z, 8 + h % 8, :] = low[:, cut]
     sent[...] = parts[...].astype(bf16)
-    back = pltpu.make_async_copy(sent, out.at[:, pl.ds(QUERY_ROW, 16), :], sem.at[1])
+    back = pltpu.make_async_copy(sent, out.at[:, pl.ds(QUERY_ROW, 16), :], sem.at[0])
     back.start()
     back.wait()
 
@@ -208,42 +203,38 @@
     return pl.pallas_call(
         query_body,
         out_shape=jax.ShapeDtypeStruct(payload.shape, bf16),
-        in_specs=[HBM, VMEM, VMEM, HBM],
+        in_specs=[VMEM, VMEM, VMEM, HBM],
         out_specs=HBM,
         input_output_aliases={3: 0},
         scratch_shapes=[
-            pltpu.VMEM((Z, 8, HEAD), bf16),
             pltpu.VMEM((2 * Z, 16, HEAD), f32),
             pltpu.VMEM((2 * Z, 16, HEAD), bf16),
-            pltpu.SemaphoreType.DMA((2,)),
+            pltpu.SemaphoreType.DMA((1,)),
         ],
         compiler_params=pltpu.CompilerParams(vmem_limit_bytes=8 << 20),
         name="query",
     )(arrived, near, far, payload)
 
 
-def attend_body(place_ref, len_ref, normed, other, cos_ref, sin_ref, parts, *refs):
-    pieces, (out_ref, w_ref, q_ref, rows_ref, sem, q_sem) = refs[:8], refs[8:]
+def attend_body(place_ref, len_ref, normed, other, cos_ref, sin_ref, parts, gathered, out_ref, w_ref, q_ref, rows_ref, sem, q_sem):
     fetch = pltpu.make_async_copy(parts.at[:, pl.ds(QUERY_ROW, 16), :], q_ref, q_sem.at[0])
     fetch.start()
     fills = [
         pltpu.make_async_copy(rows, rows_ref.at[p], q_sem.at[1 + p])
         for p, rows in enumerate((normed, other))
     ]
-    x, core, y_lo = place_ref[1], place_ref[2], place_ref[3]
-    copies = [[], []]
-    for kind in range(2):
-        for n, piece in enumerate(pieces):
-            row = y_lo if n < X else 1 - y_lo
-            column = (x + X - n % X) & (X - 1)
-            for g in range(2):
-                copies[kind].append(
-                    pltpu.make_async_copy(
-                        piece.at[:, pl.ds((kind * 2 + g) * 32, 32), :],
-                        w_ref.at[kind, row, :, column, :, pl.ds(g * HEAD, HEAD)],
-                        sem.at[kind, n, g],
-                    )
-                )
+    core, y_lo = place_ref[2], place_ref[3]
+    copies = [
+        [
+            pltpu.make_async_copy(
+                gathered.at[:, n, :, pl.ds(kind * 256, 256)],
+                w_ref.at[kind, y_lo if n == 0 else 1 - y_lo],
+                sem.at[kind, n],
+            )
+            for n in range(2)
+        ]
+        for kind in range(2)
+    ]
     for copy in fills[:1] + copies[0] + fills[1:] + copies[1]:
         copy.start()
     cosine, sine = cos_ref[...], sin_ref[...]
@@ -260,7 +251,7 @@
         queries.append((turned * (1.0 / math.sqrt(HEAD))).astype(bf16))
     for copy in copies[0]:
         copy.wait()
-    weight = w_ref[0].reshape(Y_LO * Z * X * 32, 256)
+    weight = w_ref[0].reshape(Y_LO * Z * HEAD, 256)
     sums = []
     for p in range(2):
         fills[p].wait()
@@ -289,7 +280,7 @@
     third = (rest - second.astype(f32)).astype(bf16)
     for copy in copies[1]:
         copy.wait()
-    weight = w_ref[1].reshape(Y_LO * Z * X * 32, 256)
+    weight = w_ref[1].reshape(Y_LO * Z * HEAD, 256)
     parts = [jnp.dot(t, weight, preferred_element_type=f32) for t in (third, second, first)]
     total = parts[0] + parts[1] + parts[2]
     head = lax.broadcasted_iota(jnp.int32, (16, HEAD), 0)
@@ -299,22 +290,22 @@
     out_ref[...] = jnp.broadcast_to(context[None], out_ref.shape)
 
 
-def attend(place, lengths, normed, other, cosine, sine, parts, pieces):
+def attend(place, lengths, normed, other, cosine, sine, parts, gathered):
     return pl.pallas_call(
         attend_body,
         out_shape=jax.ShapeDtypeStruct((2 * Z, 16, HEAD), bf16),
-        in_specs=[SMEM, SMEM, HBM, HBM, VMEM, VMEM] + [HBM] * 9,
+        in_specs=[SMEM, SMEM, HBM, HBM, VMEM, VMEM, HBM, HBM],
         out_specs=VMEM,
         scratch_shapes=[
-            pltpu.VMEM((2, Y_LO, Z, X, 32, 256), bf16),
+            pltpu.VMEM((2, Y_LO, Z, HEAD, 256), bf16),
             pltpu.VMEM((2 * Z, 16, HEAD), bf16),
             pltpu.VMEM((2, *normed.shape), bf16),
-            pltpu.SemaphoreType.DMA((2, 8, 2)),
+            pltpu.SemaphoreType.DMA((2, 2)),
             pltpu.SemaphoreType.DMA((3,)),
         ],
         compiler_params=pltpu.CompilerParams(vmem_limit_bytes=60 << 20),
         name="attend",
-    )(place, lengths, normed, other, cosine, sine, parts, *pieces)
+    )(place, lengths, normed, other, cosine, sine, parts, gathered)
 
 
 def local(
@@ -326,40 +317,31 @@
     y_lo = fsdp >> 4
     place = jnp.stack([lengths[0] - 1, x, core, y_lo]).astype(jnp.int32)
 
-    outgoing, last_input = open_payload(place, hidden, attn_gain, w_key, w_value)
+    unit = core_unit(place, w_key, w_value)
+    units = pair(unit, lax.ppermute(unit, "fsdp", Y_LO_SWAP))
+    gathered = lax.all_gather(units, "fsdp", axis=0, tiled=False, axis_index_groups=Z_GROUPS)
+
+    unit, hidden = lax.optimization_barrier((unit, hidden))
+    outgoing, last_input = open_payload(place, hidden, attn_gain)
+    units, outgoing = lax.optimization_barrier((units, outgoing))
+    arrived = lax.all_to_all(outgoing, "fsdp", 0, 0, tiled=True, axis_index_groups=Z_GROUPS)
 
     w_query_other = lax.ppermute(w_query, "fsdp", Y_LO_SWAP)
     both_lengths = jnp.concatenate([lengths, lax.ppermute(lengths, "dp", CORE_SWAP)])
-    rows, outgoing = lax.optimization_barrier((hidden[0], outgoing))
-    arrived = lax.all_to_all(outgoing, "fsdp", 0, 0, tiled=True, axis_index_groups=Z_GROUPS)
+    last_other = lax.ppermute(last_input, "fsdp", Y_LO_SWAP)
+    payload = fill_payload(place, w_out, last_input, last_other)
+
+    payload = query_payload(arrived, w_query, w_query_other, payload)
+    parts = lax.all_to_all(payload, BOTH, 0, 0, tiled=True, axis_index_groups=CORE_Z_GROUPS)
+
+    rows, _ = lax.optimization_barrier((hidden[0], outgoing))
     floats = rows.astype(f32)
     normed = (
         floats * lax.rsqrt(jnp.mean(floats * floats, axis=-1, keepdims=True) + 1e-05) * attn_gain
     ).astype(bf16)
     other = lax.ppermute(normed, "dp", CORE_SWAP)
     cosine, sine = rope_tables(jnp.arange(seq_len), HEAD)
-    last_other = lax.ppermute(last_input, "fsdp", Y_LO_SWAP)
-    payload = fill_payload(place, w_out, last_input, last_other)
-    arrived, w_query_other, other, both_lengths, cosine, sine, payload = lax.optimization_barrier(
-        (arrived, w_query_other, other, both_lengths, cosine, sine, payload)
-    )
-
-    plus = lax.ppermute(arrived, "dp", x_shift(1))
-    minus = lax.ppermute(arrived, "dp", x_shift(-1))
-    far = lax.ppermute(arrived, "dp", x_shift(2))
-    y_own = lax.ppermute(arrived, BOTH, y_shift(-1))
-
-    w_query_other, plus, minus = lax.optimization_barrier((w_query_other, plus, minus))
-    payload = query_payload(arrived, w_query, w_query_other, payload)
-    parts = lax.all_to_all(payload, BOTH, 0, 0, tiled=True, axis_index_groups=CORE_Z_GROUPS)
-
-    plus, minus, far, y_own = lax.optimization_barrier((plus, minus, far, y_own))
-    y_plus = lax.ppermute(plus, BOTH, y_shift(1))
-    y_minus = lax.ppermute(minus, BOTH, y_shift(-1))
-    y_far = lax.ppermute(far, BOTH, y_shift(1))
-
-    pieces = (arrived, plus, far, minus, y_own, y_plus, y_far, y_minus)
-    context = attend(place, both_lengths, normed, other, cosine, sine, parts, pieces)
+    context = attend(place, both_lengths, normed, other, cosine, sine, parts, gathered)
     contexts = lax.all_to_all(context, "fsdp", 0, 0, tiled=True)
 
     weight = jnp.transpose(parts[:, :QUERY_ROW].reshape(2, Z, 32, HEAD), (1, 0, 2, 3))

time: 214 us -> 201 us (0.939)
  starting transfers between devices: 97.8 us -> 72.3 us
  between operations: 1.02 us -> 14.3 us
  waiting for transfers between devices: 68.8 us -> 66.2 us
    ppermute x7 -> x1, waiting for transfers between devices: 37.3 us -> 2.34 us  [local(): units = pair(unit, lax.ppermute(unit, 'fsdp', Y_LO_SWAP))]
    all_to_all x1, waiting for transfers between devices: 0.01 us -> 28 us  [local(): lax.all_to_all(payload, BOTH, 0, 0, tiled=True, axis_index_groups=CORE_Z_...]
    ppermute x7 -> x1, starting transfers between devices: 24.6 us -> 4.03 us  [local(): units = pair(unit, lax.ppermute(unit, 'fsdp', Y_LO_SWAP))]
    all_gather x0 -> x1, waiting for transfers between devices: none -> 13.2 us  [local(): lax.all_gather(units, 'fsdp', axis=0, tiled=False, axis_index_groups=Z_GR...]
    all_to_all x1, starting transfers between devices: 18.5 us -> 8.15 us  [local(): lax.all_to_all(payload, BOTH, 0, 0, tiled=True, axis_index_groups=CORE_Z_...]
    ppermute x1, waiting for transfers between devices: 8.72 us -> 0.01 us  [local(): w_query_other = lax.ppermute(w_query, 'fsdp', Y_LO_SWAP)]
    all_to_all x1, waiting for transfers between devices: 5.76 us -> 0.26 us  [local(): contexts = lax.all_to_all(context, 'fsdp', 0, 0, tiled=True)]
    ppermute x1, starting transfers between devices: 5.74 us -> 11.2 us  [local(): lax.ppermute(weight, BOTH, CROSS_SWAP)]
  transfers between devices with their start and end apart: 17 -> 12, of which waited for: 11 -> 8; matrix products, arithmetic and copies ran while one was open for 3% -> 5% of each run, Pallas kernels for 1% -> 2%
where the time goes in v3:
time: 201 us; the launch traced here: 200 us
  starting transfers between devices  72.3 us (36%)
  waiting for transfers between devices  66.2 us (33%)
  Pallas kernels  15.3 us (8%)
  blocking collectives  15.2 us (8%)
  between operations  14.3 us (7%)
  other arithmetic  9.13 us (5%)
  local copies, waits for them, and re-layouts  7.24 us (4%)
    all_to_all x1, waiting for transfers between devices, local(): lax.all_to_all(payload, BOTH, 0, 0, tiled=True, axis_index_groups=CORE_Z_...  28 us
    all_to_all x1, blocking collectives, local(): lax.all_to_all(outgoing[:, None], 'dp', split_axis=0, concat_axis=1, tile...  15.2 us
    all_gather x1, waiting for transfers between devices, local(): lax.all_gather(units, 'fsdp', axis=0, tiled=False, axis_index_groups=Z_GR...  13.2 us
    all_to_all x1, waiting for transfers between devices, local(): lax.all_to_all(jnp.broadcast_to(partial[None, None, :], (slabs, 1, slabs)...  12.1 us
    ppermute x1, starting transfers between devices, local(): lax.ppermute(weight, BOTH, CROSS_SWAP)  11.2 us
    pallas_call x1, Pallas kernels, attend(): pl.pallas_call(attend_body, out_shape=jax.ShapeDtypeStruct((2 * Z, 16, HE...  10.1 us
    all_to_all x1, starting transfers between devices, local(): lax.all_to_all(outgoing, 'fsdp', 0, 0, tiled=True, axis_index_groups=Z_GR...  10 us
    ppermute x1, starting transfers between devices, local(): other = lax.ppermute(normed, 'dp', CORE_SWAP)  9.2 us
  transfers between devices with their start and end apart: 12, of which 8 were waited for; matrix products, arithmetic and copies ran while one was open for 5% of the time, Pallas kernels for 2%

profile of v3, /device:TPU:1, one launch (start us, length us, event | category | flops | bytes accessed | tf_op | source)
XLA Modules:
  0.0 200.1 jit_solution(749326209575803854)
XLA Ops:
  7.2 0.1 pad_add_fusion.place_ref
  7.3 0.9 copy-done.4
  8.2 0.9 copy-done.5
  9.1 0.6 unit.1.near
  9.7 4.0 %collective-permute-start = (bf16[128,512]{1,0:T(8,128)(2,1)S(1)}, bf16[128,512]{1,0:T(8,128)(2,1)S(1)}, u32[]{:S(2)}, u32[]{:S(2)}) collective-permute-start(bf16[128,512]{1,0:T(8,128)(2,1)S(1)} %unit.1.near), channel_id=1, source_target_pairs={{0,16},{1,17},{2,18},{3,19},{4,20},{5,21},{6,22},{7,23},{8,24},{9,... | collective-permute-start | bytes 393224 | tf_op jit(solution)/shard_map/ppermute | solution.py:321
  13.7 2.3 %collective-permute-done.far = bf16[128,512]{1,0:T(8,128)(2,1)S(1)} collective-permute-done((bf16[128,512]{1,0:T(8,128)(2,1)S(1)}, bf16[128,512]{1,0:T(8,128)(2,1)S(1)}, u32[]{:S(2)}, u32[]{:S(2)}) %collective-permute-start) | collective-permute-done | bytes 131104 | tf_op jit(solution)/shard_map/ppermute | solution.py:321
  16.1 0.7 pair.1
  16.8 3.4 %collective-permute-start.1 = (bf16[128,2048]{1,0:T(8,128)(2,1)}, bf16[128,2048]{1,0:T(8,128)(2,1)S(1)}, u32[]{:S(2)}, u32[]{:S(2)}) collective-permute-start(bf16[128,2048]{1,0:T(8,128)(2,1)} %near_ref.1), channel_id=1, source_target_pairs={{0,16},{1,17},{2,18},{3,19},{4,20},{5,21},{6,22},{7,23},{8,24},{9,... | collective-permute-start | bytes 1572872 | tf_op jit(solution)/shard_map/ppermute | solution.py:329
  20.2 1.6 copy-done
  21.8 0.7 copy-done.6
  22.5 1.4 open.1
  24.0 2.1 %fusion = f32[256]{0:T(256)S(1)} fusion(bf16[256,4096]{1,0:T(8,128)(2,1)} %bitcast.38), kind=kLoop, calls=%fused_computation.2 | loop fusion | flops 3145472 | bytes 2098176 | tf_op jit(solution)/shard_map/reduce_sum | solution.py:340
  26.2 2.0 fusion.2.normed
  28.2 9.2 %collective-permute-start.5 = (bf16[256,4096]{1,0:T(8,128)(2,1)}, bf16[256,4096]{1,0:T(8,128)(2,1)}, u32[]{:S(2)}, u32[]{:S(2)}) collective-permute-start(bf16[256,4096]{1,0:T(8,128)(2,1)} %fusion.2.normed), channel_id=1, source_target_pairs={{0,32},{32,0},{64,96},{96,64},{128,160},{160,128},{192,224},{224,1... | collective-permute-start | bytes 6291464 | tf_op jit(solution)/shard_map/ppermute | solution.py:342
  37.4 10.0 %all-to-all-start = ((bf16[16,8,128]{2,1,0:T(8,128)(2,1)}), bf16[16,8,128]{2,1,0:T(8,128)(2,1)S(1)}, u32[]{:S(2)}, u32[]{:S(2)}) async-start(bf16[16,8,128]{2,1,0:T(8,128)(2,1)} %get-tuple-element.12), calls=%async_computation | async-start | bytes 65536 | tf_op jit(solution)/shard_map/all_to_all | solution.py:327
  47.4 2.1 %collective-permute-start.2 = (bf16[1,4096]{1,0:T(2,128)(2,1)S(1)}, bf16[1,4096]{1,0:T(2,128)(2,1)S(1)}, u32[]{:S(2)}, u32[]{:S(2)}) collective-permute-start(bf16[1,4096]{1,0:T(2,128)(2,1)S(1)} %get-tuple-element.13.near_ref), channel_id=1, source_target_pairs={{0,16},{1,17},{2,18},{3,19},{4,20},{5,21},{6,22},{7,23},{8,24},{9,... | collective-permute-start | bytes 24584 | tf_op jit(solution)/shard_map/ppermute | solution.py:331
  49.5 2.8 %collective-permute-done.2.far_ref = bf16[1,4096]{1,0:T(2,128)(2,1)S(1)} collective-permute-done((bf16[1,4096]{1,0:T(2,128)(2,1)S(1)}, bf16[1,4096]{1,0:T(2,128)(2,1)S(1)}, u32[]{:S(2)}, u32[]{:S(2)}) %collective-permute-start.2) | collective-permute-done | bytes 8224 | tf_op jit(solution)/shard_map/ppermute | solution.py:331
  52.3 1.4 fill.1.payload
  53.7 5.0 %all-to-all-done.arrived_ref = bf16[16,8,128]{2,1,0:T(8,128)(2,1)S(1)} async-done(((bf16[16,8,128]{2,1,0:T(8,128)(2,1)}), bf16[16,8,128]{2,1,0:T(8,128)(2,1)S(1)}, u32[]{:S(2)}, u32[]{:S(2)}) %all-to-all-start) | async-done | bytes 32800 | tf_op jit(solution)/shard_map/all_to_all | solution.py:327
  58.7 1.0 query.1
  59.7 8.2 %all-to-all-start.1 = ((bf16[32,56,128]{2,1,0:T(8,128)(2,1)}), bf16[32,56,128]{2,1,0:T(8,128)(2,1)S(1)}, u32[]{:S(2)}, u32[]{:S(2)}) async-start(bf16[32,56,128]{2,1,0:T(8,128)(2,1)} %query.1), calls=%async_computation.1 | async-start | bytes 917504 | tf_op jit(solution)/shard_map/all_to_all | solution.py:335
  67.9 2.1 %collective-permute-start.4 = (s32[1]{0:T(128)}, s32[1]{0:T(128)}, u32[]{:S(2)}, u32[]{:S(2)}) collective-permute-start(s32[1]{0:T(128)} %param.11), channel_id=1, source_target_pairs={{0,32},{32,0},{64,96},{96,64},{128,160},{160,128},{192,224},{224,1... | collective-permute-start | bytes 20 | tf_op jit(solution)/shard_map/ppermute | solution.py:330
  70.1 0.2 select_reduce_fusion
  70.3 0.5 fusion.9
  70.8 0.9 pad_maximum_fusion
  71.7 1.3 pad_add_fusion.1.len_ref
  73.0 28.0 %all-to-all-done.1.parts = bf16[32,56,128]{2,1,0:T(8,128)(2,1)S(1)} async-done(((bf16[32,56,128]{2,1,0:T(8,128)(2,1)}), bf16[32,56,128]{2,1,0:T(8,128)(2,1)S(1)}, u32[]{:S(2)}, u32[]{:S(2)}) %all-to-all-start.1) | async-done | bytes 458784 | tf_op jit(solution)/shard_map/all_to_all | solution.py:335
  101.0 13.2 %all-gather.3.cloned.1.call-done = bf16[32,128,512]{2,1,0:T(8,128)(2,1)} async-done(((bf16[2,128,512]{2,1,0:T(8,128)(2,1)}), bf16[32,128,512]{2,1,0:T(8,128)(2,1)}) %all-gather.3.cloned.1.call-update) | async-done | bytes 4194320 | tf_op jit(solution)/shard_map/all_gather | solution.py:322
  114.2 10.1 %attend.1 = bf16[32,16,128]{2,1,0:T(8,128)(2,1)} custom-call(s32[4]{0:T(128)} %copy-done.8, s32[2]{0:T(128)} %pad_add_fusion.1.len_ref, bf16[256,4096]{1,0:T(8,128)(2,1)} %fusion.2.normed, bf16[256,4096]{1,0:T(8,128)(2,1)} %collective-permute-done.5.other, f32[256,128]{1,0:T(8,128)} %get-tuple-element.20.cos_ref, f32[256,128]{1,0:T(8,128)} %get-tuple-element.21.sin_ref, ...), custom_call_target="tpu_custom_call" | custom-call | tf_op jit(solution)/shard_map/attend/pallas_call | solution.py:294
  124.3 7.6 %all-to-all-start.2 = ((bf16[32,16,128]{2,1,0:T(8,128)(2,1)}), bf16[32,16,128]{2,1,0:T(8,128)(2,1)S(1)}, u32[]{:S(2)}, u32[]{:S(2)}) async-start(bf16[32,16,128]{2,1,0:T(8,128)(2,1)} %attend.1), calls=%async_computation.2 | async-start | bytes 262144 | tf_op jit(solution)/shard_map/all_to_all | solution.py:345
  132.0 0.1 fusion.13
  132.0 1.0 slice.4
  133.0 11.2 %collective-permute-start.3 = (bf16[1024,128]{1,0:T(8,128)(2,1)S(1)}, bf16[1024,128]{1,0:T(8,128)(2,1)S(1)}, u32[]{:S(2)}, u32[]{:S(2)}) collective-permute-start(bf16[1024,128]{1,0:T(8,128)(2,1)S(1)} %bitcast.43), channel_id=1, source_target_pairs={{16,32},{17,33},{18,34},{19,35},{20,36},{21,37},{22,38},{23,39},{2... | collective-permute-start | bytes 786440 | tf_op jit(solution)/shard_map/ppermute | solution.py:349
  144.3 0.8 dynamic_slice.16
  145.1 0.2 select_reduce_fusion.1
  145.3 0.8 dynamic-slice_convert_fusion
  146.1 0.3 all-to-all-done.2
  146.4 2.5 %collective-permute-done.3 = bf16[1024,128]{1,0:T(8,128)(2,1)S(1)} collective-permute-done((bf16[1024,128]{1,0:T(8,128)(2,1)S(1)}, bf16[1024,128]{1,0:T(8,128)(2,1)S(1)}, u32[]{:S(2)}, u32[]{:S(2)}) %collective-permute-start.3) | collective-permute-done | bytes 262176 | tf_op jit(solution)/shard_map/ppermute | solution.py:349
  148.9 0.2 fusion.4
  149.1 8.5 %collective-permute-start.6 = (f32[32,128]{1,0:T(8,128)S(1)}, f32[32,128]{1,0:T(8,128)S(1)}, u32[]{:S(2)}, u32[]{:S(2)}) collective-permute-start(f32[32,128]{1,0:T(8,128)S(1)} %dynamic-slice_bitcast_fusion), channel_id=1, source_target_pairs={{0,32},{32,0},{64,96},{96,64},{128,160},{160,128},{192,224},{224,1... | collective-permute-start | bytes 49160 | tf_op jit(solution)/shard_map/ppermute | solution.py:359
  157.6 0.8 select_bitcast_fusion
  158.4 0.1 multiply_reduce_fusion
  158.5 0.6 broadcast_in_dim.17
  159.2 6.0 %all-to-all-start.3 = ((f32[32,1,32]{2,1,0:T(1,128)}), f32[32,1,32]{2,1,0:T(1,128)S(1)}, u32[]{:S(2)}, u32[]{:S(2)}) async-start(f32[32,1,32]{2,1,0:T(1,128)} %broadcast_in_dim.17), calls=%async_computation.3 | async-start | bytes 32768 | tf_op jit(solution)/shard_map/all_to_all | solution.py:363
  165.2 12.1 %all-to-all-done.3 = f32[32,1,32]{2,1,0:T(1,128)S(1)} async-done(((f32[32,1,32]{2,1,0:T(1,128)}), f32[32,1,32]{2,1,0:T(1,128)S(1)}, u32[]{:S(2)}, u32[]{:S(2)}) %all-to-all-start.3) | async-done | bytes 4128 | tf_op jit(solution)/shard_map/all_to_all | solution.py:363
  177.3 0.2 fusion.3
  177.5 15.2 %all_to_all.32 = bf16[16,1,4,128]{3,2,1,0:T(4,128)(2,1)S(1)} all-to-all(bf16[16,1,4,128]{3,2,1,0:T(4,128)(2,1)S(1)} %copy.31), channel_id=1, replica_groups=mesh['dp'=16,'fsdp'=32] {'dp'}, dimensions={0} | all-to-all | bytes 32768 | tf_op jit(solution)/shard_map/all_to_all | solution.py:382
  192.7 0.6 copy.37
  (40 shorter events, 0.4 us)
Async XLA Ops:
  6.5 19.6 %copy-start.7 = (f32[4096]{0:T(1024)S(1)}, f32[4096]{0:T(1024)}, u32[]{:S(2)}) copy-start(f32[4096]{0:T(1024)} %param.14) | copy-start | bytes 49156
  6.5 107.7 %all-gather.3.cloned.1.call-start = ((), (), s32[]{:S(2)}) async-start(), calls=%async_computation.5 | async-start | bytes 4456448 | tf_op jit(solution)/shard_map/all_gather | solution.py:322
  7.3 0.9 copy-start.4
  8.2 0.9 copy-start.5
  9.1 43.2 %copy-start.8 = (s32[4]{0:T(128)}, s32[4]{0:T(128)S(1)}, u32[]{:S(2)}) copy-start(s32[4]{0:T(128)S(1)} %pad_add_fusion.place_ref) | copy-start | bytes 52
  9.7 6.4 %collective-permute-start = (bf16[128,512]{1,0:T(8,128)(2,1)S(1)}, bf16[128,512]{1,0:T(8,128)(2,1)S(1)}, u32[]{:S(2)}, u32[]{:S(2)}) collective-permute-start(bf16[128,512]{1,0:T(8,128)(2,1)S(1)} %unit.1.near), channel_id=1, source_target_pairs={{0,16},{1,17},{2,18},{3,19},{4,20},{5,21},{6,22},{7,23},{8,24},{9,... | collective-permute-start | bytes 393224 | tf_op jit(solution)/shard_map/ppermute | solution.py:321
  16.8 41.9 %collective-permute-start.1 = (bf16[128,2048]{1,0:T(8,128)(2,1)}, bf16[128,2048]{1,0:T(8,128)(2,1)S(1)}, u32[]{:S(2)}, u32[]{:S(2)}) collective-permute-start(bf16[128,2048]{1,0:T(8,128)(2,1)} %near_ref.1), channel_id=1, source_target_pairs={{0,16},{1,17},{2,18},{3,19},{4,20},{5,21},{6,22},{7,23},{8,24},{9,... | collective-permute-start | bytes 1572872 | tf_op jit(solution)/shard_map/ppermute | solution.py:329
  20.2 1.6 copy-start
  21.8 0.7 copy-start.6
  22.5 3.7 %copy-start.1 = (bf16[1,256,4096]{2,1,0:T(8,128)(2,1)S(1)}, bf16[1,256,4096]{2,1,0:T(8,128)(2,1)}, u32[]{:S(2)}) copy-start(bf16[1,256,4096]{2,1,0:T(8,128)(2,1)} %hidden) | copy-start | bytes 6291460
  22.5 29.8 %copy-start.2 = (bf16[64,4096]{1,0:T(8,128)(2,1)S(1)}, bf16[64,4096]{1,0:T(8,128)(2,1)}, u32[]{:S(2)}) copy-start(bf16[64,4096]{1,0:T(8,128)(2,1)} %w_out_ref.1) | copy-start | bytes 1572868
  24.0 34.7 %copy-start.3 = (bf16[128,2048]{1,0:T(8,128)(2,1)S(1)}, bf16[128,2048]{1,0:T(8,128)(2,1)}, u32[]{:S(2)}) copy-start(bf16[128,2048]{1,0:T(8,128)(2,1)} %near_ref.1) | copy-start | bytes 1572868
  26.1 44.0 %copy-start.10 = (s32[1024]{0:T(1024)S(1)}, s32[1024]{0:T(1024)}, u32[]{:S(2)}) copy-start(s32[1024]{0:T(1024)} %param.13) | copy-start | bytes 12292
  26.1 44.0 %copy-start.11 = (s32[32]{0:T(128)S(1)}, s32[32]{0:T(128)}, u32[]{:S(2)}) copy-start(s32[32]{0:T(128)} %param.12) | copy-start | bytes 388
  28.2 44.8 %collective-permute-start.5 = (bf16[256,4096]{1,0:T(8,128)(2,1)}, bf16[256,4096]{1,0:T(8,128)(2,1)}, u32[]{:S(2)}, u32[]{:S(2)}) collective-permute-start(bf16[256,4096]{1,0:T(8,128)(2,1)} %fusion.2.normed), channel_id=1, source_target_pairs={{0,32},{32,0},{64,96},{96,64},{128,160},{160,128},{192,224},{224,1... | collective-permute-start | bytes 6291464 | tf_op jit(solution)/shard_map/ppermute | solution.py:342
  37.4 21.3 %all-to-all-start = ((bf16[16,8,128]{2,1,0:T(8,128)(2,1)}), bf16[16,8,128]{2,1,0:T(8,128)(2,1)S(1)}, u32[]{:S(2)}, u32[]{:S(2)}) async-start(bf16[16,8,128]{2,1,0:T(8,128)(2,1)} %get-tuple-element.12), calls=%async_computation | async-start | bytes 65536 | tf_op jit(solution)/shard_map/all_to_all | solution.py:327
  47.4 4.9 %collective-permute-start.2 = (bf16[1,4096]{1,0:T(2,128)(2,1)S(1)}, bf16[1,4096]{1,0:T(2,128)(2,1)S(1)}, u32[]{:S(2)}, u32[]{:S(2)}) collective-permute-start(bf16[1,4096]{1,0:T(2,128)(2,1)S(1)} %get-tuple-element.13.near_ref), channel_id=1, source_target_pairs={{0,16},{1,17},{2,18},{3,19},{4,20},{5,21},{6,22},{7,23},{8,24},{9,... | collective-permute-start | bytes 24584 | tf_op jit(solution)/shard_map/ppermute | solution.py:331
  59.7 41.3 %all-to-all-start.1 = ((bf16[32,56,128]{2,1,0:T(8,128)(2,1)}), bf16[32,56,128]{2,1,0:T(8,128)(2,1)S(1)}, u32[]{:S(2)}, u32[]{:S(2)}) async-start(bf16[32,56,128]{2,1,0:T(8,128)(2,1)} %query.1), calls=%async_computation.1 | async-start | bytes 917504 | tf_op jit(solution)/shard_map/all_to_all | solution.py:335
  67.9 3.8 %collective-permute-start.4 = (s32[1]{0:T(128)}, s32[1]{0:T(128)}, u32[]{:S(2)}, u32[]{:S(2)}) collective-permute-start(s32[1]{0:T(128)} %param.11), channel_id=1, source_target_pairs={{0,32},{32,0},{64,96},{96,64},{128,160},{160,128},{192,224},{224,1... | collective-permute-start | bytes 20 | tf_op jit(solution)/shard_map/ppermute | solution.py:330
  101.0 13.2 %copy-start.9 = (bf16[32,56,128]{2,1,0:T(8,128)(2,1)}, bf16[32,56,128]{2,1,0:T(8,128)(2,1)S(1)}, u32[]{:S(2)}) copy-start(bf16[32,56,128]{2,1,0:T(8,128)(2,1)S(1)} %all-to-all-done.1.parts) | copy-start | bytes 1376260
  124.3 22.0 %all-to-all-start.2 = ((bf16[32,16,128]{2,1,0:T(8,128)(2,1)}), bf16[32,16,128]{2,1,0:T(8,128)(2,1)S(1)}, u32[]{:S(2)}, u32[]{:S(2)}) async-start(bf16[32,16,128]{2,1,0:T(8,128)(2,1)} %attend.1), calls=%async_computation.2 | async-start | bytes 262144 | tf_op jit(solution)/shard_map/all_to_all | solution.py:345
  133.0 15.9 %collective-permute-start.3 = (bf16[1024,128]{1,0:T(8,128)(2,1)S(1)}, bf16[1024,128]{1,0:T(8,128)(2,1)S(1)}, u32[]{:S(2)}, u32[]{:S(2)}) collective-permute-start(bf16[1024,128]{1,0:T(8,128)(2,1)S(1)} %bitcast.43), channel_id=1, source_target_pairs={{16,32},{17,33},{18,34},{19,35},{20,36},{21,37},{22,38},{23,39},{2... | collective-permute-start | bytes 786440 | tf_op jit(solution)/shard_map/ppermute | solution.py:349
  149.1 9.3 %collective-permute-start.6 = (f32[32,128]{1,0:T(8,128)S(1)}, f32[32,128]{1,0:T(8,128)S(1)}, u32[]{:S(2)}, u32[]{:S(2)}) collective-permute-start(f32[32,128]{1,0:T(8,128)S(1)} %dynamic-slice_bitcast_fusion), channel_id=1, source_target_pairs={{0,32},{32,0},{64,96},{96,64},{128,160},{160,128},{192,224},{224,1... | collective-permute-start | bytes 49160 | tf_op jit(solution)/shard_map/ppermute | solution.py:359
  159.2 18.1 %all-to-all-start.3 = ((f32[32,1,32]{2,1,0:T(1,128)}), f32[32,1,32]{2,1,0:T(1,128)S(1)}, u32[]{:S(2)}, u32[]{:S(2)}) async-start(f32[32,1,32]{2,1,0:T(1,128)} %broadcast_in_dim.17), calls=%async_computation.3 | async-start | bytes 32768 | tf_op jit(solution)/shard_map/all_to_all | solution.py:363
Sparse Core Ops, SparseCore 0:
  16.9 97.2 all-gather.2

commit v4 on v3

--- a/solution.py
+++ b/solution.py
@@ -51,6 +51,22 @@
 Y_LO_SWAP = [(i, i ^ Z) for i in range(32)]
 
 
+def y_shift(step):
+    pairs = []
+    for y in range(4):
+        to = (y + step) % 4
+        for x in range(X):
+            for z in range(Z):
+                for c in range(2):
+                    pairs.append(
+                        (
+                            dp_index(y // 2, x, c) * 32 + fsdp_index(y % 2, z),
+                            dp_index(to // 2, x, c) * 32 + fsdp_index(to % 2, z),
+                        )
+                    )
+    return pairs
+
+
 def rope_tables(positions, head_width):
     halfway = head_width // 2
     frequency = 10000.0 ** (-jnp.arange(halfway, dtype=f32) * 2.0 / head_width)
@@ -84,26 +100,6 @@
         compiler_params=pltpu.CompilerParams(vmem_limit_bytes=1 << 20),
         name="unit",
     )(place, w_key, w_value)
-
-
-def pair_body(near, far, out, sem):
-    copies = [pltpu.make_async_copy(rows, out.at[k], sem.at[k]) for k, rows in enumerate((near, far))]
-    for copy in copies:
-        copy.start()
-    for copy in copies:
-        copy.wait()
-
-
-def pair(near, far):
-    return pl.pallas_call(
-        pair_body,
-        out_shape=jax.ShapeDtypeStruct((2, *near.shape), bf16),
-        in_specs=[HBM, HBM],
-        out_specs=HBM,
-        scratch_shapes=[pltpu.SemaphoreType.DMA((2,))],
-        compiler_params=pltpu.CompilerParams(vmem_limit_bytes=1 << 20),
-        name="pair",
-    )(near, far)
 
 
 def open_body(place_ref, hidden, gain_ref, out_ref, last_ref, block, sem):
@@ -216,26 +212,25 @@
     )(arrived, near, far, payload)
 
 
-def attend_body(place_ref, len_ref, normed, other, cos_ref, sin_ref, parts, gathered, out_ref, w_ref, q_ref, rows_ref, sem, q_sem):
+def load_rows(own, low, high, w_ref, kind, y_lo, sem):
+    return [
+        pltpu.make_async_copy(own.at[:, :, pl.ds(kind * 256, 256)], w_ref.at[y_lo], sem.at[0]),
+        pltpu.make_async_copy(low, w_ref.at[1 - y_lo, pl.ds(0, Z // 2)], sem.at[1]),
+        pltpu.make_async_copy(high, w_ref.at[1 - y_lo, pl.ds(Z // 2, Z // 2)], sem.at[2]),
+    ]
+
+
+def attend_body(
+    place_ref, len_ref, normed, other, cos_ref, sin_ref, parts, own, low, high, out_ref, w_ref, q_ref, rows_ref, sem, q_sem
+):
+    core, y_lo = place_ref[2], place_ref[3]
+    copies = load_rows(own, low, high, w_ref, 0, y_lo, sem)
     fetch = pltpu.make_async_copy(parts.at[:, pl.ds(QUERY_ROW, 16), :], q_ref, q_sem.at[0])
-    fetch.start()
     fills = [
         pltpu.make_async_copy(rows, rows_ref.at[p], q_sem.at[1 + p])
         for p, rows in enumerate((normed, other))
     ]
-    core, y_lo = place_ref[2], place_ref[3]
-    copies = [
-        [
-            pltpu.make_async_copy(
-                gathered.at[:, n, :, pl.ds(kind * 256, 256)],
-                w_ref.at[kind, y_lo if n == 0 else 1 - y_lo],
-                sem.at[kind, n],
-            )
-            for n in range(2)
-        ]
-        for kind in range(2)
-    ]
-    for copy in fills[:1] + copies[0] + fills[1:] + copies[1]:
+    for copy in [fetch] + fills[:1] + copies + fills[1:]:
         copy.start()
     cosine, sine = cos_ref[...], sin_ref[...]
     fetch.wait()
@@ -249,10 +244,9 @@
             pl.ds(last, 1), :
         ]
         queries.append((turned * (1.0 / math.sqrt(HEAD))).astype(bf16))
-    for copy in copies[0]:
+    for copy in copies:
         copy.wait()
-    weight = w_ref[0].reshape(Y_LO * Z * HEAD, 256)
-    sums = []
+    weight = w_ref[...].reshape(Y_LO * Z * HEAD, 256)
     for p in range(2):
         fills[p].wait()
         rows = rows_ref[p]
@@ -272,15 +266,40 @@
         scores = jnp.where(place < len_ref[p], scores, -jnp.inf)
         powers = jnp.exp(scores - jnp.max(scores, axis=-1, keepdims=True))
         weights = (powers / jnp.sum(powers, axis=-1, keepdims=True)).astype(bf16)
-        sums.append(jnp.dot(weights, rows, preferred_element_type=f32))
-    u = jnp.concatenate(sums, axis=0)
+        out_ref[p * 8 : (p + 1) * 8, :] = jnp.dot(weights, rows, preferred_element_type=f32)
+
+
+def attend(place, lengths, normed, other, cosine, sine, parts, pieces):
+    return pl.pallas_call(
+        attend_body,
+        out_shape=jax.ShapeDtypeStruct((16, normed.shape[1]), f32),
+        in_specs=[SMEM, SMEM, HBM, HBM, VMEM, VMEM] + [HBM] * 4,
+        out_specs=VMEM,
+        scratch_shapes=[
+            pltpu.VMEM((Y_LO, Z, HEAD, 256), bf16),
+            pltpu.VMEM((2 * Z, 16, HEAD), bf16),
+            pltpu.VMEM((2, *normed.shape), bf16),
+            pltpu.SemaphoreType.DMA((3,)),
+            pltpu.SemaphoreType.DMA((3,)),
+        ],
+        compiler_params=pltpu.CompilerParams(vmem_limit_bytes=48 << 20),
+        name="attend",
+    )(place, lengths, normed, other, cosine, sine, parts, *pieces)
+
+
+def weigh_body(place_ref, u_ref, own, low, high, out_ref, w_ref, sem):
+    core, y_lo = place_ref[2], place_ref[3]
+    copies = load_rows(own, low, high, w_ref, 1, y_lo, sem)
+    for copy in copies:
+        copy.start()
+    u = u_ref[...]
     first = u.astype(bf16)
     rest = u - first.astype(f32)
     second = rest.astype(bf16)
     third = (rest - second.astype(f32)).astype(bf16)
-    for copy in copies[1]:
+    for copy in copies:
         copy.wait()
-    weight = w_ref[1].reshape(Y_LO * Z * HEAD, 256)
+    weight = w_ref[...].reshape(Y_LO * Z * HEAD, 256)
     parts = [jnp.dot(t, weight, preferred_element_type=f32) for t in (third, second, first)]
     total = parts[0] + parts[1] + parts[2]
     head = lax.broadcasted_iota(jnp.int32, (16, HEAD), 0)
@@ -290,22 +309,19 @@
     out_ref[...] = jnp.broadcast_to(context[None], out_ref.shape)
 
 
-def attend(place, lengths, normed, other, cosine, sine, parts, gathered):
-    return pl.pallas_call(
-        attend_body,
+def weigh(place, u, pieces):
+    return pl.pallas_call(
+        weigh_body,
         out_shape=jax.ShapeDtypeStruct((2 * Z, 16, HEAD), bf16),
-        in_specs=[SMEM, SMEM, HBM, HBM, VMEM, VMEM, HBM, HBM],
+        in_specs=[SMEM, VMEM, HBM, HBM, HBM],
         out_specs=VMEM,
         scratch_shapes=[
-            pltpu.VMEM((2, Y_LO, Z, HEAD, 256), bf16),
-            pltpu.VMEM((2 * Z, 16, HEAD), bf16),
-            pltpu.VMEM((2, *normed.shape), bf16),
-            pltpu.SemaphoreType.DMA((2, 2)),
+            pltpu.VMEM((Y_LO, Z, HEAD, 256), bf16),
             pltpu.SemaphoreType.DMA((3,)),
         ],
-        compiler_params=pltpu.CompilerParams(vmem_limit_bytes=60 << 20),
-        name="attend",
-    )(place, lengths, normed, other, cosine, sine, parts, gathered)
+        compiler_params=pltpu.CompilerParams(vmem_limit_bytes=32 << 20),
+        name="weigh",
+    )(place, u, *pieces)
 
 
 def local(
@@ -318,31 +334,26 @@
     place = jnp.stack([lengths[0] - 1, x, core, y_lo]).astype(jnp.int32)
 
     unit = core_unit(place, w_key, w_value)
-    units = pair(unit, lax.ppermute(unit, "fsdp", Y_LO_SWAP))
-    gathered = lax.all_gather(units, "fsdp", axis=0, tiled=False, axis_index_groups=Z_GROUPS)
+    gathered = lax.all_gather(unit, "fsdp", axis=0, tiled=False, axis_index_groups=Z_GROUPS)
 
     unit, hidden = lax.optimization_barrier((unit, hidden))
     outgoing, last_input = open_payload(place, hidden, attn_gain)
-    units, outgoing = lax.optimization_barrier((units, outgoing))
     arrived = lax.all_to_all(outgoing, "fsdp", 0, 0, tiled=True, axis_index_groups=Z_GROUPS)
-
     w_query_other = lax.ppermute(w_query, "fsdp", Y_LO_SWAP)
-    both_lengths = jnp.concatenate([lengths, lax.ppermute(lengths, "dp", CORE_SWAP)])
     last_other = lax.ppermute(last_input, "fsdp", Y_LO_SWAP)
     payload = fill_payload(place, w_out, last_input, last_other)
 
     payload = query_payload(arrived, w_query, w_query_other, payload)
     parts = lax.all_to_all(payload, BOTH, 0, 0, tiled=True, axis_index_groups=CORE_Z_GROUPS)
 
-    rows, _ = lax.optimization_barrier((hidden[0], outgoing))
+    rows, lengths, _ = lax.optimization_barrier((hidden[0], lengths, payload))
+    both_lengths = jnp.concatenate([lengths, lax.ppermute(lengths, "dp", CORE_SWAP)])
     floats = rows.astype(f32)
     normed = (
         floats * lax.rsqrt(jnp.mean(floats * floats, axis=-1, keepdims=True) + 1e-05) * attn_gain
     ).astype(bf16)
     other = lax.ppermute(normed, "dp", CORE_SWAP)
     cosine, sine = rope_tables(jnp.arange(seq_len), HEAD)
-    context = attend(place, both_lengths, normed, other, cosine, sine, parts, gathered)
-    contexts = lax.all_to_all(context, "fsdp", 0, 0, tiled=True)
 
     weight = jnp.transpose(parts[:, :QUERY_ROW].reshape(2, Z, 32, HEAD), (1, 0, 2, 3))
     weight = weight.reshape(2 * Z * 32, HEAD)
@@ -350,6 +361,20 @@
     inputs = lax.dynamic_slice(parts, (core * Z, HIDDEN_ROW, 0), (Z, 2, HEAD)).astype(f32)
     inputs = jnp.where(y_lo == 0, inputs, inputs[:, ::-1])
     inputs = jnp.transpose(inputs, (1, 0, 2)).reshape(2 * Z, HEAD)
+
+    half = Z // 2
+    key_rows, value_rows = gathered[:, :, :256], gathered[:, :, 256:]
+    key_low = lax.ppermute(key_rows[:half], BOTH, y_shift(-1))
+    key_high = lax.ppermute(key_rows[half:], BOTH, y_shift(1))
+    value_low = lax.ppermute(value_rows[:half], BOTH, y_shift(-1))
+    value_high = lax.ppermute(value_rows[half:], BOTH, y_shift(1))
+
+    place, weight, inputs = lax.optimization_barrier((place, weight, inputs))
+    u = attend(
+        place, both_lengths, normed, other, cosine, sine, parts, (gathered, key_low, key_high)
+    )
+    context = weigh(place, u, (gathered, value_low, value_high))
+    contexts = lax.all_to_all(context, "fsdp", 0, 0, tiled=True)
 
     slabs = width // HEAD
     contexts = contexts.reshape(slabs, 2, 8 * HEAD)

time: 201 us -> 208 us (1.035)
  waiting for transfers between devices: 66.2 us -> 74.6 us
  other arithmetic: 9.13 us -> 5.64 us
  starting transfers between devices: 72.3 us -> 69.9 us
    all_to_all x1, waiting for transfers between devices: 0.26 us -> 14.1 us  [local(): contexts = lax.all_to_all(context, 'fsdp', 0, 0, tiled=True)]
    ppermute x1, starting transfers between devices: 11.2 us -> 1.92 us  [local(): lax.ppermute(weight, BOTH, CROSS_SWAP)]
    ppermute x1 -> x4, starting transfers between devices: 4.03 us -> 13 us  [the longest x1 4.57 us: local(): key_low = lax.ppermute(key_rows[:half], BOTH, y_shift(-1))]
    all_gather x1, waiting for transfers between devices: 13.2 us -> 5.23 us  [local(): lax.all_gather(unit, 'fsdp', axis=0, tiled=False, axis_index_groups=Z_GRO...]
    ppermute x1 -> x4, waiting for transfers between devices: 2.34 us -> 9.89 us  [the longest x1 8.87 us: local(): key_high = lax.ppermute(key_rows[half:], BOTH, y_shift(1))]
    ppermute x1, starting transfers between devices: 9.2 us -> 2.13 us  [local(): other = lax.ppermute(normed, 'dp', CORE_SWAP)]
    all_to_all x1, starting transfers between devices: 10 us -> 15 us  [local(): lax.all_to_all(outgoing, 'fsdp', 0, 0, tiled=True, axis_index_groups=Z_GR...]
    all_to_all x1, waiting for transfers between devices: 28 us -> 24 us  [local(): lax.all_to_all(payload, BOTH, 0, 0, tiled=True, axis_index_groups=CORE_Z_...]
  transfers between devices with their start and end apart: 12 -> 15, of which waited for: 8 -> 9; matrix products, arithmetic and copies ran while one was open for 5% -> 4% of each run, Pallas kernels for 2% -> 6%
where the time goes in v4:
time: 208 us; the launch traced here: 207 us
  waiting for transfers between devices  74.6 us (36%)
  starting transfers between devices  69.9 us (34%)
  blocking collectives  16.8 us (8%)
  Pallas kernels  15.7 us (8%)
  between operations  14.5 us (7%)
  local copies, waits for them, and re-layouts  9.19 us (4%)
  other arithmetic  5.64 us (3%)
    all_to_all x1, waiting for transfers between devices, local(): lax.all_to_all(payload, BOTH, 0, 0, tiled=True, axis_index_groups=CORE_Z_...  24 us
    all_to_all x1, blocking collectives, local(): lax.all_to_all(outgoing[:, None], 'dp', split_axis=0, concat_axis=1, tile...  16.8 us
    all_to_all x1, starting transfers between devices, local(): lax.all_to_all(outgoing, 'fsdp', 0, 0, tiled=True, axis_index_groups=Z_GR...  15 us
    all_to_all x1, waiting for transfers between devices, local(): contexts = lax.all_to_all(context, 'fsdp', 0, 0, tiled=True)  14.1 us
    all_to_all x1, waiting for transfers between devices, local(): lax.all_to_all(jnp.broadcast_to(partial[None, None, :], (slabs, 1, slabs)...  12.1 us
    ppermute x1, starting transfers between devices, local(): residual = inputs + (kept + lax.ppermute(given, 'dp', CORE_SWAP))  11 us
    all_to_all x1, starting transfers between devices, local(): lax.all_to_all(payload, BOTH, 0, 0, tiled=True, axis_index_groups=CORE_Z_...  8.91 us
    ppermute x1, waiting for transfers between devices, local(): key_high = lax.ppermute(key_rows[half:], BOTH, y_shift(1))  8.87 us
  transfers between devices with their start and end apart: 15, of which 9 were waited for; matrix products, arithmetic and copies ran while one was open for 4% of the time, Pallas kernels for 6%

profile of v4, /device:TPU:1, one launch (start us, length us, event | category | flops | bytes accessed | tf_op | source)
XLA Modules:
  0.0 206.7 jit_solution(12012900832614084022)
XLA Ops:
  7.3 0.9 copy-done.5
  8.2 0.9 copy-done.6
  9.1 1.2 unit.1
  10.4 4.1 %collective-permute-start = (bf16[128,2048]{1,0:T(8,128)(2,1)}, bf16[128,2048]{1,0:T(8,128)(2,1)}, u32[]{:S(2)}, u32[]{:S(2)}) collective-permute-start(bf16[128,2048]{1,0:T(8,128)(2,1)} %near_ref.1), channel_id=1, source_target_pairs={{0,16},{1,17},{2,18},{3,19},{4,20},{5,21},{6,22},{7,23},{8,24},{9,... | collective-permute-start | bytes 1572872 | tf_op jit(solution)/shard_map/ppermute | solution.py:342
  14.5 1.6 copy-done
  16.1 0.7 copy-done.7
  16.8 1.4 open.1
  18.2 15.0 %all-to-all-start = ((bf16[16,8,128]{2,1,0:T(8,128)(2,1)}), bf16[16,8,128]{2,1,0:T(8,128)(2,1)S(1)}, u32[]{:S(2)}, u32[]{:S(2)}) async-start(bf16[16,8,128]{2,1,0:T(8,128)(2,1)} %get-tuple-element.14), calls=%async_computation | async-start | bytes 65536 | tf_op jit(solution)/shard_map/all_to_all | solution.py:341
  33.3 2.1 %collective-permute-start.1 = (bf16[1,4096]{1,0:T(2,128)(2,1)S(1)}, bf16[1,4096]{1,0:T(2,128)(2,1)S(1)}, u32[]{:S(2)}, u32[]{:S(2)}) collective-permute-start(bf16[1,4096]{1,0:T(2,128)(2,1)S(1)} %get-tuple-element.15.near_ref), channel_id=1, source_target_pairs={{0,16},{1,17},{2,18},{3,19},{4,20},{5,21},{6,22},{7,23},{8,24},{9,... | collective-permute-start | bytes 24584 | tf_op jit(solution)/shard_map/ppermute | solution.py:343
  35.4 2.8 %collective-permute-done.1.far_ref = bf16[1,4096]{1,0:T(2,128)(2,1)S(1)} collective-permute-done((bf16[1,4096]{1,0:T(2,128)(2,1)S(1)}, bf16[1,4096]{1,0:T(2,128)(2,1)S(1)}, u32[]{:S(2)}, u32[]{:S(2)}) %collective-permute-start.1) | collective-permute-done | bytes 8224 | tf_op jit(solution)/shard_map/ppermute | solution.py:343
  38.2 1.4 fill.1.payload
  39.6 5.2 %all-to-all-done.arrived_ref = bf16[16,8,128]{2,1,0:T(8,128)(2,1)S(1)} async-done(((bf16[16,8,128]{2,1,0:T(8,128)(2,1)}), bf16[16,8,128]{2,1,0:T(8,128)(2,1)S(1)}, u32[]{:S(2)}, u32[]{:S(2)}) %all-to-all-start) | async-done | bytes 32800 | tf_op jit(solution)/shard_map/all_to_all | solution.py:341
  44.8 2.1 %query.1 = bf16[32,56,128]{2,1,0:T(8,128)(2,1)} custom-call(bf16[16,8,128]{2,1,0:T(8,128)(2,1)S(1)} %all-to-all-done.arrived_ref, bf16[128,2048]{1,0:T(8,128)(2,1)S(1)} %copy-done.4, bf16[128,2048]{1,0:T(8,128)(2,1)} %collective-permute-done.far_ref, bf16[32,56,128]{2,1,0:T(8,128)(2,1)} %fill.1.payload), custom_call_target="tpu_custom_call", output_to_operand_aliasing={{}: (3, {})} | custom-call | tf_op jit(solution)/shard_map/query/pallas_call | solution.py:199
  46.9 8.9 %all-to-all-start.1 = ((bf16[32,56,128]{2,1,0:T(8,128)(2,1)}), bf16[32,56,128]{2,1,0:T(8,128)(2,1)S(1)}, u32[]{:S(2)}, u32[]{:S(2)}) async-start(bf16[32,56,128]{2,1,0:T(8,128)(2,1)} %query.1), calls=%async_computation.1 | async-start | bytes 917504 | tf_op jit(solution)/shard_map/all_to_all | solution.py:347
  55.8 0.5 fusion
  56.3 1.9 fusion.2.normed
  58.3 2.1 %collective-permute-start.4 = (bf16[256,4096]{1,0:T(8,128)(2,1)}, bf16[256,4096]{1,0:T(8,128)(2,1)}, u32[]{:S(2)}, u32[]{:S(2)}) collective-permute-start(bf16[256,4096]{1,0:T(8,128)(2,1)} %fusion.2.normed), channel_id=1, source_target_pairs={{0,32},{32,0},{64,96},{96,64},{128,160},{160,128},{192,224},{224,1... | collective-permute-start | bytes 6291464 | tf_op jit(solution)/shard_map/ppermute | solution.py:355
  60.4 0.5 fusion.7
  61.0 0.1 pad_maximum_fusion
  61.1 2.2 %collective-permute-start.3 = (s32[1]{0:T(128)}, s32[1]{0:T(128)}, u32[]{:S(2)}, u32[]{:S(2)}) collective-permute-start(s32[1]{0:T(128)} %param.11), channel_id=1, source_target_pairs={{0,32},{32,0},{64,96},{96,64},{128,160},{160,128},{192,224},{224,1... | collective-permute-start | bytes 20 | tf_op jit(solution)/shard_map/ppermute | solution.py:350
  63.3 1.3 collective-permute-done.3
  64.7 0.7 pad_add_fusion.1.len_ref
  65.4 24.0 %all-to-all-done.1.parts = bf16[32,56,128]{2,1,0:T(8,128)(2,1)S(1)} async-done(((bf16[32,56,128]{2,1,0:T(8,128)(2,1)}), bf16[32,56,128]{2,1,0:T(8,128)(2,1)S(1)}, u32[]{:S(2)}, u32[]{:S(2)}) %all-to-all-start.1) | async-done | bytes 458784 | tf_op jit(solution)/shard_map/all_to_all | solution.py:347
  89.5 1.9 collective-permute-start.2
  91.4 5.2 %all-gather.3.cloned.1.call-done = bf16[2048,512]{1,0:T(8,128)(2,1)} async-done(((bf16[128,512]{1,0:T(8,128)(2,1)}), bf16[2048,512]{1,0:T(8,128)(2,1)}) %all-gather.3.cloned.1.call-update) | async-done | bytes 2097168 | tf_op jit(solution)/shard_map/all_gather | solution.py:337
  96.6 2.9 %fusion.18 = (bf16[8,128,256]{2,1,0:T(8,128)(2,1)}, bf16[8,128,256]{2,1,0:T(8,128)(2,1)}, bf16[8,128,256]{2,1,0:T(8,128)(2,1)}, bf16[8,128,256]{2,1,0:T(8,128)(2,1)}) fusion(bf16[16,128,512]{2,1,0:T(8,128)(2,1)} %bitcast.39), kind=kLoop, calls=%fused_computation.42 | loop fusion | bytes 4194304 | tf_op jit(solution)/shard_map/slice | solution.py:370
  99.5 2.9 %collective-permute-start.8 = (bf16[8,128,256]{2,1,0:T(8,128)(2,1)}, bf16[8,128,256]{2,1,0:T(8,128)(2,1)S(1)}, u32[]{:S(2)}, u32[]{:S(2)}) collective-permute-start(bf16[8,128,256]{2,1,0:T(8,128)(2,1)} %get-tuple-element.23), channel_id=1, source_target_pairs={{0,16},{32,48},{1,17},{33,49},{2,18},{34,50},{3,19},{35,51},{4,20}... | collective-permute-start | bytes 1572872 | tf_op jit(solution)/shard_map/ppermute | solution.py:370
  102.4 3.6 %collective-permute-start.7 = (bf16[8,128,256]{2,1,0:T(8,128)(2,1)}, bf16[8,128,256]{2,1,0:T(8,128)(2,1)S(1)}, u32[]{:S(2)}, u32[]{:S(2)}) collective-permute-start(bf16[8,128,256]{2,1,0:T(8,128)(2,1)} %get-tuple-element.24), channel_id=1, source_target_pairs={{0,272},{32,304},{1,273},{33,305},{2,274},{34,306},{3,275},{35,307... | collective-permute-start | bytes 1572872 | tf_op jit(solution)/shard_map/ppermute | solution.py:369
  106.0 1.9 collective-permute-start.6
  108.0 4.6 %collective-permute-start.5 = (bf16[8,128,256]{2,1,0:T(8,128)(2,1)}, bf16[8,128,256]{2,1,0:T(8,128)(2,1)S(1)}, u32[]{:S(2)}, u32[]{:S(2)}) collective-permute-start(bf16[8,128,256]{2,1,0:T(8,128)(2,1)} %get-tuple-element.26), channel_id=1, source_target_pairs={{0,272},{32,304},{1,273},{33,305},{2,274},{34,306},{3,275},{35,307... | collective-permute-start | bytes 1572872 | tf_op jit(solution)/shard_map/ppermute | solution.py:367
  112.7 1.0 broadcast_select_fusion
  113.7 8.9 %collective-permute-done.6.high = bf16[8,128,256]{2,1,0:T(8,128)(2,1)S(1)} collective-permute-done((bf16[8,128,256]{2,1,0:T(8,128)(2,1)}, bf16[8,128,256]{2,1,0:T(8,128)(2,1)S(1)}, u32[]{:S(2)}, u32[]{:S(2)}) %collective-permute-start.6) | collective-permute-done | bytes 524320 | tf_op jit(solution)/shard_map/ppermute | solution.py:368
  122.6 1.0 collective-permute-done.5.low
  123.6 7.2 %attend.1.u_ref = f32[16,4096]{1,0:T(8,128)S(1)} custom-call(s32[4]{0:T(128)S(1)} %pad_add_fusion.place_ref, s32[2]{0:T(128)S(1)} %pad_add_fusion.1.len_ref, bf16[256,4096]{1,0:T(8,128)(2,1)} %fusion.2.normed, bf16[256,4096]{1,0:T(8,128)(2,1)} %collective-permute-done.4.other, f32[256,128]{1,0:T(8,128)S(1)} %get-tuple-element.30.cos_ref, ...), custom_call_target="tpu_custom_call" | custom-call | tf_op jit(solution)/shard_map/attend/pallas_call | solution.py:273
  130.8 2.4 %weigh.1 = bf16[32,16,128]{2,1,0:T(8,128)(2,1)} custom-call(s32[4]{0:T(128)S(1)} %pad_add_fusion.place_ref, f32[16,4096]{1,0:T(8,128)S(1)} %attend.1.u_ref, bf16[16,128,512]{2,1,0:T(8,128)(2,1)S(1)} %bitcast.41, bf16[8,128,256]{2,1,0:T(8,128)(2,1)S(1)} %collective-permute-done.7.low, bf16[8,128,256]{2,1,0:T(8,128)(2,1)S(1)} %collective-permute-done.8.high), custom_call_target="tpu_custom_call" | custom-call | tf_op jit(solution)/shard_map/weigh/pallas_call | solution.py:313
  133.2 5.7 %all-to-all-start.2 = ((bf16[32,16,128]{2,1,0:T(8,128)(2,1)}), bf16[32,16,128]{2,1,0:T(8,128)(2,1)S(1)}, u32[]{:S(2)}, u32[]{:S(2)}) async-start(bf16[32,16,128]{2,1,0:T(8,128)(2,1)} %weigh.1), calls=%async_computation.2 | async-start | bytes 262144 | tf_op jit(solution)/shard_map/all_to_all | solution.py:377
  138.9 0.2 select_reduce_fusion
  139.2 14.1 %all-to-all-done.2 = bf16[32,16,128]{2,1,0:T(8,128)(2,1)S(1)} async-done(((bf16[32,16,128]{2,1,0:T(8,128)(2,1)}), bf16[32,16,128]{2,1,0:T(8,128)(2,1)S(1)}, u32[]{:S(2)}, u32[]{:S(2)}) %all-to-all-start.2) | async-done | bytes 131104 | tf_op jit(solution)/shard_map/all_to_all | solution.py:377
  153.3 0.2 fusion.4
  153.5 11.0 %collective-permute-start.9 = (f32[32,128]{1,0:T(8,128)S(1)}, f32[32,128]{1,0:T(8,128)S(1)}, u32[]{:S(2)}, u32[]{:S(2)}) collective-permute-start(f32[32,128]{1,0:T(8,128)S(1)} %dynamic-slice_bitcast_fusion), channel_id=1, source_target_pairs={{0,32},{32,0},{64,96},{96,64},{128,160},{160,128},{192,224},{224,1... | collective-permute-start | bytes 49160 | tf_op jit(solution)/shard_map/ppermute | solution.py:384
  164.6 0.2 select_reduce_fusion.1
  164.7 0.8 dynamic_slice.16
  165.6 0.6 broadcast_in_dim.17
  166.2 3.8 %all-to-all-start.3 = ((f32[32,1,32]{2,1,0:T(1,128)}), f32[32,1,32]{2,1,0:T(1,128)S(1)}, u32[]{:S(2)}, u32[]{:S(2)}) async-start(f32[32,1,32]{2,1,0:T(1,128)} %broadcast_in_dim.17), calls=%async_computation.3 | async-start | bytes 32768 | tf_op jit(solution)/shard_map/all_to_all | solution.py:388
  170.1 12.1 %all-to-all-done.3 = f32[32,1,32]{2,1,0:T(1,128)S(1)} async-done(((f32[32,1,32]{2,1,0:T(1,128)}), f32[32,1,32]{2,1,0:T(1,128)S(1)}, u32[]{:S(2)}, u32[]{:S(2)}) %all-to-all-start.3) | async-done | bytes 4128 | tf_op jit(solution)/shard_map/all_to_all | solution.py:388
  182.2 0.2 fusion.3
  182.4 16.8 %all_to_all.32 = bf16[16,1,4,128]{3,2,1,0:T(4,128)(2,1)S(1)} all-to-all(bf16[16,1,4,128]{3,2,1,0:T(4,128)(2,1)S(1)} %copy.31), channel_id=1, replica_groups=mesh['dp'=16,'fsdp'=32] {'dp'}, dimensions={0} | all-to-all | bytes 32768 | tf_op jit(solution)/shard_map/all_to_all | solution.py:407
  199.3 0.6 copy.37
  (48 shorter events, 0.6 us)
Async XLA Ops:
  6.5 31.6 %copy-start.3 = (bf16[64,4096]{1,0:T(8,128)(2,1)S(1)}, bf16[64,4096]{1,0:T(8,128)(2,1)}, u32[]{:S(2)}) copy-start(bf16[64,4096]{1,0:T(8,128)(2,1)} %w_out_ref.1) | copy-start | bytes 1572868
  6.5 90.1 %all-gather.3.cloned.1.call-start = ((), (), s32[]{:S(2)}) async-start(), calls=%async_computation.5 | async-start | bytes 2228224 | tf_op jit(solution)/shard_map/all_gather | solution.py:337
  7.3 0.9 copy-start.5
  8.2 0.9 copy-start.6
  10.4 34.4 %collective-permute-start = (bf16[128,2048]{1,0:T(8,128)(2,1)}, bf16[128,2048]{1,0:T(8,128)(2,1)}, u32[]{:S(2)}, u32[]{:S(2)}) collective-permute-start(bf16[128,2048]{1,0:T(8,128)(2,1)} %near_ref.1), channel_id=1, source_target_pairs={{0,16},{1,17},{2,18},{3,19},{4,20},{5,21},{6,22},{7,23},{8,24},{9,... | collective-permute-start | bytes 1572872 | tf_op jit(solution)/shard_map/ppermute | solution.py:342
  14.5 1.6 copy-start
  16.1 0.7 copy-start.7
  16.8 28.0 %copy-start.4 = (bf16[128,2048]{1,0:T(8,128)(2,1)S(1)}, bf16[128,2048]{1,0:T(8,128)(2,1)}, u32[]{:S(2)}) copy-start(bf16[128,2048]{1,0:T(8,128)(2,1)} %near_ref.1) | copy-start | bytes 1572868
  18.2 37.6 %copy-start.1 = (bf16[1,256,4096]{2,1,0:T(8,128)(2,1)S(1)}, bf16[1,256,4096]{2,1,0:T(8,128)(2,1)}, u32[]{:S(2)}) copy-start(bf16[1,256,4096]{2,1,0:T(8,128)(2,1)} %hidden) | copy-start | bytes 6291460
  18.2 26.5 %all-to-all-start = ((bf16[16,8,128]{2,1,0:T(8,128)(2,1)}), bf16[16,8,128]{2,1,0:T(8,128)(2,1)S(1)}, u32[]{:S(2)}, u32[]{:S(2)}) async-start(bf16[16,8,128]{2,1,0:T(8,128)(2,1)} %get-tuple-element.14), calls=%async_computation | async-start | bytes 65536 | tf_op jit(solution)/shard_map/all_to_all | solution.py:341
  33.3 4.9 %collective-permute-start.1 = (bf16[1,4096]{1,0:T(2,128)(2,1)S(1)}, bf16[1,4096]{1,0:T(2,128)(2,1)S(1)}, u32[]{:S(2)}, u32[]{:S(2)}) collective-permute-start(bf16[1,4096]{1,0:T(2,128)(2,1)S(1)} %get-tuple-element.15.near_ref), channel_id=1, source_target_pairs={{0,16},{1,17},{2,18},{3,19},{4,20},{5,21},{6,22},{7,23},{8,24},{9,... | collective-permute-start | bytes 24584 | tf_op jit(solution)/shard_map/ppermute | solution.py:343
  39.6 16.7 %copy-start.8 = (f32[4096]{0:T(1024)S(1)}, f32[4096]{0:T(1024)}, u32[]{:S(2)}) copy-start(f32[4096]{0:T(1024)} %param.14) | copy-start | bytes 49156
  46.9 42.6 %all-to-all-start.1 = ((bf16[32,56,128]{2,1,0:T(8,128)(2,1)}), bf16[32,56,128]{2,1,0:T(8,128)(2,1)S(1)}, u32[]{:S(2)}, u32[]{:S(2)}) async-start(bf16[32,56,128]{2,1,0:T(8,128)(2,1)} %query.1), calls=%async_computation.1 | async-start | bytes 917504 | tf_op jit(solution)/shard_map/all_to_all | solution.py:347
  58.3 55.4 %collective-permute-start.4 = (bf16[256,4096]{1,0:T(8,128)(2,1)}, bf16[256,4096]{1,0:T(8,128)(2,1)}, u32[]{:S(2)}, u32[]{:S(2)}) collective-permute-start(bf16[256,4096]{1,0:T(8,128)(2,1)} %fusion.2.normed), channel_id=1, source_target_pairs={{0,32},{32,0},{64,96},{96,64},{128,160},{160,128},{192,224},{224,1... | collective-permute-start | bytes 6291464 | tf_op jit(solution)/shard_map/ppermute | solution.py:355
  61.1 3.5 %collective-permute-start.3 = (s32[1]{0:T(128)}, s32[1]{0:T(128)}, u32[]{:S(2)}, u32[]{:S(2)}) collective-permute-start(s32[1]{0:T(128)} %param.11), channel_id=1, source_target_pairs={{0,32},{32,0},{64,96},{96,64},{128,160},{160,128},{192,224},{224,1... | collective-permute-start | bytes 20 | tf_op jit(solution)/shard_map/ppermute | solution.py:350
  89.5 18.5 %collective-permute-start.2 = (bf16[1024,128]{1,0:T(8,128)(2,1)S(1)}, bf16[1024,128]{1,0:T(8,128)(2,1)S(1)}, u32[]{:S(2)}, u32[]{:S(2)}) collective-permute-start(bf16[1024,128]{1,0:T(8,128)(2,1)S(1)} %bitcast.44), channel_id=1, source_target_pairs={{16,32},{17,33},{18,34},{19,35},{20,36},{21,37},{22,38},{23,39},{2... | collective-permute-start | bytes 786440 | tf_op jit(solution)/shard_map/ppermute | solution.py:360
  99.5 31.2 %collective-permute-start.8 = (bf16[8,128,256]{2,1,0:T(8,128)(2,1)}, bf16[8,128,256]{2,1,0:T(8,128)(2,1)S(1)}, u32[]{:S(2)}, u32[]{:S(2)}) collective-permute-start(bf16[8,128,256]{2,1,0:T(8,128)(2,1)} %get-tuple-element.23), channel_id=1, source_target_pairs={{0,16},{32,48},{1,17},{33,49},{2,18},{34,50},{3,19},{35,51},{4,20}... | collective-permute-start | bytes 1572872 | tf_op jit(solution)/shard_map/ppermute | solution.py:370
  102.4 28.3 %collective-permute-start.7 = (bf16[8,128,256]{2,1,0:T(8,128)(2,1)}, bf16[8,128,256]{2,1,0:T(8,128)(2,1)S(1)}, u32[]{:S(2)}, u32[]{:S(2)}) collective-permute-start(bf16[8,128,256]{2,1,0:T(8,128)(2,1)} %get-tuple-element.24), channel_id=1, source_target_pairs={{0,272},{32,304},{1,273},{33,305},{2,274},{34,306},{3,275},{35,307... | collective-permute-start | bytes 1572872 | tf_op jit(solution)/shard_map/ppermute | solution.py:369
  106.0 16.5 %collective-permute-start.6 = (bf16[8,128,256]{2,1,0:T(8,128)(2,1)}, bf16[8,128,256]{2,1,0:T(8,128)(2,1)S(1)}, u32[]{:S(2)}, u32[]{:S(2)}) collective-permute-start(bf16[8,128,256]{2,1,0:T(8,128)(2,1)} %get-tuple-element.25), channel_id=1, source_target_pairs={{0,16},{32,48},{1,17},{33,49},{2,18},{34,50},{3,19},{35,51},{4,20}... | collective-permute-start | bytes 1572872 | tf_op jit(solution)/shard_map/ppermute | solution.py:368
  108.0 4.7 %copy-start.9 = (bf16[1024,128]{1,0:T(8,128)(2,1)}, bf16[1024,128]{1,0:T(8,128)(2,1)S(1)}, u32[]{:S(2)}) copy-start(bf16[1024,128]{1,0:T(8,128)(2,1)S(1)} %collective-permute-done.2) | copy-start | bytes 786436
  108.0 15.6 %collective-permute-start.5 = (bf16[8,128,256]{2,1,0:T(8,128)(2,1)}, bf16[8,128,256]{2,1,0:T(8,128)(2,1)S(1)}, u32[]{:S(2)}, u32[]{:S(2)}) collective-permute-start(bf16[8,128,256]{2,1,0:T(8,128)(2,1)} %get-tuple-element.26), channel_id=1, source_target_pairs={{0,272},{32,304},{1,273},{33,305},{2,274},{34,306},{3,275},{35,307... | collective-permute-start | bytes 1572872 | tf_op jit(solution)/shard_map/ppermute | solution.py:367
  123.6 7.2 %copy-start.2 = (bf16[2048,512]{1,0:T(8,128)(2,1)S(1)}, bf16[2048,512]{1,0:T(8,128)(2,1)}, u32[]{:S(2)}) copy-start(bf16[2048,512]{1,0:T(8,128)(2,1)} %all-gather.3.cloned.1.call-done) | copy-start | bytes 6291460
  130.7 8.1 %copy-start.10 = (s32[1024]{0:T(1024)S(1)}, s32[1024]{0:T(1024)}, u32[]{:S(2)}) copy-start(s32[1024]{0:T(1024)} %param.13) | copy-start | bytes 12292
  130.8 8.1 %copy-start.11 = (s32[32]{0:T(128)S(1)}, s32[32]{0:T(128)}, u32[]{:S(2)}) copy-start(s32[32]{0:T(128)} %param.12) | copy-start | bytes 388
  133.2 20.1 %all-to-all-start.2 = ((bf16[32,16,128]{2,1,0:T(8,128)(2,1)}), bf16[32,16,128]{2,1,0:T(8,128)(2,1)S(1)}, u32[]{:S(2)}, u32[]{:S(2)}) async-start(bf16[32,16,128]{2,1,0:T(8,128)(2,1)} %weigh.1), calls=%async_computation.2 | async-start | bytes 262144 | tf_op jit(solution)/shard_map/all_to_all | solution.py:377
  153.5 12.0 %collective-permute-start.9 = (f32[32,128]{1,0:T(8,128)S(1)}, f32[32,128]{1,0:T(8,128)S(1)}, u32[]{:S(2)}, u32[]{:S(2)}) collective-permute-start(f32[32,128]{1,0:T(8,128)S(1)} %dynamic-slice_bitcast_fusion), channel_id=1, source_target_pairs={{0,32},{32,0},{64,96},{96,64},{128,160},{160,128},{192,224},{224,1... | collective-permute-start | bytes 49160 | tf_op jit(solution)/shard_map/ppermute | solution.py:384
  166.2 16.0 %all-to-all-start.3 = ((f32[32,1,32]{2,1,0:T(1,128)}), f32[32,1,32]{2,1,0:T(1,128)S(1)}, u32[]{:S(2)}, u32[]{:S(2)}) async-start(f32[32,1,32]{2,1,0:T(1,128)} %broadcast_in_dim.17), calls=%async_computation.3 | async-start | bytes 32768 | tf_op jit(solution)/shard_map/all_to_all | solution.py:388
Sparse Core Ops, SparseCore 0:
  10.5 86.0 all-gather.2

commit v5 on v3

--- a/solution.py
+++ b/solution.py
@@ -31,6 +31,7 @@
 
 
 Z_GROUPS = [[fsdp_index(yl, z) for z in range(Z)] for yl in range(Y_LO)]
+X_GROUPS = [[dp_index(yh, x, c) for x in range(X)] for yh in range(2) for c in range(2)]
 CORE_Z_GROUPS = [
     [dp_index(yh, x, c) * 32 + fsdp_index(yl, z) for c in range(2) for z in range(Z)]
     for yh in range(2)
@@ -145,30 +146,31 @@
     )(place, hidden, gain[None, :])
 
 
-ROWS = 56
-QUERY_ROW = 32
-HIDDEN_ROW = 48
+ROWS = 32
+WEIGHT_ROW = 16
+HIDDEN_ROW = 24
 
 
 def fill_body(place_ref, w_out_ref, near_ref, far_ref, out_ref):
-    core, y_lo = place_ref[2], place_ref[3]
-    weight = w_out_ref[...].astype(f32)
-    weight = jnp.where(core == 0, weight[:32], weight[32:]).astype(bf16)
+    x, core, y_lo = place_ref[1], place_ref[2], place_ref[3]
+    rows = w_out_ref[...].astype(f32)
+    weight = rows[:8]
+    for n in range(1, 2 * X):
+        weight = jnp.where(core * X + x == n, rows[n * 8 : n * 8 + 8], weight)
     row = lax.broadcasted_iota(jnp.int32, (8, HEAD), 0)
     half = Z * HEAD
     near, far = (
         jnp.where(y_lo == 0, rows[:, :half], rows[:, half:])
         for rows in (near_ref[...].astype(f32), far_ref[...].astype(f32))
     )
-    zeros = jnp.zeros((HIDDEN_ROW - QUERY_ROW, HEAD), bf16)
     for z in range(Z):
         cut = slice(z * HEAD, (z + 1) * HEAD)
-        tile = jnp.where(row == 0, near[:, cut], jnp.where(row == 1, far[:, cut], 0.0)).astype(bf16)
+        tile = jnp.where(row == 0, near[:, cut], jnp.where(row == 1, far[:, cut], 0.0))
         for c in range(2):
             n = c * Z + z
-            out_ref[n, :QUERY_ROW, :] = weight[:, n * HEAD : (n + 1) * HEAD]
-            out_ref[n, QUERY_ROW:HIDDEN_ROW, :] = zeros
-            out_ref[n, HIDDEN_ROW:, :] = tile
+            both = jnp.concatenate([weight[:, n * HEAD : (n + 1) * HEAD], tile], axis=0)
+            out_ref[n, :WEIGHT_ROW, :] = jnp.zeros((WEIGHT_ROW, HEAD), bf16)
+            out_ref[n, WEIGHT_ROW:, :] = both.astype(bf16)
 
 
 def fill_payload(place, w_out, near, far):
@@ -194,7 +196,7 @@
         parts[c * Z : (c + 1) * Z, h % 8, :] = high[:, cut]
         parts[c * Z : (c + 1) * Z, 8 + h % 8, :] = low[:, cut]
     sent[...] = parts[...].astype(bf16)
-    back = pltpu.make_async_copy(sent, out.at[:, pl.ds(QUERY_ROW, 16), :], sem.at[0])
+    back = pltpu.make_async_copy(sent, out.at[:, pl.ds(0, 16), :], sem.at[0])
     back.start()
     back.wait()
 
@@ -216,13 +218,11 @@
     )(arrived, near, far, payload)
 
 
-def attend_body(place_ref, len_ref, normed, other, cos_ref, sin_ref, parts, gathered, out_ref, w_ref, q_ref, rows_ref, sem, q_sem):
-    fetch = pltpu.make_async_copy(parts.at[:, pl.ds(QUERY_ROW, 16), :], q_ref, q_sem.at[0])
+def attend_body(
+    place_ref, len_ref, normed_ref, other_ref, cos_ref, sin_ref, parts, gathered, out_ref, w_ref, q_ref, sem, q_sem
+):
+    fetch = pltpu.make_async_copy(parts.at[:, pl.ds(0, 16), :], q_ref, q_sem.at[0])
     fetch.start()
-    fills = [
-        pltpu.make_async_copy(rows, rows_ref.at[p], q_sem.at[1 + p])
-        for p, rows in enumerate((normed, other))
-    ]
     core, y_lo = place_ref[2], place_ref[3]
     copies = [
         [
@@ -235,7 +235,7 @@
         ]
         for kind in range(2)
     ]
-    for copy in fills[:1] + copies[0] + fills[1:] + copies[1]:
+    for copy in copies[0] + copies[1]:
         copy.start()
     cosine, sine = cos_ref[...], sin_ref[...]
     fetch.wait()
@@ -253,9 +253,8 @@
         copy.wait()
     weight = w_ref[0].reshape(Y_LO * Z * HEAD, 256)
     sums = []
-    for p in range(2):
-        fills[p].wait()
-        rows = rows_ref[p]
+    for p, rows_ref in enumerate((normed_ref, other_ref)):
+        rows = rows_ref[...]
         keys = jnp.dot(rows, weight, preferred_element_type=f32)
         scores = []
         for g in range(2):
@@ -294,16 +293,15 @@
     return pl.pallas_call(
         attend_body,
         out_shape=jax.ShapeDtypeStruct((2 * Z, 16, HEAD), bf16),
-        in_specs=[SMEM, SMEM, HBM, HBM, VMEM, VMEM, HBM, HBM],
+        in_specs=[SMEM, SMEM, VMEM, VMEM, VMEM, VMEM, HBM, HBM],
         out_specs=VMEM,
         scratch_shapes=[
             pltpu.VMEM((2, Y_LO, Z, HEAD, 256), bf16),
             pltpu.VMEM((2 * Z, 16, HEAD), bf16),
-            pltpu.VMEM((2, *normed.shape), bf16),
             pltpu.SemaphoreType.DMA((2, 2)),
-            pltpu.SemaphoreType.DMA((3,)),
+            pltpu.SemaphoreType.DMA((1,)),
         ],
-        compiler_params=pltpu.CompilerParams(vmem_limit_bytes=60 << 20),
+        compiler_params=pltpu.CompilerParams(vmem_limit_bytes=48 << 20),
         name="attend",
     )(place, lengths, normed, other, cosine, sine, parts, gathered)
 
@@ -325,31 +323,36 @@
     outgoing, last_input = open_payload(place, hidden, attn_gain)
     units, outgoing = lax.optimization_barrier((units, outgoing))
     arrived = lax.all_to_all(outgoing, "fsdp", 0, 0, tiled=True, axis_index_groups=Z_GROUPS)
-
     w_query_other = lax.ppermute(w_query, "fsdp", Y_LO_SWAP)
-    both_lengths = jnp.concatenate([lengths, lax.ppermute(lengths, "dp", CORE_SWAP)])
     last_other = lax.ppermute(last_input, "fsdp", Y_LO_SWAP)
     payload = fill_payload(place, w_out, last_input, last_other)
 
     payload = query_payload(arrived, w_query, w_query_other, payload)
     parts = lax.all_to_all(payload, BOTH, 0, 0, tiled=True, axis_index_groups=CORE_Z_GROUPS)
 
-    rows, _ = lax.optimization_barrier((hidden[0], outgoing))
+    rows, lengths, _ = lax.optimization_barrier((hidden[0], lengths, payload))
+    both_lengths = jnp.concatenate([lengths, lax.ppermute(lengths, "dp", CORE_SWAP)])
     floats = rows.astype(f32)
     normed = (
         floats * lax.rsqrt(jnp.mean(floats * floats, axis=-1, keepdims=True) + 1e-05) * attn_gain
     ).astype(bf16)
     other = lax.ppermute(normed, "dp", CORE_SWAP)
     cosine, sine = rope_tables(jnp.arange(seq_len), HEAD)
-    context = attend(place, both_lengths, normed, other, cosine, sine, parts, gathered)
-    contexts = lax.all_to_all(context, "fsdp", 0, 0, tiled=True)
-
-    weight = jnp.transpose(parts[:, :QUERY_ROW].reshape(2, Z, 32, HEAD), (1, 0, 2, 3))
-    weight = weight.reshape(2 * Z * 32, HEAD)
+
+    weight = lax.all_gather(
+        parts[:, WEIGHT_ROW:HIDDEN_ROW], "dp", axis=0, tiled=False, axis_index_groups=X_GROUPS
+    ).reshape(X, 2, Z, 8, HEAD)
+    weight = jnp.transpose(weight, (2, 1, 0, 3, 4)).reshape(2 * Z * 32, HEAD)
     weight = jnp.where(core == y_lo, weight, lax.ppermute(weight, BOTH, CROSS_SWAP))
     inputs = lax.dynamic_slice(parts, (core * Z, HIDDEN_ROW, 0), (Z, 2, HEAD)).astype(f32)
     inputs = jnp.where(y_lo == 0, inputs, inputs[:, ::-1])
     inputs = jnp.transpose(inputs, (1, 0, 2)).reshape(2 * Z, HEAD)
+
+    gathered, weight, inputs, both_lengths, normed, other, cosine, sine = lax.optimization_barrier(
+        (gathered, weight, inputs, both_lengths, normed, other, cosine, sine)
+    )
+    context = attend(place, both_lengths, normed, other, cosine, sine, parts, gathered)
+    contexts = lax.all_to_all(context, "fsdp", 0, 0, tiled=True)
 
     slabs = width // HEAD
     contexts = contexts.reshape(slabs, 2, 8 * HEAD)

time: 201 us -> 190 us (0.945)
  starting transfers between devices: 72.3 us -> 60.8 us
  blocking collectives: 15.2 us -> 26.3 us
  waiting for transfers between devices: 66.2 us -> 60.3 us
  other arithmetic: 9.13 us -> 4.69 us
    all_to_all x1, waiting for transfers between devices: 0.26 us -> 14.2 us  [local(): contexts = lax.all_to_all(context, 'fsdp', 0, 0, tiled=True)]
    all_gather x1, waiting for transfers between devices: 13.2 us -> 0.02 us  [local(): lax.all_gather(units, 'fsdp', axis=0, tiled=False, axis_index_groups=Z_GR...]
    all_gather x0 -> x1, blocking collectives: none -> 11.1 us  [local(): lax.all_gather(parts[:, WEIGHT_ROW:HIDDEN_ROW], 'dp', axis=0, tiled=False...]
    all_to_all x1, waiting for transfers between devices: 28 us -> 19.2 us  [local(): lax.all_to_all(payload, BOTH, 0, 0, tiled=True, axis_index_groups=CORE_Z_...]
    ppermute x1, starting transfers between devices: 11.2 us -> 3.73 us  [local(): lax.ppermute(weight, BOTH, CROSS_SWAP)]
    all_to_all x1, starting transfers between devices: 10 us -> 15.5 us  [local(): lax.all_to_all(outgoing, 'fsdp', 0, 0, tiled=True, axis_index_groups=Z_GR...]
    ppermute x1, starting transfers between devices: 9.2 us -> 5.35 us  [local(): other = lax.ppermute(normed, 'dp', CORE_SWAP)]
    all_to_all x1, starting transfers between devices: 7.62 us -> 3.87 us  [local(): contexts = lax.all_to_all(context, 'fsdp', 0, 0, tiled=True)]
  transfers between devices with their start and end apart: 12 -> 12, of which waited for: 8 -> 8; matrix products, arithmetic and copies ran while one was open for 5% -> 3% of each run, Pallas kernels for 2% -> 2%
where the time goes in v5:
time: 190 us; the launch traced here: 189 us
  starting transfers between devices  60.8 us (32%)
  waiting for transfers between devices  60.3 us (32%)
  blocking collectives  26.3 us (14%)
  Pallas kernels  14.9 us (8%)
  between operations  14.4 us (8%)
  local copies, waits for them, and re-layouts  7.35 us (4%)
  other arithmetic  4.69 us (2%)
    all_to_all x1, waiting for transfers between devices, local(): lax.all_to_all(payload, BOTH, 0, 0, tiled=True, axis_index_groups=CORE_Z_...  19.2 us
    all_to_all x1, starting transfers between devices, local(): lax.all_to_all(outgoing, 'fsdp', 0, 0, tiled=True, axis_index_groups=Z_GR...  15.5 us
    all_to_all x1, blocking collectives, local(): lax.all_to_all(outgoing[:, None], 'dp', split_axis=0, concat_axis=1, tile...  15.2 us
    all_to_all x1, waiting for transfers between devices, local(): contexts = lax.all_to_all(context, 'fsdp', 0, 0, tiled=True)  14.2 us
    all_to_all x1, waiting for transfers between devices, local(): lax.all_to_all(jnp.broadcast_to(partial[None, None, :], (slabs, 1, slabs)...  12.1 us
    all_gather x1, blocking collectives, local(): lax.all_gather(parts[:, WEIGHT_ROW:HIDDEN_ROW], 'dp', axis=0, tiled=False...  11.1 us
    pallas_call x1, Pallas kernels, attend(): pl.pallas_call(attend_body, out_shape=jax.ShapeDtypeStruct((2 * Z, 16, HE...  9.75 us
    ppermute x1, starting transfers between devices, local(): residual = inputs + (kept + lax.ppermute(given, 'dp', CORE_SWAP))  9.47 us
  transfers between devices with their start and end apart: 12, of which 8 were waited for; matrix products, arithmetic and copies ran while one was open for 3% of the time, Pallas kernels for 2%

profile of v5, /device:TPU:1, one launch (start us, length us, event | category | flops | bytes accessed | tf_op | source)
XLA Modules:
  0.0 189.1 jit_solution(15599469391473043648)
XLA Ops:
  7.3 0.1 pad_add_fusion.place_ref
  7.3 0.9 copy-done.4
  8.2 0.9 copy-done.5
  9.1 0.6 unit.1.near
  9.7 4.0 %collective-permute-start = (bf16[128,512]{1,0:T(8,128)(2,1)S(1)}, bf16[128,512]{1,0:T(8,128)(2,1)S(1)}, u32[]{:S(2)}, u32[]{:S(2)}) collective-permute-start(bf16[128,512]{1,0:T(8,128)(2,1)S(1)} %unit.1.near), channel_id=1, source_target_pairs={{0,16},{1,17},{2,18},{3,19},{4,20},{5,21},{6,22},{7,23},{8,24},{9,... | collective-permute-start | bytes 393224 | tf_op jit(solution)/shard_map/ppermute | solution.py:319
  13.8 2.3 %collective-permute-done.far = bf16[128,512]{1,0:T(8,128)(2,1)S(1)} collective-permute-done((bf16[128,512]{1,0:T(8,128)(2,1)S(1)}, bf16[128,512]{1,0:T(8,128)(2,1)S(1)}, u32[]{:S(2)}, u32[]{:S(2)}) %collective-permute-start) | collective-permute-done | bytes 131104 | tf_op jit(solution)/shard_map/ppermute | solution.py:319
  16.1 0.7 pair.1
  16.9 3.4 %collective-permute-start.1 = (bf16[128,2048]{1,0:T(8,128)(2,1)}, bf16[128,2048]{1,0:T(8,128)(2,1)S(1)}, u32[]{:S(2)}, u32[]{:S(2)}) collective-permute-start(bf16[128,2048]{1,0:T(8,128)(2,1)} %near_ref.1), channel_id=1, source_target_pairs={{0,16},{1,17},{2,18},{3,19},{4,20},{5,21},{6,22},{7,23},{8,24},{9,... | collective-permute-start | bytes 1572872 | tf_op jit(solution)/shard_map/ppermute | solution.py:326
  20.2 1.6 copy-done
  21.8 0.7 copy-done.6
  22.5 1.4 open.1
  24.0 15.5 %all-to-all-start = ((bf16[16,8,128]{2,1,0:T(8,128)(2,1)}), bf16[16,8,128]{2,1,0:T(8,128)(2,1)S(1)}, u32[]{:S(2)}, u32[]{:S(2)}) async-start(bf16[16,8,128]{2,1,0:T(8,128)(2,1)} %get-tuple-element.21), calls=%async_computation | async-start | bytes 65536 | tf_op jit(solution)/shard_map/all_to_all | solution.py:325
  39.5 2.1 %collective-permute-start.2 = (bf16[1,4096]{1,0:T(2,128)(2,1)S(1)}, bf16[1,4096]{1,0:T(2,128)(2,1)S(1)}, u32[]{:S(2)}, u32[]{:S(2)}) collective-permute-start(bf16[1,4096]{1,0:T(2,128)(2,1)S(1)} %get-tuple-element.22.near_ref), channel_id=1, source_target_pairs={{0,16},{1,17},{2,18},{3,19},{4,20},{5,21},{6,22},{7,23},{8,24},{9,... | collective-permute-start | bytes 24584 | tf_op jit(solution)/shard_map/ppermute | solution.py:327
  41.6 2.8 %collective-permute-done.2.far_ref = bf16[1,4096]{1,0:T(2,128)(2,1)S(1)} collective-permute-done((bf16[1,4096]{1,0:T(2,128)(2,1)S(1)}, bf16[1,4096]{1,0:T(2,128)(2,1)S(1)}, u32[]{:S(2)}, u32[]{:S(2)}) %collective-permute-start.2) | collective-permute-done | bytes 8224 | tf_op jit(solution)/shard_map/ppermute | solution.py:327
  44.4 1.0 copy-done.3
  45.4 1.3 fill.1.payload
  46.7 4.2 %all-to-all-done.arrived_ref = bf16[16,8,128]{2,1,0:T(8,128)(2,1)S(1)} async-done(((bf16[16,8,128]{2,1,0:T(8,128)(2,1)}), bf16[16,8,128]{2,1,0:T(8,128)(2,1)S(1)}, u32[]{:S(2)}, u32[]{:S(2)}) %all-to-all-start) | async-done | bytes 32800 | tf_op jit(solution)/shard_map/all_to_all | solution.py:325
  51.0 1.0 query.1
  52.0 0.5 fusion
  52.5 2.0 %fusion.2.normed_ref = bf16[256,4096]{1,0:T(8,128)(2,1)} fusion(bf16[256,4096]{1,0:T(8,128)(2,1)S(1)} %bitcast.38, f32[4096]{0:T(1024)S(1)} %copy-done.7, f32[256]{0:T(256)S(1)} %add_rsqrt_fusion), kind=kLoop, calls=%fused_computation.4 | loop fusion | flops 4194304 | bytes 4211712 | tf_op jit(solution)/shard_map/convert_element_type | solution.py:338
  54.5 5.4 %collective-permute-start.5 = (bf16[256,4096]{1,0:T(8,128)(2,1)}, bf16[256,4096]{1,0:T(8,128)(2,1)S(1)}, u32[]{:S(2)}, u32[]{:S(2)}) collective-permute-start(bf16[256,4096]{1,0:T(8,128)(2,1)} %fusion.2.normed_ref), channel_id=1, source_target_pairs={{0,32},{32,0},{64,96},{96,64},{128,160},{160,128},{192,224},{224,1... | collective-permute-start | bytes 6291464 | tf_op jit(solution)/shard_map/ppermute | solution.py:339
  59.9 7.4 %all-to-all-start.1 = ((bf16[32,32,128]{2,1,0:T(8,128)(2,1)}), bf16[32,32,128]{2,1,0:T(8,128)(2,1)S(1)}, u32[]{:S(2)}, u32[]{:S(2)}) async-start(bf16[32,32,128]{2,1,0:T(8,128)(2,1)} %query.1), calls=%async_computation.1 | async-start | bytes 524288 | tf_op jit(solution)/shard_map/all_to_all | solution.py:331
  67.3 0.5 fusion.7
  67.8 0.1 pad_maximum_fusion
  68.0 2.1 %collective-permute-start.4 = (s32[1]{0:T(128)}, s32[1]{0:T(128)}, u32[]{:S(2)}, u32[]{:S(2)}) collective-permute-start(s32[1]{0:T(128)} %param.11), channel_id=1, source_target_pairs={{0,32},{32,0},{64,96},{96,64},{128,160},{160,128},{192,224},{224,1... | collective-permute-start | bytes 20 | tf_op jit(solution)/shard_map/ppermute | solution.py:334
  70.1 1.1 collective-permute-done.4
  71.3 0.7 pad_add_fusion.1.len_ref
  72.0 19.2 %all-to-all-done.1.parts = bf16[32,32,128]{2,1,0:T(8,128)(2,1)S(1)} async-done(((bf16[32,32,128]{2,1,0:T(8,128)(2,1)}), bf16[32,32,128]{2,1,0:T(8,128)(2,1)S(1)}, u32[]{:S(2)}, u32[]{:S(2)}) %all-to-all-start.1) | async-done | bytes 262176 | tf_op jit(solution)/shard_map/all_to_all | solution.py:331
  91.2 11.1 %all-gather.1 = bf16[128,8,128]{2,1,0:T(8,128)(2,1)S(1)} all-gather(bf16[32,8,128]{2,1,0:T(8,128)(2,1)S(1)} %slice.4), channel_id=3, replica_groups={{0,64,128,192},{32,96,160,224},{256,320,384,448},{288,352,416,480},{1,6..., dimensions={0}, use_global_device_ids=true | all-gather | bytes 327680 | tf_op jit(solution)/shard_map/all_gather | solution.py:342
  102.3 0.1 copy.27
  102.4 3.7 %collective-permute-start.3 = (bf16[1024,128]{1,0:T(8,128)(2,1)S(1)}, bf16[1024,128]{1,0:T(8,128)(2,1)S(1)}, u32[]{:S(2)}, u32[]{:S(2)}) collective-permute-start(bf16[1024,128]{1,0:T(8,128)(2,1)S(1)} %bitcast.42), channel_id=1, source_target_pairs={{16,32},{17,33},{18,34},{19,35},{20,36},{21,37},{22,38},{23,39},{2... | collective-permute-start | bytes 786440 | tf_op jit(solution)/shard_map/ppermute | solution.py:346
  106.2 4.3 %collective-permute-done.3 = bf16[1024,128]{1,0:T(8,128)(2,1)S(1)} collective-permute-done((bf16[1024,128]{1,0:T(8,128)(2,1)S(1)}, bf16[1024,128]{1,0:T(8,128)(2,1)S(1)}, u32[]{:S(2)}, u32[]{:S(2)}) %collective-permute-start.3) | collective-permute-done | bytes 262176 | tf_op jit(solution)/shard_map/ppermute | solution.py:346
  110.7 9.8 %attend.1 = bf16[32,16,128]{2,1,0:T(8,128)(2,1)} custom-call(s32[4]{0:T(128)S(1)} %pad_add_fusion.place_ref, s32[2]{0:T(128)S(1)} %pad_add_fusion.1.len_ref, bf16[256,4096]{1,0:T(8,128)(2,1)} %fusion.2.normed_ref, bf16[256,4096]{1,0:T(8,128)(2,1)S(1)} %collective-permute-done.5.other_ref, f32[256,128]{1,0:T(8,128)S(1)} %get-tuple-element.30.cos_ref, ...), custom_call_target="tpu_custom_call" | custom-call | tf_op jit(solution)/shard_map/attend/pallas_call | solution.py:293
  120.5 3.9 %all-to-all-start.2 = ((bf16[32,16,128]{2,1,0:T(8,128)(2,1)}), bf16[32,16,128]{2,1,0:T(8,128)(2,1)S(1)}, u32[]{:S(2)}, u32[]{:S(2)}) async-start(bf16[32,16,128]{2,1,0:T(8,128)(2,1)} %attend.1), calls=%async_computation.2 | async-start | bytes 262144 | tf_op jit(solution)/shard_map/all_to_all | solution.py:355
  124.3 0.2 select_reduce_fusion
  124.5 0.1 fusion.11
  124.7 14.2 %all-to-all-done.2 = bf16[32,16,128]{2,1,0:T(8,128)(2,1)S(1)} async-done(((bf16[32,16,128]{2,1,0:T(8,128)(2,1)}), bf16[32,16,128]{2,1,0:T(8,128)(2,1)S(1)}, u32[]{:S(2)}, u32[]{:S(2)}) %all-to-all-start.2) | async-done | bytes 131104 | tf_op jit(solution)/shard_map/all_to_all | solution.py:355
  138.9 0.2 fusion.4
  139.1 9.5 %collective-permute-start.6 = (f32[32,128]{1,0:T(8,128)S(1)}, f32[32,128]{1,0:T(8,128)S(1)}, u32[]{:S(2)}, u32[]{:S(2)}) collective-permute-start(f32[32,128]{1,0:T(8,128)S(1)} %dynamic-slice_bitcast_fusion), channel_id=1, source_target_pairs={{0,32},{32,0},{64,96},{96,64},{128,160},{160,128},{192,224},{224,1... | collective-permute-start | bytes 49160 | tf_op jit(solution)/shard_map/ppermute | solution.py:362
  148.6 0.2 select_reduce_fusion.1
  148.7 0.8 dynamic_slice.16
  149.5 0.1 multiply_reduce_fusion
  149.6 0.6 broadcast_in_dim.17
  150.2 3.8 %all-to-all-start.3 = ((f32[32,1,32]{2,1,0:T(1,128)}), f32[32,1,32]{2,1,0:T(1,128)S(1)}, u32[]{:S(2)}, u32[]{:S(2)}) async-start(f32[32,1,32]{2,1,0:T(1,128)} %broadcast_in_dim.17), calls=%async_computation.3 | async-start | bytes 32768 | tf_op jit(solution)/shard_map/all_to_all | solution.py:366
  154.1 12.1 %all-to-all-done.3 = f32[32,1,32]{2,1,0:T(1,128)S(1)} async-done(((f32[32,1,32]{2,1,0:T(1,128)}), f32[32,1,32]{2,1,0:T(1,128)S(1)}, u32[]{:S(2)}, u32[]{:S(2)}) %all-to-all-start.3) | async-done | bytes 4128 | tf_op jit(solution)/shard_map/all_to_all | solution.py:366
  166.2 0.2 fusion.3
  166.4 15.2 %all_to_all.32 = bf16[16,1,4,128]{3,2,1,0:T(4,128)(2,1)S(1)} all-to-all(bf16[16,1,4,128]{3,2,1,0:T(4,128)(2,1)S(1)} %copy.31), channel_id=1, replica_groups=mesh['dp'=16,'fsdp'=32] {'dp'}, dimensions={0} | all-to-all | bytes 32768 | tf_op jit(solution)/shard_map/all_to_all | solution.py:385
  181.6 0.6 copy.37
  (38 shorter events, 0.4 us)
Async XLA Ops:
  6.5 44.4 %copy-start.2 = (bf16[128,2048]{1,0:T(8,128)(2,1)S(1)}, bf16[128,2048]{1,0:T(8,128)(2,1)}, u32[]{:S(2)}) copy-start(bf16[128,2048]{1,0:T(8,128)(2,1)} %near_ref.1) | copy-start | bytes 1572868
  6.5 104.1 %all-gather.4.cloned.1.call-start = ((), (), s32[]{:S(2)}) async-start(), calls=%async_computation.5 | async-start | bytes 4456448 | tf_op jit(solution)/shard_map/all_gather | solution.py:320
  7.3 0.9 copy-start.4
  8.2 0.9 copy-start.5
  9.1 43.4 %copy-start.7 = (f32[4096]{0:T(1024)S(1)}, f32[4096]{0:T(1024)}, u32[]{:S(2)}) copy-start(f32[4096]{0:T(1024)} %param.14) | copy-start | bytes 49156
  9.7 6.4 %collective-permute-start = (bf16[128,512]{1,0:T(8,128)(2,1)S(1)}, bf16[128,512]{1,0:T(8,128)(2,1)S(1)}, u32[]{:S(2)}, u32[]{:S(2)}) collective-permute-start(bf16[128,512]{1,0:T(8,128)(2,1)S(1)} %unit.1.near), channel_id=1, source_target_pairs={{0,16},{1,17},{2,18},{3,19},{4,20},{5,21},{6,22},{7,23},{8,24},{9,... | collective-permute-start | bytes 393224 | tf_op jit(solution)/shard_map/ppermute | solution.py:319
  16.9 34.1 %collective-permute-start.1 = (bf16[128,2048]{1,0:T(8,128)(2,1)}, bf16[128,2048]{1,0:T(8,128)(2,1)S(1)}, u32[]{:S(2)}, u32[]{:S(2)}) collective-permute-start(bf16[128,2048]{1,0:T(8,128)(2,1)} %near_ref.1), channel_id=1, source_target_pairs={{0,16},{1,17},{2,18},{3,19},{4,20},{5,21},{6,22},{7,23},{8,24},{9,... | collective-permute-start | bytes 1572872 | tf_op jit(solution)/shard_map/ppermute | solution.py:326
  20.2 1.6 copy-start
  21.8 0.7 copy-start.6
  22.5 29.5 %copy-start.1 = (bf16[1,256,4096]{2,1,0:T(8,128)(2,1)S(1)}, bf16[1,256,4096]{2,1,0:T(8,128)(2,1)}, u32[]{:S(2)}) copy-start(bf16[1,256,4096]{2,1,0:T(8,128)(2,1)} %hidden) | copy-start | bytes 6291460
  24.0 26.9 %all-to-all-start = ((bf16[16,8,128]{2,1,0:T(8,128)(2,1)}), bf16[16,8,128]{2,1,0:T(8,128)(2,1)S(1)}, u32[]{:S(2)}, u32[]{:S(2)}) async-start(bf16[16,8,128]{2,1,0:T(8,128)(2,1)} %get-tuple-element.21), calls=%async_computation | async-start | bytes 65536 | tf_op jit(solution)/shard_map/all_to_all | solution.py:325
  39.5 4.9 %collective-permute-start.2 = (bf16[1,4096]{1,0:T(2,128)(2,1)S(1)}, bf16[1,4096]{1,0:T(2,128)(2,1)S(1)}, u32[]{:S(2)}, u32[]{:S(2)}) collective-permute-start(bf16[1,4096]{1,0:T(2,128)(2,1)S(1)} %get-tuple-element.22.near_ref), channel_id=1, source_target_pairs={{0,16},{1,17},{2,18},{3,19},{4,20},{5,21},{6,22},{7,23},{8,24},{9,... | collective-permute-start | bytes 24584 | tf_op jit(solution)/shard_map/ppermute | solution.py:327
  44.4 1.0 copy-start.3
  54.5 56.1 %collective-permute-start.5 = (bf16[256,4096]{1,0:T(8,128)(2,1)}, bf16[256,4096]{1,0:T(8,128)(2,1)S(1)}, u32[]{:S(2)}, u32[]{:S(2)}) collective-permute-start(bf16[256,4096]{1,0:T(8,128)(2,1)} %fusion.2.normed_ref), channel_id=1, source_target_pairs={{0,32},{32,0},{64,96},{96,64},{128,160},{160,128},{192,224},{224,1... | collective-permute-start | bytes 6291464 | tf_op jit(solution)/shard_map/ppermute | solution.py:339
  59.9 31.4 %all-to-all-start.1 = ((bf16[32,32,128]{2,1,0:T(8,128)(2,1)}), bf16[32,32,128]{2,1,0:T(8,128)(2,1)S(1)}, u32[]{:S(2)}, u32[]{:S(2)}) async-start(bf16[32,32,128]{2,1,0:T(8,128)(2,1)} %query.1), calls=%async_computation.1 | async-start | bytes 524288 | tf_op jit(solution)/shard_map/all_to_all | solution.py:331
  68.0 3.3 %collective-permute-start.4 = (s32[1]{0:T(128)}, s32[1]{0:T(128)}, u32[]{:S(2)}, u32[]{:S(2)}) collective-permute-start(s32[1]{0:T(128)} %param.11), channel_id=1, source_target_pairs={{0,32},{32,0},{64,96},{96,64},{128,160},{160,128},{192,224},{224,1... | collective-permute-start | bytes 20 | tf_op jit(solution)/shard_map/ppermute | solution.py:334
  102.4 8.2 %collective-permute-start.3 = (bf16[1024,128]{1,0:T(8,128)(2,1)S(1)}, bf16[1024,128]{1,0:T(8,128)(2,1)S(1)}, u32[]{:S(2)}, u32[]{:S(2)}) collective-permute-start(bf16[1024,128]{1,0:T(8,128)(2,1)S(1)} %bitcast.42), channel_id=1, source_target_pairs={{16,32},{17,33},{18,34},{19,35},{20,36},{21,37},{22,38},{23,39},{2... | collective-permute-start | bytes 786440 | tf_op jit(solution)/shard_map/ppermute | solution.py:346
  110.7 13.7 %copy-start.8 = (s32[1024]{0:T(1024)S(1)}, s32[1024]{0:T(1024)}, u32[]{:S(2)}) copy-start(s32[1024]{0:T(1024)} %param.13) | copy-start | bytes 12292
  110.7 13.7 %copy-start.9 = (s32[32]{0:T(128)S(1)}, s32[32]{0:T(128)}, u32[]{:S(2)}) copy-start(s32[32]{0:T(128)} %param.12) | copy-start | bytes 388
  120.5 18.4 %all-to-all-start.2 = ((bf16[32,16,128]{2,1,0:T(8,128)(2,1)}), bf16[32,16,128]{2,1,0:T(8,128)(2,1)S(1)}, u32[]{:S(2)}, u32[]{:S(2)}) async-start(bf16[32,16,128]{2,1,0:T(8,128)(2,1)} %attend.1), calls=%async_computation.2 | async-start | bytes 262144 | tf_op jit(solution)/shard_map/all_to_all | solution.py:355
  139.1 10.4 %collective-permute-start.6 = (f32[32,128]{1,0:T(8,128)S(1)}, f32[32,128]{1,0:T(8,128)S(1)}, u32[]{:S(2)}, u32[]{:S(2)}) collective-permute-start(f32[32,128]{1,0:T(8,128)S(1)} %dynamic-slice_bitcast_fusion), channel_id=1, source_target_pairs={{0,32},{32,0},{64,96},{96,64},{128,160},{160,128},{192,224},{224,1... | collective-permute-start | bytes 49160 | tf_op jit(solution)/shard_map/ppermute | solution.py:362
  150.2 16.0 %all-to-all-start.3 = ((f32[32,1,32]{2,1,0:T(1,128)}), f32[32,1,32]{2,1,0:T(1,128)S(1)}, u32[]{:S(2)}, u32[]{:S(2)}) async-start(f32[32,1,32]{2,1,0:T(1,128)} %broadcast_in_dim.17), calls=%async_computation.3 | async-start | bytes 32768 | tf_op jit(solution)/shard_map/all_to_all | solution.py:366
Sparse Core Ops, SparseCore 0:
  17.0 88.3 all-gather.3

commit v6 on v2

--- a/solution.py
+++ b/solution.py
@@ -87,11 +87,11 @@
     )
 
 
-PIECE = 136
+UNIT = 128
 
 
 def open_body(place_ref, hidden, gain_ref, w_key, w_value, out_ref, last_ref, block, keys, values, sem):
-    last, x, core, y_lo = place_ref[0], place_ref[1], place_ref[2], place_ref[3]
+    last, x, core = place_ref[0], place_ref[1], place_ref[2]
     first = pl.multiple_of((last >> 3) << 3, 8)
     rows = pl.ds(pl.multiple_of(x * 32, 32), 32)
     columns = pl.ds(pl.multiple_of(core * 256, 256), 256)
@@ -108,30 +108,22 @@
     row = jnp.sum(jnp.where(pick, floats, 0.0), axis=0, keepdims=True)
     last_ref[...] = row.astype(bf16)
     normed = row * lax.rsqrt(jnp.mean(row * row, axis=-1, keepdims=True) + 1e-05) * gain_ref[...]
-    normed = normed.astype(bf16).astype(f32)
-    half = normed.shape[1] // 2
-    place = lax.broadcasted_iota(jnp.int32, (8, HEAD), 0)
+    tokens = [normed[:, n * HEAD : (n + 1) * HEAD] for n in range(2 * Z)]
+    out_ref[UNIT:, :] = jnp.concatenate(tokens, axis=0).astype(bf16)
     copies[1].wait()
     copies[2].wait()
-    unit = jnp.concatenate(
-        [w[:, g * HEAD : (g + 1) * HEAD] for w in (keys[...], values[...]) for g in range(2)], axis=0
-    )
-    for z in range(Z):
-        low = normed[:, z * HEAD : (z + 1) * HEAD]
-        high = normed[:, half + z * HEAD : half + (z + 1) * HEAD]
-        mine = jnp.where(y_lo == 0, low, high)
-        other = jnp.where(y_lo == 0, high, low)
-        tile = jnp.where(place == 0, mine, jnp.where(place == 1, other, 0.0))
-        out_ref[z, :128, :] = unit
-        out_ref[z, 128:, :] = tile.astype(bf16)
-
-
-def open_payload(place, hidden, gain, w_key, w_value):
+    for k, w in enumerate((keys, values)):
+        for g in range(2):
+            n = (2 * k + g) * 32
+            out_ref[n : n + 32, :] = w[:, g * HEAD : (g + 1) * HEAD]
+
+
+def open_unit(place, hidden, gain, w_key, w_value):
     width = hidden.shape[2]
     return pl.pallas_call(
         open_body,
         out_shape=(
-            jax.ShapeDtypeStruct((Z, PIECE, HEAD), bf16),
+            jax.ShapeDtypeStruct((UNIT + 2 * Z, HEAD), bf16),
             jax.ShapeDtypeStruct((1, width), bf16),
         ),
         in_specs=[SMEM, HBM, VMEM, HBM, HBM],
@@ -142,87 +134,52 @@
             pltpu.VMEM((32, 256), bf16),
             pltpu.SemaphoreType.DMA((3,)),
         ],
-        compiler_params=pltpu.CompilerParams(vmem_limit_bytes=8 << 20),
+        compiler_params=pltpu.CompilerParams(vmem_limit_bytes=62 << 20),
         name="open",
     )(place, hidden, gain[None, :], w_key, w_value)
 
 
-ROWS = 56
+ROWS = 48
 QUERY_ROW = 32
-HIDDEN_ROW = 48
-
-
-def fill_body(place_ref, w_out_ref, near_ref, far_ref, out_ref):
-    core, y_lo = place_ref[2], place_ref[3]
-    weight = w_out_ref[...].astype(f32)
-    weight = jnp.where(core == 0, weight[:32], weight[32:]).astype(bf16)
-    row = lax.broadcasted_iota(jnp.int32, (8, HEAD), 0)
-    half = Z * HEAD
+
+
+def query_body(place_ref, tokens_ref, near_ref, far_ref, w_out_ref, out_ref, parts):
+    core, y_lo, z = place_ref[2], place_ref[3], place_ref[4]
+    rows = w_out_ref[...].astype(f32)
+    weight = jnp.where(core == 0, rows[:32], rows[32:]).astype(bf16)
+    tokens = tokens_ref[...].astype(f32)
+    place = lax.broadcasted_iota(jnp.int32, tokens.shape, 1)
     near, far = (
-        jnp.where(y_lo == 0, rows[:, :half], rows[:, half:])
-        for rows in (near_ref[...].astype(f32), far_ref[...].astype(f32))
-    )
-    zeros = jnp.zeros((HIDDEN_ROW - QUERY_ROW, HEAD), bf16)
-    for z in range(Z):
-        cut = slice(z * HEAD, (z + 1) * HEAD)
-        tile = jnp.where(row == 0, near[:, cut], jnp.where(row == 1, far[:, cut], 0.0)).astype(bf16)
-        for c in range(2):
-            n = c * Z + z
-            out_ref[n, :QUERY_ROW, :] = weight[:, n * HEAD : (n + 1) * HEAD]
-            out_ref[n, QUERY_ROW:HIDDEN_ROW, :] = zeros
-            out_ref[n, HIDDEN_ROW:, :] = tile
-
-
-def fill_payload(place, w_out, near, far):
-    return pl.pallas_call(
-        fill_body,
-        out_shape=jax.ShapeDtypeStruct((2 * Z, ROWS, HEAD), bf16),
-        in_specs=[SMEM, VMEM, VMEM, VMEM],
-        out_specs=VMEM,
-        compiler_params=pltpu.CompilerParams(vmem_limit_bytes=8 << 20),
-        name="fill",
-    )(place, w_out, near, far)
-
-
-def query_body(arrived, near_ref, far_ref, payload, out, tile, parts, sent, sem):
-    copy = pltpu.make_async_copy(arrived.at[:, pl.ds(128, 8), :], tile, sem.at[0])
-    copy.start()
-    copy.wait()
-    features = tile[...].astype(f32)
-    total = jnp.dot(
-        features[:, 0, :].astype(bf16), near_ref[...], preferred_element_type=f32
-    ) + jnp.dot(features[:, 1, :].astype(bf16), far_ref[...], preferred_element_type=f32)
+        jnp.sum(jnp.where(place == y * Z + z, tokens, 0.0), axis=1).astype(bf16)
+        for y in (y_lo, 1 - y_lo)
+    )
+    total = jnp.dot(near, near_ref[...], preferred_element_type=f32) + jnp.dot(
+        far, far_ref[...], preferred_element_type=f32
+    )
     high = total.astype(bf16).astype(f32)
     low = total - high
     for h in range(HEADS):
         c, cut = h // 8, slice(h * HEAD, (h + 1) * HEAD)
         parts[c * Z : (c + 1) * Z, h % 8, :] = high[:, cut]
         parts[c * Z : (c + 1) * Z, 8 + h % 8, :] = low[:, cut]
-    sent[...] = parts[...].astype(bf16)
-    back = pltpu.make_async_copy(sent, out.at[:, pl.ds(QUERY_ROW, 16), :], sem.at[1])
-    back.start()
-    back.wait()
-
-
-def query_payload(arrived, near, far, payload):
+    out_ref[:, QUERY_ROW:, :] = parts[...].astype(bf16)
+    for n in range(2 * Z):
+        out_ref[n, :QUERY_ROW, :] = weight[:, n * HEAD : (n + 1) * HEAD]
+
+
+def query_payload(place, tokens, near, far, w_out):
     return pl.pallas_call(
         query_body,
-        out_shape=jax.ShapeDtypeStruct(payload.shape, bf16),
-        in_specs=[HBM, VMEM, VMEM, HBM],
-        out_specs=HBM,
-        input_output_aliases={3: 0},
-        scratch_shapes=[
-            pltpu.VMEM((Z, 8, HEAD), bf16),
-            pltpu.VMEM((2 * Z, 16, HEAD), f32),
-            pltpu.VMEM((2 * Z, 16, HEAD), bf16),
-            pltpu.SemaphoreType.DMA((2,)),
-        ],
-        compiler_params=pltpu.CompilerParams(vmem_limit_bytes=8 << 20),
+        out_shape=jax.ShapeDtypeStruct((2 * Z, ROWS, HEAD), bf16),
+        in_specs=[SMEM, VMEM, VMEM, VMEM, VMEM],
+        out_specs=VMEM,
+        scratch_shapes=[pltpu.VMEM((2 * Z, 16, HEAD), f32)],
+        compiler_params=pltpu.CompilerParams(vmem_limit_bytes=12 << 20),
         name="query",
-    )(arrived, near, far, payload)
-
-
-def attend_body(place_ref, len_ref, normed, other, cos_ref, sin_ref, parts, *refs):
+    )(place, tokens, near, far, w_out)
+
+
+def attend_body(place_ref, len_ref, normed, other, cos_ref, sin_ref, last_ref, parts, *refs):
     pieces, (out_ref, w_ref, q_ref, rows_ref, sem, q_sem) = refs[:8], refs[8:]
     fetch = pltpu.make_async_copy(parts.at[:, pl.ds(QUERY_ROW, 16), :], q_ref, q_sem.at[0])
     fetch.start()
@@ -296,14 +253,18 @@
     context = jnp.where((head & 7) < 4, total[:, :HEAD], total[:, HEAD:])
     turned = jnp.concatenate([context[8:], context[:8]], axis=0)
     context = jnp.where(core == 0, context, turned).astype(bf16)
-    out_ref[...] = jnp.broadcast_to(context[None], out_ref.shape)
-
-
-def attend(place, lengths, normed, other, cosine, sine, parts, pieces):
+    last = last_ref[...].astype(f32)
+    for n in range(2 * Z):
+        out_ref[n, :16, :] = context
+        tile = jnp.broadcast_to(last[:, n * HEAD : (n + 1) * HEAD], (8, HEAD))
+        out_ref[n, 16:, :] = tile.astype(bf16)
+
+
+def attend(place, lengths, normed, other, cosine, sine, last, parts, pieces):
     return pl.pallas_call(
         attend_body,
-        out_shape=jax.ShapeDtypeStruct((2 * Z, 16, HEAD), bf16),
-        in_specs=[SMEM, SMEM, HBM, HBM, VMEM, VMEM] + [HBM] * 9,
+        out_shape=jax.ShapeDtypeStruct((2 * Z, 24, HEAD), bf16),
+        in_specs=[SMEM, SMEM, HBM, HBM, VMEM, VMEM, VMEM] + [HBM] * 9,
         out_specs=VMEM,
         scratch_shapes=[
             pltpu.VMEM((2, Y_LO, Z, X, 32, 256), bf16),
@@ -314,7 +275,7 @@
         ],
         compiler_params=pltpu.CompilerParams(vmem_limit_bytes=60 << 20),
         name="attend",
-    )(place, lengths, normed, other, cosine, sine, parts, *pieces)
+    )(place, lengths, normed, other, cosine, sine, last, parts, *pieces)
 
 
 def local(
@@ -324,53 +285,49 @@
     dp, fsdp = lax.axis_index("dp"), lax.axis_index("fsdp")
     core, x = dp & 1, (dp >> 1) & (X - 1)
     y_lo = fsdp >> 4
-    place = jnp.stack([lengths[0] - 1, x, core, y_lo]).astype(jnp.int32)
-
-    outgoing, last_input = open_payload(place, hidden, attn_gain, w_key, w_value)
+    z = fsdp & (Z - 1)
+    place = jnp.stack([lengths[0] - 1, x, core, y_lo, z]).astype(jnp.int32)
 
     w_query_other = lax.ppermute(w_query, "fsdp", Y_LO_SWAP)
+    unit, last_input = open_unit(place, hidden, attn_gain, w_key, w_value)
+    arrived = lax.all_gather(unit, "fsdp", axis=0, tiled=False, axis_index_groups=Z_GROUPS)
+    own, tokens = arrived[:, :UNIT], arrived[:, UNIT:]
+
+    payload = query_payload(place, tokens, w_query, w_query_other, w_out)
+    own, payload = lax.optimization_barrier((own, payload))
+    parts = lax.all_to_all(payload, BOTH, 0, 0, tiled=True, axis_index_groups=CORE_Z_GROUPS)
+
+    plus = lax.ppermute(own, "dp", x_shift(1))
+    minus = lax.ppermute(own, "dp", x_shift(-1))
+    far = lax.ppermute(own, "dp", x_shift(2))
+    y_own = lax.ppermute(own, BOTH, y_shift(-1))
+    y_plus = lax.ppermute(plus, BOTH, y_shift(1))
+    y_minus = lax.ppermute(minus, BOTH, y_shift(1))
+    y_far = lax.ppermute(far, BOTH, y_shift(-1))
+
+    rows, lengths, _ = lax.optimization_barrier((hidden[0], lengths, payload))
     both_lengths = jnp.concatenate([lengths, lax.ppermute(lengths, "dp", CORE_SWAP)])
-    rows, outgoing = lax.optimization_barrier((hidden[0], outgoing))
-    arrived = lax.all_to_all(outgoing, "fsdp", 0, 0, tiled=True, axis_index_groups=Z_GROUPS)
     floats = rows.astype(f32)
     normed = (
         floats * lax.rsqrt(jnp.mean(floats * floats, axis=-1, keepdims=True) + 1e-05) * attn_gain
     ).astype(bf16)
     other = lax.ppermute(normed, "dp", CORE_SWAP)
     cosine, sine = rope_tables(jnp.arange(seq_len), HEAD)
-    last_other = lax.ppermute(last_input, "fsdp", Y_LO_SWAP)
-    payload = fill_payload(place, w_out, last_input, last_other)
-    arrived, w_query_other, other, both_lengths, cosine, sine, payload = lax.optimization_barrier(
-        (arrived, w_query_other, other, both_lengths, cosine, sine, payload)
-    )
-
-    plus = lax.ppermute(arrived, "dp", x_shift(1))
-    minus = lax.ppermute(arrived, "dp", x_shift(-1))
-    far = lax.ppermute(arrived, "dp", x_shift(2))
-    y_own = lax.ppermute(arrived, BOTH, y_shift(-1))
-
-    w_query_other, plus, minus = lax.optimization_barrier((w_query_other, plus, minus))
-    payload = query_payload(arrived, w_query, w_query_other, payload)
-    parts = lax.all_to_all(payload, BOTH, 0, 0, tiled=True, axis_index_groups=CORE_Z_GROUPS)
-
-    plus, minus, far, y_own = lax.optimization_barrier((plus, minus, far, y_own))
-    y_plus = lax.ppermute(plus, BOTH, y_shift(1))
-    y_minus = lax.ppermute(minus, BOTH, y_shift(-1))
-    y_far = lax.ppermute(far, BOTH, y_shift(1))
-
-    pieces = (arrived, plus, far, minus, y_own, y_plus, y_far, y_minus)
-    context = attend(place, both_lengths, normed, other, cosine, sine, parts, pieces)
-    contexts = lax.all_to_all(context, "fsdp", 0, 0, tiled=True)
 
     weight = jnp.transpose(parts[:, :QUERY_ROW].reshape(2, Z, 32, HEAD), (1, 0, 2, 3))
     weight = weight.reshape(2 * Z * 32, HEAD)
     weight = jnp.where(core == y_lo, weight, lax.ppermute(weight, BOTH, CROSS_SWAP))
-    inputs = lax.dynamic_slice(parts, (core * Z, HIDDEN_ROW, 0), (Z, 2, HEAD)).astype(f32)
-    inputs = jnp.where(y_lo == 0, inputs, inputs[:, ::-1])
-    inputs = jnp.transpose(inputs, (1, 0, 2)).reshape(2 * Z, HEAD)
+
+    place, weight = lax.optimization_barrier((place, weight))
+    pieces = (own, plus, far, minus, y_own, y_plus, y_far, y_minus)
+    context = attend(
+        place, both_lengths, normed, other, cosine, sine, last_input, parts, pieces
+    )
+    contexts = lax.all_to_all(context, "fsdp", 0, 0, tiled=True)
 
     slabs = width // HEAD
-    contexts = contexts.reshape(slabs, 2, 8 * HEAD)
+    inputs = contexts[:, 16].astype(f32)
+    contexts = contexts[:, :16].reshape(slabs, 2, 8 * HEAD)
     halves = jnp.einsum("sad,dn->asn", contexts, weight, preferred_element_type=f32)
     kept = lax.dynamic_index_in_dim(halves, core, 0, keepdims=False)
     given = lax.dynamic_index_in_dim(halves, 1 - core, 0, keepdims=False)

time: 214 us -> 197 us (0.921)
  blocking collectives: 13.6 us -> 44.6 us
  starting transfers between devices: 97.8 us -> 69.7 us
  waiting for transfers between devices: 68.8 us -> 51 us
  local copies, waits for them, and re-layouts: 8.91 us -> 4.41 us
  other arithmetic: 7.33 us -> 10.4 us
    all_gather x0 -> x1, blocking collectives: none -> 32.7 us  [local(): lax.all_gather(unit, 'fsdp', axis=0, tiled=False, axis_index_groups=Z_GRO...]
    ppermute x7 -> x6, waiting for transfers between devices: 27 us -> 15.4 us  [the longest x1 6.51 us: local(): y_minus = lax.ppermute(minus, BOTH, y_shift(1))]
    all_to_all x1 -> x0, starting transfers between devices: 9.55 us -> none  [local(): lax.all_to_all(outgoing, 'fsdp', 0, 0, tiled=True, axis_index_groups=Z_GR...]
    all_to_all x1, waiting for transfers between devices: 5.76 us -> 15.1 us  [local(): contexts = lax.all_to_all(context, 'fsdp', 0, 0, tiled=True)]
    ppermute x1, waiting for transfers between devices: 10.3 us -> 1.24 us  [local(): y_plus = lax.ppermute(plus, BOTH, y_shift(1))]
    ppermute x1, waiting for transfers between devices: 8.72 us -> 0.01 us  [local(): w_query_other = lax.ppermute(w_query, 'fsdp', Y_LO_SWAP)]
    ppermute x1, starting transfers between devices: 8.91 us -> 2.14 us  [local(): other = lax.ppermute(normed, 'dp', CORE_SWAP)]
    ppermute x7 -> x6, starting transfers between devices: 25.9 us -> 19.4 us  [the longest x1 4.42 us: local(): y_far = lax.ppermute(far, BOTH, y_shift(-1))]
  transfers between devices with their start and end apart: 17 -> 15, of which waited for: 11 -> 8; matrix products, arithmetic and copies ran while one was open for 3% -> 6% of each run, Pallas kernels for 1% -> 1%
where the time goes in v6:
time: 197 us; the launch traced here: 196 us
  starting transfers between devices  69.7 us (35%)
  waiting for transfers between devices  51 us (26%)
  blocking collectives  44.6 us (23%)
  Pallas kernels  14.7 us (7%)
  other arithmetic  10.4 us (5%)
  local copies, waits for them, and re-layouts  4.41 us (2%)
    all_gather x1, blocking collectives, local(): lax.all_gather(unit, 'fsdp', axis=0, tiled=False, axis_index_groups=Z_GRO...  32.7 us
    all_to_all x1, waiting for transfers between devices, local(): contexts = lax.all_to_all(context, 'fsdp', 0, 0, tiled=True)  15.1 us
    all_to_all x1, starting transfers between devices, local(): lax.all_to_all(payload, BOTH, 0, 0, tiled=True, axis_index_groups=CORE_Z_...  14.9 us
    all_to_all x1, starting transfers between devices, local(): contexts = lax.all_to_all(context, 'fsdp', 0, 0, tiled=True)  12.2 us
    all_to_all x1, waiting for transfers between devices, local(): lax.all_to_all(jnp.broadcast_to(partial[None, None, :], (slabs, 1, slabs)...  12.1 us
    all_to_all x1, blocking collectives, local(): lax.all_to_all(outgoing[:, None], 'dp', split_axis=0, concat_axis=1, tile...  11.9 us
    pallas_call x1, Pallas kernels, attend(): pl.pallas_call(attend_body, out_shape=jax.ShapeDtypeStruct((2 * Z, 24, HE...  10.3 us
    ppermute x1, waiting for transfers between devices, local(): y_minus = lax.ppermute(minus, BOTH, y_shift(1))  6.51 us
  transfers between devices with their start and end apart: 15, of which 8 were waited for; matrix products, arithmetic and copies ran while one was open for 6% of the time, Pallas kernels for 1%

profile of v6, /device:TPU:1, one launch (start us, length us, event | category | flops | bytes accessed | tf_op | source)
XLA Modules:
  0.0 196.1 jit_solution(11412672699992339794)
XLA Ops:
  0.0 4.0 %collective-permute-start = (bf16[128,2048]{1,0:T(8,128)(2,1)}, bf16[128,2048]{1,0:T(8,128)(2,1)S(1)}, u32[]{:S(2)}, u32[]{:S(2)}) collective-permute-start(bf16[128,2048]{1,0:T(8,128)(2,1)} %near_ref.1), channel_id=1, source_target_pairs={{0,16},{1,17},{2,18},{3,19},{4,20},{5,21},{6,22},{7,23},{8,24},{9,... | collective-permute-start | bytes 1572872 | tf_op jit(solution)/shard_map/ppermute | solution.py:291
  4.7 0.7 stack.20.place_ref
  5.4 2.5 %open.1 = (bf16[160,128]{1,0:T(8,128)(2,1)}, bf16[1,4096]{1,0:T(2,128)(2,1)}) custom-call(s32[5]{0:T(128)} %stack.20.place_ref, bf16[1,256,4096]{2,1,0:T(8,128)(2,1)} %hidden.1, f32[1,4096]{1,0:T(1,128)} %bitcast.45, bf16[128,512]{1,0:T(8,128)(2,1)} %w_key.1, bf16[128,512]{1,0:T(8,128)(2,1)} %w_value.1), custom_call_target="tpu_custom_call" | custom-call | tf_op jit(solution)/shard_map/open/pallas_call | solution.py:123
  7.9 32.7 %all-gather = bf16[2560,128]{1,0:T(8,128)(2,1)S(1)} all-gather(bf16[160,128]{1,0:T(8,128)(2,1)} %get-tuple-element.13), channel_id=2, replica_groups={{0,1,2,3,4,5,6,7,8,9,10,11,12,13,14,15},{16,17,18,19,20,21,22,23,24,25,..., dimensions={0}, use_global_device_ids=true | all-gather | bytes 696320 | tf_op jit(solution)/shard_map/all_gather | solution.py:293
  40.6 0.9 slice.20.refs_0_
  41.4 0.0 copy-start.7
  41.5 1.8 query.1
  43.3 14.9 %all-to-all-start = ((bf16[32,48,128]{2,1,0:T(8,128)(2,1)}), bf16[32,48,128]{2,1,0:T(8,128)(2,1)S(1)}, u32[]{:S(2)}, u32[]{:S(2)}) async-start(bf16[32,48,128]{2,1,0:T(8,128)(2,1)} %query.1), calls=%async_computation | async-start | bytes 786432 | tf_op jit(solution)/shard_map/all_to_all | solution.py:298
  58.2 2.1 %fusion = f32[256]{0:T(256)S(1)} fusion(bf16[256,4096]{1,0:T(8,128)(2,1)} %bitcast.36), kind=kLoop, calls=%fused_computation.2 | loop fusion | flops 3145472 | bytes 2098176 | tf_op jit(solution)/shard_map/reduce_sum | solution.py:312
  60.4 2.3 %fusion.2.normed = bf16[256,4096]{1,0:T(8,128)(2,1)S(1)} fusion(bf16[256,4096]{1,0:T(8,128)(2,1)} %bitcast.37, f32[4096]{0:T(1024)S(1)} %copy-done.7, f32[256]{0:T(256)S(1)} %add_rsqrt_fusion), kind=kLoop, calls=%fused_computation.4 | loop fusion | flops 4194304 | bytes 4211712 | tf_op jit(solution)/shard_map/convert_element_type | solution.py:313
  62.7 2.1 %collective-permute-start.3 = (bf16[256,4096]{1,0:T(8,128)(2,1)S(1)}, bf16[256,4096]{1,0:T(8,128)(2,1)}, u32[]{:S(2)}, u32[]{:S(2)}) collective-permute-start(bf16[256,4096]{1,0:T(8,128)(2,1)S(1)} %fusion.2.normed), channel_id=1, source_target_pairs={{0,32},{32,0},{64,96},{96,64},{128,160},{160,128},{192,224},{224,1... | collective-permute-start | bytes 6291464 | tf_op jit(solution)/shard_map/ppermute | solution.py:314
  64.8 3.1 %collective-permute-start.4 = (bf16[16,128,128]{2,1,0:T(8,128)(2,1)S(1)}, bf16[16,128,128]{2,1,0:T(8,128)(2,1)}, u32[]{:S(2)}, u32[]{:S(2)}) collective-permute-start(bf16[16,128,128]{2,1,0:T(8,128)(2,1)S(1)} %copy-done.5), channel_id=1, source_target_pairs={{0,64},{32,96},{64,128},{96,160},{128,192},{160,224},{192,0},{224,... | collective-permute-start | bytes 1572872 | tf_op jit(solution)/shard_map/ppermute | solution.py:300
  67.9 4.4 %collective-permute-start.5 = (bf16[16,128,128]{2,1,0:T(8,128)(2,1)S(1)}, bf16[16,128,128]{2,1,0:T(8,128)(2,1)}, u32[]{:S(2)}, u32[]{:S(2)}) collective-permute-start(bf16[16,128,128]{2,1,0:T(8,128)(2,1)S(1)} %copy-done.5), channel_id=1, source_target_pairs={{0,128},{32,160},{64,192},{96,224},{128,0},{160,32},{192,64},{224,... | collective-permute-start | bytes 1572872 | tf_op jit(solution)/shard_map/ppermute | solution.py:302
  72.3 3.1 %collective-permute-start.6 = (bf16[16,128,128]{2,1,0:T(8,128)(2,1)S(1)}, bf16[16,128,128]{2,1,0:T(8,128)(2,1)}, u32[]{:S(2)}, u32[]{:S(2)}) collective-permute-start(bf16[16,128,128]{2,1,0:T(8,128)(2,1)S(1)} %copy-done.5), channel_id=1, source_target_pairs={{0,192},{32,224},{64,0},{96,32},{128,64},{160,96},{192,128},{224,1... | collective-permute-start | bytes 1572872 | tf_op jit(solution)/shard_map/ppermute | solution.py:301
  75.4 3.0 %collective-permute-start.2 = (s32[1]{0:T(128)}, s32[1]{0:T(128)}, u32[]{:S(2)}, u32[]{:S(2)}) collective-permute-start(s32[1]{0:T(128)} %param.11), channel_id=1, source_target_pairs={{0,32},{32,0},{64,96},{96,64},{128,160},{160,128},{192,224},{224,1... | collective-permute-start | bytes 20 | tf_op jit(solution)/shard_map/ppermute | solution.py:309
  78.4 6.3 %all-to-all-done.parts = bf16[32,48,128]{2,1,0:T(8,128)(2,1)S(1)} async-done(((bf16[32,48,128]{2,1,0:T(8,128)(2,1)}), bf16[32,48,128]{2,1,0:T(8,128)(2,1)S(1)}, u32[]{:S(2)}, u32[]{:S(2)}) %all-to-all-start) | async-done | bytes 393248 | tf_op jit(solution)/shard_map/all_to_all | solution.py:298
  84.7 1.9 collective-permute-start.1
  86.7 2.6 %collective-permute-start.7 = (bf16[16,128,128]{2,1,0:T(8,128)(2,1)S(1)}, bf16[16,128,128]{2,1,0:T(8,128)(2,1)}, u32[]{:S(2)}, u32[]{:S(2)}) collective-permute-start(bf16[16,128,128]{2,1,0:T(8,128)(2,1)S(1)} %copy-done.5), channel_id=1, source_target_pairs={{0,272},{32,304},{1,273},{33,305},{2,274},{34,306},{3,275},{35,307... | collective-permute-start | bytes 1572872 | tf_op jit(solution)/shard_map/ppermute | solution.py:303
  89.3 4.2 %collective-permute-done.5.refs_2_ = bf16[16,128,128]{2,1,0:T(8,128)(2,1)} collective-permute-done((bf16[16,128,128]{2,1,0:T(8,128)(2,1)S(1)}, bf16[16,128,128]{2,1,0:T(8,128)(2,1)}, u32[]{:S(2)}, u32[]{:S(2)}) %collective-permute-start.5) | collective-permute-done | bytes 524320 | tf_op jit(solution)/shard_map/ppermute | solution.py:302
  93.5 2.1 %collective-permute-start.8 = (bf16[16,128,128]{2,1,0:T(8,128)(2,1)}, bf16[16,128,128]{2,1,0:T(8,128)(2,1)}, u32[]{:S(2)}, u32[]{:S(2)}) collective-permute-start(bf16[16,128,128]{2,1,0:T(8,128)(2,1)} %collective-permute-done.4.refs_1_), channel_id=1, source_target_pairs={{0,16},{32,48},{1,17},{33,49},{2,18},{34,50},{3,19},{35,51},{4,20}... | collective-permute-start | bytes 1572872 | tf_op jit(solution)/shard_map/ppermute | solution.py:304
  95.6 4.4 %collective-permute-start.9 = (bf16[16,128,128]{2,1,0:T(8,128)(2,1)}, bf16[16,128,128]{2,1,0:T(8,128)(2,1)}, u32[]{:S(2)}, u32[]{:S(2)}) collective-permute-start(bf16[16,128,128]{2,1,0:T(8,128)(2,1)} %collective-permute-done.5.refs_2_), channel_id=1, source_target_pairs={{0,272},{32,304},{1,273},{33,305},{2,274},{34,306},{3,275},{35,307... | collective-permute-start | bytes 1572872 | tf_op jit(solution)/shard_map/ppermute | solution.py:306
  100.0 0.7 copy-done.6
  100.7 1.9 collective-permute-start.10
  102.6 1.2 fusion.7
  103.8 1.8 pad_maximum_fusion
  105.7 1.3 pad_add_fusion.len_ref
  107.0 1.0 broadcast_select_fusion
  108.0 1.2 collective-permute-done.8.refs_5_
  109.2 4.7 %collective-permute-done.9.refs_6_ = bf16[16,128,128]{2,1,0:T(8,128)(2,1)} collective-permute-done((bf16[16,128,128]{2,1,0:T(8,128)(2,1)}, bf16[16,128,128]{2,1,0:T(8,128)(2,1)}, u32[]{:S(2)}, u32[]{:S(2)}) %collective-permute-start.9) | collective-permute-done | bytes 524320 | tf_op jit(solution)/shard_map/ppermute | solution.py:306
  113.9 6.5 %collective-permute-done.10.refs_7_ = bf16[16,128,128]{2,1,0:T(8,128)(2,1)} collective-permute-done((bf16[16,128,128]{2,1,0:T(8,128)(2,1)}, bf16[16,128,128]{2,1,0:T(8,128)(2,1)}, u32[]{:S(2)}, u32[]{:S(2)}) %collective-permute-start.10) | collective-permute-done | bytes 524320 | tf_op jit(solution)/shard_map/ppermute | solution.py:305
  120.5 10.3 %attend.1 = bf16[32,24,128]{2,1,0:T(8,128)(2,1)} custom-call(s32[5]{0:T(128)} %stack.20.place_ref, s32[2]{0:T(128)} %pad_add_fusion.len_ref, bf16[256,4096]{1,0:T(8,128)(2,1)} %copy-done.3, bf16[256,4096]{1,0:T(8,128)(2,1)} %collective-permute-done.3.other, f32[256,128]{1,0:T(8,128)} %get-tuple-element.26.cos_ref, f32[256,128]{1,0:T(8,128)} %get-tuple-element.27.sin_ref, ...), custom_call_target="tpu_custom_call" | custom-call | tf_op jit(solution)/shard_map/attend/pallas_call | solution.py:264
  130.8 12.2 %all-to-all-start.1 = ((bf16[32,24,128]{2,1,0:T(8,128)(2,1)}), bf16[32,24,128]{2,1,0:T(8,128)(2,1)S(1)}, u32[]{:S(2)}, u32[]{:S(2)}) async-start(bf16[32,24,128]{2,1,0:T(8,128)(2,1)} %attend.1), calls=%async_computation.1 | async-start | bytes 393216 | tf_op jit(solution)/shard_map/all_to_all | solution.py:326
  143.1 0.2 select_reduce_fusion
  143.3 0.1 fusion.11
  143.3 0.1 reduce_window_sum.11
  143.4 0.8 dynamic_slice.12
  144.1 0.2 select_reduce_fusion.1
  144.3 15.1 %all-to-all-done.1 = bf16[32,24,128]{2,1,0:T(8,128)(2,1)S(1)} async-done(((bf16[32,24,128]{2,1,0:T(8,128)(2,1)}), bf16[32,24,128]{2,1,0:T(8,128)(2,1)S(1)}, u32[]{:S(2)}, u32[]{:S(2)}) %all-to-all-start.1) | async-done | bytes 196640 | tf_op jit(solution)/shard_map/all_to_all | solution.py:326
  159.5 0.2 fusion.4
  159.7 6.1 %collective-permute-start.11 = (f32[32,128]{1,0:T(8,128)S(1)}, f32[32,128]{1,0:T(8,128)S(1)}, u32[]{:S(2)}, u32[]{:S(2)}) collective-permute-start(f32[32,128]{1,0:T(8,128)S(1)} %dynamic-slice_bitcast_fusion), channel_id=1, source_target_pairs={{0,32},{32,0},{64,96},{96,64},{128,160},{160,128},{192,224},{224,1... | collective-permute-start | bytes 49160 | tf_op jit(solution)/shard_map/ppermute | solution.py:334
  165.8 0.8 collective-permute-done.11
  166.6 0.1 multiply_reduce_fusion
  166.8 0.6 broadcast_in_dim.17
  167.4 3.8 %all-to-all-start.2 = ((f32[32,1,32]{2,1,0:T(1,128)}), f32[32,1,32]{2,1,0:T(1,128)S(1)}, u32[]{:S(2)}, u32[]{:S(2)}) async-start(f32[32,1,32]{2,1,0:T(1,128)} %broadcast_in_dim.17), calls=%async_computation.2 | async-start | bytes 32768 | tf_op jit(solution)/shard_map/all_to_all | solution.py:338
  171.2 12.1 %all-to-all-done.2 = f32[32,1,32]{2,1,0:T(1,128)S(1)} async-done(((f32[32,1,32]{2,1,0:T(1,128)}), f32[32,1,32]{2,1,0:T(1,128)S(1)}, u32[]{:S(2)}, u32[]{:S(2)}) %all-to-all-start.2) | async-done | bytes 4128 | tf_op jit(solution)/shard_map/all_to_all | solution.py:338
  183.4 0.2 fusion.3
  183.6 11.9 %all_to_all.27 = bf16[16,1,4,128]{3,2,1,0:T(4,128)(2,1)S(1)} all-to-all(bf16[16,1,4,128]{3,2,1,0:T(4,128)(2,1)S(1)} %copy.23), channel_id=1, replica_groups=mesh['dp'=16,'fsdp'=32] {'dp'}, dimensions={0} | all-to-all | bytes 32768 | tf_op jit(solution)/shard_map/all_to_all | solution.py:357
  195.5 0.6 copy.28
  (40 shorter events, 0.3 us)
Async XLA Ops:
  0.0 41.4 %collective-permute-start = (bf16[128,2048]{1,0:T(8,128)(2,1)}, bf16[128,2048]{1,0:T(8,128)(2,1)S(1)}, u32[]{:S(2)}, u32[]{:S(2)}) collective-permute-start(bf16[128,2048]{1,0:T(8,128)(2,1)} %near_ref.1), channel_id=1, source_target_pairs={{0,16},{1,17},{2,18},{3,19},{4,20},{5,21},{6,22},{7,23},{8,24},{9,... | collective-permute-start | bytes 1572872 | tf_op jit(solution)/shard_map/ppermute | solution.py:291
  5.4 36.1 %copy-start = (bf16[128,2048]{1,0:T(8,128)(2,1)S(1)}, bf16[128,2048]{1,0:T(8,128)(2,1)}, u32[]{:S(2)}) copy-start(bf16[128,2048]{1,0:T(8,128)(2,1)} %near_ref.1) | copy-start | bytes 1572868
  5.4 36.1 %copy-start.1 = (bf16[64,4096]{1,0:T(8,128)(2,1)S(1)}, bf16[64,4096]{1,0:T(8,128)(2,1)}, u32[]{:S(2)}) copy-start(bf16[64,4096]{1,0:T(8,128)(2,1)} %w_out_ref.1) | copy-start | bytes 1572868
  5.4 36.1 %copy-start.2 = (s32[5]{0:T(128)S(1)}, s32[5]{0:T(128)}, u32[]{:S(2)}) copy-start(s32[5]{0:T(128)} %stack.20.place_ref) | copy-start | bytes 64
  41.4 18.9 %copy-start.7 = (f32[4096]{0:T(1024)S(1)}, f32[4096]{0:T(1024)}, u32[]{:S(2)}) copy-start(f32[4096]{0:T(1024)} %param.14) | copy-start | bytes 49156
  43.3 41.4 %all-to-all-start = ((bf16[32,48,128]{2,1,0:T(8,128)(2,1)}), bf16[32,48,128]{2,1,0:T(8,128)(2,1)S(1)}, u32[]{:S(2)}, u32[]{:S(2)}) async-start(bf16[32,48,128]{2,1,0:T(8,128)(2,1)} %query.1), calls=%async_computation | async-start | bytes 786432 | tf_op jit(solution)/shard_map/all_to_all | solution.py:298
  60.4 4.5 %copy-start.5 = (bf16[16,128,128]{2,1,0:T(8,128)(2,1)S(1)}, bf16[16,128,128]{2,1,0:T(8,128)(2,1)}, u32[]{:S(2)}) copy-start(bf16[16,128,128]{2,1,0:T(8,128)(2,1)} %slice.20.refs_0_) | copy-start | bytes 1572868
  62.6 57.8 %copy-start.3 = (bf16[256,4096]{1,0:T(8,128)(2,1)}, bf16[256,4096]{1,0:T(8,128)(2,1)S(1)}, u32[]{:S(2)}) copy-start(bf16[256,4096]{1,0:T(8,128)(2,1)S(1)} %fusion.2.normed) | copy-start | bytes 6291460
  62.7 57.8 %collective-permute-start.3 = (bf16[256,4096]{1,0:T(8,128)(2,1)S(1)}, bf16[256,4096]{1,0:T(8,128)(2,1)}, u32[]{:S(2)}, u32[]{:S(2)}) collective-permute-start(bf16[256,4096]{1,0:T(8,128)(2,1)S(1)} %fusion.2.normed), channel_id=1, source_target_pairs={{0,32},{32,0},{64,96},{96,64},{128,160},{160,128},{192,224},{224,1... | collective-permute-start | bytes 6291464 | tf_op jit(solution)/shard_map/ppermute | solution.py:314
  64.8 21.9 %collective-permute-start.4 = (bf16[16,128,128]{2,1,0:T(8,128)(2,1)S(1)}, bf16[16,128,128]{2,1,0:T(8,128)(2,1)}, u32[]{:S(2)}, u32[]{:S(2)}) collective-permute-start(bf16[16,128,128]{2,1,0:T(8,128)(2,1)S(1)} %copy-done.5), channel_id=1, source_target_pairs={{0,64},{32,96},{64,128},{96,160},{128,192},{160,224},{192,0},{224,... | collective-permute-start | bytes 1572872 | tf_op jit(solution)/shard_map/ppermute | solution.py:300
  67.9 25.5 %collective-permute-start.5 = (bf16[16,128,128]{2,1,0:T(8,128)(2,1)S(1)}, bf16[16,128,128]{2,1,0:T(8,128)(2,1)}, u32[]{:S(2)}, u32[]{:S(2)}) collective-permute-start(bf16[16,128,128]{2,1,0:T(8,128)(2,1)S(1)} %copy-done.5), channel_id=1, source_target_pairs={{0,128},{32,160},{64,192},{96,224},{128,0},{160,32},{192,64},{224,... | collective-permute-start | bytes 1572872 | tf_op jit(solution)/shard_map/ppermute | solution.py:302
  72.3 23.2 %collective-permute-start.6 = (bf16[16,128,128]{2,1,0:T(8,128)(2,1)S(1)}, bf16[16,128,128]{2,1,0:T(8,128)(2,1)}, u32[]{:S(2)}, u32[]{:S(2)}) collective-permute-start(bf16[16,128,128]{2,1,0:T(8,128)(2,1)S(1)} %copy-done.5), channel_id=1, source_target_pairs={{0,192},{32,224},{64,0},{96,32},{128,64},{160,96},{192,128},{224,1... | collective-permute-start | bytes 1572872 | tf_op jit(solution)/shard_map/ppermute | solution.py:301
  75.4 9.3 %collective-permute-start.2 = (s32[1]{0:T(128)}, s32[1]{0:T(128)}, u32[]{:S(2)}, u32[]{:S(2)}) collective-permute-start(s32[1]{0:T(128)} %param.11), channel_id=1, source_target_pairs={{0,32},{32,0},{64,96},{96,64},{128,160},{160,128},{192,224},{224,1... | collective-permute-start | bytes 20 | tf_op jit(solution)/shard_map/ppermute | solution.py:309
  84.7 35.8 %copy-start.4 = (bf16[32,48,128]{2,1,0:T(8,128)(2,1)}, bf16[32,48,128]{2,1,0:T(8,128)(2,1)S(1)}, u32[]{:S(2)}) copy-start(bf16[32,48,128]{2,1,0:T(8,128)(2,1)S(1)} %all-to-all-done.parts) | copy-start | bytes 1179652
  84.7 15.3 %collective-permute-start.1 = (bf16[1024,128]{1,0:T(8,128)(2,1)S(1)}, bf16[1024,128]{1,0:T(8,128)(2,1)S(1)}, u32[]{:S(2)}, u32[]{:S(2)}) collective-permute-start(bf16[1024,128]{1,0:T(8,128)(2,1)S(1)} %bitcast.41), channel_id=1, source_target_pairs={{16,32},{17,33},{18,34},{19,35},{20,36},{21,37},{22,38},{23,39},{2... | collective-permute-start | bytes 786440 | tf_op jit(solution)/shard_map/ppermute | solution.py:319
  86.7 21.3 %collective-permute-start.7 = (bf16[16,128,128]{2,1,0:T(8,128)(2,1)S(1)}, bf16[16,128,128]{2,1,0:T(8,128)(2,1)}, u32[]{:S(2)}, u32[]{:S(2)}) collective-permute-start(bf16[16,128,128]{2,1,0:T(8,128)(2,1)S(1)} %copy-done.5), channel_id=1, source_target_pairs={{0,272},{32,304},{1,273},{33,305},{2,274},{34,306},{3,275},{35,307... | collective-permute-start | bytes 1572872 | tf_op jit(solution)/shard_map/ppermute | solution.py:303
  93.5 15.7 %collective-permute-start.8 = (bf16[16,128,128]{2,1,0:T(8,128)(2,1)}, bf16[16,128,128]{2,1,0:T(8,128)(2,1)}, u32[]{:S(2)}, u32[]{:S(2)}) collective-permute-start(bf16[16,128,128]{2,1,0:T(8,128)(2,1)} %collective-permute-done.4.refs_1_), channel_id=1, source_target_pairs={{0,16},{32,48},{1,17},{33,49},{2,18},{34,50},{3,19},{35,51},{4,20}... | collective-permute-start | bytes 1572872 | tf_op jit(solution)/shard_map/ppermute | solution.py:304
  95.6 18.4 %collective-permute-start.9 = (bf16[16,128,128]{2,1,0:T(8,128)(2,1)}, bf16[16,128,128]{2,1,0:T(8,128)(2,1)}, u32[]{:S(2)}, u32[]{:S(2)}) collective-permute-start(bf16[16,128,128]{2,1,0:T(8,128)(2,1)} %collective-permute-done.5.refs_2_), channel_id=1, source_target_pairs={{0,272},{32,304},{1,273},{33,305},{2,274},{34,306},{3,275},{35,307... | collective-permute-start | bytes 1572872 | tf_op jit(solution)/shard_map/ppermute | solution.py:306
  100.0 0.7 copy-start.6
  100.7 19.7 %collective-permute-start.10 = (bf16[16,128,128]{2,1,0:T(8,128)(2,1)}, bf16[16,128,128]{2,1,0:T(8,128)(2,1)}, u32[]{:S(2)}, u32[]{:S(2)}) collective-permute-start(bf16[16,128,128]{2,1,0:T(8,128)(2,1)} %collective-permute-done.6.refs_3_), channel_id=1, source_target_pairs={{0,16},{32,48},{1,17},{33,49},{2,18},{34,50},{3,19},{35,51},{4,20}... | collective-permute-start | bytes 1572872 | tf_op jit(solution)/shard_map/ppermute | solution.py:305
  120.4 22.6 %copy-start.8 = (s32[1024]{0:T(1024)S(1)}, s32[1024]{0:T(1024)}, u32[]{:S(2)}) copy-start(s32[1024]{0:T(1024)} %param.13) | copy-start | bytes 12292
  120.5 22.6 %copy-start.9 = (s32[32]{0:T(128)S(1)}, s32[32]{0:T(128)}, u32[]{:S(2)}) copy-start(s32[32]{0:T(128)} %param.12) | copy-start | bytes 388
  130.8 28.6 %all-to-all-start.1 = ((bf16[32,24,128]{2,1,0:T(8,128)(2,1)}), bf16[32,24,128]{2,1,0:T(8,128)(2,1)S(1)}, u32[]{:S(2)}, u32[]{:S(2)}) async-start(bf16[32,24,128]{2,1,0:T(8,128)(2,1)} %attend.1), calls=%async_computation.1 | async-start | bytes 393216 | tf_op jit(solution)/shard_map/all_to_all | solution.py:326
  159.7 6.9 %collective-permute-start.11 = (f32[32,128]{1,0:T(8,128)S(1)}, f32[32,128]{1,0:T(8,128)S(1)}, u32[]{:S(2)}, u32[]{:S(2)}) collective-permute-start(f32[32,128]{1,0:T(8,128)S(1)} %dynamic-slice_bitcast_fusion), channel_id=1, source_target_pairs={{0,32},{32,0},{64,96},{96,64},{128,160},{160,128},{192,224},{224,1... | collective-permute-start | bytes 49160 | tf_op jit(solution)/shard_map/ppermute | solution.py:334
  167.4 16.0 %all-to-all-start.2 = ((f32[32,1,32]{2,1,0:T(1,128)}), f32[32,1,32]{2,1,0:T(1,128)S(1)}, u32[]{:S(2)}, u32[]{:S(2)}) async-start(f32[32,1,32]{2,1,0:T(1,128)} %broadcast_in_dim.17), calls=%async_computation.2 | async-start | bytes 32768 | tf_op jit(solution)/shard_map/all_to_all | solution.py:338

commit v7 on v5

--- a/solution.py
+++ b/solution.py
@@ -82,7 +82,7 @@
         in_specs=[SMEM, HBM, HBM],
         out_specs=HBM,
         scratch_shapes=[pltpu.SemaphoreType.DMA((2,))],
-        compiler_params=pltpu.CompilerParams(vmem_limit_bytes=1 << 20),
+        compiler_params=pltpu.CompilerParams(vmem_limit_bytes=62 << 20),
         name="unit",
     )(place, w_key, w_value)
 
@@ -102,7 +102,7 @@
         in_specs=[HBM, HBM],
         out_specs=HBM,
         scratch_shapes=[pltpu.SemaphoreType.DMA((2,))],
-        compiler_params=pltpu.CompilerParams(vmem_limit_bytes=1 << 20),
+        compiler_params=pltpu.CompilerParams(vmem_limit_bytes=62 << 20),
         name="pair",
     )(near, far)
 
@@ -141,50 +141,22 @@
         in_specs=[SMEM, HBM, VMEM],
         out_specs=(VMEM, VMEM),
         scratch_shapes=[pltpu.VMEM((8, width), bf16), pltpu.SemaphoreType.DMA((1,))],
-        compiler_params=pltpu.CompilerParams(vmem_limit_bytes=4 << 20),
+        compiler_params=pltpu.CompilerParams(vmem_limit_bytes=62 << 20),
         name="open",
     )(place, hidden, gain[None, :])
 
 
-ROWS = 32
+ROWS = 24
 WEIGHT_ROW = 16
-HIDDEN_ROW = 24
-
-
-def fill_body(place_ref, w_out_ref, near_ref, far_ref, out_ref):
-    x, core, y_lo = place_ref[1], place_ref[2], place_ref[3]
+
+
+def query_body(place_ref, arrived_ref, near_ref, far_ref, w_out_ref, out_ref, parts):
+    x, core = place_ref[1], place_ref[2]
     rows = w_out_ref[...].astype(f32)
     weight = rows[:8]
     for n in range(1, 2 * X):
         weight = jnp.where(core * X + x == n, rows[n * 8 : n * 8 + 8], weight)
-    row = lax.broadcasted_iota(jnp.int32, (8, HEAD), 0)
-    half = Z * HEAD
-    near, far = (
-        jnp.where(y_lo == 0, rows[:, :half], rows[:, half:])
-        for rows in (near_ref[...].astype(f32), far_ref[...].astype(f32))
-    )
-    for z in range(Z):
-        cut = slice(z * HEAD, (z + 1) * HEAD)
-        tile = jnp.where(row == 0, near[:, cut], jnp.where(row == 1, far[:, cut], 0.0))
-        for c in range(2):
-            n = c * Z + z
-            both = jnp.concatenate([weight[:, n * HEAD : (n + 1) * HEAD], tile], axis=0)
-            out_ref[n, :WEIGHT_ROW, :] = jnp.zeros((WEIGHT_ROW, HEAD), bf16)
-            out_ref[n, WEIGHT_ROW:, :] = both.astype(bf16)
-
-
-def fill_payload(place, w_out, near, far):
-    return pl.pallas_call(
-        fill_body,
-        out_shape=jax.ShapeDtypeStruct((2 * Z, ROWS, HEAD), bf16),
-        in_specs=[SMEM, VMEM, VMEM, VMEM],
-        out_specs=VMEM,
-        compiler_params=pltpu.CompilerParams(vmem_limit_bytes=8 << 20),
-        name="fill",
-    )(place, w_out, near, far)
-
-
-def query_body(arrived_ref, near_ref, far_ref, payload, out, parts, sent, sem):
+    weight = weight.astype(bf16)
     features = arrived_ref[...].astype(f32)
     total = jnp.dot(
         features[:, 0, :].astype(bf16), near_ref[...], preferred_element_type=f32
@@ -195,31 +167,25 @@
         c, cut = h // 8, slice(h * HEAD, (h + 1) * HEAD)
         parts[c * Z : (c + 1) * Z, h % 8, :] = high[:, cut]
         parts[c * Z : (c + 1) * Z, 8 + h % 8, :] = low[:, cut]
-    sent[...] = parts[...].astype(bf16)
-    back = pltpu.make_async_copy(sent, out.at[:, pl.ds(0, 16), :], sem.at[0])
-    back.start()
-    back.wait()
-
-
-def query_payload(arrived, near, far, payload):
+    out_ref[:, :WEIGHT_ROW, :] = parts[...].astype(bf16)
+    for n in range(2 * Z):
+        out_ref[n, WEIGHT_ROW:, :] = weight[:, n * HEAD : (n + 1) * HEAD]
+
+
+def query_payload(place, arrived, near, far, w_out):
     return pl.pallas_call(
         query_body,
-        out_shape=jax.ShapeDtypeStruct(payload.shape, bf16),
-        in_specs=[VMEM, VMEM, VMEM, HBM],
-        out_specs=HBM,
-        input_output_aliases={3: 0},
-        scratch_shapes=[
-            pltpu.VMEM((2 * Z, 16, HEAD), f32),
-            pltpu.VMEM((2 * Z, 16, HEAD), bf16),
-            pltpu.SemaphoreType.DMA((1,)),
-        ],
-        compiler_params=pltpu.CompilerParams(vmem_limit_bytes=8 << 20),
+        out_shape=jax.ShapeDtypeStruct((2 * Z, ROWS, HEAD), bf16),
+        in_specs=[SMEM, VMEM, VMEM, VMEM, VMEM],
+        out_specs=VMEM,
+        scratch_shapes=[pltpu.VMEM((2 * Z, 16, HEAD), f32)],
+        compiler_params=pltpu.CompilerParams(vmem_limit_bytes=12 << 20),
         name="query",
-    )(arrived, near, far, payload)
+    )(place, arrived, near, far, w_out)
 
 
 def attend_body(
-    place_ref, len_ref, normed_ref, other_ref, cos_ref, sin_ref, parts, gathered, out_ref, w_ref, q_ref, sem, q_sem
+    place_ref, len_ref, normed_ref, other_ref, cos_ref, sin_ref, last_ref, parts, gathered, out_ref, w_ref, q_ref, sem, q_sem
 ):
     fetch = pltpu.make_async_copy(parts.at[:, pl.ds(0, 16), :], q_ref, q_sem.at[0])
     fetch.start()
@@ -280,20 +246,26 @@
     for copy in copies[1]:
         copy.wait()
     weight = w_ref[1].reshape(Y_LO * Z * HEAD, 256)
-    parts = [jnp.dot(t, weight, preferred_element_type=f32) for t in (third, second, first)]
-    total = parts[0] + parts[1] + parts[2]
+    stacked = jnp.dot(
+        jnp.concatenate([third, second, first], axis=0), weight, preferred_element_type=f32
+    )
+    total = stacked[:16] + stacked[16:32] + stacked[32:]
     head = lax.broadcasted_iota(jnp.int32, (16, HEAD), 0)
     context = jnp.where((head & 7) < 4, total[:, :HEAD], total[:, HEAD:])
     turned = jnp.concatenate([context[8:], context[:8]], axis=0)
     context = jnp.where(core == 0, context, turned).astype(bf16)
-    out_ref[...] = jnp.broadcast_to(context[None], out_ref.shape)
-
-
-def attend(place, lengths, normed, other, cosine, sine, parts, gathered):
+    last = last_ref[...].astype(f32)
+    for n in range(2 * Z):
+        out_ref[n, :16, :] = context
+        tile = jnp.broadcast_to(last[:, n * HEAD : (n + 1) * HEAD], (8, HEAD))
+        out_ref[n, 16:, :] = tile.astype(bf16)
+
+
+def attend(place, lengths, normed, other, cosine, sine, last, parts, gathered):
     return pl.pallas_call(
         attend_body,
-        out_shape=jax.ShapeDtypeStruct((2 * Z, 16, HEAD), bf16),
-        in_specs=[SMEM, SMEM, VMEM, VMEM, VMEM, VMEM, HBM, HBM],
+        out_shape=jax.ShapeDtypeStruct((2 * Z, 24, HEAD), bf16),
+        in_specs=[SMEM, SMEM, VMEM, VMEM, VMEM, VMEM, VMEM, HBM, HBM],
         out_specs=VMEM,
         scratch_shapes=[
             pltpu.VMEM((2, Y_LO, Z, HEAD, 256), bf16),
@@ -303,7 +275,7 @@
         ],
         compiler_params=pltpu.CompilerParams(vmem_limit_bytes=48 << 20),
         name="attend",
-    )(place, lengths, normed, other, cosine, sine, parts, gathered)
+    )(place, lengths, normed, other, cosine, sine, last, parts, gathered)
 
 
 def local(
@@ -324,13 +296,11 @@
     units, outgoing = lax.optimization_barrier((units, outgoing))
     arrived = lax.all_to_all(outgoing, "fsdp", 0, 0, tiled=True, axis_index_groups=Z_GROUPS)
     w_query_other = lax.ppermute(w_query, "fsdp", Y_LO_SWAP)
-    last_other = lax.ppermute(last_input, "fsdp", Y_LO_SWAP)
-    payload = fill_payload(place, w_out, last_input, last_other)
-
-    payload = query_payload(arrived, w_query, w_query_other, payload)
+
+    payload = query_payload(place, arrived, w_query, w_query_other, w_out)
     parts = lax.all_to_all(payload, BOTH, 0, 0, tiled=True, axis_index_groups=CORE_Z_GROUPS)
 
-    rows, lengths, _ = lax.optimization_barrier((hidden[0], lengths, payload))
+    rows, lengths, parts = lax.optimization_barrier((hidden[0], lengths, parts))
     both_lengths = jnp.concatenate([lengths, lax.ppermute(lengths, "dp", CORE_SWAP)])
     floats = rows.astype(f32)
     normed = (
@@ -340,22 +310,19 @@
     cosine, sine = rope_tables(jnp.arange(seq_len), HEAD)
 
     weight = lax.all_gather(
-        parts[:, WEIGHT_ROW:HIDDEN_ROW], "dp", axis=0, tiled=False, axis_index_groups=X_GROUPS
+        parts[:, WEIGHT_ROW:], "dp", axis=0, tiled=False, axis_index_groups=X_GROUPS
     ).reshape(X, 2, Z, 8, HEAD)
     weight = jnp.transpose(weight, (2, 1, 0, 3, 4)).reshape(2 * Z * 32, HEAD)
     weight = jnp.where(core == y_lo, weight, lax.ppermute(weight, BOTH, CROSS_SWAP))
-    inputs = lax.dynamic_slice(parts, (core * Z, HIDDEN_ROW, 0), (Z, 2, HEAD)).astype(f32)
-    inputs = jnp.where(y_lo == 0, inputs, inputs[:, ::-1])
-    inputs = jnp.transpose(inputs, (1, 0, 2)).reshape(2 * Z, HEAD)
-
-    gathered, weight, inputs, both_lengths, normed, other, cosine, sine = lax.optimization_barrier(
-        (gathered, weight, inputs, both_lengths, normed, other, cosine, sine)
-    )
-    context = attend(place, both_lengths, normed, other, cosine, sine, parts, gathered)
+    gathered, weight, both_lengths, normed, other, cosine, sine = lax.optimization_barrier(
+        (gathered, weight, both_lengths, normed, other, cosine, sine)
+    )
+    context = attend(place, both_lengths, normed, other, cosine, sine, last_input, parts, gathered)
     contexts = lax.all_to_all(context, "fsdp", 0, 0, tiled=True)
 
     slabs = width // HEAD
-    contexts = contexts.reshape(slabs, 2, 8 * HEAD)
+    inputs = contexts[:, 16].astype(f32)
+    contexts = contexts[:, :16].reshape(slabs, 2, 8 * HEAD)
     halves = jnp.einsum("sad,dn->asn", contexts, weight, preferred_element_type=f32)
     kept = lax.dynamic_index_in_dim(halves, core, 0, keepdims=False)
     given = lax.dynamic_index_in_dim(halves, 1 - core, 0, keepdims=False)

time: 190 us -> 201 us (1.058)
  blocking collectives: 26.3 us -> 78.9 us
  waiting for transfers between devices: 60.3 us -> 31.2 us
  starting transfers between devices: 60.8 us -> 36.9 us
  Pallas kernels: 14.9 us -> 26.9 us
    all_to_all x0 -> x2, blocking collectives: none -> 53.5 us  [the longest x1 27 us: local(): lax.all_to_all(outgoing, 'fsdp', 0, 0, tiled=True, axis_index_groups=Z_GR...]
    all_to_all x2 -> x0, waiting for transfers between devices: 23.4 us -> none  [the longest x1 19.2 us: local(): lax.all_to_all(payload, BOTH, 0, 0, tiled=True, axis_index_groups=CORE_Z_...]
    all_to_all x2 -> x0, starting transfers between devices: 22.9 us -> none  [the longest x1 15.5 us: local(): lax.all_to_all(outgoing, 'fsdp', 0, 0, tiled=True, axis_index_groups=Z_GR...]
    pallas_call x1, Pallas kernels: 0.71 us -> 9.06 us  [pair(): pl.pallas_call(pair_body, out_shape=jax.ShapeDtypeStruct((2, *near.shape)...]
    pallas_call x1, Pallas kernels: 0.58 us -> 5.75 us  [core_unit(): pl.pallas_call(unit_body, out_shape=jax.ShapeDtypeStruct((w_key.shape[0],...]
    ppermute x1, waiting for transfers between devices: 4.33 us -> 0.01 us  [local(): lax.ppermute(weight, BOTH, CROSS_SWAP)]
    ppermute x1, starting transfers between devices: 5.35 us -> 1.95 us  [local(): other = lax.ppermute(normed, 'dp', CORE_SWAP)]
    ppermute x1 -> x0, waiting for transfers between devices: 2.8 us -> none  [local(): last_other = lax.ppermute(last_input, 'fsdp', Y_LO_SWAP)]
  transfers between devices with their start and end apart: 12 -> 9, of which waited for: 8 -> 5; matrix products, arithmetic and copies ran while one was open for 3% -> 3% of each run, Pallas kernels for 2% -> 2%
where the time goes in v7:
time: 201 us; the launch traced here: 200 us
  blocking collectives  78.9 us (39%)
  starting transfers between devices  36.9 us (18%)
  waiting for transfers between devices  31.2 us (16%)
  Pallas kernels  26.9 us (13%)
  between operations  14.3 us (7%)
  local copies, waits for them, and re-layouts  5.58 us (3%)
  other arithmetic  5.48 us (3%)
    all_to_all x1, blocking collectives, local(): lax.all_to_all(outgoing, 'fsdp', 0, 0, tiled=True, axis_index_groups=Z_GR...  27 us
    all_to_all x1, blocking collectives, local(): lax.all_to_all(payload, BOTH, 0, 0, tiled=True, axis_index_groups=CORE_Z_...  26.5 us
    all_to_all x1, blocking collectives, local(): lax.all_to_all(outgoing[:, None], 'dp', split_axis=0, concat_axis=1, tile...  14.5 us
    all_to_all x1, waiting for transfers between devices, local(): contexts = lax.all_to_all(context, 'fsdp', 0, 0, tiled=True)  14.3 us
    ppermute x1, starting transfers between devices, local(): residual = inputs + (kept + lax.ppermute(given, 'dp', CORE_SWAP))  12.3 us
    all_to_all x1, waiting for transfers between devices, local(): lax.all_to_all(jnp.broadcast_to(partial[None, None, :], (slabs, 1, slabs)...  12.1 us
    all_gather x1, blocking collectives, local(): lax.all_gather(parts[:, WEIGHT_ROW:], 'dp', axis=0, tiled=False, axis_ind...  10.9 us
    pallas_call x1, Pallas kernels, pair(): pl.pallas_call(pair_body, out_shape=jax.ShapeDtypeStruct((2, *near.shape)...  9.06 us
  transfers between devices with their start and end apart: 9, of which 5 were waited for; matrix products, arithmetic and copies ran while one was open for 3% of the time, Pallas kernels for 2%

profile of v7, /device:TPU:1, one launch (start us, length us, event | category | flops | bytes accessed | tf_op | source)
XLA Modules:
  0.0 199.7 jit_solution(9049879994296155979)
XLA Ops:
  7.2 0.7 pad_add_fusion.place_ref
  7.9 5.8 %unit.1.near = bf16[128,512]{1,0:T(8,128)(2,1)} custom-call(s32[4]{0:T(128)} %pad_add_fusion.place_ref, bf16[128,512]{1,0:T(8,128)(2,1)} %w_key.1, bf16[128,512]{1,0:T(8,128)(2,1)} %w_value.1), custom_call_target="tpu_custom_call" | custom-call | tf_op jit(solution)/shard_map/unit/pallas_call | solution.py:79
  13.6 4.0 %collective-permute-start = (bf16[128,512]{1,0:T(8,128)(2,1)}, bf16[128,512]{1,0:T(8,128)(2,1)S(1)}, u32[]{:S(2)}, u32[]{:S(2)}) collective-permute-start(bf16[128,512]{1,0:T(8,128)(2,1)} %unit.1.near), channel_id=1, source_target_pairs={{0,16},{1,17},{2,18},{3,19},{4,20},{5,21},{6,22},{7,23},{8,24},{9,... | collective-permute-start | bytes 393224 | tf_op jit(solution)/shard_map/ppermute | solution.py:291
  17.7 2.6 %collective-permute-done.far = bf16[128,512]{1,0:T(8,128)(2,1)S(1)} collective-permute-done((bf16[128,512]{1,0:T(8,128)(2,1)}, bf16[128,512]{1,0:T(8,128)(2,1)S(1)}, u32[]{:S(2)}, u32[]{:S(2)}) %collective-permute-start) | collective-permute-done | bytes 131104 | tf_op jit(solution)/shard_map/ppermute | solution.py:291
  20.2 0.7 copy-done.6
  20.9 9.1 %pair.1 = bf16[2,128,512]{2,1,0:T(8,128)(2,1)} custom-call(bf16[128,512]{1,0:T(8,128)(2,1)} %unit.1.near, bf16[128,512]{1,0:T(8,128)(2,1)} %copy-done.6), custom_call_target="tpu_custom_call" | custom-call | tf_op jit(solution)/shard_map/pair/pallas_call | solution.py:99
  29.9 0.0 all-gather.4.cloned.1.call-update
  30.0 3.4 %collective-permute-start.1 = (bf16[128,2048]{1,0:T(8,128)(2,1)}, bf16[128,2048]{1,0:T(8,128)(2,1)S(1)}, u32[]{:S(2)}, u32[]{:S(2)}) collective-permute-start(bf16[128,2048]{1,0:T(8,128)(2,1)} %near_ref.1), channel_id=1, source_target_pairs={{0,16},{1,17},{2,18},{3,19},{4,20},{5,21},{6,22},{7,23},{8,24},{9,... | collective-permute-start | bytes 1572872 | tf_op jit(solution)/shard_map/ppermute | solution.py:298
  33.3 2.4 %open.1 = (bf16[16,8,128]{2,1,0:T(8,128)(2,1)}, bf16[1,4096]{1,0:T(2,128)(2,1)}) custom-call(s32[4]{0:T(128)} %pad_add_fusion.place_ref, bf16[1,256,4096]{2,1,0:T(8,128)(2,1)} %hidden, f32[1,4096]{1,0:T(1,128)} %bitcast.40), custom_call_target="tpu_custom_call" | custom-call | tf_op jit(solution)/shard_map/open/pallas_call | solution.py:135
  35.7 27.0 %all_to_all.32.arrived_ref = bf16[16,8,128]{2,1,0:T(8,128)(2,1)S(1)} all-to-all(bf16[16,8,128]{2,1,0:T(8,128)(2,1)} %get-tuple-element.21), channel_id=1, replica_groups={{0,1,2,3,4,5,6,7,8,9,10,11,12,13,14,15},{16,17,18,19,20,21,22,23,24,25,..., dimensions={0} | all-to-all | bytes 65536 | tf_op jit(solution)/shard_map/all_to_all | solution.py:297
  62.7 1.0 copy-done
  63.8 1.0 copy-done.1
  64.8 0.7 copy-done.3
  65.5 1.0 query.1
  66.5 26.5 %all_to_all.33.parts = bf16[32,24,128]{2,1,0:T(8,128)(2,1)S(1)} all-to-all(bf16[32,24,128]{2,1,0:T(8,128)(2,1)S(1)} %query.1), channel_id=1, replica_groups={{0,1,2,3,4,5,6,7,8,9,10,11,12,13,14,15,32,33,34,35,36,37,38,39,40,41,42..., dimensions={0} | all-to-all | bytes 393216 | tf_op jit(solution)/shard_map/all_to_all | solution.py:301
  93.0 2.1 %fusion = f32[256]{0:T(256)S(1)} fusion(bf16[256,4096]{1,0:T(8,128)(2,1)} %bitcast.35), kind=kLoop, calls=%fused_computation.2 | loop fusion | flops 3145472 | bytes 2098176 | tf_op jit(solution)/shard_map/reduce_sum | solution.py:307
  95.2 0.6 fusion.2.normed_ref
  95.8 2.0 collective-permute-start.4
  97.8 10.9 %all-gather.1 = bf16[128,8,128]{2,1,0:T(8,128)(2,1)S(1)} all-gather(bf16[32,8,128]{2,1,0:T(8,128)(2,1)S(1)} %slice.9), channel_id=3, replica_groups={{0,64,128,192},{32,96,160,224},{256,320,384,448},{288,352,416,480},{1,6..., dimensions={0}, use_global_device_ids=true | all-gather | bytes 327680 | tf_op jit(solution)/shard_map/all_gather | solution.py:312
  108.7 0.1 copy.20
  108.8 4.3 %collective-permute-start.2 = (bf16[1024,128]{1,0:T(8,128)(2,1)S(1)}, bf16[1024,128]{1,0:T(8,128)(2,1)S(1)}, u32[]{:S(2)}, u32[]{:S(2)}) collective-permute-start(bf16[1024,128]{1,0:T(8,128)(2,1)S(1)} %bitcast.39), channel_id=1, source_target_pairs={{16,32},{17,33},{18,34},{19,35},{20,36},{21,37},{22,38},{23,39},{2... | collective-permute-start | bytes 786440 | tf_op jit(solution)/shard_map/ppermute | solution.py:316
  113.1 0.5 fusion.7
  113.7 0.1 pad_maximum_fusion
  113.8 1.9 collective-permute-start.3
  115.8 1.4 collective-permute-done.3
  117.1 0.6 pad_add_fusion.1.len_ref
  117.8 0.1 broadcast_select_fusion
  117.8 0.0 all-gather.4.cloned.1.call-done
  117.9 0.0 copy-start.8
  117.9 0.0 copy-start.9
  117.9 8.7 %attend.1 = bf16[32,24,128]{2,1,0:T(8,128)(2,1)} custom-call(s32[4]{0:T(128)S(1)} %copy-done.4, s32[2]{0:T(128)S(1)} %pad_add_fusion.1.len_ref, bf16[256,4096]{1,0:T(8,128)(2,1)S(1)} %fusion.2.normed_ref, bf16[256,4096]{1,0:T(8,128)(2,1)} %collective-permute-done.4.other_ref, f32[256,128]{1,0:T(8,128)S(1)} %get-tuple-element.28.cos_ref, ...), custom_call_target="tpu_custom_call" | custom-call | tf_op jit(solution)/shard_map/attend/pallas_call | solution.py:265
  126.6 5.2 %all-to-all-start.2 = ((bf16[32,24,128]{2,1,0:T(8,128)(2,1)}), bf16[32,24,128]{2,1,0:T(8,128)(2,1)S(1)}, u32[]{:S(2)}, u32[]{:S(2)}) async-start(bf16[32,24,128]{2,1,0:T(8,128)(2,1)} %attend.1), calls=%async_computation.2 | async-start | bytes 393216 | tf_op jit(solution)/shard_map/all_to_all | solution.py:321
  131.8 0.2 select_reduce_fusion
  132.0 0.1 fusion.11
  132.1 0.1 reduce_window_sum.11
  132.1 0.8 dynamic_slice.12
  132.9 0.2 select_reduce_fusion.1
  133.1 14.3 %all-to-all-done.2 = bf16[32,24,128]{2,1,0:T(8,128)(2,1)S(1)} async-done(((bf16[32,24,128]{2,1,0:T(8,128)(2,1)}), bf16[32,24,128]{2,1,0:T(8,128)(2,1)S(1)}, u32[]{:S(2)}, u32[]{:S(2)}) %all-to-all-start.2) | async-done | bytes 196640 | tf_op jit(solution)/shard_map/all_to_all | solution.py:321
  147.5 0.2 fusion.4
  147.7 12.3 %collective-permute-start.5 = (f32[32,128]{1,0:T(8,128)S(1)}, f32[32,128]{1,0:T(8,128)S(1)}, u32[]{:S(2)}, u32[]{:S(2)}) collective-permute-start(f32[32,128]{1,0:T(8,128)S(1)} %dynamic-slice_bitcast_fusion), channel_id=1, source_target_pairs={{0,32},{32,0},{64,96},{96,64},{128,160},{160,128},{192,224},{224,1... | collective-permute-start | bytes 49160 | tf_op jit(solution)/shard_map/ppermute | solution.py:329
  160.0 0.8 collective-permute-done.5
  160.8 0.1 multiply_reduce_fusion
  160.9 0.6 broadcast_in_dim.17
  161.5 3.8 %all-to-all-start.3 = ((f32[32,1,32]{2,1,0:T(1,128)}), f32[32,1,32]{2,1,0:T(1,128)S(1)}, u32[]{:S(2)}, u32[]{:S(2)}) async-start(f32[32,1,32]{2,1,0:T(1,128)} %broadcast_in_dim.17), calls=%async_computation.3 | async-start | bytes 32768 | tf_op jit(solution)/shard_map/all_to_all | solution.py:333
  165.4 12.1 %all-to-all-done.3 = f32[32,1,32]{2,1,0:T(1,128)S(1)} async-done(((f32[32,1,32]{2,1,0:T(1,128)}), f32[32,1,32]{2,1,0:T(1,128)S(1)}, u32[]{:S(2)}, u32[]{:S(2)}) %all-to-all-start.3) | async-done | bytes 4128 | tf_op jit(solution)/shard_map/all_to_all | solution.py:333
  177.5 0.2 fusion.3
  177.7 14.5 %all_to_all.34 = bf16[16,1,4,128]{3,2,1,0:T(4,128)(2,1)S(1)} all-to-all(bf16[16,1,4,128]{3,2,1,0:T(4,128)(2,1)S(1)} %copy.23), channel_id=1, replica_groups=mesh['dp'=16,'fsdp'=32] {'dp'}, dimensions={0} | all-to-all | bytes 32768 | tf_op jit(solution)/shard_map/all_to_all | solution.py:352
  192.2 0.6 copy.28
  (31 shorter events, 0.2 us)
Async XLA Ops:
  6.5 88.6 %copy-start.7 = (f32[4096]{0:T(1024)S(1)}, f32[4096]{0:T(1024)}, u32[]{:S(2)}) copy-start(f32[4096]{0:T(1024)} %param.14) | copy-start | bytes 49156
  6.5 111.3 %all-gather.4.cloned.1.call-start = ((), (), s32[]{:S(2)}) async-start(), calls=%async_computation.5 | async-start | bytes 4456448 | tf_op jit(solution)/shard_map/all_gather | solution.py:292
  13.6 6.6 %collective-permute-start = (bf16[128,512]{1,0:T(8,128)(2,1)}, bf16[128,512]{1,0:T(8,128)(2,1)S(1)}, u32[]{:S(2)}, u32[]{:S(2)}) collective-permute-start(bf16[128,512]{1,0:T(8,128)(2,1)} %unit.1.near), channel_id=1, source_target_pairs={{0,16},{1,17},{2,18},{3,19},{4,20},{5,21},{6,22},{7,23},{8,24},{9,... | collective-permute-start | bytes 393224 | tf_op jit(solution)/shard_map/ppermute | solution.py:291
  20.2 0.7 copy-start.6
  30.0 32.8 %collective-permute-start.1 = (bf16[128,2048]{1,0:T(8,128)(2,1)}, bf16[128,2048]{1,0:T(8,128)(2,1)S(1)}, u32[]{:S(2)}, u32[]{:S(2)}) collective-permute-start(bf16[128,2048]{1,0:T(8,128)(2,1)} %near_ref.1), channel_id=1, source_target_pairs={{0,16},{1,17},{2,18},{3,19},{4,20},{5,21},{6,22},{7,23},{8,24},{9,... | collective-permute-start | bytes 1572872 | tf_op jit(solution)/shard_map/ppermute | solution.py:298
  62.7 1.0 copy-start
  63.8 1.0 copy-start.1
  64.8 0.7 copy-start.3
  65.5 29.6 %copy-start.5 = (bf16[1,256,4096]{2,1,0:T(8,128)(2,1)S(1)}, bf16[1,256,4096]{2,1,0:T(8,128)(2,1)}, u32[]{:S(2)}) copy-start(bf16[1,256,4096]{2,1,0:T(8,128)(2,1)} %hidden) | copy-start | bytes 6291460
  93.0 24.9 %copy-start.2 = (bf16[1,4096]{1,0:T(2,128)(2,1)S(1)}, bf16[1,4096]{1,0:T(2,128)(2,1)}, u32[]{:S(2)}) copy-start(bf16[1,4096]{1,0:T(2,128)(2,1)} %get-tuple-element.30.last_ref) | copy-start | bytes 24580
  93.0 24.9 %copy-start.4 = (s32[4]{0:T(128)S(1)}, s32[4]{0:T(128)}, u32[]{:S(2)}) copy-start(s32[4]{0:T(128)} %pad_add_fusion.place_ref) | copy-start | bytes 52
  95.8 22.0 %collective-permute-start.4 = (bf16[256,4096]{1,0:T(8,128)(2,1)S(1)}, bf16[256,4096]{1,0:T(8,128)(2,1)}, u32[]{:S(2)}, u32[]{:S(2)}) collective-permute-start(bf16[256,4096]{1,0:T(8,128)(2,1)S(1)} %fusion.2.normed_ref), channel_id=1, source_target_pairs={{0,32},{32,0},{64,96},{96,64},{128,160},{160,128},{192,224},{224,1... | collective-permute-start | bytes 6291464 | tf_op jit(solution)/shard_map/ppermute | solution.py:309
  108.8 9.0 %collective-permute-start.2 = (bf16[1024,128]{1,0:T(8,128)(2,1)S(1)}, bf16[1024,128]{1,0:T(8,128)(2,1)S(1)}, u32[]{:S(2)}, u32[]{:S(2)}) collective-permute-start(bf16[1024,128]{1,0:T(8,128)(2,1)S(1)} %bitcast.39), channel_id=1, source_target_pairs={{16,32},{17,33},{18,34},{19,35},{20,36},{21,37},{22,38},{23,39},{2... | collective-permute-start | bytes 786440 | tf_op jit(solution)/shard_map/ppermute | solution.py:316
  113.8 3.3 %collective-permute-start.3 = (s32[1]{0:T(128)}, s32[1]{0:T(128)}, u32[]{:S(2)}, u32[]{:S(2)}) collective-permute-start(s32[1]{0:T(128)} %param.11), channel_id=1, source_target_pairs={{0,32},{32,0},{64,96},{96,64},{128,160},{160,128},{192,224},{224,1... | collective-permute-start | bytes 20 | tf_op jit(solution)/shard_map/ppermute | solution.py:304
  117.9 13.9 %copy-start.8 = (s32[1024]{0:T(1024)S(1)}, s32[1024]{0:T(1024)}, u32[]{:S(2)}) copy-start(s32[1024]{0:T(1024)} %param.13) | copy-start | bytes 12292
  117.9 13.9 %copy-start.9 = (s32[32]{0:T(128)S(1)}, s32[32]{0:T(128)}, u32[]{:S(2)}) copy-start(s32[32]{0:T(128)} %param.12) | copy-start | bytes 388
  126.6 20.8 %all-to-all-start.2 = ((bf16[32,24,128]{2,1,0:T(8,128)(2,1)}), bf16[32,24,128]{2,1,0:T(8,128)(2,1)S(1)}, u32[]{:S(2)}, u32[]{:S(2)}) async-start(bf16[32,24,128]{2,1,0:T(8,128)(2,1)} %attend.1), calls=%async_computation.2 | async-start | bytes 393216 | tf_op jit(solution)/shard_map/all_to_all | solution.py:321
  147.7 13.1 %collective-permute-start.5 = (f32[32,128]{1,0:T(8,128)S(1)}, f32[32,128]{1,0:T(8,128)S(1)}, u32[]{:S(2)}, u32[]{:S(2)}) collective-permute-start(f32[32,128]{1,0:T(8,128)S(1)} %dynamic-slice_bitcast_fusion), channel_id=1, source_target_pairs={{0,32},{32,0},{64,96},{96,64},{128,160},{160,128},{192,224},{224,1... | collective-permute-start | bytes 49160 | tf_op jit(solution)/shard_map/ppermute | solution.py:329
  161.5 16.0 %all-to-all-start.3 = ((f32[32,1,32]{2,1,0:T(1,128)}), f32[32,1,32]{2,1,0:T(1,128)S(1)}, u32[]{:S(2)}, u32[]{:S(2)}) async-start(f32[32,1,32]{2,1,0:T(1,128)} %broadcast_in_dim.17), calls=%async_computation.3 | async-start | bytes 32768 | tf_op jit(solution)/shard_map/all_to_all | solution.py:333
Sparse Core Ops, SparseCore 0:
  30.1 84.2 all-gather.3

commit v8 on v7

--- a/solution.py
+++ b/solution.py
@@ -63,46 +63,36 @@
     )
 
 
-def unit_body(place_ref, w_key, w_value, out, sem):
-    columns = pl.ds(pl.multiple_of(place_ref[2] * 256, 256), 256)
-    copies = [
-        pltpu.make_async_copy(w.at[:, columns], out.at[:, pl.ds(k * 256, 256)], sem.at[k])
-        for k, w in enumerate((w_key, w_value))
-    ]
-    for copy in copies:
-        copy.start()
-    for copy in copies:
-        copy.wait()
+def unit_body(place_ref, key_ref, value_ref, out_ref):
+    core = place_ref[2]
+    for k, w in enumerate((key_ref, value_ref)):
+        columns = pl.multiple_of(core * 256, 256)
+        out_ref[:, k * 256 : (k + 1) * 256] = w[:, pl.ds(columns, 256)]
 
 
 def core_unit(place, w_key, w_value):
     return pl.pallas_call(
         unit_body,
         out_shape=jax.ShapeDtypeStruct((w_key.shape[0], 512), bf16),
-        in_specs=[SMEM, HBM, HBM],
-        out_specs=HBM,
-        scratch_shapes=[pltpu.SemaphoreType.DMA((2,))],
+        in_specs=[SMEM, VMEM, VMEM],
+        out_specs=VMEM,
         compiler_params=pltpu.CompilerParams(vmem_limit_bytes=62 << 20),
         name="unit",
     )(place, w_key, w_value)
 
 
-def pair_body(near, far, out, sem):
-    copies = [pltpu.make_async_copy(rows, out.at[k], sem.at[k]) for k, rows in enumerate((near, far))]
-    for copy in copies:
-        copy.start()
-    for copy in copies:
-        copy.wait()
+def pair_body(near_ref, far_ref, out_ref):
+    out_ref[0] = near_ref[...]
+    out_ref[1] = far_ref[...]
 
 
 def pair(near, far):
     return pl.pallas_call(
         pair_body,
         out_shape=jax.ShapeDtypeStruct((2, *near.shape), bf16),
-        in_specs=[HBM, HBM],
-        out_specs=HBM,
-        scratch_shapes=[pltpu.SemaphoreType.DMA((2,))],
-        compiler_params=pltpu.CompilerParams(vmem_limit_bytes=62 << 20),
+        in_specs=[VMEM, VMEM],
+        out_specs=VMEM,
+        compiler_params=pltpu.CompilerParams(vmem_limit_bytes=8 << 20),
         name="pair",
     )(near, far)
 

time: 201 us -> 188 us (0.935)
  Pallas kernels: 26.9 us -> 14.5 us
    pallas_call x1, Pallas kernels: 9.06 us -> 0.72 us  [pair(): pl.pallas_call(pair_body, out_shape=jax.ShapeDtypeStruct((2, *near.shape)...]
    pallas_call x1, Pallas kernels: 5.75 us -> 1.63 us  [core_unit(): pl.pallas_call(unit_body, out_shape=jax.ShapeDtypeStruct((w_key.shape[0],...]
where the time goes in v8:
time: 188 us; the launch traced here: 187 us
  blocking collectives  78.9 us (42%)
  starting transfers between devices  36.8 us (20%)
  waiting for transfers between devices  31.2 us (17%)
  Pallas kernels  14.5 us (8%)
  between operations  14.3 us (8%)
  local copies, waits for them, and re-layouts  5.83 us (3%)
  other arithmetic  5.48 us (3%)
    all_to_all x1, blocking collectives, local(): lax.all_to_all(outgoing, 'fsdp', 0, 0, tiled=True, axis_index_groups=Z_GR...  27 us
    all_to_all x1, blocking collectives, local(): lax.all_to_all(payload, BOTH, 0, 0, tiled=True, axis_index_groups=CORE_Z_...  26.5 us
    all_to_all x1, blocking collectives, local(): lax.all_to_all(outgoing[:, None], 'dp', split_axis=0, concat_axis=1, tile...  14.5 us
    all_to_all x1, waiting for transfers between devices, local(): contexts = lax.all_to_all(context, 'fsdp', 0, 0, tiled=True)  14.3 us
    ppermute x1, starting transfers between devices, local(): residual = inputs + (kept + lax.ppermute(given, 'dp', CORE_SWAP))  12.3 us
    all_to_all x1, waiting for transfers between devices, local(): lax.all_to_all(jnp.broadcast_to(partial[None, None, :], (slabs, 1, slabs)...  12.1 us
    all_gather x1, blocking collectives, local(): lax.all_gather(parts[:, WEIGHT_ROW:], 'dp', axis=0, tiled=False, axis_ind...  10.9 us
    pallas_call x1, Pallas kernels, attend(): pl.pallas_call(attend_body, out_shape=jax.ShapeDtypeStruct((2 * Z, 24, HE...  8.73 us
  transfers between devices with their start and end apart: 9, of which 5 were waited for; matrix products, arithmetic and copies ran while one was open for 3% of the time, Pallas kernels for 2%

profile of v8, /device:TPU:1, one launch (start us, length us, event | category | flops | bytes accessed | tf_op | source)
XLA Modules:
  0.0 187.4 jit_solution(11008656966619235227)
XLA Ops:
  7.2 0.7 pad_add_fusion.place_ref
  7.9 1.6 unit.1.near_ref
  9.5 4.0 %collective-permute-start = (bf16[128,512]{1,0:T(8,128)(2,1)}, bf16[128,512]{1,0:T(8,128)(2,1)S(1)}, u32[]{:S(2)}, u32[]{:S(2)}) collective-permute-start(bf16[128,512]{1,0:T(8,128)(2,1)} %unit.1.near_ref), channel_id=1, source_target_pairs={{0,16},{1,17},{2,18},{3,19},{4,20},{5,21},{6,22},{7,23},{8,24},{9,... | collective-permute-start | bytes 393224 | tf_op jit(solution)/shard_map/ppermute | solution.py:281
  13.5 2.6 %collective-permute-done.far_ref = bf16[128,512]{1,0:T(8,128)(2,1)S(1)} collective-permute-done((bf16[128,512]{1,0:T(8,128)(2,1)}, bf16[128,512]{1,0:T(8,128)(2,1)S(1)}, u32[]{:S(2)}, u32[]{:S(2)}) %collective-permute-start) | collective-permute-done | bytes 131104 | tf_op jit(solution)/shard_map/ppermute | solution.py:281
  16.1 0.9 copy-done
  17.0 0.7 pair.1
  17.7 0.0 all-gather.4.cloned.1.call-update
  17.7 3.4 %collective-permute-start.1 = (bf16[128,2048]{1,0:T(8,128)(2,1)}, bf16[128,2048]{1,0:T(8,128)(2,1)S(1)}, u32[]{:S(2)}, u32[]{:S(2)}) collective-permute-start(bf16[128,2048]{1,0:T(8,128)(2,1)} %near_ref.1), channel_id=1, source_target_pairs={{0,16},{1,17},{2,18},{3,19},{4,20},{5,21},{6,22},{7,23},{8,24},{9,... | collective-permute-start | bytes 1572872 | tf_op jit(solution)/shard_map/ppermute | solution.py:288
  21.1 2.4 %open.1 = (bf16[16,8,128]{2,1,0:T(8,128)(2,1)}, bf16[1,4096]{1,0:T(2,128)(2,1)}) custom-call(s32[4]{0:T(128)} %pad_add_fusion.place_ref, bf16[1,256,4096]{2,1,0:T(8,128)(2,1)} %hidden, f32[1,4096]{1,0:T(1,128)} %bitcast.40), custom_call_target="tpu_custom_call" | custom-call | tf_op jit(solution)/shard_map/open/pallas_call | solution.py:125
  23.5 27.0 %all_to_all.32.arrived_ref = bf16[16,8,128]{2,1,0:T(8,128)(2,1)S(1)} all-to-all(bf16[16,8,128]{2,1,0:T(8,128)(2,1)} %get-tuple-element.21), channel_id=1, replica_groups={{0,1,2,3,4,5,6,7,8,9,10,11,12,13,14,15},{16,17,18,19,20,21,22,23,24,25,..., dimensions={0} | all-to-all | bytes 65536 | tf_op jit(solution)/shard_map/all_to_all | solution.py:287
  50.5 1.0 copy-done.1
  51.6 1.0 copy-done.2
  52.6 0.7 copy-done.4
  53.3 1.0 query.1
  54.3 26.5 %all_to_all.33.parts = bf16[32,24,128]{2,1,0:T(8,128)(2,1)S(1)} all-to-all(bf16[32,24,128]{2,1,0:T(8,128)(2,1)S(1)} %query.1), channel_id=1, replica_groups={{0,1,2,3,4,5,6,7,8,9,10,11,12,13,14,15,32,33,34,35,36,37,38,39,40,41,42..., dimensions={0} | all-to-all | bytes 393216 | tf_op jit(solution)/shard_map/all_to_all | solution.py:291
  80.8 2.1 %fusion = f32[256]{0:T(256)S(1)} fusion(bf16[256,4096]{1,0:T(8,128)(2,1)} %bitcast.35), kind=kLoop, calls=%fused_computation.2 | loop fusion | flops 3145472 | bytes 2098176 | tf_op jit(solution)/shard_map/reduce_sum | solution.py:297
  82.9 0.6 fusion.2.normed_ref
  83.6 2.0 %collective-permute-start.4 = (bf16[256,4096]{1,0:T(8,128)(2,1)S(1)}, bf16[256,4096]{1,0:T(8,128)(2,1)}, u32[]{:S(2)}, u32[]{:S(2)}) collective-permute-start(bf16[256,4096]{1,0:T(8,128)(2,1)S(1)} %fusion.2.normed_ref), channel_id=1, source_target_pairs={{0,32},{32,0},{64,96},{96,64},{128,160},{160,128},{192,224},{224,1... | collective-permute-start | bytes 6291464 | tf_op jit(solution)/shard_map/ppermute | solution.py:299
  85.6 10.9 %all-gather.1 = bf16[128,8,128]{2,1,0:T(8,128)(2,1)S(1)} all-gather(bf16[32,8,128]{2,1,0:T(8,128)(2,1)S(1)} %slice.9), channel_id=3, replica_groups={{0,64,128,192},{32,96,160,224},{256,320,384,448},{288,352,416,480},{1,6..., dimensions={0}, use_global_device_ids=true | all-gather | bytes 327680 | tf_op jit(solution)/shard_map/all_gather | solution.py:302
  96.5 0.1 copy.20
  96.6 4.3 %collective-permute-start.2 = (bf16[1024,128]{1,0:T(8,128)(2,1)S(1)}, bf16[1024,128]{1,0:T(8,128)(2,1)S(1)}, u32[]{:S(2)}, u32[]{:S(2)}) collective-permute-start(bf16[1024,128]{1,0:T(8,128)(2,1)S(1)} %bitcast.39), channel_id=1, source_target_pairs={{16,32},{17,33},{18,34},{19,35},{20,36},{21,37},{22,38},{23,39},{2... | collective-permute-start | bytes 786440 | tf_op jit(solution)/shard_map/ppermute | solution.py:306
  100.9 0.5 fusion.7
  101.4 0.1 pad_maximum_fusion
  101.6 1.9 %collective-permute-start.3 = (s32[1]{0:T(128)}, s32[1]{0:T(128)}, u32[]{:S(2)}, u32[]{:S(2)}) collective-permute-start(s32[1]{0:T(128)} %param.11), channel_id=1, source_target_pairs={{0,32},{32,0},{64,96},{96,64},{128,160},{160,128},{192,224},{224,1... | collective-permute-start | bytes 20 | tf_op jit(solution)/shard_map/ppermute | solution.py:294
  103.5 1.4 collective-permute-done.3
  104.9 0.6 pad_add_fusion.1.len_ref
  105.5 0.1 broadcast_select_fusion
  105.6 0.0 all-gather.4.cloned.1.call-done
  105.6 0.0 copy-start.8
  105.7 0.0 copy-start.9
  105.7 8.7 %attend.1 = bf16[32,24,128]{2,1,0:T(8,128)(2,1)} custom-call(s32[4]{0:T(128)S(1)} %copy-done.5, s32[2]{0:T(128)S(1)} %pad_add_fusion.1.len_ref, bf16[256,4096]{1,0:T(8,128)(2,1)S(1)} %fusion.2.normed_ref, bf16[256,4096]{1,0:T(8,128)(2,1)} %collective-permute-done.4.other_ref, f32[256,128]{1,0:T(8,128)S(1)} %get-tuple-element.28.cos_ref, ...), custom_call_target="tpu_custom_call" | custom-call | tf_op jit(solution)/shard_map/attend/pallas_call | solution.py:255
  114.4 5.2 %all-to-all-start.2 = ((bf16[32,24,128]{2,1,0:T(8,128)(2,1)}), bf16[32,24,128]{2,1,0:T(8,128)(2,1)S(1)}, u32[]{:S(2)}, u32[]{:S(2)}) async-start(bf16[32,24,128]{2,1,0:T(8,128)(2,1)} %attend.1), calls=%async_computation.2 | async-start | bytes 393216 | tf_op jit(solution)/shard_map/all_to_all | solution.py:311
  119.6 0.2 select_reduce_fusion
  119.8 0.1 fusion.11
  119.8 0.1 reduce_window_sum.11
  119.9 0.8 dynamic_slice.12
  120.7 0.2 select_reduce_fusion.1
  120.9 14.3 %all-to-all-done.2 = bf16[32,24,128]{2,1,0:T(8,128)(2,1)S(1)} async-done(((bf16[32,24,128]{2,1,0:T(8,128)(2,1)}), bf16[32,24,128]{2,1,0:T(8,128)(2,1)S(1)}, u32[]{:S(2)}, u32[]{:S(2)}) %all-to-all-start.2) | async-done | bytes 196640 | tf_op jit(solution)/shard_map/all_to_all | solution.py:311
  135.2 0.2 fusion.4
  135.4 12.3 %collective-permute-start.5 = (f32[32,128]{1,0:T(8,128)S(1)}, f32[32,128]{1,0:T(8,128)S(1)}, u32[]{:S(2)}, u32[]{:S(2)}) collective-permute-start(f32[32,128]{1,0:T(8,128)S(1)} %dynamic-slice_bitcast_fusion), channel_id=1, source_target_pairs={{0,32},{32,0},{64,96},{96,64},{128,160},{160,128},{192,224},{224,1... | collective-permute-start | bytes 49160 | tf_op jit(solution)/shard_map/ppermute | solution.py:319
  147.7 0.8 collective-permute-done.5
  148.5 0.1 multiply_reduce_fusion
  148.6 0.6 broadcast_in_dim.17
  149.3 3.8 %all-to-all-start.3 = ((f32[32,1,32]{2,1,0:T(1,128)}), f32[32,1,32]{2,1,0:T(1,128)S(1)}, u32[]{:S(2)}, u32[]{:S(2)}) async-start(f32[32,1,32]{2,1,0:T(1,128)} %broadcast_in_dim.17), calls=%async_computation.3 | async-start | bytes 32768 | tf_op jit(solution)/shard_map/all_to_all | solution.py:323
  153.1 12.1 %all-to-all-done.3 = f32[32,1,32]{2,1,0:T(1,128)S(1)} async-done(((f32[32,1,32]{2,1,0:T(1,128)}), f32[32,1,32]{2,1,0:T(1,128)S(1)}, u32[]{:S(2)}, u32[]{:S(2)}) %all-to-all-start.3) | async-done | bytes 4128 | tf_op jit(solution)/shard_map/all_to_all | solution.py:323
  165.3 0.2 fusion.3
  165.5 14.5 %all_to_all.34 = bf16[16,1,4,128]{3,2,1,0:T(4,128)(2,1)S(1)} all-to-all(bf16[16,1,4,128]{3,2,1,0:T(4,128)(2,1)S(1)} %copy.23), channel_id=1, replica_groups=mesh['dp'=16,'fsdp'=32] {'dp'}, dimensions={0} | all-to-all | bytes 32768 | tf_op jit(solution)/shard_map/all_to_all | solution.py:342
  180.0 0.6 copy.28
  (31 shorter events, 0.2 us)
Async XLA Ops:
  6.5 76.4 %copy-start.7 = (f32[4096]{0:T(1024)S(1)}, f32[4096]{0:T(1024)}, u32[]{:S(2)}) copy-start(f32[4096]{0:T(1024)} %param.14) | copy-start | bytes 49156
  6.5 99.1 %all-gather.4.cloned.1.call-start = ((), (), s32[]{:S(2)}) async-start(), calls=%async_computation.5 | async-start | bytes 4456448 | tf_op jit(solution)/shard_map/all_gather | solution.py:282
  9.5 6.6 %collective-permute-start = (bf16[128,512]{1,0:T(8,128)(2,1)}, bf16[128,512]{1,0:T(8,128)(2,1)S(1)}, u32[]{:S(2)}, u32[]{:S(2)}) collective-permute-start(bf16[128,512]{1,0:T(8,128)(2,1)} %unit.1.near_ref), channel_id=1, source_target_pairs={{0,16},{1,17},{2,18},{3,19},{4,20},{5,21},{6,22},{7,23},{8,24},{9,... | collective-permute-start | bytes 393224 | tf_op jit(solution)/shard_map/ppermute | solution.py:281
  16.1 0.9 copy-start
  17.7 32.8 %collective-permute-start.1 = (bf16[128,2048]{1,0:T(8,128)(2,1)}, bf16[128,2048]{1,0:T(8,128)(2,1)S(1)}, u32[]{:S(2)}, u32[]{:S(2)}) collective-permute-start(bf16[128,2048]{1,0:T(8,128)(2,1)} %near_ref.1), channel_id=1, source_target_pairs={{0,16},{1,17},{2,18},{3,19},{4,20},{5,21},{6,22},{7,23},{8,24},{9,... | collective-permute-start | bytes 1572872 | tf_op jit(solution)/shard_map/ppermute | solution.py:288
  50.5 1.0 copy-start.1
  51.6 1.0 copy-start.2
  52.6 0.7 copy-start.4
  53.3 29.6 %copy-start.6 = (bf16[1,256,4096]{2,1,0:T(8,128)(2,1)S(1)}, bf16[1,256,4096]{2,1,0:T(8,128)(2,1)}, u32[]{:S(2)}) copy-start(bf16[1,256,4096]{2,1,0:T(8,128)(2,1)} %hidden) | copy-start | bytes 6291460
  80.8 24.8 %copy-start.3 = (bf16[1,4096]{1,0:T(2,128)(2,1)S(1)}, bf16[1,4096]{1,0:T(2,128)(2,1)}, u32[]{:S(2)}) copy-start(bf16[1,4096]{1,0:T(2,128)(2,1)} %get-tuple-element.30.last_ref) | copy-start | bytes 24580
  80.8 24.9 %copy-start.5 = (s32[4]{0:T(128)S(1)}, s32[4]{0:T(128)}, u32[]{:S(2)}) copy-start(s32[4]{0:T(128)} %pad_add_fusion.place_ref) | copy-start | bytes 52
  83.6 22.0 %collective-permute-start.4 = (bf16[256,4096]{1,0:T(8,128)(2,1)S(1)}, bf16[256,4096]{1,0:T(8,128)(2,1)}, u32[]{:S(2)}, u32[]{:S(2)}) collective-permute-start(bf16[256,4096]{1,0:T(8,128)(2,1)S(1)} %fusion.2.normed_ref), channel_id=1, source_target_pairs={{0,32},{32,0},{64,96},{96,64},{128,160},{160,128},{192,224},{224,1... | collective-permute-start | bytes 6291464 | tf_op jit(solution)/shard_map/ppermute | solution.py:299
  96.6 9.0 %collective-permute-start.2 = (bf16[1024,128]{1,0:T(8,128)(2,1)S(1)}, bf16[1024,128]{1,0:T(8,128)(2,1)S(1)}, u32[]{:S(2)}, u32[]{:S(2)}) collective-permute-start(bf16[1024,128]{1,0:T(8,128)(2,1)S(1)} %bitcast.39), channel_id=1, source_target_pairs={{16,32},{17,33},{18,34},{19,35},{20,36},{21,37},{22,38},{23,39},{2... | collective-permute-start | bytes 786440 | tf_op jit(solution)/shard_map/ppermute | solution.py:306
  101.6 3.3 %collective-permute-start.3 = (s32[1]{0:T(128)}, s32[1]{0:T(128)}, u32[]{:S(2)}, u32[]{:S(2)}) collective-permute-start(s32[1]{0:T(128)} %param.11), channel_id=1, source_target_pairs={{0,32},{32,0},{64,96},{96,64},{128,160},{160,128},{192,224},{224,1... | collective-permute-start | bytes 20 | tf_op jit(solution)/shard_map/ppermute | solution.py:294
  105.6 13.9 %copy-start.8 = (s32[1024]{0:T(1024)S(1)}, s32[1024]{0:T(1024)}, u32[]{:S(2)}) copy-start(s32[1024]{0:T(1024)} %param.13) | copy-start | bytes 12292
  105.7 13.9 %copy-start.9 = (s32[32]{0:T(128)S(1)}, s32[32]{0:T(128)}, u32[]{:S(2)}) copy-start(s32[32]{0:T(128)} %param.12) | copy-start | bytes 388
  114.4 20.8 %all-to-all-start.2 = ((bf16[32,24,128]{2,1,0:T(8,128)(2,1)}), bf16[32,24,128]{2,1,0:T(8,128)(2,1)S(1)}, u32[]{:S(2)}, u32[]{:S(2)}) async-start(bf16[32,24,128]{2,1,0:T(8,128)(2,1)} %attend.1), calls=%async_computation.2 | async-start | bytes 393216 | tf_op jit(solution)/shard_map/all_to_all | solution.py:311
  135.4 13.1 %collective-permute-start.5 = (f32[32,128]{1,0:T(8,128)S(1)}, f32[32,128]{1,0:T(8,128)S(1)}, u32[]{:S(2)}, u32[]{:S(2)}) collective-permute-start(f32[32,128]{1,0:T(8,128)S(1)} %dynamic-slice_bitcast_fusion), channel_id=1, source_target_pairs={{0,32},{32,0},{64,96},{96,64},{128,160},{160,128},{192,224},{224,1... | collective-permute-start | bytes 49160 | tf_op jit(solution)/shard_map/ppermute | solution.py:319
  149.3 16.0 %all-to-all-start.3 = ((f32[32,1,32]{2,1,0:T(1,128)}), f32[32,1,32]{2,1,0:T(1,128)S(1)}, u32[]{:S(2)}, u32[]{:S(2)}) async-start(f32[32,1,32]{2,1,0:T(1,128)} %broadcast_in_dim.17), calls=%async_computation.3 | async-start | bytes 32768 | tf_op jit(solution)/shard_map/all_to_all | solution.py:323
Sparse Core Ops, SparseCore 0:
  17.9 84.2 all-gather.3

commit v9 on v8

--- a/solution.py
+++ b/solution.py
@@ -97,7 +97,7 @@
     )(near, far)
 
 
-def open_body(place_ref, hidden, gain_ref, out_ref, last_ref, block, sem):
+def open_body(place_ref, hidden, gain_ref, out_ref, block, sem):
     last, y_lo = place_ref[0], place_ref[3]
     first = pl.multiple_of((last >> 3) << 3, 8)
     copy = pltpu.make_async_copy(hidden.at[0, pl.ds(first, 8)], block, sem.at[0])
@@ -106,17 +106,17 @@
     floats = block[...].astype(f32)
     pick = lax.broadcasted_iota(jnp.int32, floats.shape, 0) == (last & 7)
     row = jnp.sum(jnp.where(pick, floats, 0.0), axis=0, keepdims=True)
-    last_ref[...] = row.astype(bf16)
     normed = row * lax.rsqrt(jnp.mean(row * row, axis=-1, keepdims=True) + 1e-05) * gain_ref[...]
     normed = normed.astype(bf16).astype(f32)
     half = normed.shape[1] // 2
     place = lax.broadcasted_iota(jnp.int32, (8, HEAD), 0)
+    near, far = (
+        [jnp.where(y_lo == y, v[:, :half], v[:, half:]) for v in (normed, row)] for y in range(2)
+    )
     for z in range(Z):
-        low = normed[:, z * HEAD : (z + 1) * HEAD]
-        high = normed[:, half + z * HEAD : half + (z + 1) * HEAD]
-        mine = jnp.where(y_lo == 0, low, high)
-        other = jnp.where(y_lo == 0, high, low)
-        tile = jnp.where(place == 0, mine, jnp.where(place == 1, other, 0.0))
+        tile = jnp.zeros((8, HEAD), f32)
+        for n, v in enumerate((near[0], far[0], near[1], far[1])):
+            tile = jnp.where(place == n, v[:, z * HEAD : (z + 1) * HEAD], tile)
         out_ref[z] = tile.astype(bf16)
 
 
@@ -124,12 +124,9 @@
     width = hidden.shape[2]
     return pl.pallas_call(
         open_body,
-        out_shape=(
-            jax.ShapeDtypeStruct((Z, 8, HEAD), bf16),
-            jax.ShapeDtypeStruct((1, width), bf16),
-        ),
+        out_shape=jax.ShapeDtypeStruct((Z, 8, HEAD), bf16),
         in_specs=[SMEM, HBM, VMEM],
-        out_specs=(VMEM, VMEM),
+        out_specs=VMEM,
         scratch_shapes=[pltpu.VMEM((8, width), bf16), pltpu.SemaphoreType.DMA((1,))],
         compiler_params=pltpu.CompilerParams(vmem_limit_bytes=62 << 20),
         name="open",
@@ -175,7 +172,7 @@
 
 
 def attend_body(
-    place_ref, len_ref, normed_ref, other_ref, cos_ref, sin_ref, last_ref, parts, gathered, out_ref, w_ref, q_ref, sem, q_sem
+    place_ref, len_ref, normed_ref, other_ref, cos_ref, sin_ref, parts, gathered, out_ref, w_ref, q_ref, sem, q_sem
 ):
     fetch = pltpu.make_async_copy(parts.at[:, pl.ds(0, 16), :], q_ref, q_sem.at[0])
     fetch.start()
@@ -244,18 +241,14 @@
     context = jnp.where((head & 7) < 4, total[:, :HEAD], total[:, HEAD:])
     turned = jnp.concatenate([context[8:], context[:8]], axis=0)
     context = jnp.where(core == 0, context, turned).astype(bf16)
-    last = last_ref[...].astype(f32)
-    for n in range(2 * Z):
-        out_ref[n, :16, :] = context
-        tile = jnp.broadcast_to(last[:, n * HEAD : (n + 1) * HEAD], (8, HEAD))
-        out_ref[n, 16:, :] = tile.astype(bf16)
-
-
-def attend(place, lengths, normed, other, cosine, sine, last, parts, gathered):
+    out_ref[...] = jnp.broadcast_to(context[None], out_ref.shape)
+
+
+def attend(place, lengths, normed, other, cosine, sine, parts, gathered):
     return pl.pallas_call(
         attend_body,
-        out_shape=jax.ShapeDtypeStruct((2 * Z, 24, HEAD), bf16),
-        in_specs=[SMEM, SMEM, VMEM, VMEM, VMEM, VMEM, VMEM, HBM, HBM],
+        out_shape=jax.ShapeDtypeStruct((2 * Z, 16, HEAD), bf16),
+        in_specs=[SMEM, SMEM, VMEM, VMEM, VMEM, VMEM, HBM, HBM],
         out_specs=VMEM,
         scratch_shapes=[
             pltpu.VMEM((2, Y_LO, Z, HEAD, 256), bf16),
@@ -265,7 +258,7 @@
         ],
         compiler_params=pltpu.CompilerParams(vmem_limit_bytes=48 << 20),
         name="attend",
-    )(place, lengths, normed, other, cosine, sine, last, parts, gathered)
+    )(place, lengths, normed, other, cosine, sine, parts, gathered)
 
 
 def local(
@@ -282,7 +275,7 @@
     gathered = lax.all_gather(units, "fsdp", axis=0, tiled=False, axis_index_groups=Z_GROUPS)
 
     unit, hidden = lax.optimization_barrier((unit, hidden))
-    outgoing, last_input = open_payload(place, hidden, attn_gain)
+    outgoing = open_payload(place, hidden, attn_gain)
     units, outgoing = lax.optimization_barrier((units, outgoing))
     arrived = lax.all_to_all(outgoing, "fsdp", 0, 0, tiled=True, axis_index_groups=Z_GROUPS)
     w_query_other = lax.ppermute(w_query, "fsdp", Y_LO_SWAP)
@@ -304,27 +297,10 @@
     ).reshape(X, 2, Z, 8, HEAD)
     weight = jnp.transpose(weight, (2, 1, 0, 3, 4)).reshape(2 * Z * 32, HEAD)
     weight = jnp.where(core == y_lo, weight, lax.ppermute(weight, BOTH, CROSS_SWAP))
-    gathered, weight, both_lengths, normed, other, cosine, sine = lax.optimization_barrier(
-        (gathered, weight, both_lengths, normed, other, cosine, sine)
-    )
-    context = attend(place, both_lengths, normed, other, cosine, sine, last_input, parts, gathered)
-    contexts = lax.all_to_all(context, "fsdp", 0, 0, tiled=True)
-
-    slabs = width // HEAD
-    inputs = contexts[:, 16].astype(f32)
-    contexts = contexts[:, :16].reshape(slabs, 2, 8 * HEAD)
-    halves = jnp.einsum("sad,dn->asn", contexts, weight, preferred_element_type=f32)
-    kept = lax.dynamic_index_in_dim(halves, core, 0, keepdims=False)
-    given = lax.dynamic_index_in_dim(halves, 1 - core, 0, keepdims=False)
-    residual = inputs + (kept + lax.ppermute(given, "dp", CORE_SWAP))
+    near, far = arrived[:, 2], lax.ppermute(arrived[:, 3], "fsdp", Y_LO_SWAP)
+    inputs = jnp.concatenate([jnp.where(y_lo == 0, near, far), jnp.where(y_lo == 0, far, near)])
+    inputs = inputs.astype(f32)
     gain = lax.dynamic_slice(final_gain, (fsdp * HEAD,), (HEAD,))
-    scaled = residual * gain
-    partial = jnp.sum(scaled * scaled, axis=-1)
-    squares = lax.all_to_all(
-        jnp.broadcast_to(partial[None, None, :], (slabs, 1, slabs)), "fsdp", 0, 0, tiled=True
-    )
-    mean = jnp.sum(squares, axis=0)[0] / width
-    slab = (scaled * lax.rsqrt(mean + 1e-06)[:, None]).astype(bf16)
 
     owner_count = lax.axis_size("dp")
     capacity = 4
@@ -338,6 +314,29 @@
         (owners[None, None, :] == jnp.arange(owner_count)[:, None, None])
         & (slot_rank[None, None, :] == jnp.arange(capacity)[None, :, None])
     ).astype(bf16)
+
+    (
+        gathered, weight, both_lengths, normed, other, cosine, sine, inputs, gain, select
+    ) = lax.optimization_barrier(
+        (gathered, weight, both_lengths, normed, other, cosine, sine, inputs, gain, select)
+    )
+    context = attend(place, both_lengths, normed, other, cosine, sine, parts, gathered)
+    contexts = lax.all_to_all(context, "fsdp", 0, 0, tiled=True)
+
+    slabs = width // HEAD
+    contexts = contexts.reshape(slabs, 2, 8 * HEAD)
+    halves = jnp.einsum("sad,dn->asn", contexts, weight, preferred_element_type=f32)
+    kept = lax.dynamic_index_in_dim(halves, core, 0, keepdims=False)
+    given = lax.dynamic_index_in_dim(halves, 1 - core, 0, keepdims=False)
+    residual = inputs + (kept + lax.ppermute(given, "dp", CORE_SWAP))
+    scaled = residual * gain
+    partial = jnp.sum(scaled * scaled, axis=-1)
+    squares = lax.all_to_all(
+        jnp.broadcast_to(partial[None, None, :], (slabs, 1, slabs)), "fsdp", 0, 0, tiled=True
+    )
+    mean = jnp.sum(squares, axis=0)[0] / width
+    slab = (scaled * lax.rsqrt(mean + 1e-06)[:, None]).astype(bf16)
+
     outgoing = jnp.einsum("osr,rd->osd", select, slab, preferred_element_type=f32).astype(bf16)
     return lax.all_to_all(outgoing[:, None], "dp", split_axis=0, concat_axis=1, tiled=True)
 

time: 188 us -> 186 us (0.989)
  blocking collectives: 78.9 us -> 67.6 us
  waiting for transfers between devices: 31.2 us -> 39.8 us
    all_to_all x1, blocking collectives: 26.5 us -> 15.2 us  [local(): lax.all_to_all(jnp.broadcast_to(partial[None, None, :], (slabs, 1, slabs)...]
    all_to_all x1, waiting for transfers between devices: 12.1 us -> 20.4 us  [local(): lax.all_to_all(payload, BOTH, 0, 0, tiled=True, axis_index_groups=CORE_Z_...]
    ppermute x1, starting transfers between devices: 12.3 us -> 5.72 us  [local(): residual = inputs + (kept + lax.ppermute(given, 'dp', CORE_SWAP))]
    all_to_all x1, starting transfers between devices: 3.83 us -> 7.04 us  [local(): lax.all_to_all(payload, BOTH, 0, 0, tiled=True, axis_index_groups=CORE_Z_...]
    ppermute x0 -> x1, starting transfers between devices: none -> 1.94 us  [local(): near, far = (arrived[:, 2], lax.ppermute(arrived[:, 3], 'fsdp', Y_LO_SWAP))]
    unnamed x21 -> x18, local copies, waits for them, and re-layouts: 4.3 us -> 4.29 us
  transfers between devices with their start and end apart: 9 -> 10, of which waited for: 5 -> 6; matrix products, arithmetic and copies ran while one was open for 3% -> 4% of each run, Pallas kernels for 2% -> 2%
where the time goes in v9:
time: 186 us; the launch traced here: 185 us
  blocking collectives  67.6 us (36%)
  waiting for transfers between devices  39.8 us (21%)
  starting transfers between devices  35.5 us (19%)
  Pallas kernels  15.1 us (8%)
  between operations  14.4 us (8%)
  other arithmetic  7.1 us (4%)
  local copies, waits for them, and re-layouts  5.22 us (3%)
    all_to_all x1, blocking collectives, local(): lax.all_to_all(outgoing, 'fsdp', 0, 0, tiled=True, axis_index_groups=Z_GR...  27 us
    all_to_all x1, waiting for transfers between devices, local(): lax.all_to_all(payload, BOTH, 0, 0, tiled=True, axis_index_groups=CORE_Z_...  20.4 us
    all_to_all x1, blocking collectives, local(): lax.all_to_all(jnp.broadcast_to(partial[None, None, :], (slabs, 1, slabs)...  15.2 us
    all_to_all x1, blocking collectives, local(): lax.all_to_all(outgoing[:, None], 'dp', split_axis=0, concat_axis=1, tile...  14.8 us
    all_to_all x1, waiting for transfers between devices, local(): contexts = lax.all_to_all(context, 'fsdp', 0, 0, tiled=True)  14.5 us
    all_gather x1, blocking collectives, local(): lax.all_gather(parts[:, WEIGHT_ROW:], 'dp', axis=0, tiled=False, axis_ind...  10.6 us
    pallas_call x1, Pallas kernels, attend(): pl.pallas_call(attend_body, out_shape=jax.ShapeDtypeStruct((2 * Z, 16, HE...  8.72 us
    all_to_all x1, starting transfers between devices, local(): lax.all_to_all(payload, BOTH, 0, 0, tiled=True, axis_index_groups=CORE_Z_...  7.04 us
  transfers between devices with their start and end apart: 10, of which 6 were waited for; matrix products, arithmetic and copies ran while one was open for 4% of the time, Pallas kernels for 2%

profile of v9, /device:TPU:1, one launch (start us, length us, event | category | flops | bytes accessed | tf_op | source)
XLA Modules:
  0.0 185.0 jit_solution(12274673266534056534)
XLA Ops:
  7.2 0.7 pad_add_fusion.place_ref
  7.9 1.6 unit.1.near_ref
  9.5 4.0 %collective-permute-start = (bf16[128,512]{1,0:T(8,128)(2,1)}, bf16[128,512]{1,0:T(8,128)(2,1)S(1)}, u32[]{:S(2)}, u32[]{:S(2)}) collective-permute-start(bf16[128,512]{1,0:T(8,128)(2,1)} %unit.1.near_ref), channel_id=1, source_target_pairs={{0,16},{1,17},{2,18},{3,19},{4,20},{5,21},{6,22},{7,23},{8,24},{9,... | collective-permute-start | bytes 393224 | tf_op jit(solution)/shard_map/ppermute | solution.py:274
  13.6 2.6 %collective-permute-done.far_ref = bf16[128,512]{1,0:T(8,128)(2,1)S(1)} collective-permute-done((bf16[128,512]{1,0:T(8,128)(2,1)}, bf16[128,512]{1,0:T(8,128)(2,1)S(1)}, u32[]{:S(2)}, u32[]{:S(2)}) %collective-permute-start) | collective-permute-done | bytes 131104 | tf_op jit(solution)/shard_map/ppermute | solution.py:274
  16.1 0.9 copy-done
  17.0 0.7 pair.1
  17.7 0.0 all-gather.4.cloned.1.call-update
  17.8 3.4 %collective-permute-start.1 = (bf16[128,2048]{1,0:T(8,128)(2,1)}, bf16[128,2048]{1,0:T(8,128)(2,1)S(1)}, u32[]{:S(2)}, u32[]{:S(2)}) collective-permute-start(bf16[128,2048]{1,0:T(8,128)(2,1)} %near_ref.1), channel_id=1, source_target_pairs={{0,16},{1,17},{2,18},{3,19},{4,20},{5,21},{6,22},{7,23},{8,24},{9,... | collective-permute-start | bytes 1572872 | tf_op jit(solution)/shard_map/ppermute | solution.py:281
  21.1 2.4 %open.1 = bf16[16,8,128]{2,1,0:T(8,128)(2,1)} custom-call(s32[4]{0:T(128)} %pad_add_fusion.place_ref, bf16[1,256,4096]{2,1,0:T(8,128)(2,1)} %hidden, f32[1,4096]{1,0:T(1,128)} %bitcast.46), custom_call_target="tpu_custom_call" | custom-call | tf_op jit(solution)/shard_map/open/pallas_call | solution.py:125
  23.5 27.0 %all_to_all.32.arrived_ref = bf16[16,8,128]{2,1,0:T(8,128)(2,1)S(1)} all-to-all(bf16[16,8,128]{2,1,0:T(8,128)(2,1)} %open.1), channel_id=1, replica_groups={{0,1,2,3,4,5,6,7,8,9,10,11,12,13,14,15},{16,17,18,19,20,21,22,23,24,25,..., dimensions={0} | all-to-all | bytes 65536 | tf_op jit(solution)/shard_map/all_to_all | solution.py:280
  50.5 0.0 collective-permute-done.1.far_ref
  50.5 1.0 copy-done.1
  51.6 1.0 copy-done.2
  52.6 0.7 copy-done.3
  53.3 1.7 query.1
  55.0 7.0 %all-to-all-start.1 = ((bf16[32,24,128]{2,1,0:T(8,128)(2,1)}), bf16[32,24,128]{2,1,0:T(8,128)(2,1)S(1)}, u32[]{:S(2)}, u32[]{:S(2)}) async-start(bf16[32,24,128]{2,1,0:T(8,128)(2,1)} %query.1), calls=%async_computation.1 | async-start | bytes 393216 | tf_op jit(solution)/shard_map/all_to_all | solution.py:284
  62.1 0.2 select_reduce_fusion
  62.2 0.1 fusion.10
  62.3 0.1 reduce_window_sum.11
  62.4 0.2 select_reduce_fusion.1
  62.6 20.4 %all-to-all-done.1.parts = bf16[32,24,128]{2,1,0:T(8,128)(2,1)S(1)} async-done(((bf16[32,24,128]{2,1,0:T(8,128)(2,1)}), bf16[32,24,128]{2,1,0:T(8,128)(2,1)S(1)}, u32[]{:S(2)}, u32[]{:S(2)}) %all-to-all-start.1) | async-done | bytes 196640 | tf_op jit(solution)/shard_map/all_to_all | solution.py:284
  83.0 2.1 %fusion = f32[256]{0:T(256)S(1)} fusion(bf16[256,4096]{1,0:T(8,128)(2,1)} %bitcast.41), kind=kLoop, calls=%fused_computation.2 | loop fusion | flops 3145472 | bytes 2098176 | tf_op jit(solution)/shard_map/reduce_sum | solution.py:290
  85.1 2.2 %fusion.2.normed_ref = bf16[256,4096]{1,0:T(8,128)(2,1)S(1)} fusion(bf16[256,4096]{1,0:T(8,128)(2,1)} %bitcast.42, f32[4096]{0:T(1024)S(1)} %copy-done.5, f32[256]{0:T(256)S(1)} %add_rsqrt_fusion), kind=kLoop, calls=%fused_computation.4 | loop fusion | flops 4194304 | bytes 4211712 | tf_op jit(solution)/shard_map/convert_element_type | solution.py:291
  87.4 2.3 %collective-permute-start.4 = (bf16[256,4096]{1,0:T(8,128)(2,1)S(1)}, bf16[256,4096]{1,0:T(8,128)(2,1)}, u32[]{:S(2)}, u32[]{:S(2)}) collective-permute-start(bf16[256,4096]{1,0:T(8,128)(2,1)S(1)} %fusion.2.normed_ref), channel_id=1, source_target_pairs={{0,32},{32,0},{64,96},{96,64},{128,160},{160,128},{192,224},{224,1... | collective-permute-start | bytes 6291464 | tf_op jit(solution)/shard_map/ppermute | solution.py:292
  89.7 0.8 dynamic_slice.10
  90.5 0.5 fusion.7
  91.0 0.1 pad_maximum_fusion
  91.2 1.9 %collective-permute-start.5 = (bf16[16,128]{1,0:T(8,128)(2,1)S(1)}, bf16[16,128]{1,0:T(8,128)(2,1)S(1)}, u32[]{:S(2)}, u32[]{:S(2)}) collective-permute-start(bf16[16,128]{1,0:T(8,128)(2,1)S(1)} %bitcast.49), channel_id=1, source_target_pairs={{0,16},{1,17},{2,18},{3,19},{4,20},{5,21},{6,22},{7,23},{8,24},{9,... | collective-permute-start | bytes 12296 | tf_op jit(solution)/shard_map/ppermute | solution.py:300
  93.2 10.6 %all-gather.1 = bf16[128,8,128]{2,1,0:T(8,128)(2,1)S(1)} all-gather(bf16[32,8,128]{2,1,0:T(8,128)(2,1)S(1)} %slice.9), channel_id=3, replica_groups={{0,64,128,192},{32,96,160,224},{256,320,384,448},{288,352,416,480},{1,6..., dimensions={0}, use_global_device_ids=true | all-gather | bytes 327680 | tf_op jit(solution)/shard_map/all_gather | solution.py:295
  103.8 0.1 copy.27
  103.8 5.3 %collective-permute-start.2 = (bf16[1024,128]{1,0:T(8,128)(2,1)S(1)}, bf16[1024,128]{1,0:T(8,128)(2,1)S(1)}, u32[]{:S(2)}, u32[]{:S(2)}) collective-permute-start(bf16[1024,128]{1,0:T(8,128)(2,1)S(1)} %bitcast.45), channel_id=1, source_target_pairs={{16,32},{17,33},{18,34},{19,35},{20,36},{21,37},{22,38},{23,39},{2... | collective-permute-start | bytes 786440 | tf_op jit(solution)/shard_map/ppermute | solution.py:299
  109.2 1.9 %collective-permute-start.3 = (s32[1]{0:T(128)}, s32[1]{0:T(128)}, u32[]{:S(2)}, u32[]{:S(2)}) collective-permute-start(s32[1]{0:T(128)} %param.11), channel_id=1, source_target_pairs={{0,32},{32,0},{64,96},{96,64},{128,160},{160,128},{192,224},{224,1... | collective-permute-start | bytes 20 | tf_op jit(solution)/shard_map/ppermute | solution.py:287
  111.1 1.4 collective-permute-done.3
  112.5 0.6 pad_add_fusion.1.len_ref
  113.1 0.1 collective-permute-done.2
  113.2 0.1 broadcast_select_fusion
  113.3 0.0 all-gather.4.cloned.1.call-done
  113.3 8.7 %attend.1 = bf16[32,16,128]{2,1,0:T(8,128)(2,1)} custom-call(s32[4]{0:T(128)S(1)} %copy-done.4, s32[2]{0:T(128)S(1)} %pad_add_fusion.1.len_ref, bf16[256,4096]{1,0:T(8,128)(2,1)S(1)} %fusion.2.normed_ref, bf16[256,4096]{1,0:T(8,128)(2,1)} %collective-permute-done.4.other_ref, f32[256,128]{1,0:T(8,128)S(1)} %get-tuple-element.31.cos_ref, ...), custom_call_target="tpu_custom_call" | custom-call | tf_op jit(solution)/shard_map/attend/pallas_call | solution.py:248
  122.0 3.9 %all-to-all-start.2 = ((bf16[32,16,128]{2,1,0:T(8,128)(2,1)}), bf16[32,16,128]{2,1,0:T(8,128)(2,1)S(1)}, u32[]{:S(2)}, u32[]{:S(2)}) async-start(bf16[32,16,128]{2,1,0:T(8,128)(2,1)} %attend.1), calls=%async_computation.2 | async-start | bytes 262144 | tf_op jit(solution)/shard_map/all_to_all | solution.py:324
  125.9 14.5 %all-to-all-done.2 = bf16[32,16,128]{2,1,0:T(8,128)(2,1)S(1)} async-done(((bf16[32,16,128]{2,1,0:T(8,128)(2,1)}), bf16[32,16,128]{2,1,0:T(8,128)(2,1)S(1)}, u32[]{:S(2)}, u32[]{:S(2)}) %all-to-all-start.2) | async-done | bytes 131104 | tf_op jit(solution)/shard_map/all_to_all | solution.py:324
  140.5 0.2 fusion.4
  140.7 5.7 %collective-permute-start.6 = (f32[32,128]{1,0:T(8,128)S(1)}, f32[32,128]{1,0:T(8,128)S(1)}, u32[]{:S(2)}, u32[]{:S(2)}) collective-permute-start(f32[32,128]{1,0:T(8,128)S(1)} %dynamic-slice_bitcast_fusion), channel_id=1, source_target_pairs={{0,32},{32,0},{64,96},{96,64},{128,160},{160,128},{192,224},{224,1... | collective-permute-start | bytes 49160 | tf_op jit(solution)/shard_map/ppermute | solution.py:331
  146.4 0.8 collective-permute-done.6
  147.2 0.1 multiply_reduce_fusion
  147.3 15.2 %all_to_all.33 = f32[32,1,32]{2,1,0:T(1,128)S(1)} all-to-all(f32[32,1,32]{2,1,0:T(1,128)S(1)} %broadcast_in_dim.21), channel_id=1, replica_groups=mesh['dp'=16,'fsdp'=32] {'fsdp'}, dimensions={0} | all-to-all | bytes 8192 | tf_op jit(solution)/shard_map/all_to_all | solution.py:334
  162.5 0.2 fusion.3
  162.7 14.8 %all_to_all.34 = bf16[16,1,4,128]{3,2,1,0:T(4,128)(2,1)S(1)} all-to-all(bf16[16,1,4,128]{3,2,1,0:T(4,128)(2,1)S(1)} %copy.30), channel_id=1, replica_groups=mesh['dp'=16,'fsdp'=32] {'dp'}, dimensions={0} | all-to-all | bytes 32768 | tf_op jit(solution)/shard_map/all_to_all | solution.py:341
  177.6 0.6 copy.41
  (32 shorter events, 0.2 us)
Async XLA Ops:
  6.5 78.6 %copy-start.5 = (f32[4096]{0:T(1024)S(1)}, f32[4096]{0:T(1024)}, u32[]{:S(2)}) copy-start(f32[4096]{0:T(1024)} %param.14) | copy-start | bytes 49156
  6.5 55.5 %copy-start.6 = (s32[1024]{0:T(1024)S(1)}, s32[1024]{0:T(1024)}, u32[]{:S(2)}) copy-start(s32[1024]{0:T(1024)} %param.13) | copy-start | bytes 12292
  6.5 55.5 %copy-start.7 = (s32[32]{0:T(128)S(1)}, s32[32]{0:T(128)}, u32[]{:S(2)}) copy-start(s32[32]{0:T(128)} %param.12) | copy-start | bytes 388
  6.5 106.8 %all-gather.4.cloned.1.call-start = ((), (), s32[]{:S(2)}) async-start(), calls=%async_computation.5 | async-start | bytes 4456448 | tf_op jit(solution)/shard_map/all_gather | solution.py:275
  9.5 6.6 %collective-permute-start = (bf16[128,512]{1,0:T(8,128)(2,1)}, bf16[128,512]{1,0:T(8,128)(2,1)S(1)}, u32[]{:S(2)}, u32[]{:S(2)}) collective-permute-start(bf16[128,512]{1,0:T(8,128)(2,1)} %unit.1.near_ref), channel_id=1, source_target_pairs={{0,16},{1,17},{2,18},{3,19},{4,20},{5,21},{6,22},{7,23},{8,24},{9,... | collective-permute-start | bytes 393224 | tf_op jit(solution)/shard_map/ppermute | solution.py:274
  16.1 0.9 copy-start
  17.8 32.8 %collective-permute-start.1 = (bf16[128,2048]{1,0:T(8,128)(2,1)}, bf16[128,2048]{1,0:T(8,128)(2,1)S(1)}, u32[]{:S(2)}, u32[]{:S(2)}) collective-permute-start(bf16[128,2048]{1,0:T(8,128)(2,1)} %near_ref.1), channel_id=1, source_target_pairs={{0,16},{1,17},{2,18},{3,19},{4,20},{5,21},{6,22},{7,23},{8,24},{9,... | collective-permute-start | bytes 1572872 | tf_op jit(solution)/shard_map/ppermute | solution.py:281
  50.5 1.0 copy-start.1
  51.6 1.0 copy-start.2
  52.6 0.7 copy-start.3
  55.0 28.0 %all-to-all-start.1 = ((bf16[32,24,128]{2,1,0:T(8,128)(2,1)}), bf16[32,24,128]{2,1,0:T(8,128)(2,1)S(1)}, u32[]{:S(2)}, u32[]{:S(2)}) async-start(bf16[32,24,128]{2,1,0:T(8,128)(2,1)} %query.1), calls=%async_computation.1 | async-start | bytes 393216 | tf_op jit(solution)/shard_map/all_to_all | solution.py:284
  83.0 30.3 %copy-start.4 = (s32[4]{0:T(128)S(1)}, s32[4]{0:T(128)}, u32[]{:S(2)}) copy-start(s32[4]{0:T(128)} %pad_add_fusion.place_ref) | copy-start | bytes 52
  87.4 25.9 %collective-permute-start.4 = (bf16[256,4096]{1,0:T(8,128)(2,1)S(1)}, bf16[256,4096]{1,0:T(8,128)(2,1)}, u32[]{:S(2)}, u32[]{:S(2)}) collective-permute-start(bf16[256,4096]{1,0:T(8,128)(2,1)S(1)} %fusion.2.normed_ref), channel_id=1, source_target_pairs={{0,32},{32,0},{64,96},{96,64},{128,160},{160,128},{192,224},{224,1... | collective-permute-start | bytes 6291464 | tf_op jit(solution)/shard_map/ppermute | solution.py:292
  91.2 18.0 %collective-permute-start.5 = (bf16[16,128]{1,0:T(8,128)(2,1)S(1)}, bf16[16,128]{1,0:T(8,128)(2,1)S(1)}, u32[]{:S(2)}, u32[]{:S(2)}) collective-permute-start(bf16[16,128]{1,0:T(8,128)(2,1)S(1)} %bitcast.49), channel_id=1, source_target_pairs={{0,16},{1,17},{2,18},{3,19},{4,20},{5,21},{6,22},{7,23},{8,24},{9,... | collective-permute-start | bytes 12296 | tf_op jit(solution)/shard_map/ppermute | solution.py:300
  103.8 9.4 %collective-permute-start.2 = (bf16[1024,128]{1,0:T(8,128)(2,1)S(1)}, bf16[1024,128]{1,0:T(8,128)(2,1)S(1)}, u32[]{:S(2)}, u32[]{:S(2)}) collective-permute-start(bf16[1024,128]{1,0:T(8,128)(2,1)S(1)} %bitcast.45), channel_id=1, source_target_pairs={{16,32},{17,33},{18,34},{19,35},{20,36},{21,37},{22,38},{23,39},{2... | collective-permute-start | bytes 786440 | tf_op jit(solution)/shard_map/ppermute | solution.py:299
  109.2 3.3 %collective-permute-start.3 = (s32[1]{0:T(128)}, s32[1]{0:T(128)}, u32[]{:S(2)}, u32[]{:S(2)}) collective-permute-start(s32[1]{0:T(128)} %param.11), channel_id=1, source_target_pairs={{0,32},{32,0},{64,96},{96,64},{128,160},{160,128},{192,224},{224,1... | collective-permute-start | bytes 20 | tf_op jit(solution)/shard_map/ppermute | solution.py:287
  122.0 18.4 %all-to-all-start.2 = ((bf16[32,16,128]{2,1,0:T(8,128)(2,1)}), bf16[32,16,128]{2,1,0:T(8,128)(2,1)S(1)}, u32[]{:S(2)}, u32[]{:S(2)}) async-start(bf16[32,16,128]{2,1,0:T(8,128)(2,1)} %attend.1), calls=%async_computation.2 | async-start | bytes 262144 | tf_op jit(solution)/shard_map/all_to_all | solution.py:324
  140.7 6.5 %collective-permute-start.6 = (f32[32,128]{1,0:T(8,128)S(1)}, f32[32,128]{1,0:T(8,128)S(1)}, u32[]{:S(2)}, u32[]{:S(2)}) collective-permute-start(f32[32,128]{1,0:T(8,128)S(1)} %dynamic-slice_bitcast_fusion), channel_id=1, source_target_pairs={{0,32},{32,0},{64,96},{96,64},{128,160},{160,128},{192,224},{224,1... | collective-permute-start | bytes 49160 | tf_op jit(solution)/shard_map/ppermute | solution.py:331
Sparse Core Ops, SparseCore 0:
  17.9 84.9 all-gather.3

commit v10 on v9

--- a/solution.py
+++ b/solution.py
@@ -92,7 +92,7 @@
         out_shape=jax.ShapeDtypeStruct((2, *near.shape), bf16),
         in_specs=[VMEM, VMEM],
         out_specs=VMEM,
-        compiler_params=pltpu.CompilerParams(vmem_limit_bytes=8 << 20),
+        compiler_params=pltpu.CompilerParams(vmem_limit_bytes=62 << 20),
         name="pair",
     )(near, far)
 
@@ -166,7 +166,7 @@
         in_specs=[SMEM, VMEM, VMEM, VMEM, VMEM],
         out_specs=VMEM,
         scratch_shapes=[pltpu.VMEM((2 * Z, 16, HEAD), f32)],
-        compiler_params=pltpu.CompilerParams(vmem_limit_bytes=12 << 20),
+        compiler_params=pltpu.CompilerParams(vmem_limit_bytes=62 << 20),
         name="query",
     )(place, arrived, near, far, w_out)
 
@@ -283,13 +283,17 @@
     payload = query_payload(place, arrived, w_query, w_query_other, w_out)
     parts = lax.all_to_all(payload, BOTH, 0, 0, tiled=True, axis_index_groups=CORE_Z_GROUPS)
 
-    rows, lengths, parts = lax.optimization_barrier((hidden[0], lengths, parts))
     both_lengths = jnp.concatenate([lengths, lax.ppermute(lengths, "dp", CORE_SWAP)])
-    floats = rows.astype(f32)
-    normed = (
-        floats * lax.rsqrt(jnp.mean(floats * floats, axis=-1, keepdims=True) + 1e-05) * attn_gain
-    ).astype(bf16)
-    other = lax.ppermute(normed, "dp", CORE_SWAP)
+    rows, _ = lax.optimization_barrier((hidden[0], payload))
+
+    def norm(values):
+        floats = values.astype(f32)
+        return (
+            floats * lax.rsqrt(jnp.mean(floats * floats, axis=-1, keepdims=True) + 1e-05) * attn_gain
+        ).astype(bf16)
+
+    normed, other = norm(rows), norm(lax.ppermute(rows, "dp", CORE_SWAP))
+    parts, normed, other = lax.optimization_barrier((parts, normed, other))
     cosine, sine = rope_tables(jnp.arange(seq_len), HEAD)
 
     weight = lax.all_gather(

time: 186 us -> 188 us (1.011)
  blocking collectives: 67.6 us -> 41.2 us
  starting transfers between devices: 35.5 us -> 51.1 us
  waiting for transfers between devices: 39.8 us -> 46.5 us
  other arithmetic: 7.1 us -> 10.4 us
    all_to_all x1 -> x0, blocking collectives: 27 us -> none  [local(): lax.all_to_all(outgoing, 'fsdp', 0, 0, tiled=True, axis_index_groups=Z_GR...]
    all_to_all x0 -> x1, waiting for transfers between devices: none -> 11.5 us  [local(): lax.all_to_all(outgoing, 'fsdp', 0, 0, tiled=True, axis_index_groups=Z_GR...]
    all_to_all x0 -> x1, starting transfers between devices: none -> 11.4 us  [local(): lax.all_to_all(outgoing, 'fsdp', 0, 0, tiled=True, axis_index_groups=Z_GR...]
    all_to_all x1, waiting for transfers between devices: 20.4 us -> 13.1 us  [local(): lax.all_to_all(payload, BOTH, 0, 0, tiled=True, axis_index_groups=CORE_Z_...]
    ppermute x1, starting transfers between devices: 1.92 us -> 7.83 us  [local(): lax.ppermute(lengths, 'dp', CORE_SWAP)]
    ppermute x1, waiting for transfers between devices: 0.07 us -> 4 us  [local(): lax.ppermute(weight, BOTH, CROSS_SWAP)]
    all_to_all x1, starting transfers between devices: 7.04 us -> 3.92 us  [local(): lax.all_to_all(payload, BOTH, 0, 0, tiled=True, axis_index_groups=CORE_Z_...]
    convert_element_type x1, other arithmetic: 2.24 us -> 4.35 us  [norm(): return (floats * lax.rsqrt(jnp.mean(floats * floats, axis=-1, keepdims=Tr...]
  transfers between devices with their start and end apart: 10 -> 11, of which waited for: 6 -> 6; matrix products, arithmetic and copies ran while one was open for 4% -> 6% of each run, Pallas kernels for 2% -> 3%
where the time goes in v10:
time: 188 us; the launch traced here: 187 us
  starting transfers between devices  51.1 us (27%)
  waiting for transfers between devices  46.5 us (25%)
  blocking collectives  41.2 us (22%)
  Pallas kernels  15.9 us (8%)
  between operations  14.3 us (8%)
  other arithmetic  10.4 us (6%)
  local copies, waits for them, and re-layouts  6.87 us (4%)
    all_to_all x1, blocking collectives, local(): lax.all_to_all(outgoing[:, None], 'dp', split_axis=0, concat_axis=1, tile...  15.2 us
    all_to_all x1, blocking collectives, local(): lax.all_to_all(jnp.broadcast_to(partial[None, None, :], (slabs, 1, slabs)...  15.2 us
    all_to_all x1, waiting for transfers between devices, local(): contexts = lax.all_to_all(context, 'fsdp', 0, 0, tiled=True)  14.4 us
    all_to_all x1, waiting for transfers between devices, local(): lax.all_to_all(payload, BOTH, 0, 0, tiled=True, axis_index_groups=CORE_Z_...  13.1 us
    all_to_all x1, waiting for transfers between devices, local(): lax.all_to_all(outgoing, 'fsdp', 0, 0, tiled=True, axis_index_groups=Z_GR...  11.5 us
    all_to_all x1, starting transfers between devices, local(): lax.all_to_all(outgoing, 'fsdp', 0, 0, tiled=True, axis_index_groups=Z_GR...  11.4 us
    all_gather x1, blocking collectives, local(): lax.all_gather(parts[:, WEIGHT_ROW:], 'dp', axis=0, tiled=False, axis_ind...  10.9 us
    ppermute x1, starting transfers between devices, local(): lax.ppermute(lengths, 'dp', CORE_SWAP)  7.83 us
  transfers between devices with their start and end apart: 11, of which 6 were waited for; matrix products, arithmetic and copies ran while one was open for 6% of the time, Pallas kernels for 3%

profile of v10, /device:TPU:1, one launch (start us, length us, event | category | flops | bytes accessed | tf_op | source)
XLA Modules:
  0.0 186.7 jit_solution(11539865736334379172)
XLA Ops:
  7.2 0.6 pad_add_fusion.place_ref
  7.8 1.6 unit.1.near_ref
  9.4 4.0 %collective-permute-start = (bf16[128,512]{1,0:T(8,128)(2,1)}, bf16[128,512]{1,0:T(8,128)(2,1)S(1)}, u32[]{:S(2)}, u32[]{:S(2)}) collective-permute-start(bf16[128,512]{1,0:T(8,128)(2,1)} %unit.1.near_ref), channel_id=1, source_target_pairs={{0,16},{1,17},{2,18},{3,19},{4,20},{5,21},{6,22},{7,23},{8,24},{9,... | collective-permute-start | bytes 393224 | tf_op jit(solution)/shard_map/ppermute | solution.py:274
  13.5 2.6 %collective-permute-done.far_ref = bf16[128,512]{1,0:T(8,128)(2,1)S(1)} collective-permute-done((bf16[128,512]{1,0:T(8,128)(2,1)}, bf16[128,512]{1,0:T(8,128)(2,1)S(1)}, u32[]{:S(2)}, u32[]{:S(2)}) %collective-permute-start) | collective-permute-done | bytes 131104 | tf_op jit(solution)/shard_map/ppermute | solution.py:274
  16.0 0.7 copy-done.6
  16.7 1.7 pair.1
  18.4 3.4 %collective-permute-start.1 = (bf16[128,2048]{1,0:T(8,128)(2,1)}, bf16[128,2048]{1,0:T(8,128)(2,1)S(1)}, u32[]{:S(2)}, u32[]{:S(2)}) collective-permute-start(bf16[128,2048]{1,0:T(8,128)(2,1)} %near_ref.1), channel_id=1, source_target_pairs={{0,16},{1,17},{2,18},{3,19},{4,20},{5,21},{6,22},{7,23},{8,24},{9,... | collective-permute-start | bytes 1572872 | tf_op jit(solution)/shard_map/ppermute | solution.py:281
  21.8 7.8 %collective-permute-start.4 = (s32[1]{0:T(128)}, s32[1]{0:T(128)}, u32[]{:S(2)}, u32[]{:S(2)}) collective-permute-start(s32[1]{0:T(128)} %param.11), channel_id=1, source_target_pairs={{0,32},{32,0},{64,96},{96,64},{128,160},{160,128},{192,224},{224,1... | collective-permute-start | bytes 20 | tf_op jit(solution)/shard_map/ppermute | solution.py:286
  29.6 2.4 %open.1 = bf16[16,8,128]{2,1,0:T(8,128)(2,1)} custom-call(s32[4]{0:T(128)} %pad_add_fusion.place_ref, bf16[1,256,4096]{2,1,0:T(8,128)(2,1)} %hidden, f32[1,4096]{1,0:T(1,128)} %bitcast.47), custom_call_target="tpu_custom_call" | custom-call | tf_op jit(solution)/shard_map/open/pallas_call | solution.py:125
  32.0 0.9 select_reduce_fusion
  32.9 11.4 %all-to-all-start = ((bf16[16,8,128]{2,1,0:T(8,128)(2,1)}), bf16[16,8,128]{2,1,0:T(8,128)(2,1)S(1)}, u32[]{:S(2)}, u32[]{:S(2)}) async-start(bf16[16,8,128]{2,1,0:T(8,128)(2,1)} %open.1), calls=%async_computation | async-start | bytes 65536 | tf_op jit(solution)/shard_map/all_to_all | solution.py:280
  44.3 0.1 fusion.13
  44.3 11.5 %all-to-all-done.arrived_ref = bf16[16,8,128]{2,1,0:T(8,128)(2,1)S(1)} async-done(((bf16[16,8,128]{2,1,0:T(8,128)(2,1)}), bf16[16,8,128]{2,1,0:T(8,128)(2,1)S(1)}, u32[]{:S(2)}, u32[]{:S(2)}) %all-to-all-start) | async-done | bytes 32800 | tf_op jit(solution)/shard_map/all_to_all | solution.py:280
  55.8 0.6 copy-done.5
  56.4 0.8 copy-done.4
  57.2 2.5 %query.1 = bf16[32,24,128]{2,1,0:T(8,128)(2,1)} custom-call(s32[4]{0:T(128)} %pad_add_fusion.place_ref, bf16[16,8,128]{2,1,0:T(8,128)(2,1)} %copy-done.5, bf16[128,2048]{1,0:T(8,128)(2,1)} %near_ref.1, bf16[128,2048]{1,0:T(8,128)(2,1)} %copy-done.4, bf16[64,4096]{1,0:T(8,128)(2,1)} %w_out_ref.1), custom_call_target="tpu_custom_call" | custom-call | tf_op jit(solution)/shard_map/query/pallas_call | solution.py:163
  59.8 3.3 %collective-permute-start.2 = (bf16[256,4096]{1,0:T(8,128)(2,1)}, bf16[256,4096]{1,0:T(8,128)(2,1)S(1)}, u32[]{:S(2)}, u32[]{:S(2)}) collective-permute-start(bf16[256,4096]{1,0:T(8,128)(2,1)} %bitcast.41), channel_id=1, source_target_pairs={{0,32},{32,0},{64,96},{96,64},{128,160},{160,128},{192,224},{224,1... | collective-permute-start | bytes 6291464 | tf_op jit(solution)/shard_map/ppermute | solution.py:295
  63.0 0.1 reduce_window_sum.11
  63.1 0.8 dynamic_slice.10
  63.9 0.2 select_reduce_fusion.1
  64.0 0.5 fusion.10
  64.6 0.1 pad_maximum_fusion
  64.8 0.6 pad_add_fusion.1.len_ref
  65.4 0.9 fusion.18
  66.3 2.5 %collective-permute-start.5 = (bf16[16,128]{1,0:T(8,128)(2,1)S(1)}, bf16[16,128]{1,0:T(8,128)(2,1)S(1)}, u32[]{:S(2)}, u32[]{:S(2)}) collective-permute-start(bf16[16,128]{1,0:T(8,128)(2,1)S(1)} %bitcast.50), channel_id=1, source_target_pairs={{0,16},{1,17},{2,18},{3,19},{4,20},{5,21},{6,22},{7,23},{8,24},{9,... | collective-permute-start | bytes 12296 | tf_op jit(solution)/shard_map/ppermute | solution.py:304
  68.8 3.9 %all-to-all-start.1 = ((bf16[32,24,128]{2,1,0:T(8,128)(2,1)}), bf16[32,24,128]{2,1,0:T(8,128)(2,1)S(1)}, u32[]{:S(2)}, u32[]{:S(2)}) async-start(bf16[32,24,128]{2,1,0:T(8,128)(2,1)} %query.1), calls=%async_computation.1 | async-start | bytes 393216 | tf_op jit(solution)/shard_map/all_to_all | solution.py:284
  72.7 2.2 %fusion = f32[256]{0:T(256)S(1)} fusion(bf16[256,4096]{1,0:T(8,128)(2,1)} %bitcast.42), kind=kLoop, calls=%fused_computation.4 | loop fusion | flops 3145472 | bytes 2098176 | tf_op jit(solution)/shard_map/reduce_sum | solution.py:292
  75.0 0.5 fusion.3
  75.5 0.8 copy-done.3
  76.4 4.4 %fusion.5 = (bf16[256,4096]{1,0:T(8,128)(2,1)S(1)}, bf16[256,4096]{1,0:T(8,128)(2,1)}) fusion(bf16[256,4096]{1,0:T(8,128)(2,1)} %copy-done.3, f32[256]{0:T(256)S(1)} %add_rsqrt_fusion, f32[4096]{0:T(1024)S(1)} %copy-done.7, f32[256]{0:T(256)S(1)} %add_rsqrt_fusion.1, bf16[256,4096]{1,0:T(8,128)(2,1)S(1)} %bitcast.43), kind=kLoop, calls=%fused_computation.9 | loop fusion | flops 8388608 | bytes 8407040 | tf_op jit(solution)/shard_map/convert_element_type | solution.py:293
  80.7 13.1 %all-to-all-done.1.parts = bf16[32,24,128]{2,1,0:T(8,128)(2,1)S(1)} async-done(((bf16[32,24,128]{2,1,0:T(8,128)(2,1)}), bf16[32,24,128]{2,1,0:T(8,128)(2,1)S(1)}, u32[]{:S(2)}, u32[]{:S(2)}) %all-to-all-start.1) | async-done | bytes 196640 | tf_op jit(solution)/shard_map/all_to_all | solution.py:284
  93.9 10.9 %all-gather.1 = bf16[128,8,128]{2,1,0:T(8,128)(2,1)S(1)} all-gather(bf16[32,8,128]{2,1,0:T(8,128)(2,1)S(1)} %slice.9), channel_id=3, replica_groups={{0,64,128,192},{32,96,160,224},{256,320,384,448},{288,352,416,480},{1,6..., dimensions={0}, use_global_device_ids=true | all-gather | bytes 327680 | tf_op jit(solution)/shard_map/all_gather | solution.py:299
  104.7 0.1 copy.27
  104.8 4.4 %collective-permute-start.3 = (bf16[1024,128]{1,0:T(8,128)(2,1)S(1)}, bf16[1024,128]{1,0:T(8,128)(2,1)S(1)}, u32[]{:S(2)}, u32[]{:S(2)}) collective-permute-start(bf16[1024,128]{1,0:T(8,128)(2,1)S(1)} %bitcast.46), channel_id=1, source_target_pairs={{16,32},{17,33},{18,34},{19,35},{20,36},{21,37},{22,38},{23,39},{2... | collective-permute-start | bytes 786440 | tf_op jit(solution)/shard_map/ppermute | solution.py:303
  109.3 4.0 %collective-permute-done.3 = bf16[1024,128]{1,0:T(8,128)(2,1)S(1)} collective-permute-done((bf16[1024,128]{1,0:T(8,128)(2,1)S(1)}, bf16[1024,128]{1,0:T(8,128)(2,1)S(1)}, u32[]{:S(2)}, u32[]{:S(2)}) %collective-permute-start.3) | collective-permute-done | bytes 262176 | tf_op jit(solution)/shard_map/ppermute | solution.py:303
  113.3 0.1 broadcast_select_fusion
  113.4 1.6 copy-done
  114.9 7.6 %attend.1 = bf16[32,16,128]{2,1,0:T(8,128)(2,1)} custom-call(s32[4]{0:T(128)S(1)} %copy-done.1, s32[2]{0:T(128)S(1)} %pad_add_fusion.1.len_ref, bf16[256,4096]{1,0:T(8,128)(2,1)S(1)} %copy-done, bf16[256,4096]{1,0:T(8,128)(2,1)S(1)} %get-tuple-element.32.other_ref, f32[256,128]{1,0:T(8,128)S(1)} %get-tuple-element.33.cos_ref, ...), custom_call_target="tpu_custom_call" | custom-call | tf_op jit(solution)/shard_map/attend/pallas_call | solution.py:248
  122.6 3.9 %all-to-all-start.2 = ((bf16[32,16,128]{2,1,0:T(8,128)(2,1)}), bf16[32,16,128]{2,1,0:T(8,128)(2,1)S(1)}, u32[]{:S(2)}, u32[]{:S(2)}) async-start(bf16[32,16,128]{2,1,0:T(8,128)(2,1)} %attend.1), calls=%async_computation.2 | async-start | bytes 262144 | tf_op jit(solution)/shard_map/all_to_all | solution.py:328
  126.5 14.4 %all-to-all-done.2 = bf16[32,16,128]{2,1,0:T(8,128)(2,1)S(1)} async-done(((bf16[32,16,128]{2,1,0:T(8,128)(2,1)}), bf16[32,16,128]{2,1,0:T(8,128)(2,1)S(1)}, u32[]{:S(2)}, u32[]{:S(2)}) %all-to-all-start.2) | async-done | bytes 131104 | tf_op jit(solution)/shard_map/all_to_all | solution.py:328
  141.0 0.2 fusion.7
  141.2 6.5 %collective-permute-start.6 = (f32[32,128]{1,0:T(8,128)S(1)}, f32[32,128]{1,0:T(8,128)S(1)}, u32[]{:S(2)}, u32[]{:S(2)}) collective-permute-start(f32[32,128]{1,0:T(8,128)S(1)} %dynamic-slice_bitcast_fusion), channel_id=1, source_target_pairs={{0,32},{32,0},{64,96},{96,64},{128,160},{160,128},{192,224},{224,1... | collective-permute-start | bytes 49160 | tf_op jit(solution)/shard_map/ppermute | solution.py:335
  147.7 0.8 collective-permute-done.6
  148.5 0.1 multiply_reduce_fusion
  148.6 15.2 %all_to_all.32 = f32[32,1,32]{2,1,0:T(1,128)S(1)} all-to-all(f32[32,1,32]{2,1,0:T(1,128)S(1)} %broadcast_in_dim.21), channel_id=1, replica_groups=mesh['dp'=16,'fsdp'=32] {'fsdp'}, dimensions={0} | all-to-all | bytes 8192 | tf_op jit(solution)/shard_map/all_to_all | solution.py:338
  163.8 0.2 fusion.6
  164.0 15.2 %all_to_all.33 = bf16[16,1,4,128]{3,2,1,0:T(4,128)(2,1)S(1)} all-to-all(bf16[16,1,4,128]{3,2,1,0:T(4,128)(2,1)S(1)} %copy.30), channel_id=1, replica_groups=mesh['dp'=16,'fsdp'=32] {'dp'}, dimensions={0} | all-to-all | bytes 32768 | tf_op jit(solution)/shard_map/all_to_all | solution.py:345
  179.2 0.6 copy.41
  (35 shorter events, 0.3 us)
Async XLA Ops:
  6.5 106.8 %all-gather.4.cloned.1.call-start = ((), (), s32[]{:S(2)}) async-start(), calls=%async_computation.5 | async-start | bytes 4456448 | tf_op jit(solution)/shard_map/all_gather | solution.py:275
  9.4 6.6 %collective-permute-start = (bf16[128,512]{1,0:T(8,128)(2,1)}, bf16[128,512]{1,0:T(8,128)(2,1)S(1)}, u32[]{:S(2)}, u32[]{:S(2)}) collective-permute-start(bf16[128,512]{1,0:T(8,128)(2,1)} %unit.1.near_ref), channel_id=1, source_target_pairs={{0,16},{1,17},{2,18},{3,19},{4,20},{5,21},{6,22},{7,23},{8,24},{9,... | collective-permute-start | bytes 393224 | tf_op jit(solution)/shard_map/ppermute | solution.py:274
  16.0 0.7 copy-start.6
  18.4 37.4 %collective-permute-start.1 = (bf16[128,2048]{1,0:T(8,128)(2,1)}, bf16[128,2048]{1,0:T(8,128)(2,1)S(1)}, u32[]{:S(2)}, u32[]{:S(2)}) collective-permute-start(bf16[128,2048]{1,0:T(8,128)(2,1)} %near_ref.1), channel_id=1, source_target_pairs={{0,16},{1,17},{2,18},{3,19},{4,20},{5,21},{6,22},{7,23},{8,24},{9,... | collective-permute-start | bytes 1572872 | tf_op jit(solution)/shard_map/ppermute | solution.py:281
  21.8 43.0 %collective-permute-start.4 = (s32[1]{0:T(128)}, s32[1]{0:T(128)}, u32[]{:S(2)}, u32[]{:S(2)}) collective-permute-start(s32[1]{0:T(128)} %param.11), channel_id=1, source_target_pairs={{0,32},{32,0},{64,96},{96,64},{128,160},{160,128},{192,224},{224,1... | collective-permute-start | bytes 20 | tf_op jit(solution)/shard_map/ppermute | solution.py:286
  32.0 44.4 %copy-start.7 = (f32[4096]{0:T(1024)S(1)}, f32[4096]{0:T(1024)}, u32[]{:S(2)}) copy-start(f32[4096]{0:T(1024)} %param.14) | copy-start | bytes 49156
  32.9 22.9 %all-to-all-start = ((bf16[16,8,128]{2,1,0:T(8,128)(2,1)}), bf16[16,8,128]{2,1,0:T(8,128)(2,1)S(1)}, u32[]{:S(2)}, u32[]{:S(2)}) async-start(bf16[16,8,128]{2,1,0:T(8,128)(2,1)} %open.1), calls=%async_computation | async-start | bytes 65536 | tf_op jit(solution)/shard_map/all_to_all | solution.py:280
  55.8 0.6 copy-start.5
  56.4 0.8 copy-start.4
  59.8 15.2 %collective-permute-start.2 = (bf16[256,4096]{1,0:T(8,128)(2,1)}, bf16[256,4096]{1,0:T(8,128)(2,1)S(1)}, u32[]{:S(2)}, u32[]{:S(2)}) collective-permute-start(bf16[256,4096]{1,0:T(8,128)(2,1)} %bitcast.41), channel_id=1, source_target_pairs={{0,32},{32,0},{64,96},{96,64},{128,160},{160,128},{192,224},{224,1... | collective-permute-start | bytes 6291464 | tf_op jit(solution)/shard_map/ppermute | solution.py:295
  66.3 43.0 %collective-permute-start.5 = (bf16[16,128]{1,0:T(8,128)(2,1)S(1)}, bf16[16,128]{1,0:T(8,128)(2,1)S(1)}, u32[]{:S(2)}, u32[]{:S(2)}) collective-permute-start(bf16[16,128]{1,0:T(8,128)(2,1)S(1)} %bitcast.50), channel_id=1, source_target_pairs={{0,16},{1,17},{2,18},{3,19},{4,20},{5,21},{6,22},{7,23},{8,24},{9,... | collective-permute-start | bytes 12296 | tf_op jit(solution)/shard_map/ppermute | solution.py:304
  68.8 25.1 %all-to-all-start.1 = ((bf16[32,24,128]{2,1,0:T(8,128)(2,1)}), bf16[32,24,128]{2,1,0:T(8,128)(2,1)S(1)}, u32[]{:S(2)}, u32[]{:S(2)}) async-start(bf16[32,24,128]{2,1,0:T(8,128)(2,1)} %query.1), calls=%async_computation.1 | async-start | bytes 393216 | tf_op jit(solution)/shard_map/all_to_all | solution.py:284
  72.7 3.6 %copy-start.2 = (bf16[1,256,4096]{2,1,0:T(8,128)(2,1)S(1)}, bf16[1,256,4096]{2,1,0:T(8,128)(2,1)}, u32[]{:S(2)}) copy-start(bf16[1,256,4096]{2,1,0:T(8,128)(2,1)} %hidden) | copy-start | bytes 6291460
  75.0 1.4 copy-start.3
  76.4 37.0 %copy-start.1 = (s32[4]{0:T(128)S(1)}, s32[4]{0:T(128)}, u32[]{:S(2)}) copy-start(s32[4]{0:T(128)} %pad_add_fusion.place_ref) | copy-start | bytes 52
  104.8 8.5 %collective-permute-start.3 = (bf16[1024,128]{1,0:T(8,128)(2,1)S(1)}, bf16[1024,128]{1,0:T(8,128)(2,1)S(1)}, u32[]{:S(2)}, u32[]{:S(2)}) collective-permute-start(bf16[1024,128]{1,0:T(8,128)(2,1)S(1)} %bitcast.46), channel_id=1, source_target_pairs={{16,32},{17,33},{18,34},{19,35},{20,36},{21,37},{22,38},{23,39},{2... | collective-permute-start | bytes 786440 | tf_op jit(solution)/shard_map/ppermute | solution.py:303
  113.4 1.6 copy-start
  122.6 18.3 %all-to-all-start.2 = ((bf16[32,16,128]{2,1,0:T(8,128)(2,1)}), bf16[32,16,128]{2,1,0:T(8,128)(2,1)S(1)}, u32[]{:S(2)}, u32[]{:S(2)}) async-start(bf16[32,16,128]{2,1,0:T(8,128)(2,1)} %attend.1), calls=%async_computation.2 | async-start | bytes 262144 | tf_op jit(solution)/shard_map/all_to_all | solution.py:328
  141.2 7.3 %collective-permute-start.6 = (f32[32,128]{1,0:T(8,128)S(1)}, f32[32,128]{1,0:T(8,128)S(1)}, u32[]{:S(2)}, u32[]{:S(2)}) collective-permute-start(f32[32,128]{1,0:T(8,128)S(1)} %dynamic-slice_bitcast_fusion), channel_id=1, source_target_pairs={{0,32},{32,0},{64,96},{96,64},{128,160},{160,128},{192,224},{224,1... | collective-permute-start | bytes 49160 | tf_op jit(solution)/shard_map/ppermute | solution.py:335
Sparse Core Ops, SparseCore 0:
  18.5 86.4 all-gather.3

commit v11 on v9

--- a/solution.py
+++ b/solution.py
@@ -283,21 +283,25 @@
     payload = query_payload(place, arrived, w_query, w_query_other, w_out)
     parts = lax.all_to_all(payload, BOTH, 0, 0, tiled=True, axis_index_groups=CORE_Z_GROUPS)
 
-    rows, lengths, parts = lax.optimization_barrier((hidden[0], lengths, parts))
+    lengths, arrived, _ = lax.optimization_barrier((lengths, arrived, payload))
+    far_inputs = lax.ppermute(arrived[:, 3], "fsdp", Y_LO_SWAP)
     both_lengths = jnp.concatenate([lengths, lax.ppermute(lengths, "dp", CORE_SWAP)])
+    cosine, sine = rope_tables(jnp.arange(seq_len), HEAD)
+    rows, parts, far_inputs, both_lengths, cosine, sine = lax.optimization_barrier(
+        (hidden[0], parts, far_inputs, both_lengths, cosine, sine)
+    )
     floats = rows.astype(f32)
     normed = (
         floats * lax.rsqrt(jnp.mean(floats * floats, axis=-1, keepdims=True) + 1e-05) * attn_gain
     ).astype(bf16)
     other = lax.ppermute(normed, "dp", CORE_SWAP)
-    cosine, sine = rope_tables(jnp.arange(seq_len), HEAD)
 
     weight = lax.all_gather(
         parts[:, WEIGHT_ROW:], "dp", axis=0, tiled=False, axis_index_groups=X_GROUPS
     ).reshape(X, 2, Z, 8, HEAD)
     weight = jnp.transpose(weight, (2, 1, 0, 3, 4)).reshape(2 * Z * 32, HEAD)
     weight = jnp.where(core == y_lo, weight, lax.ppermute(weight, BOTH, CROSS_SWAP))
-    near, far = arrived[:, 2], lax.ppermute(arrived[:, 3], "fsdp", Y_LO_SWAP)
+    near, far = arrived[:, 2], far_inputs
     inputs = jnp.concatenate([jnp.where(y_lo == 0, near, far), jnp.where(y_lo == 0, far, near)])
     inputs = inputs.astype(f32)
     gain = lax.dynamic_slice(final_gain, (fsdp * HEAD,), (HEAD,))

time: 186 us -> 186 us (level)
  blocking collectives: 67.6 us -> 40.3 us
  starting transfers between devices: 35.5 us -> 54 us
  waiting for transfers between devices: 39.8 us -> 48.6 us
    all_to_all x1 -> x0, blocking collectives: 27 us -> none  [local(): lax.all_to_all(outgoing, 'fsdp', 0, 0, tiled=True, axis_index_groups=Z_GR...]
    all_to_all x0 -> x1, starting transfers between devices: none -> 15.5 us  [local(): lax.all_to_all(outgoing, 'fsdp', 0, 0, tiled=True, axis_index_groups=Z_GR...]
    all_to_all x0 -> x1, waiting for transfers between devices: none -> 11.5 us  [local(): lax.all_to_all(outgoing, 'fsdp', 0, 0, tiled=True, axis_index_groups=Z_GR...]
    all_to_all x1, waiting for transfers between devices: 20.4 us -> 14.2 us  [local(): lax.all_to_all(payload, BOTH, 0, 0, tiled=True, axis_index_groups=CORE_Z_...]
    ppermute x1, waiting for transfers between devices: 0.07 us -> 4.01 us  [local(): lax.ppermute(weight, BOTH, CROSS_SWAP)]
    ppermute x1, starting transfers between devices: 5.72 us -> 8.8 us  [local(): residual = inputs + (kept + lax.ppermute(given, 'dp', CORE_SWAP))]
  transfers between devices with their start and end apart: 10 -> 11, of which waited for: 6 -> 7; matrix products, arithmetic and copies ran while one was open for 4% -> 4% of each run, Pallas kernels for 2% -> 2%
where the time goes in v11:
time: 186 us; the launch traced here: 185 us
  starting transfers between devices  54 us (29%)
  waiting for transfers between devices  48.6 us (26%)
  blocking collectives  40.3 us (22%)
  Pallas kernels  15.1 us (8%)
  between operations  14.3 us (8%)
  other arithmetic  7.05 us (4%)
  local copies, waits for them, and re-layouts  5.21 us (3%)
    all_to_all x1, starting transfers between devices, local(): lax.all_to_all(outgoing, 'fsdp', 0, 0, tiled=True, axis_index_groups=Z_GR...  15.5 us
    all_to_all x1, blocking collectives, local(): lax.all_to_all(jnp.broadcast_to(partial[None, None, :], (slabs, 1, slabs)...  15.2 us
    all_to_all x1, blocking collectives, local(): lax.all_to_all(outgoing[:, None], 'dp', split_axis=0, concat_axis=1, tile...  14.9 us
    all_to_all x1, waiting for transfers between devices, local(): contexts = lax.all_to_all(context, 'fsdp', 0, 0, tiled=True)  14.4 us
    all_to_all x1, waiting for transfers between devices, local(): lax.all_to_all(payload, BOTH, 0, 0, tiled=True, axis_index_groups=CORE_Z_...  14.2 us
    all_to_all x1, waiting for transfers between devices, local(): lax.all_to_all(outgoing, 'fsdp', 0, 0, tiled=True, axis_index_groups=Z_GR...  11.5 us
    all_gather x1, blocking collectives, local(): lax.all_gather(parts[:, WEIGHT_ROW:], 'dp', axis=0, tiled=False, axis_ind...  10.2 us
    ppermute x1, starting transfers between devices, local(): residual = inputs + (kept + lax.ppermute(given, 'dp', CORE_SWAP))  8.8 us
  transfers between devices with their start and end apart: 11, of which 7 were waited for; matrix products, arithmetic and copies ran while one was open for 4% of the time, Pallas kernels for 2%

profile of v11, /device:TPU:1, one launch (start us, length us, event | category | flops | bytes accessed | tf_op | source)
XLA Modules:
  0.0 185.0 jit_solution(7756222231219838548)
XLA Ops:
  7.2 0.7 pad_add_fusion.place_ref
  7.8 1.6 unit.1.near_ref
  9.5 4.0 %collective-permute-start = (bf16[128,512]{1,0:T(8,128)(2,1)}, bf16[128,512]{1,0:T(8,128)(2,1)S(1)}, u32[]{:S(2)}, u32[]{:S(2)}) collective-permute-start(bf16[128,512]{1,0:T(8,128)(2,1)} %unit.1.near_ref), channel_id=1, source_target_pairs={{0,16},{1,17},{2,18},{3,19},{4,20},{5,21},{6,22},{7,23},{8,24},{9,... | collective-permute-start | bytes 393224 | tf_op jit(solution)/shard_map/ppermute | solution.py:274
  13.5 2.6 %collective-permute-done.far_ref = bf16[128,512]{1,0:T(8,128)(2,1)S(1)} collective-permute-done((bf16[128,512]{1,0:T(8,128)(2,1)}, bf16[128,512]{1,0:T(8,128)(2,1)S(1)}, u32[]{:S(2)}, u32[]{:S(2)}) %collective-permute-start) | collective-permute-done | bytes 131104 | tf_op jit(solution)/shard_map/ppermute | solution.py:274
  16.1 0.9 copy-done
  17.0 0.7 pair.1
  17.7 0.0 all-gather.4.cloned.1.call-update
  17.7 3.4 %collective-permute-start.1 = (bf16[128,2048]{1,0:T(8,128)(2,1)}, bf16[128,2048]{1,0:T(8,128)(2,1)S(1)}, u32[]{:S(2)}, u32[]{:S(2)}) collective-permute-start(bf16[128,2048]{1,0:T(8,128)(2,1)} %near_ref.1), channel_id=1, source_target_pairs={{0,16},{1,17},{2,18},{3,19},{4,20},{5,21},{6,22},{7,23},{8,24},{9,... | collective-permute-start | bytes 1572872 | tf_op jit(solution)/shard_map/ppermute | solution.py:281
  21.1 2.4 %open.1 = bf16[16,8,128]{2,1,0:T(8,128)(2,1)} custom-call(s32[4]{0:T(128)} %pad_add_fusion.place_ref, bf16[1,256,4096]{2,1,0:T(8,128)(2,1)} %hidden, f32[1,4096]{1,0:T(1,128)} %bitcast.46), custom_call_target="tpu_custom_call" | custom-call | tf_op jit(solution)/shard_map/open/pallas_call | solution.py:125
  23.4 15.5 %all-to-all-start = ((bf16[16,8,128]{2,1,0:T(8,128)(2,1)}), bf16[16,8,128]{2,1,0:T(8,128)(2,1)S(1)}, u32[]{:S(2)}, u32[]{:S(2)}) async-start(bf16[16,8,128]{2,1,0:T(8,128)(2,1)} %open.1), calls=%async_computation | async-start | bytes 65536 | tf_op jit(solution)/shard_map/all_to_all | solution.py:280
  38.9 11.5 %all-to-all-done.arrived_ref = bf16[16,8,128]{2,1,0:T(8,128)(2,1)S(1)} async-done(((bf16[16,8,128]{2,1,0:T(8,128)(2,1)}), bf16[16,8,128]{2,1,0:T(8,128)(2,1)S(1)}, u32[]{:S(2)}, u32[]{:S(2)}) %all-to-all-start) | async-done | bytes 32800 | tf_op jit(solution)/shard_map/all_to_all | solution.py:280
  50.5 1.0 copy-done.1
  51.5 1.0 copy-done.2
  52.6 0.7 copy-done.3
  53.2 1.7 query.1
  54.9 7.0 %all-to-all-start.1 = ((bf16[32,24,128]{2,1,0:T(8,128)(2,1)}), bf16[32,24,128]{2,1,0:T(8,128)(2,1)S(1)}, u32[]{:S(2)}, u32[]{:S(2)}) async-start(bf16[32,24,128]{2,1,0:T(8,128)(2,1)} %query.1), calls=%async_computation.1 | async-start | bytes 393216 | tf_op jit(solution)/shard_map/all_to_all | solution.py:284
  61.9 0.5 fusion.7
  62.5 0.1 pad_maximum_fusion
  62.7 2.2 %collective-permute-start.2 = (bf16[16,128]{1,0:T(8,128)(2,1)S(1)}, bf16[16,128]{1,0:T(8,128)(2,1)S(1)}, u32[]{:S(2)}, u32[]{:S(2)}) collective-permute-start(bf16[16,128]{1,0:T(8,128)(2,1)S(1)} %bitcast.49), channel_id=1, source_target_pairs={{0,16},{1,17},{2,18},{3,19},{4,20},{5,21},{6,22},{7,23},{8,24},{9,... | collective-permute-start | bytes 12296 | tf_op jit(solution)/shard_map/ppermute | solution.py:287
  64.8 2.4 %collective-permute-start.3 = (s32[1]{0:T(128)}, s32[1]{0:T(128)}, u32[]{:S(2)}, u32[]{:S(2)}) collective-permute-start(s32[1]{0:T(128)} %param.11), channel_id=1, source_target_pairs={{0,32},{32,0},{64,96},{96,64},{128,160},{160,128},{192,224},{224,1... | collective-permute-start | bytes 20 | tf_op jit(solution)/shard_map/ppermute | solution.py:288
  67.3 1.1 collective-permute-done.3
  68.4 0.6 pad_add_fusion.1.len_ref
  69.0 14.2 %all-to-all-done.1.parts = bf16[32,24,128]{2,1,0:T(8,128)(2,1)S(1)} async-done(((bf16[32,24,128]{2,1,0:T(8,128)(2,1)}), bf16[32,24,128]{2,1,0:T(8,128)(2,1)S(1)}, u32[]{:S(2)}, u32[]{:S(2)}) %all-to-all-start.1) | async-done | bytes 196640 | tf_op jit(solution)/shard_map/all_to_all | solution.py:284
  83.2 2.1 %fusion = f32[256]{0:T(256)S(1)} fusion(bf16[256,4096]{1,0:T(8,128)(2,1)} %bitcast.41), kind=kLoop, calls=%fused_computation.2 | loop fusion | flops 3145472 | bytes 2098176 | tf_op jit(solution)/shard_map/reduce_sum | solution.py:295
  85.3 2.2 %fusion.2.normed_ref = bf16[256,4096]{1,0:T(8,128)(2,1)S(1)} fusion(bf16[256,4096]{1,0:T(8,128)(2,1)} %bitcast.42, f32[4096]{0:T(1024)S(1)} %copy-done.5, f32[256]{0:T(256)S(1)} %add_rsqrt_fusion), kind=kLoop, calls=%fused_computation.4 | loop fusion | flops 4194304 | bytes 4211712 | tf_op jit(solution)/shard_map/convert_element_type | solution.py:296
  87.5 2.3 %collective-permute-start.5 = (bf16[256,4096]{1,0:T(8,128)(2,1)S(1)}, bf16[256,4096]{1,0:T(8,128)(2,1)}, u32[]{:S(2)}, u32[]{:S(2)}) collective-permute-start(bf16[256,4096]{1,0:T(8,128)(2,1)S(1)} %fusion.2.normed_ref), channel_id=1, source_target_pairs={{0,32},{32,0},{64,96},{96,64},{128,160},{160,128},{192,224},{224,1... | collective-permute-start | bytes 6291464 | tf_op jit(solution)/shard_map/ppermute | solution.py:297
  89.8 0.2 select_reduce_fusion
  90.0 0.1 fusion.10
  90.1 0.1 reduce_window_sum.11
  90.2 0.8 dynamic_slice.10
  90.9 0.2 select_reduce_fusion.1
  91.2 10.2 %all-gather.1 = bf16[128,8,128]{2,1,0:T(8,128)(2,1)S(1)} all-gather(bf16[32,8,128]{2,1,0:T(8,128)(2,1)S(1)} %slice.10), channel_id=3, replica_groups={{0,64,128,192},{32,96,160,224},{256,320,384,448},{288,352,416,480},{1,6..., dimensions={0}, use_global_device_ids=true | all-gather | bytes 327680 | tf_op jit(solution)/shard_map/all_gather | solution.py:299
  101.4 0.1 copy.27
  101.4 4.6 %collective-permute-start.4 = (bf16[1024,128]{1,0:T(8,128)(2,1)S(1)}, bf16[1024,128]{1,0:T(8,128)(2,1)S(1)}, u32[]{:S(2)}, u32[]{:S(2)}) collective-permute-start(bf16[1024,128]{1,0:T(8,128)(2,1)S(1)} %bitcast.45), channel_id=1, source_target_pairs={{16,32},{17,33},{18,34},{19,35},{20,36},{21,37},{22,38},{23,39},{2... | collective-permute-start | bytes 786440 | tf_op jit(solution)/shard_map/ppermute | solution.py:303
  106.0 4.0 %collective-permute-done.4 = bf16[1024,128]{1,0:T(8,128)(2,1)S(1)} collective-permute-done((bf16[1024,128]{1,0:T(8,128)(2,1)S(1)}, bf16[1024,128]{1,0:T(8,128)(2,1)S(1)}, u32[]{:S(2)}, u32[]{:S(2)}) %collective-permute-start.4) | collective-permute-done | bytes 262176 | tf_op jit(solution)/shard_map/ppermute | solution.py:303
  110.1 0.1 broadcast_select_fusion
  110.1 0.0 all-gather.4.cloned.1.call-done
  110.2 8.7 %attend.1 = bf16[32,16,128]{2,1,0:T(8,128)(2,1)} custom-call(s32[4]{0:T(128)S(1)} %copy-done.4, s32[2]{0:T(128)S(1)} %pad_add_fusion.1.len_ref, bf16[256,4096]{1,0:T(8,128)(2,1)S(1)} %fusion.2.normed_ref, bf16[256,4096]{1,0:T(8,128)(2,1)} %collective-permute-done.5.other_ref, f32[256,128]{1,0:T(8,128)S(1)} %get-tuple-element.41.cos_ref, ...), custom_call_target="tpu_custom_call" | custom-call | tf_op jit(solution)/shard_map/attend/pallas_call | solution.py:248
  118.9 3.9 %all-to-all-start.2 = ((bf16[32,16,128]{2,1,0:T(8,128)(2,1)}), bf16[32,16,128]{2,1,0:T(8,128)(2,1)S(1)}, u32[]{:S(2)}, u32[]{:S(2)}) async-start(bf16[32,16,128]{2,1,0:T(8,128)(2,1)} %attend.1), calls=%async_computation.2 | async-start | bytes 262144 | tf_op jit(solution)/shard_map/all_to_all | solution.py:328
  122.8 14.4 %all-to-all-done.2 = bf16[32,16,128]{2,1,0:T(8,128)(2,1)S(1)} async-done(((bf16[32,16,128]{2,1,0:T(8,128)(2,1)}), bf16[32,16,128]{2,1,0:T(8,128)(2,1)S(1)}, u32[]{:S(2)}, u32[]{:S(2)}) %all-to-all-start.2) | async-done | bytes 131104 | tf_op jit(solution)/shard_map/all_to_all | solution.py:328
  137.2 0.2 fusion.4
  137.4 8.8 %collective-permute-start.6 = (f32[32,128]{1,0:T(8,128)S(1)}, f32[32,128]{1,0:T(8,128)S(1)}, u32[]{:S(2)}, u32[]{:S(2)}) collective-permute-start(f32[32,128]{1,0:T(8,128)S(1)} %dynamic-slice_bitcast_fusion), channel_id=1, source_target_pairs={{0,32},{32,0},{64,96},{96,64},{128,160},{160,128},{192,224},{224,1... | collective-permute-start | bytes 49160 | tf_op jit(solution)/shard_map/ppermute | solution.py:335
  146.2 0.8 collective-permute-done.6
  147.0 0.1 multiply_reduce_fusion
  147.2 15.2 %all_to_all.32 = f32[32,1,32]{2,1,0:T(1,128)S(1)} all-to-all(f32[32,1,32]{2,1,0:T(1,128)S(1)} %broadcast_in_dim.21), channel_id=1, replica_groups=mesh['dp'=16,'fsdp'=32] {'fsdp'}, dimensions={0} | all-to-all | bytes 8192 | tf_op jit(solution)/shard_map/all_to_all | solution.py:338
  162.4 0.2 fusion.3
  162.6 14.9 %all_to_all.33 = bf16[16,1,4,128]{3,2,1,0:T(4,128)(2,1)S(1)} all-to-all(bf16[16,1,4,128]{3,2,1,0:T(4,128)(2,1)S(1)} %copy.30), channel_id=1, replica_groups=mesh['dp'=16,'fsdp'=32] {'dp'}, dimensions={0} | all-to-all | bytes 32768 | tf_op jit(solution)/shard_map/all_to_all | solution.py:345
  177.5 0.6 copy.41
  (33 shorter events, 0.2 us)
Async XLA Ops:
  6.5 103.6 %all-gather.4.cloned.1.call-start = ((), (), s32[]{:S(2)}) async-start(), calls=%async_computation.5 | async-start | bytes 4456448 | tf_op jit(solution)/shard_map/all_gather | solution.py:275
  7.8 77.4 %copy-start.5 = (f32[4096]{0:T(1024)S(1)}, f32[4096]{0:T(1024)}, u32[]{:S(2)}) copy-start(f32[4096]{0:T(1024)} %param.14) | copy-start | bytes 49156
  9.5 6.6 %collective-permute-start = (bf16[128,512]{1,0:T(8,128)(2,1)}, bf16[128,512]{1,0:T(8,128)(2,1)S(1)}, u32[]{:S(2)}, u32[]{:S(2)}) collective-permute-start(bf16[128,512]{1,0:T(8,128)(2,1)} %unit.1.near_ref), channel_id=1, source_target_pairs={{0,16},{1,17},{2,18},{3,19},{4,20},{5,21},{6,22},{7,23},{8,24},{9,... | collective-permute-start | bytes 393224 | tf_op jit(solution)/shard_map/ppermute | solution.py:274
  16.1 0.9 copy-start
  17.7 32.8 %collective-permute-start.1 = (bf16[128,2048]{1,0:T(8,128)(2,1)}, bf16[128,2048]{1,0:T(8,128)(2,1)S(1)}, u32[]{:S(2)}, u32[]{:S(2)}) collective-permute-start(bf16[128,2048]{1,0:T(8,128)(2,1)} %near_ref.1), channel_id=1, source_target_pairs={{0,16},{1,17},{2,18},{3,19},{4,20},{5,21},{6,22},{7,23},{8,24},{9,... | collective-permute-start | bytes 1572872 | tf_op jit(solution)/shard_map/ppermute | solution.py:281
  23.4 27.0 %all-to-all-start = ((bf16[16,8,128]{2,1,0:T(8,128)(2,1)}), bf16[16,8,128]{2,1,0:T(8,128)(2,1)S(1)}, u32[]{:S(2)}, u32[]{:S(2)}) async-start(bf16[16,8,128]{2,1,0:T(8,128)(2,1)} %open.1), calls=%async_computation | async-start | bytes 65536 | tf_op jit(solution)/shard_map/all_to_all | solution.py:280
  50.5 1.0 copy-start.1
  51.5 1.0 copy-start.2
  52.6 0.7 copy-start.3
  54.9 34.9 %copy-start.6 = (s32[1024]{0:T(1024)S(1)}, s32[1024]{0:T(1024)}, u32[]{:S(2)}) copy-start(s32[1024]{0:T(1024)} %param.13) | copy-start | bytes 12292
  54.9 34.9 %copy-start.7 = (s32[32]{0:T(128)S(1)}, s32[32]{0:T(128)}, u32[]{:S(2)}) copy-start(s32[32]{0:T(128)} %param.12) | copy-start | bytes 388
  54.9 28.2 %all-to-all-start.1 = ((bf16[32,24,128]{2,1,0:T(8,128)(2,1)}), bf16[32,24,128]{2,1,0:T(8,128)(2,1)S(1)}, u32[]{:S(2)}, u32[]{:S(2)}) async-start(bf16[32,24,128]{2,1,0:T(8,128)(2,1)} %query.1), calls=%async_computation.1 | async-start | bytes 393216 | tf_op jit(solution)/shard_map/all_to_all | solution.py:284
  62.6 47.5 %copy-start.4 = (s32[4]{0:T(128)S(1)}, s32[4]{0:T(128)}, u32[]{:S(2)}) copy-start(s32[4]{0:T(128)} %pad_add_fusion.place_ref) | copy-start | bytes 52
  62.7 6.3 %collective-permute-start.2 = (bf16[16,128]{1,0:T(8,128)(2,1)S(1)}, bf16[16,128]{1,0:T(8,128)(2,1)S(1)}, u32[]{:S(2)}, u32[]{:S(2)}) collective-permute-start(bf16[16,128]{1,0:T(8,128)(2,1)S(1)} %bitcast.49), channel_id=1, source_target_pairs={{0,16},{1,17},{2,18},{3,19},{4,20},{5,21},{6,22},{7,23},{8,24},{9,... | collective-permute-start | bytes 12296 | tf_op jit(solution)/shard_map/ppermute | solution.py:287
  64.8 3.5 %collective-permute-start.3 = (s32[1]{0:T(128)}, s32[1]{0:T(128)}, u32[]{:S(2)}, u32[]{:S(2)}) collective-permute-start(s32[1]{0:T(128)} %param.11), channel_id=1, source_target_pairs={{0,32},{32,0},{64,96},{96,64},{128,160},{160,128},{192,224},{224,1... | collective-permute-start | bytes 20 | tf_op jit(solution)/shard_map/ppermute | solution.py:288
  87.5 22.6 %collective-permute-start.5 = (bf16[256,4096]{1,0:T(8,128)(2,1)S(1)}, bf16[256,4096]{1,0:T(8,128)(2,1)}, u32[]{:S(2)}, u32[]{:S(2)}) collective-permute-start(bf16[256,4096]{1,0:T(8,128)(2,1)S(1)} %fusion.2.normed_ref), channel_id=1, source_target_pairs={{0,32},{32,0},{64,96},{96,64},{128,160},{160,128},{192,224},{224,1... | collective-permute-start | bytes 6291464 | tf_op jit(solution)/shard_map/ppermute | solution.py:297
  101.4 8.6 %collective-permute-start.4 = (bf16[1024,128]{1,0:T(8,128)(2,1)S(1)}, bf16[1024,128]{1,0:T(8,128)(2,1)S(1)}, u32[]{:S(2)}, u32[]{:S(2)}) collective-permute-start(bf16[1024,128]{1,0:T(8,128)(2,1)S(1)} %bitcast.45), channel_id=1, source_target_pairs={{16,32},{17,33},{18,34},{19,35},{20,36},{21,37},{22,38},{23,39},{2... | collective-permute-start | bytes 786440 | tf_op jit(solution)/shard_map/ppermute | solution.py:303
  118.9 18.3 %all-to-all-start.2 = ((bf16[32,16,128]{2,1,0:T(8,128)(2,1)}), bf16[32,16,128]{2,1,0:T(8,128)(2,1)S(1)}, u32[]{:S(2)}, u32[]{:S(2)}) async-start(bf16[32,16,128]{2,1,0:T(8,128)(2,1)} %attend.1), calls=%async_computation.2 | async-start | bytes 262144 | tf_op jit(solution)/shard_map/all_to_all | solution.py:328
  137.4 9.6 %collective-permute-start.6 = (f32[32,128]{1,0:T(8,128)S(1)}, f32[32,128]{1,0:T(8,128)S(1)}, u32[]{:S(2)}, u32[]{:S(2)}) collective-permute-start(f32[32,128]{1,0:T(8,128)S(1)} %dynamic-slice_bitcast_fusion), channel_id=1, source_target_pairs={{0,32},{32,0},{64,96},{96,64},{128,160},{160,128},{192,224},{224,1... | collective-permute-start | bytes 49160 | tf_op jit(solution)/shard_map/ppermute | solution.py:335
Sparse Core Ops, SparseCore 0:
  17.8 84.9 all-gather.3

commit v12 on v11

--- a/solution.py
+++ b/solution.py
@@ -172,7 +172,7 @@
 
 
 def attend_body(
-    place_ref, len_ref, normed_ref, other_ref, cos_ref, sin_ref, parts, gathered, out_ref, w_ref, q_ref, sem, q_sem
+    place_ref, len_ref, normed_ref, other, cos_ref, sin_ref, parts, gathered, out_ref, w_ref, q_ref, other_ref, sem, q_sem
 ):
     fetch = pltpu.make_async_copy(parts.at[:, pl.ds(0, 16), :], q_ref, q_sem.at[0])
     fetch.start()
@@ -188,7 +188,8 @@
         ]
         for kind in range(2)
     ]
-    for copy in copies[0] + copies[1]:
+    fill = pltpu.make_async_copy(other, other_ref, q_sem.at[1])
+    for copy in copies[0] + [fill] + copies[1]:
         copy.start()
     cosine, sine = cos_ref[...], sin_ref[...]
     fetch.wait()
@@ -207,6 +208,8 @@
     weight = w_ref[0].reshape(Y_LO * Z * HEAD, 256)
     sums = []
     for p, rows_ref in enumerate((normed_ref, other_ref)):
+        if p == 1:
+            fill.wait()
         rows = rows_ref[...]
         keys = jnp.dot(rows, weight, preferred_element_type=f32)
         scores = []
@@ -248,13 +251,14 @@
     return pl.pallas_call(
         attend_body,
         out_shape=jax.ShapeDtypeStruct((2 * Z, 16, HEAD), bf16),
-        in_specs=[SMEM, SMEM, VMEM, VMEM, VMEM, VMEM, HBM, HBM],
+        in_specs=[SMEM, SMEM, VMEM, HBM, VMEM, VMEM, HBM, HBM],
         out_specs=VMEM,
         scratch_shapes=[
             pltpu.VMEM((2, Y_LO, Z, HEAD, 256), bf16),
             pltpu.VMEM((2 * Z, 16, HEAD), bf16),
+            pltpu.VMEM(other.shape, bf16),
             pltpu.SemaphoreType.DMA((2, 2)),
-            pltpu.SemaphoreType.DMA((1,)),
+            pltpu.SemaphoreType.DMA((2,)),
         ],
         compiler_params=pltpu.CompilerParams(vmem_limit_bytes=48 << 20),
         name="attend",

time: 186 us -> 185 us (level)
  no operation moved by 1% of the time
where the time goes in v12:
time: 185 us; the launch traced here: 184 us
  starting transfers between devices  54 us (29%)
  waiting for transfers between devices  48.6 us (26%)
  blocking collectives  40.3 us (22%)
  between operations  14.3 us (8%)
  Pallas kernels  14.2 us (8%)
  other arithmetic  7.05 us (4%)
  local copies, waits for them, and re-layouts  5.21 us (3%)
    all_to_all x1, starting transfers between devices, local(): lax.all_to_all(outgoing, 'fsdp', 0, 0, tiled=True, axis_index_groups=Z_GR...  15.5 us
    all_to_all x1, blocking collectives, local(): lax.all_to_all(jnp.broadcast_to(partial[None, None, :], (slabs, 1, slabs)...  15.2 us
    all_to_all x1, blocking collectives, local(): lax.all_to_all(outgoing[:, None], 'dp', split_axis=0, concat_axis=1, tile...  14.9 us
    all_to_all x1, waiting for transfers between devices, local(): contexts = lax.all_to_all(context, 'fsdp', 0, 0, tiled=True)  14.4 us
    all_to_all x1, waiting for transfers between devices, local(): lax.all_to_all(payload, BOTH, 0, 0, tiled=True, axis_index_groups=CORE_Z_...  14.2 us
    all_to_all x1, waiting for transfers between devices, local(): lax.all_to_all(outgoing, 'fsdp', 0, 0, tiled=True, axis_index_groups=Z_GR...  11.5 us
    all_gather x1, blocking collectives, local(): lax.all_gather(parts[:, WEIGHT_ROW:], 'dp', axis=0, tiled=False, axis_ind...  10.2 us
    ppermute x1, starting transfers between devices, local(): residual = inputs + (kept + lax.ppermute(given, 'dp', CORE_SWAP))  8.8 us
  transfers between devices with their start and end apart: 11, of which 7 were waited for; matrix products, arithmetic and copies ran while one was open for 4% of the time, Pallas kernels for 2%

profile of v12, /device:TPU:1, one launch (start us, length us, event | category | flops | bytes accessed | tf_op | source)
XLA Modules:
  0.0 184.0 jit_solution(9390749181263894438)
XLA Ops:
  7.2 0.7 pad_add_fusion.place_ref
  7.8 1.6 unit.1.near_ref
  9.5 4.0 %collective-permute-start = (bf16[128,512]{1,0:T(8,128)(2,1)}, bf16[128,512]{1,0:T(8,128)(2,1)S(1)}, u32[]{:S(2)}, u32[]{:S(2)}) collective-permute-start(bf16[128,512]{1,0:T(8,128)(2,1)} %unit.1.near_ref), channel_id=1, source_target_pairs={{0,16},{1,17},{2,18},{3,19},{4,20},{5,21},{6,22},{7,23},{8,24},{9,... | collective-permute-start | bytes 393224 | tf_op jit(solution)/shard_map/ppermute | solution.py:278
  13.5 2.6 %collective-permute-done.far_ref = bf16[128,512]{1,0:T(8,128)(2,1)S(1)} collective-permute-done((bf16[128,512]{1,0:T(8,128)(2,1)}, bf16[128,512]{1,0:T(8,128)(2,1)S(1)}, u32[]{:S(2)}, u32[]{:S(2)}) %collective-permute-start) | collective-permute-done | bytes 131104 | tf_op jit(solution)/shard_map/ppermute | solution.py:278
  16.1 0.9 copy-done
  17.0 0.7 pair.1
  17.7 0.0 all-gather.4.cloned.1.call-update
  17.7 3.4 %collective-permute-start.1 = (bf16[128,2048]{1,0:T(8,128)(2,1)}, bf16[128,2048]{1,0:T(8,128)(2,1)S(1)}, u32[]{:S(2)}, u32[]{:S(2)}) collective-permute-start(bf16[128,2048]{1,0:T(8,128)(2,1)} %near_ref.1), channel_id=1, source_target_pairs={{0,16},{1,17},{2,18},{3,19},{4,20},{5,21},{6,22},{7,23},{8,24},{9,... | collective-permute-start | bytes 1572872 | tf_op jit(solution)/shard_map/ppermute | solution.py:285
  21.1 2.4 %open.1 = bf16[16,8,128]{2,1,0:T(8,128)(2,1)} custom-call(s32[4]{0:T(128)} %pad_add_fusion.place_ref, bf16[1,256,4096]{2,1,0:T(8,128)(2,1)} %hidden, f32[1,4096]{1,0:T(1,128)} %bitcast.46), custom_call_target="tpu_custom_call" | custom-call | tf_op jit(solution)/shard_map/open/pallas_call | solution.py:125
  23.4 15.5 %all-to-all-start = ((bf16[16,8,128]{2,1,0:T(8,128)(2,1)}), bf16[16,8,128]{2,1,0:T(8,128)(2,1)S(1)}, u32[]{:S(2)}, u32[]{:S(2)}) async-start(bf16[16,8,128]{2,1,0:T(8,128)(2,1)} %open.1), calls=%async_computation | async-start | bytes 65536 | tf_op jit(solution)/shard_map/all_to_all | solution.py:284
  38.9 11.5 %all-to-all-done.arrived_ref = bf16[16,8,128]{2,1,0:T(8,128)(2,1)S(1)} async-done(((bf16[16,8,128]{2,1,0:T(8,128)(2,1)}), bf16[16,8,128]{2,1,0:T(8,128)(2,1)S(1)}, u32[]{:S(2)}, u32[]{:S(2)}) %all-to-all-start) | async-done | bytes 32800 | tf_op jit(solution)/shard_map/all_to_all | solution.py:284
  50.5 1.0 copy-done.1
  51.5 1.0 copy-done.2
  52.6 0.7 copy-done.3
  53.2 1.7 query.1
  54.9 7.0 %all-to-all-start.1 = ((bf16[32,24,128]{2,1,0:T(8,128)(2,1)}), bf16[32,24,128]{2,1,0:T(8,128)(2,1)S(1)}, u32[]{:S(2)}, u32[]{:S(2)}) async-start(bf16[32,24,128]{2,1,0:T(8,128)(2,1)} %query.1), calls=%async_computation.1 | async-start | bytes 393216 | tf_op jit(solution)/shard_map/all_to_all | solution.py:288
  61.9 0.5 fusion.7
  62.5 0.1 pad_maximum_fusion
  62.7 2.2 %collective-permute-start.2 = (bf16[16,128]{1,0:T(8,128)(2,1)S(1)}, bf16[16,128]{1,0:T(8,128)(2,1)S(1)}, u32[]{:S(2)}, u32[]{:S(2)}) collective-permute-start(bf16[16,128]{1,0:T(8,128)(2,1)S(1)} %bitcast.49), channel_id=1, source_target_pairs={{0,16},{1,17},{2,18},{3,19},{4,20},{5,21},{6,22},{7,23},{8,24},{9,... | collective-permute-start | bytes 12296 | tf_op jit(solution)/shard_map/ppermute | solution.py:291
  64.8 2.4 %collective-permute-start.3 = (s32[1]{0:T(128)}, s32[1]{0:T(128)}, u32[]{:S(2)}, u32[]{:S(2)}) collective-permute-start(s32[1]{0:T(128)} %param.11), channel_id=1, source_target_pairs={{0,32},{32,0},{64,96},{96,64},{128,160},{160,128},{192,224},{224,1... | collective-permute-start | bytes 20 | tf_op jit(solution)/shard_map/ppermute | solution.py:292
  67.3 1.1 collective-permute-done.3
  68.4 0.6 pad_add_fusion.1.len_ref
  69.0 14.2 %all-to-all-done.1.parts = bf16[32,24,128]{2,1,0:T(8,128)(2,1)S(1)} async-done(((bf16[32,24,128]{2,1,0:T(8,128)(2,1)}), bf16[32,24,128]{2,1,0:T(8,128)(2,1)S(1)}, u32[]{:S(2)}, u32[]{:S(2)}) %all-to-all-start.1) | async-done | bytes 196640 | tf_op jit(solution)/shard_map/all_to_all | solution.py:288
  83.2 2.1 %fusion = f32[256]{0:T(256)S(1)} fusion(bf16[256,4096]{1,0:T(8,128)(2,1)} %bitcast.41), kind=kLoop, calls=%fused_computation.2 | loop fusion | flops 3145472 | bytes 2098176 | tf_op jit(solution)/shard_map/reduce_sum | solution.py:299
  85.3 2.2 %fusion.2.normed_ref = bf16[256,4096]{1,0:T(8,128)(2,1)S(1)} fusion(bf16[256,4096]{1,0:T(8,128)(2,1)} %bitcast.42, f32[4096]{0:T(1024)S(1)} %copy-done.5, f32[256]{0:T(256)S(1)} %add_rsqrt_fusion), kind=kLoop, calls=%fused_computation.4 | loop fusion | flops 4194304 | bytes 4211712 | tf_op jit(solution)/shard_map/convert_element_type | solution.py:300
  87.5 2.3 %collective-permute-start.5 = (bf16[256,4096]{1,0:T(8,128)(2,1)S(1)}, bf16[256,4096]{1,0:T(8,128)(2,1)}, u32[]{:S(2)}, u32[]{:S(2)}) collective-permute-start(bf16[256,4096]{1,0:T(8,128)(2,1)S(1)} %fusion.2.normed_ref), channel_id=1, source_target_pairs={{0,32},{32,0},{64,96},{96,64},{128,160},{160,128},{192,224},{224,1... | collective-permute-start | bytes 6291464 | tf_op jit(solution)/shard_map/ppermute | solution.py:301
  89.8 0.2 select_reduce_fusion
  90.0 0.1 fusion.10
  90.1 0.1 reduce_window_sum.11
  90.2 0.8 dynamic_slice.10
  90.9 0.2 select_reduce_fusion.1
  91.2 10.2 %all-gather.1 = bf16[128,8,128]{2,1,0:T(8,128)(2,1)S(1)} all-gather(bf16[32,8,128]{2,1,0:T(8,128)(2,1)S(1)} %slice.10), channel_id=3, replica_groups={{0,64,128,192},{32,96,160,224},{256,320,384,448},{288,352,416,480},{1,6..., dimensions={0}, use_global_device_ids=true | all-gather | bytes 327680 | tf_op jit(solution)/shard_map/all_gather | solution.py:303
  101.4 0.1 copy.27
  101.4 4.6 %collective-permute-start.4 = (bf16[1024,128]{1,0:T(8,128)(2,1)S(1)}, bf16[1024,128]{1,0:T(8,128)(2,1)S(1)}, u32[]{:S(2)}, u32[]{:S(2)}) collective-permute-start(bf16[1024,128]{1,0:T(8,128)(2,1)S(1)} %bitcast.45), channel_id=1, source_target_pairs={{16,32},{17,33},{18,34},{19,35},{20,36},{21,37},{22,38},{23,39},{2... | collective-permute-start | bytes 786440 | tf_op jit(solution)/shard_map/ppermute | solution.py:307
  106.0 4.0 %collective-permute-done.4 = bf16[1024,128]{1,0:T(8,128)(2,1)S(1)} collective-permute-done((bf16[1024,128]{1,0:T(8,128)(2,1)S(1)}, bf16[1024,128]{1,0:T(8,128)(2,1)S(1)}, u32[]{:S(2)}, u32[]{:S(2)}) %collective-permute-start.4) | collective-permute-done | bytes 262176 | tf_op jit(solution)/shard_map/ppermute | solution.py:307
  110.1 0.1 broadcast_select_fusion
  110.1 0.0 all-gather.4.cloned.1.call-done
  110.2 7.8 %attend.1 = bf16[32,16,128]{2,1,0:T(8,128)(2,1)} custom-call(s32[4]{0:T(128)S(1)} %copy-done.4, s32[2]{0:T(128)S(1)} %pad_add_fusion.1.len_ref, bf16[256,4096]{1,0:T(8,128)(2,1)S(1)} %fusion.2.normed_ref, bf16[256,4096]{1,0:T(8,128)(2,1)} %collective-permute-done.5.other, f32[256,128]{1,0:T(8,128)S(1)} %get-tuple-element.41.cos_ref, ...), custom_call_target="tpu_custom_call" | custom-call | tf_op jit(solution)/shard_map/attend/pallas_call | solution.py:251
  118.0 3.9 %all-to-all-start.2 = ((bf16[32,16,128]{2,1,0:T(8,128)(2,1)}), bf16[32,16,128]{2,1,0:T(8,128)(2,1)S(1)}, u32[]{:S(2)}, u32[]{:S(2)}) async-start(bf16[32,16,128]{2,1,0:T(8,128)(2,1)} %attend.1), calls=%async_computation.2 | async-start | bytes 262144 | tf_op jit(solution)/shard_map/all_to_all | solution.py:332
  121.8 14.4 %all-to-all-done.2 = bf16[32,16,128]{2,1,0:T(8,128)(2,1)S(1)} async-done(((bf16[32,16,128]{2,1,0:T(8,128)(2,1)}), bf16[32,16,128]{2,1,0:T(8,128)(2,1)S(1)}, u32[]{:S(2)}, u32[]{:S(2)}) %all-to-all-start.2) | async-done | bytes 131104 | tf_op jit(solution)/shard_map/all_to_all | solution.py:332
  136.3 0.2 fusion.4
  136.5 8.8 %collective-permute-start.6 = (f32[32,128]{1,0:T(8,128)S(1)}, f32[32,128]{1,0:T(8,128)S(1)}, u32[]{:S(2)}, u32[]{:S(2)}) collective-permute-start(f32[32,128]{1,0:T(8,128)S(1)} %dynamic-slice_bitcast_fusion), channel_id=1, source_target_pairs={{0,32},{32,0},{64,96},{96,64},{128,160},{160,128},{192,224},{224,1... | collective-permute-start | bytes 49160 | tf_op jit(solution)/shard_map/ppermute | solution.py:339
  145.3 0.8 collective-permute-done.6
  146.1 0.1 multiply_reduce_fusion
  146.2 15.2 %all_to_all.32 = f32[32,1,32]{2,1,0:T(1,128)S(1)} all-to-all(f32[32,1,32]{2,1,0:T(1,128)S(1)} %broadcast_in_dim.21), channel_id=1, replica_groups=mesh['dp'=16,'fsdp'=32] {'fsdp'}, dimensions={0} | all-to-all | bytes 8192 | tf_op jit(solution)/shard_map/all_to_all | solution.py:342
  161.4 0.2 fusion.3
  161.6 14.9 %all_to_all.33 = bf16[16,1,4,128]{3,2,1,0:T(4,128)(2,1)S(1)} all-to-all(bf16[16,1,4,128]{3,2,1,0:T(4,128)(2,1)S(1)} %copy.30), channel_id=1, replica_groups=mesh['dp'=16,'fsdp'=32] {'dp'}, dimensions={0} | all-to-all | bytes 32768 | tf_op jit(solution)/shard_map/all_to_all | solution.py:349
  176.6 0.6 copy.41
  (33 shorter events, 0.2 us)
Async XLA Ops:
  6.5 103.6 %all-gather.4.cloned.1.call-start = ((), (), s32[]{:S(2)}) async-start(), calls=%async_computation.5 | async-start | bytes 4456448 | tf_op jit(solution)/shard_map/all_gather | solution.py:279
  7.8 77.4 %copy-start.5 = (f32[4096]{0:T(1024)S(1)}, f32[4096]{0:T(1024)}, u32[]{:S(2)}) copy-start(f32[4096]{0:T(1024)} %param.14) | copy-start | bytes 49156
  9.5 6.6 %collective-permute-start = (bf16[128,512]{1,0:T(8,128)(2,1)}, bf16[128,512]{1,0:T(8,128)(2,1)S(1)}, u32[]{:S(2)}, u32[]{:S(2)}) collective-permute-start(bf16[128,512]{1,0:T(8,128)(2,1)} %unit.1.near_ref), channel_id=1, source_target_pairs={{0,16},{1,17},{2,18},{3,19},{4,20},{5,21},{6,22},{7,23},{8,24},{9,... | collective-permute-start | bytes 393224 | tf_op jit(solution)/shard_map/ppermute | solution.py:278
  16.1 0.9 copy-start
  17.7 32.8 %collective-permute-start.1 = (bf16[128,2048]{1,0:T(8,128)(2,1)}, bf16[128,2048]{1,0:T(8,128)(2,1)S(1)}, u32[]{:S(2)}, u32[]{:S(2)}) collective-permute-start(bf16[128,2048]{1,0:T(8,128)(2,1)} %near_ref.1), channel_id=1, source_target_pairs={{0,16},{1,17},{2,18},{3,19},{4,20},{5,21},{6,22},{7,23},{8,24},{9,... | collective-permute-start | bytes 1572872 | tf_op jit(solution)/shard_map/ppermute | solution.py:285
  23.4 27.0 %all-to-all-start = ((bf16[16,8,128]{2,1,0:T(8,128)(2,1)}), bf16[16,8,128]{2,1,0:T(8,128)(2,1)S(1)}, u32[]{:S(2)}, u32[]{:S(2)}) async-start(bf16[16,8,128]{2,1,0:T(8,128)(2,1)} %open.1), calls=%async_computation | async-start | bytes 65536 | tf_op jit(solution)/shard_map/all_to_all | solution.py:284
  50.5 1.0 copy-start.1
  51.5 1.0 copy-start.2
  52.6 0.7 copy-start.3
  54.9 34.9 %copy-start.6 = (s32[1024]{0:T(1024)S(1)}, s32[1024]{0:T(1024)}, u32[]{:S(2)}) copy-start(s32[1024]{0:T(1024)} %param.13) | copy-start | bytes 12292
  54.9 34.9 %copy-start.7 = (s32[32]{0:T(128)S(1)}, s32[32]{0:T(128)}, u32[]{:S(2)}) copy-start(s32[32]{0:T(128)} %param.12) | copy-start | bytes 388
  54.9 28.2 %all-to-all-start.1 = ((bf16[32,24,128]{2,1,0:T(8,128)(2,1)}), bf16[32,24,128]{2,1,0:T(8,128)(2,1)S(1)}, u32[]{:S(2)}, u32[]{:S(2)}) async-start(bf16[32,24,128]{2,1,0:T(8,128)(2,1)} %query.1), calls=%async_computation.1 | async-start | bytes 393216 | tf_op jit(solution)/shard_map/all_to_all | solution.py:288
  62.6 47.5 %copy-start.4 = (s32[4]{0:T(128)S(1)}, s32[4]{0:T(128)}, u32[]{:S(2)}) copy-start(s32[4]{0:T(128)} %pad_add_fusion.place_ref) | copy-start | bytes 52
  62.7 6.3 %collective-permute-start.2 = (bf16[16,128]{1,0:T(8,128)(2,1)S(1)}, bf16[16,128]{1,0:T(8,128)(2,1)S(1)}, u32[]{:S(2)}, u32[]{:S(2)}) collective-permute-start(bf16[16,128]{1,0:T(8,128)(2,1)S(1)} %bitcast.49), channel_id=1, source_target_pairs={{0,16},{1,17},{2,18},{3,19},{4,20},{5,21},{6,22},{7,23},{8,24},{9,... | collective-permute-start | bytes 12296 | tf_op jit(solution)/shard_map/ppermute | solution.py:291
  64.8 3.5 %collective-permute-start.3 = (s32[1]{0:T(128)}, s32[1]{0:T(128)}, u32[]{:S(2)}, u32[]{:S(2)}) collective-permute-start(s32[1]{0:T(128)} %param.11), channel_id=1, source_target_pairs={{0,32},{32,0},{64,96},{96,64},{128,160},{160,128},{192,224},{224,1... | collective-permute-start | bytes 20 | tf_op jit(solution)/shard_map/ppermute | solution.py:292
  87.5 22.6 %collective-permute-start.5 = (bf16[256,4096]{1,0:T(8,128)(2,1)S(1)}, bf16[256,4096]{1,0:T(8,128)(2,1)}, u32[]{:S(2)}, u32[]{:S(2)}) collective-permute-start(bf16[256,4096]{1,0:T(8,128)(2,1)S(1)} %fusion.2.normed_ref), channel_id=1, source_target_pairs={{0,32},{32,0},{64,96},{96,64},{128,160},{160,128},{192,224},{224,1... | collective-permute-start | bytes 6291464 | tf_op jit(solution)/shard_map/ppermute | solution.py:301
  101.4 8.6 %collective-permute-start.4 = (bf16[1024,128]{1,0:T(8,128)(2,1)S(1)}, bf16[1024,128]{1,0:T(8,128)(2,1)S(1)}, u32[]{:S(2)}, u32[]{:S(2)}) collective-permute-start(bf16[1024,128]{1,0:T(8,128)(2,1)S(1)} %bitcast.45), channel_id=1, source_target_pairs={{16,32},{17,33},{18,34},{19,35},{20,36},{21,37},{22,38},{23,39},{2... | collective-permute-start | bytes 786440 | tf_op jit(solution)/shard_map/ppermute | solution.py:307
  118.0 18.3 %all-to-all-start.2 = ((bf16[32,16,128]{2,1,0:T(8,128)(2,1)}), bf16[32,16,128]{2,1,0:T(8,128)(2,1)S(1)}, u32[]{:S(2)}, u32[]{:S(2)}) async-start(bf16[32,16,128]{2,1,0:T(8,128)(2,1)} %attend.1), calls=%async_computation.2 | async-start | bytes 262144 | tf_op jit(solution)/shard_map/all_to_all | solution.py:332
  136.5 9.6 %collective-permute-start.6 = (f32[32,128]{1,0:T(8,128)S(1)}, f32[32,128]{1,0:T(8,128)S(1)}, u32[]{:S(2)}, u32[]{:S(2)}) collective-permute-start(f32[32,128]{1,0:T(8,128)S(1)} %dynamic-slice_bitcast_fusion), channel_id=1, source_target_pairs={{0,32},{32,0},{64,96},{96,64},{128,160},{160,128},{192,224},{224,1... | collective-permute-start | bytes 49160 | tf_op jit(solution)/shard_map/ppermute | solution.py:339
Sparse Core Ops, SparseCore 0:
  17.8 84.9 all-gather.3
